TPU v7x, 128 devices: a whole 4x4x4 slice. The times are simulated.
128 devices in a mesh: bx: 8 (over y_hi, z), by: 16 (over x, y_lo, core).
Axes of the slice: x: 4, y: 4 (y_hi: 2, y_lo: 2; y = y_hi * 2 + y_lo), z: 4, core: 2. Of those that a mesh axis runs over, the one named last changes fastest.
Arguments:
- state: float32 [384, 64, 2048], P(None, 'bx', 'by'), may hold values from -6 to 6
- target: bfloat16 [384, 64, 2048], P(None, 'bx', 'by'), may hold values from -6 to 6
- land_mask: int32 [64, 2048], P('bx', 'by'), may hold values 0 or 1
- batch_map: int32 [64, 2048], P('bx', 'by'), may hold values from 0 to 63
- diffusion: float32 [384], replicated, may hold values from 0.05 to 0.2
- speed_x: float32 [384], replicated, may hold values from -0.3 to 0.3
- speed_y: float32 [384], replicated, may hold values from -0.3 to 0.3
- w_in: bfloat16 [384, 4096], replicated, may hold values from -0.3125 to 0.3125
- w_out: bfloat16 [4096, 384], replicated, may hold values from -0.09375 to 0.09375
Outputs:
- new_state: float32 [384, 64, 2048], P(None, 'bx', 'by')
- grad_in: float32 [4096, 384], P(('bx', 'by'))
- grad_out: float32 [4096, 384], P(('bx', 'by'))
- batch_loss: float32 [64], replicated
All inputs are finite; a program needn't handle non-finite values. No bound on the sum of `land_mask` on one device may be relied on, other than what follows from the above.
Results may differ from a plain program's by a relative error of at most 0.0017.
Values sent between devices are 32-bit elements; how exact they have to be, the bound alone decides.
No kernel may reach another device: no remote copies, remote signals or barrier semaphores. Data moves between devices by JAX's collectives and lax.ppermute only.
A program may use at most 128 MiB of HBM per device.

v0:
```python
import jax
import jax.numpy as jnp
from jax import lax
from jax.sharding import Mesh
from jax.sharding import PartitionSpec as P

SUB = 3
BATCHES = 64
BX_BY = ("bx_0", "bx_1", "by_0", "by_1", "by_2")
BX = ("bx_0", "bx_1")
BY = ("by_0", "by_1", "by_2")


def extended(cells, sides, width):
    for axis, dim in sides:
        count = lax.axis_size(axis)
        ends = count - 1
        head = lax.slice_in_dim(cells, 0, width, axis=dim)
        tail = lax.slice_in_dim(cells, cells.shape[dim] - width, cells.shape[dim], axis=dim)
        cells = jnp.concatenate(
            [
                lax.ppermute(tail, axis, [(i, (i + 1) % count) for i in range(ends)]),
                cells,
                lax.ppermute(head, axis, [((i + 1) % count, i) for i in range(ends)]),
            ],
            axis=dim,
        )
    return cells


def over_axes(value, axes):
    for axis in axes:
        value = lax.psum(value, axis)
    return value


def in_blocks(value, dim, count):
    before, after = (value.shape[:dim], value.shape[dim + 1 :])
    return jnp.moveaxis(value.reshape(*before, count, -1, *after), dim, 0)


def summed_rows(value, chips, core, dim):
    sizes = (lax.axis_size(chips), lax.axis_size(core))
    pieces = in_blocks(value, dim, sizes[0] * sizes[1])
    inside = pieces.shape[1:]
    pieces = pieces.reshape(*sizes, *inside).swapaxes(0, 1).reshape(-1, *inside)
    pieces = lax.psum_scatter(pieces, core, scatter_dimension=0, tiled=True)
    return lax.psum_scatter(pieces, chips, scatter_dimension=0, tiled=True)[0]


def advance(padded, kap, sxx, syy):
    centre = padded[:, 1:-1, 1:-1]
    east = padded[:, 2:, 1:-1]
    west = padded[:, :-2, 1:-1]
    north = padded[:, 1:-1, 2:]
    south = padded[:, 1:-1, :-2]
    return (
        centre
        + kap * (east + west + north + south - 4.0 * centre)
        - 0.5 * sxx * (east - west)
        - 0.5 * syy * (north - south)
    )


def on_device(state, target, land_mask, batch_map, diffusion, speed_x, speed_y, w_in, w_out):
    feats, rows_x, rows_y = state.shape
    kap = diffusion[:, None, None]
    sxx = speed_x[:, None, None]
    syy = speed_y[:, None, None]
    field = extended(state, ((BX, 1), (BY, 2)), SUB)
    for substep in range(SUB):
        field = advance(field, kap, sxx, syy)
        margin = SUB - substep - 1
        if margin > 0:
            along_x = (
                lax.axis_index(BX) * rows_x
                + jnp.arange(rows_x + 2 * margin, dtype=jnp.int32)
                - margin
            )
            along_y = (
                lax.axis_index(BY) * rows_y
                + jnp.arange(rows_y + 2 * margin, dtype=jnp.int32)
                - margin
            )
            inside_x = ((along_x >= 0) & (along_x < rows_x * lax.axis_size(BX))).astype(jnp.float32)
            inside_y = ((along_y >= 0) & (along_y < rows_y * lax.axis_size(BY))).astype(jnp.float32)
            field = field * inside_x[None, :, None] * inside_y[None, None, :]
    local_cols = rows_x * rows_y
    total = local_cols * lax.axis_size(BX) * lax.axis_size(BY)
    inputs = field.reshape(feats, local_cols).T.astype(jnp.bfloat16)
    pre = jnp.dot(inputs, w_in, preferred_element_type=jnp.float32)
    hidden = jax.nn.silu(pre).astype(jnp.bfloat16)
    tend = jnp.dot(hidden, w_out, preferred_element_type=jnp.float32)
    weights = land_mask.reshape(local_cols).astype(jnp.float32)[:, None]
    err = weights * (tend - target.reshape(feats, local_cols).T.astype(jnp.float32))
    new_state = field + 0.5 * (weights * tend).T.reshape(feats, rows_x, rows_y)
    persq = 0.5 * jnp.sum(err * err, axis=1)
    onehot = (
        batch_map.reshape(local_cols)[:, None] == jnp.arange(BATCHES, dtype=jnp.int32)[None, :]
    ).astype(jnp.float32)
    partial_loss = jnp.dot(persq, onehot, precision=lax.Precision.HIGHEST) * (
        BATCHES / (total * feats)
    )
    batch_loss = over_axes(partial_loss, BX_BY)
    dtend = (err * total ** (-0.5)).astype(jnp.bfloat16)
    dhid = jnp.dot(dtend, w_out.T, preferred_element_type=jnp.float32)
    sig = jax.nn.sigmoid(pre)
    dpre = (dhid * sig * (1.0 + pre * (1.0 - sig))).astype(jnp.bfloat16)
    joined = summed_rows(
        jnp.concatenate(
            [
                jnp.dot(hidden.T, dtend, preferred_element_type=jnp.float32),
                jnp.dot(dpre.T, inputs, preferred_element_type=jnp.float32),
            ],
            axis=1,
        ),
        ("bx_0", "bx_1", "by_0", "by_1"),
        "by_2",
        0,
    )
    grad_out = joined[:, :feats]
    grad_in = joined[:, feats:]
    return (new_state, grad_in, grad_out, batch_loss)


def solution(mesh):
    torus = Mesh(mesh.devices.reshape(2, 4, 4, 2, 2), ("bx_0", "bx_1", "by_0", "by_1", "by_2"))
    return jax.shard_map(
        on_device,
        mesh=torus,
        in_specs=(P(None, BX, BY), P(None, BX, BY), P(BX, BY), P(BX, BY), P(), P(), P(), P(), P()),
        out_specs=(P(None, BX, BY), P(BX_BY, None), P(BX_BY, None), P()),
        check_vma=False,
    )
```

profile of v0, /device:TPU:0, one launch (start us, length us, event | category | flops | bytes accessed | tf_op | source)
XLA Modules:
  0.0 532.6 jit_solution(17666337754188688891)
XLA Ops:
  7.2 0.0 copy-start
  7.2 0.0 reduce-scatter.3.cloned.1.call-start
  7.2 2.3 fusion.9
  9.5 0.9 copy.35
  10.4 4.7 collective-permute-start
  15.1 0.9 copy.36
  16.0 1.3 collective-permute-start.1
  17.3 0.0 copy-start.4
  17.3 0.0 copy-start.5
  17.3 0.0 copy-start.6
  17.3 3.1 copy.26
  20.4 2.9 copy.31
  23.3 0.0 copy-done.4
  23.3 0.0 copy-done.5
  23.3 0.0 copy-done.6
  23.3 3.9 collective-permute-done
  27.2 2.2 copy.25
  29.4 3.6 collective-permute-done.1
  33.0 2.2 copy.27
  35.2 2.4 pad_maximum_fusion.1
  37.6 1.3 collective-permute-start.2
  38.9 1.5 collective-permute-start.3
  40.4 0.9 copy.29
  41.3 0.0 collective-permute-done.2
  41.3 2.5 collective-permute-done.3
  43.9 0.0 copy-start.3
  43.9 0.2 pad_maximum_fusion.2
  44.2 0.4 copy-done.3
  44.6 1.9 multiply_multiply_fusion
  46.5 1.3 multiply_multiply_fusion.1
  47.8 2.1 fusion.7
  49.9 0.0 copy-done
  49.9 0.0 copy-start.2
  49.9 0.0 copy-start.7
  49.9 9.1 %multiply_convert_fusion.1 = (bf16[1024,4096]{1,0:T(8,128)(2,1)S(1)}, f32[1024,4096]{1,0:T(8,128)}) fusion(bf16[384,1024]{0,1:T(8,128)(2,1)S(1)} %bitcast.36, bf16[384,4096]{1,0:T(8,128)(2,1)S(1)} %copy-done), kind=kOutput, calls=%fused_computation.1 | convolution fusion | flops 3242196992 | bytes 29097984 | tf_op jit(solution)/shard_map/dot_general | solution.py:91
  59.0 0.0 copy-done.2
  59.0 0.0 copy-done.7
  59.0 5.7 %multiply_reduce_fusion = (f32[1024]{0:T(1024)S(1)}, f32[1024,384]{1,0:T(8,128)S(1)}, f32[1024,384]{1,0:T(8,128)}) fusion(f32[384,8,128]{0,2,1:T(8,128)S(1)} %copy-done.2, f32[1024]{0:T(1024)S(1)} %convert_bitcast_fusion, bf16[1024,4096]{1,0:T(8,128)(2,1)S(1)} %get-tuple-element.19, bf16[4096,384]{1,0:T(8,128)(2,1)S(1)} %copy-done.7), kind=kOutput, calls=%fused_computation.10 | convolution fusion | flops 3223583744 | bytes 16261120 | tf_op jit(solution)/shard_map/dot_general | solution.py:93
  64.7 5.4 %fusion.2 = f32[4096,384]{0,1:T(8,128)} fusion(bf16[1024,4096]{1,0:T(8,128)(2,1)S(1)} %get-tuple-element.19, f32[1024,384]{1,0:T(8,128)S(1)} %get-tuple-element.9), kind=kOutput, calls=%fused_computation.17 | convolution fusion | flops 3222011904 | bytes 16252928 | tf_op jit(solution)/shard_map/dot_general | solution.py:112
  70.1 13.0 %multiply_convert_fusion = bf16[1024,4096]{1,0:T(8,128)(2,1)} fusion(f32[1024,4096]{1,0:T(8,128)} %get-tuple-element.20, bf16[4096,384]{1,0:T(8,128)(2,1)S(1)} %copy-done.7, f32[1024,384]{1,0:T(8,128)S(1)} %get-tuple-element.9), kind=kOutput, calls=%fused_computation | convolution fusion | flops 3259760640 | bytes 29884416 | tf_op jit(solution)/shard_map/dot_general | solution.py:106
  83.1 9.5 %fusion.11 = f32[4096,384]{0,1:T(8,128)} fusion(bf16[1024,4096]{1,0:T(8,128)(2,1)} %multiply_convert_fusion, bf16[384,1024]{0,1:T(8,128)(2,1)S(1)} %bitcast.37), kind=kOutput, calls=%fused_computation.33 | convolution fusion | flops 3221225472 | bytes 15466496 | tf_op jit(solution)/shard_map/dot_general | solution.py:113
  92.7 10.8 %pad_maximum_fusion = f32[4096,768]{0,1:T(8,128)} fusion(f32[4096,384]{0,1:T(8,128)} %fusion.11, f32[4096,384]{0,1:T(8,128)} %fusion.2), kind=kLoop, calls=%fused_computation.3 | loop fusion | flops 3145728 | bytes 25165824 | tf_op jit(solution)/shard_map/concatenate | solution.py:110
  103.4 12.6 %copy.32 = f32[4096,768]{1,0:T(8,128)} copy(f32[4096,768]{0,1:T(8,128)} %pad_maximum_fusion) | data formatting | bytes 25165824 | tf_op jit(solution)/shard_map/concatenate | solution.py:110
  116.0 10.7 %copy.33 = f32[2,64,32,768]{3,2,1,0:T(8,128)} copy(f32[2,64,32,768]{3,2,0,1:T(8,128)} %bitcast.34) | data formatting | bytes 25165824 | tf_op jit(solution)/shard_map/transpose | solution.py:46
  126.7 0.0 reduce-scatter.3.cloned.1.call-update
  126.8 0.0 reduce-scatter.5.cloned.1.call-start
  126.8 30.7 %reduce-scatter.3.cloned.1.call-done = f32[64,32,768]{2,1,0:T(8,128)} async-done(((f32[128,32,768]{2,1,0:T(8,128)}), f32[64,32,768]{2,1,0:T(8,128)}) %reduce-scatter.3.cloned.1.call-update) | async-done | bytes 6291472 | tf_op jit(solution)/shard_map/reduce_scatter | solution.py:47
  157.6 0.0 reduce-scatter.5.cloned.1.call-update
  157.6 0.0 copy-start.1
  157.6 3.4 add.157
  161.0 0.0 copy-start.8
  161.0 3.0 copy.34
  164.1 0.0 copy-done.8
  164.1 0.4 fusion.1
  164.5 6.4 %psum.35 = f32[64]{0:T(128)S(1)} all-reduce(f32[64]{0:T(128)S(1)} %fusion.1), channel_id=1, replica_groups=mesh['bx_0'=2,'bx_1'=4,'by_0'=4,'by_1'=2,'by_2'=2] {'bx_0'}, use_global_device_ids=true, to_apply=%region_3.4 | all-reduce | flops 64 | bytes 512 | tf_op jit(solution)/shard_map/psum | solution.py:33
  170.9 11.2 %psum.36 = f32[64]{0:T(128)S(1)} all-reduce(f32[64]{0:T(128)S(1)} %psum.35), channel_id=1, replica_groups=mesh['bx_0'=2,'bx_1'=4,'by_0'=4,'by_1'=2,'by_2'=2] {'bx_1'}, use_global_device_ids=true, to_apply=%region_4.5 | all-reduce | flops 64 | bytes 512 | tf_op jit(solution)/shard_map/psum | solution.py:33
  182.1 10.0 %psum.37 = f32[64]{0:T(128)S(1)} all-reduce(f32[64]{0:T(128)S(1)} %psum.36), channel_id=1, replica_groups=mesh['bx_0'=2,'bx_1'=4,'by_0'=4,'by_1'=2,'by_2'=2] {'by_0'}, use_global_device_ids=true, to_apply=%region_5.6 | all-reduce | flops 64 | bytes 512 | tf_op jit(solution)/shard_map/psum | solution.py:33
  192.1 4.9 psum.38
  197.0 2.9 psum.39
  200.0 324.3 %reduce-scatter.5.cloned.1.call-done = f32[1,32,768]{2,1,0:T(8,128)} async-done(((f32[64,32,768]{2,1,0:T(8,128)}), f32[1,32,768]{2,1,0:T(8,128)}) %reduce-scatter.5.cloned.1.call-update) | async-done | bytes 98320 | tf_op jit(solution)/shard_map/reduce_scatter | solution.py:48
  524.3 1.5 fusion.10
  525.7 0.0 copy-done.1
  (10 shorter events, 0.1 us)
Async XLA Ops:
  7.2 42.7 %copy-start = (bf16[384,4096]{1,0:T(8,128)(2,1)S(1)}, bf16[384,4096]{1,0:T(8,128)(2,1)}, u32[]{:S(2)}) copy-start(bf16[384,4096]{1,0:T(8,128)(2,1)} %param.16) | copy-start | bytes 9437188
  7.2 150.4 %reduce-scatter.3.cloned.1.call-start = ((), (), s32[]{:S(2)}) async-start(), calls=%async_computation.2 | async-start | bytes 18874368 | tf_op jit(solution)/shard_map/reduce_scatter | solution.py:47
  10.4 16.8 %collective-permute-start = (f32[384,3,128]{2,0,1:T(8,128)}, f32[384,3,128]{2,0,1:T(8,128)}, u32[]{:S(2)}, u32[]{:S(2)}) collective-permute-start(f32[384,3,128]{2,0,1:T(8,128)} %copy.35), channel_id=1, source_target_pairs={{0,16},{16,32},{32,48},{48,64},{64,80},{80,96},{96,112},{1,17},{17... | collective-permute-start | bytes 1769480 | tf_op jit(solution)/shard_map/ppermute | solution.py:22
  16.0 17.0 %collective-permute-start.1 = (f32[384,3,128]{2,0,1:T(8,128)}, f32[384,3,128]{2,0,1:T(8,128)}, u32[]{:S(2)}, u32[]{:S(2)}) collective-permute-start(f32[384,3,128]{2,0,1:T(8,128)} %copy.36), channel_id=1, source_target_pairs={{16,0},{32,16},{48,32},{64,48},{80,64},{96,80},{112,96},{17,1},{33... | collective-permute-start | bytes 1769480 | tf_op jit(solution)/shard_map/ppermute | solution.py:24
  17.3 6.0 %copy-start.4 = (s32[8,128]{1,0:T(8,128)S(1)}, s32[8,128]{1,0:T(8,128)}, u32[]{:S(2)}) copy-start(s32[8,128]{1,0:T(8,128)} %param.11) | copy-start | bytes 12292
  17.3 6.0 %copy-start.5 = (f32[384]{0:T(512)S(1)}, f32[384]{0:T(512)}, u32[]{:S(2)}) copy-start(f32[384]{0:T(512)} %param.15) | copy-start | bytes 4612
  17.3 6.0 %copy-start.6 = (f32[384]{0:T(512)S(1)}, f32[384]{0:T(512)}, u32[]{:S(2)}) copy-start(f32[384]{0:T(512)} %param.14) | copy-start | bytes 4612
  37.6 3.7 collective-permute-start.2
  38.9 5.0 collective-permute-start.3
  43.9 0.7 copy-start.3
  49.9 9.1 %copy-start.2 = (f32[384,8,128]{0,2,1:T(8,128)S(1)}, f32[384,8,128]{0,2,1:T(8,128)}, u32[]{:S(2)}) copy-start(f32[384,8,128]{0,2,1:T(8,128)} %copy.31) | copy-start | bytes 4718596
  49.9 9.1 %copy-start.7 = (bf16[4096,384]{1,0:T(8,128)(2,1)S(1)}, bf16[4096,384]{1,0:T(8,128)(2,1)}, u32[]{:S(2)}) copy-start(bf16[4096,384]{1,0:T(8,128)(2,1)} %param.17) | copy-start | bytes 9437188
  126.8 397.5 %reduce-scatter.5.cloned.1.call-start = ((), (), s32[]{:S(2)}) async-start(), calls=%async_computation.3 | async-start | bytes 6389760 | tf_op jit(solution)/shard_map/reduce_scatter | solution.py:48
  157.6 368.1 %copy-start.1 = (bf16[384,4096]{1,0:T(8,128)(2,1)S(1)}, bf16[384,4096]{1,0:T(8,128)(2,1)}, u32[]{:S(2)}) copy-start(bf16[384,4096]{1,0:T(8,128)(2,1)} %param.16) | copy-start | bytes 9437188
  161.0 3.0 copy-start.8
Sparse Core Ops, SparseCore 0:
  126.9 30.6 reduce-scatter.2
  160.0 364.2 reduce-scatter.4
where the time goes:
time: 533 us
  waiting for transfers between devices  365 us (68%)
  local copies, waits for them, and re-layouts  43.6 us (8%)
  matrix products  43.1 us (8%)
  blocking collectives  35.5 us (7%)
  other arithmetic  22.2 us (4%)
  between operations  14.3 us (3%)
  starting transfers between devices  8.85 us (2%)
    reduce_scatter x1, waiting for transfers between devices, summed_rows(): return lax.psum_scatter(pieces, chips, scatter_dimension=0, tiled=True)[0]  324 us
    psum x5, blocking collectives, over_axes(): value = lax.psum(value, axis)  35.5 us
    reduce_scatter x1, waiting for transfers between devices, summed_rows(): pieces = lax.psum_scatter(pieces, core, scatter_dimension=0, tiled=True)  30.7 us
    dot_general x1, matrix products, on_device(): dhid = jnp.dot(dtend, w_out.T, preferred_element_type=jnp.float32)  13 us
    concatenate x1, local copies, waits for them, and re-layouts, on_device(): jnp.concatenate([jnp.dot(hidden.T, dtend, preferred_element_type=jnp.floa...  12.6 us
    concatenate x1, other arithmetic, on_device(): jnp.concatenate([jnp.dot(hidden.T, dtend, preferred_element_type=jnp.floa...  10.8 us
    transpose x1, local copies, waits for them, and re-layouts, summed_rows(): pieces = pieces.reshape(*sizes, *inside).swapaxes(0, 1).reshape(-1, *inside)  10.7 us
  transfers between devices with their start and end apart: 6, of which 5 were waited for; matrix products, arithmetic and copies ran while one was open for 3% of the time, Pallas kernels for 0%

commit v1 on v0

--- a/solution.py
+++ b/solution.py
@@ -6,9 +6,17 @@
 
 SUB = 3
 BATCHES = 64
-BX_BY = ("bx_0", "bx_1", "by_0", "by_1", "by_2")
 BX = ("bx_0", "bx_1")
 BY = ("by_0", "by_1", "by_2")
+CORE = "by_2"
+AXES = {"x": ("by_0", CORE), "y": ("bx_0", "by_1", CORE), "z": ("bx_1", CORE)}
+ORDERS = ("xyz", "yzx", "zxy")
+DIGITS = ((0, 3, 1, 2), (0, 1, 2, 3))
+RING = {
+    1: [(2 * p + c, 2 * (p ^ 1 if c == 0 else 3 - p) + c) for p in range(4) for c in range(2)],
+    2: [(2 * p + c, 2 * (3 - p if c == 0 else p ^ 1) + c) for p in range(4) for c in range(2)],
+}
+PAIR = [(0, 1), (1, 0)]
 
 
 def extended(cells, sides, width):
@@ -28,26 +36,6 @@
     return cells
 
 
-def over_axes(value, axes):
-    for axis in axes:
-        value = lax.psum(value, axis)
-    return value
-
-
-def in_blocks(value, dim, count):
-    before, after = (value.shape[:dim], value.shape[dim + 1 :])
-    return jnp.moveaxis(value.reshape(*before, count, -1, *after), dim, 0)
-
-
-def summed_rows(value, chips, core, dim):
-    sizes = (lax.axis_size(chips), lax.axis_size(core))
-    pieces = in_blocks(value, dim, sizes[0] * sizes[1])
-    inside = pieces.shape[1:]
-    pieces = pieces.reshape(*sizes, *inside).swapaxes(0, 1).reshape(-1, *inside)
-    pieces = lax.psum_scatter(pieces, core, scatter_dimension=0, tiled=True)
-    return lax.psum_scatter(pieces, chips, scatter_dimension=0, tiled=True)[0]
-
-
 def advance(padded, kap, sxx, syy):
     centre = padded[:, 1:-1, 1:-1]
     east = padded[:, 2:, 1:-1]
@@ -60,6 +48,67 @@
         - 0.5 * sxx * (east - west)
         - 0.5 * syy * (north - south)
     )
+
+
+def position(axis):
+    if axis == "y":
+        return lax.axis_index("bx_0") * 2 + lax.axis_index("by_1")
+    return lax.axis_index("by_0" if axis == "x" else "bx_1")
+
+
+def ring_places():
+    core = lax.axis_index(CORE)
+    places = {}
+    for axis in "xyz":
+        at = position(axis)
+        folded = jnp.where(at == 0, 0, jnp.where(at == 3, 1, at + 1))
+        places[axis] = jnp.where(core == 0, folded, at)
+    return places
+
+
+def half_of(rows, bit):
+    size = rows.shape[0] // 2
+    return lax.dynamic_slice_in_dim(rows, bit * size, size, 0)
+
+
+def scatter_sums(kept, sent, places):
+    received = lax.ppermute(sent, CORE, PAIR)
+    done = []
+    rows = kept.shape[0] // len(ORDERS)
+    for stream, order in enumerate(ORDERS):
+        mine = kept[stream * rows : (stream + 1) * rows] + received[stream * rows : (stream + 1) * rows]
+        for axis in order:
+            for turn in (1, 2):
+                bit = places[axis] // 2 if turn == 1 else places[axis] % 2
+                coming = lax.ppermute(half_of(mine, 1 - bit), AXES[axis], RING[turn])
+                mine = half_of(mine, bit) + coming
+        done.append(mine)
+    return jnp.concatenate(done, axis=1)
+
+
+def over_all(value):
+    value = value + lax.ppermute(value, CORE, PAIR)
+    for axis in "xyz":
+        for turn in (1, 2):
+            value = value + lax.ppermute(value, AXES[axis], RING[turn])
+    return value
+
+
+def in_ring_order(grad):
+    split = grad.reshape(2, 4, 4, 2, 2, 32, 3, 128)
+    cores = []
+    for core in range(2):
+        streams = []
+        for stream, order in enumerate(ORDERS):
+            part = split[:, :, :, :, core, :, stream].transpose(2, 0, 3, 1, 4, 5).reshape(4, 4, 4, 32, 128)
+            part = part.transpose(*["xyz".index(axis) for axis in order], 3, 4)
+            for dim in range(3):
+                part = jnp.concatenate([lax.slice_in_dim(part, d, d + 1, axis=dim) for d in DIGITS[core]], axis=dim)
+            streams.append(part.reshape(2048, 128))
+        cores.append(jnp.concatenate(streams, axis=0))
+    core = lax.axis_index(CORE)
+    both = jnp.stack(cores)
+    return lax.dynamic_index_in_dim(both, core, 0, False), lax.dynamic_index_in_dim(both, 1 - core, 0, False)
 
 
 def on_device(state, target, land_mask, batch_map, diffusion, speed_x, speed_y, w_in, w_out):
@@ -101,34 +150,27 @@
     partial_loss = jnp.dot(persq, onehot, precision=lax.Precision.HIGHEST) * (
         BATCHES / (total * feats)
     )
-    batch_loss = over_axes(partial_loss, BX_BY)
+    batch_loss = over_all(partial_loss)
     dtend = (err * total ** (-0.5)).astype(jnp.bfloat16)
+    places = ring_places()
+    grad_out = scatter_sums(
+        *in_ring_order(jnp.dot(hidden.T, dtend, preferred_element_type=jnp.float32)), places
+    )
     dhid = jnp.dot(dtend, w_out.T, preferred_element_type=jnp.float32)
     sig = jax.nn.sigmoid(pre)
     dpre = (dhid * sig * (1.0 + pre * (1.0 - sig))).astype(jnp.bfloat16)
-    joined = summed_rows(
-        jnp.concatenate(
-            [
-                jnp.dot(hidden.T, dtend, preferred_element_type=jnp.float32),
-                jnp.dot(dpre.T, inputs, preferred_element_type=jnp.float32),
-            ],
-            axis=1,
-        ),
-        ("bx_0", "bx_1", "by_0", "by_1"),
-        "by_2",
-        0,
+    grad_in = scatter_sums(
+        *in_ring_order(jnp.dot(dpre.T, inputs, preferred_element_type=jnp.float32)), places
     )
-    grad_out = joined[:, :feats]
-    grad_in = joined[:, feats:]
     return (new_state, grad_in, grad_out, batch_loss)
 
 
 def solution(mesh):
-    torus = Mesh(mesh.devices.reshape(2, 4, 4, 2, 2), ("bx_0", "bx_1", "by_0", "by_1", "by_2"))
+    torus = Mesh(mesh.devices.reshape(2, 4, 4, 2, 2), BX + BY)
     return jax.shard_map(
         on_device,
         mesh=torus,
         in_specs=(P(None, BX, BY), P(None, BX, BY), P(BX, BY), P(BX, BY), P(), P(), P(), P(), P()),
-        out_specs=(P(None, BX, BY), P(BX_BY, None), P(BX_BY, None), P()),
+        out_specs=(P(None, BX, BY), P(BX + BY, None), P(BX + BY, None), P()),
         check_vma=False,
     )

time: 533 us -> 272 us (0.51)
  waiting for transfers between devices: 365 us -> 48.2 us
  starting transfers between devices: 8.85 us -> 66.7 us
  blocking collectives: 35.5 us -> 0 us
  local copies, waits for them, and re-layouts: 43.6 us -> 78 us
  between operations: 14.3 us -> 2.56 us
  other arithmetic: 22.2 us -> 27.6 us
    reduce_scatter x2 -> x0, waiting for transfers between devices: 355 us -> none  [the longest x1 324 us: summed_rows(): return lax.psum_scatter(pieces, chips, scatter_dimension=0, tiled=True)[0]]
    ppermute x0 -> x45, starting transfers between devices: none -> 58.1 us  [the longest x36 37.2 us: scatter_sums(): coming = lax.ppermute(half_of(mine, 1 - bit), AXES[axis], RING[turn])]
    ppermute x0 -> x45, waiting for transfers between devices: none -> 38 us  [the longest x36 23.3 us: scatter_sums(): coming = lax.ppermute(half_of(mine, 1 - bit), AXES[axis], RING[turn])]
    psum x5 -> x0, blocking collectives: 35.5 us -> none  [over_axes(): value = lax.psum(value, axis)]
    slice x1 -> x48, local copies, waits for them, and re-layouts: 1.46 us -> 32 us  [the longest x2 25.2 us: in_ring_order(): split[:, :, :, :, core, :, stream].transpose(2, 0, 3, 1, 4, 5)]
    reshape x0 -> x2, local copies, waits for them, and re-layouts: none -> 20.6 us  [in_ring_order(): split = grad.reshape(2, 4, 4, 2, 2, 32, 3, 128)]
    concatenate x1 -> x4, local copies, waits for them, and re-layouts: 12.6 us -> 0.35 us  [in_ring_order(): jnp.concatenate([lax.slice_in_dim(part, d, d + 1, axis=dim) for d in DIGI...]
    transpose x1 -> x12, local copies, waits for them, and re-layouts: 10.7 us -> 0.98 us  [the longest x8 0.63 us: in_ring_order(): split[:, :, :, :, core, :, stream].transpose(2, 0, 3, 1, 4, 5)]
  transfers between devices with their start and end apart: 6 -> 49, of which waited for: 5 -> 22; matrix products, arithmetic and copies ran while one was open for 3% -> 11% of each run, Pallas kernels for 0% -> 0%
where the time goes in v1:
time: 272 us; the launch traced here: 268 us
  local copies, waits for them, and re-layouts  78 us (29%)
  starting transfers between devices  66.7 us (25%)
  waiting for transfers between devices  48.2 us (18%)
  matrix products  44.5 us (16%)
  other arithmetic  27.6 us (10%)
    ppermute x36, starting transfers between devices, scatter_sums(): coming = lax.ppermute(half_of(mine, 1 - bit), AXES[axis], RING[turn])  37.2 us
    slice x2, local copies, waits for them, and re-layouts, in_ring_order(): split[:, :, :, :, core, :, stream].transpose(2, 0, 3, 1, 4, 5)  25.2 us
    ppermute x36, waiting for transfers between devices, scatter_sums(): coming = lax.ppermute(half_of(mine, 1 - bit), AXES[axis], RING[turn])  23.3 us
    reshape x2, local copies, waits for them, and re-layouts, in_ring_order(): split = grad.reshape(2, 4, 4, 2, 2, 32, 3, 128)  20.6 us
    ppermute x6, starting transfers between devices, over_all(): value = value + lax.ppermute(value, AXES[axis], RING[turn])  17.3 us
    dot_general x1, matrix products, on_device(): dhid = jnp.dot(dtend, w_out.T, preferred_element_type=jnp.float32)  13.2 us
    unnamed x58, local copies, waits for them, and re-layouts  12.8 us
    ppermute x6, waiting for transfers between devices, over_all(): value = value + lax.ppermute(value, AXES[axis], RING[turn])  10.1 us
  transfers between devices with their start and end apart: 49, of which 22 were waited for; matrix products, arithmetic and copies ran while one was open for 11% of the time, Pallas kernels for 0%

profile of v1, /device:TPU:0, one launch (start us, length us, event | category | flops | bytes accessed | tf_op | source)
XLA Modules:
  0.0 267.6 jit_solution(2955008938453823542)
XLA Ops:
  0.6 2.3 fusion.38
  3.8 4.7 %collective-permute-start = (f32[384,3,128]{2,0,1:T(8,128)}, f32[384,3,128]{2,0,1:T(8,128)}, u32[]{:S(2)}, u32[]{:S(2)}) collective-permute-start(f32[384,3,128]{2,0,1:T(8,128)} %copy.117), channel_id=1, source_target_pairs={{0,16},{16,32},{32,48},{48,64},{64,80},{80,96},{96,112},{1,17},{17... | collective-permute-start | bytes 1769480 | tf_op jit(solution)/shard_map/ppermute | solution.py:30
  10.8 3.0 %copy.78 = f32[384,8,128]{0,1,2:T(8,128)} copy(f32[384,8,128]{2,1,0:T(8,128)} %param.9) | data formatting | bytes 3145728 | tf_op args[0]
  13.8 2.8 %copy.83 = f32[384,8,128]{0,2,1:T(8,128)} copy(bf16[384,8,128]{2,1,0:T(8,128)(2,1)} %param.10) | data formatting | bytes 2359296 | tf_op jit(solution)/shard_map/convert_element_type | solution.py:144
  16.7 3.9 %collective-permute-done = f32[384,3,128]{2,0,1:T(8,128)} collective-permute-done((f32[384,3,128]{2,0,1:T(8,128)}, f32[384,3,128]{2,0,1:T(8,128)}, u32[]{:S(2)}, u32[]{:S(2)}) %collective-permute-start) | collective-permute-done | bytes 589856 | tf_op jit(solution)/shard_map/ppermute | solution.py:30
  20.6 2.2 copy.77
  22.8 3.6 %collective-permute-done.1 = f32[384,3,128]{2,0,1:T(8,128)} collective-permute-done((f32[384,3,128]{2,0,1:T(8,128)}, f32[384,3,128]{2,0,1:T(8,128)}, u32[]{:S(2)}, u32[]{:S(2)}) %collective-permute-start.1) | collective-permute-done | bytes 589856 | tf_op jit(solution)/shard_map/ppermute | solution.py:32
  26.4 2.2 copy.79
  28.6 2.4 pad_maximum_fusion
  31.1 1.3 collective-permute-start.2
  32.4 1.3 collective-permute-start.3
  34.6 2.7 %collective-permute-done.3 = f32[384,14,3]{0,1,2:T(8,128)S(1)} collective-permute-done((f32[384,14,3]{0,1,2:T(8,128)S(1)}, f32[384,14,3]{0,1,2:T(8,128)S(1)}, u32[]{:S(2)}, u32[]{:S(2)}) %collective-permute-start.3) | collective-permute-done | bytes 64544 | tf_op jit(solution)/shard_map/ppermute | solution.py:32
  37.6 2.4 multiply_multiply_fusion
  40.0 1.3 multiply_multiply_fusion.1
  41.4 2.1 fusion.34
  43.4 9.1 %multiply_convert_fusion.1 = (bf16[1024,4096]{1,0:T(8,128)(2,1)S(1)}, f32[1024,4096]{1,0:T(8,128)}) fusion(bf16[384,1024]{0,1:T(8,128)(2,1)S(1)} %bitcast.205, bf16[384,4096]{1,0:T(8,128)(2,1)S(1)} %copy-done), kind=kOutput, calls=%fused_computation.1 | convolution fusion | flops 3242196992 | bytes 29097984 | tf_op jit(solution)/shard_map/dot_general | solution.py:140
  52.5 5.7 %multiply_reduce_fusion = (f32[1024]{0:T(1024)S(1)}, f32[1024,384]{1,0:T(8,128)S(1)}, f32[1024,384]{1,0:T(8,128)}) fusion(f32[384,8,128]{0,2,1:T(8,128)S(1)} %copy-done.10, f32[1024]{0:T(1024)S(1)} %convert_bitcast_fusion, bf16[1024,4096]{1,0:T(8,128)(2,1)S(1)} %get-tuple-element.75, bf16[4096,384]{1,0:T(8,128)(2,1)S(1)} %copy-done.22), kind=kOutput, calls=%fused_computation.33 | convolution fusion | flops 3223583744 | bytes 16261120 | tf_op jit(solution)/shard_map/dot_general | solution.py:142
  58.2 6.4 %fusion.23 = f32[4096,384]{1,0:T(8,128)} fusion(bf16[1024,4096]{1,0:T(8,128)(2,1)S(1)} %get-tuple-element.75, f32[1024,384]{1,0:T(8,128)S(1)} %get-tuple-element.9), kind=kOutput, calls=%fused_computation.129 | convolution fusion | flops 3222011904 | bytes 16252928 | tf_op jit(solution)/shard_map/dot_general | solution.py:157
  64.6 10.3 %reshape.168 = f32[2,4,4,2,2,32,3,128]{7,6,5,4,3,2,1,0:T(4,128)} reshape(f32[4096,384]{1,0:T(8,128)} %fusion.23) | data formatting | bytes 12582912 | tf_op jit(solution)/shard_map/reshape | solution.py:98
  75.0 12.3 %fusion.35 = (f32[2,4,4,2,1,32,1,128]{7,6,5,4,3,2,1,0:T(1,128)S(1)}, f32[2,4,4,2,1,32,1,128]{7,6,5,4,3,2,1,0:T(1,128)S(1)}, f32[2,4,4,2,1,32,1,128]{7,6,5,4,3,2,...) fusion(f32[2,4,4,2,2,32,3,128]{7,6,5,4,3,2,1,0:T(4,128)} %resha, ...), kind=kLoop, calls=%fused_computation.216 | loop fusion | bytes 12582912 | tf_op jit(solution)/shard_map/slice | solution.py:103
  92.7 13.2 %multiply_convert_fusion = bf16[1024,4096]{1,0:T(8,128)(2,1)} fusion(f32[1024,4096]{1,0:T(8,128)} %get-tuple-element.76, bf16[4096,384]{1,0:T(8,128)(2,1)S(1)} %copy-done.23, f32[1024,384]{1,0:T(8,128)S(1)} %copy-done.26), kind=kOutput, calls=%fused_computation | convolution fusion | flops 3259760640 | bytes 29884416 | tf_op jit(solution)/shard_map/dot_general | solution.py:159
  105.8 9.7 %fusion.53 = f32[4096,384]{1,0:T(8,128)} fusion(bf16[1024,4096]{1,0:T(8,128)(2,1)} %multiply_convert_fusion, bf16[384,1024]{0,1:T(8,128)(2,1)S(1)} %bitcast.206), kind=kOutput, calls=%fused_computation.234 | convolution fusion | flops 3221225472 | bytes 15466496 | tf_op jit(solution)/shard_map/dot_general | solution.py:163
  115.6 10.3 %reshape.157 = f32[2,4,4,2,2,32,3,128]{7,6,5,4,3,2,1,0:T(4,128)} reshape(f32[4096,384]{1,0:T(8,128)} %fusion.53) | data formatting | bytes 12582912 | tf_op jit(solution)/shard_map/reshape | solution.py:98
  125.9 12.9 %fusion.36 = (f32[2,4,4,2,1,32,1,128]{7,6,5,4,3,2,1,0:T(1,128)S(1)}, f32[2,4,4,2,1,32,1,128]{7,6,5,4,3,2,1,0:T(1,128)S(1)}, f32[2,4,4,2,1,32,1,128]{7,6,5,4,3,2,...) fusion(f32[2,4,4,2,2,32,3,128]{7,6,5,4,3,2,1,0:T(4,128)} %resha, ...), kind=kLoop, calls=%fused_computation.217 | loop fusion | bytes 12582912 | tf_op jit(solution)/shard_map/slice | solution.py:103
  145.6 3.4 %fusion.2 = (f32[1,6144,128]{2,1,0:T(8,128)}, f32[6144,128]{1,0:T(8,128)}) fusion(s32[]{:T(128)S(6)} %select_n.251, f32[1,6144,128]{2,1,0:T(8,128)S(1)} %maximum_bitcast_fusion.2, f32[1,6144,128]{2,1,0:T(8,128)S(1)} %maximum_bitcast_fusion.3, s32[]{:T(128)S(6)} %select_n.252), kind=kLoop, calls=%fused_computation.13 | loop fusion | flops 1572864 | bytes 12582920 | tf_op jit(solution)/shard_map/stack | solution.py:110
  149.0 3.0 %collective-permute-start.23 = (f32[6144,128]{1,0:T(8,128)}, f32[6144,128]{1,0:T(8,128)}, u32[]{:S(2)}, u32[]{:S(2)}) collective-permute-start(f32[6144,128]{1,0:T(8,128)} %get-tuple-element.28), channel_id=1, source_target_pairs={{0,1},{1,0},{2,3},{3,2},{4,5},{5,4},{6,7},{7,6},{8,9},{9,8},{10,11... | collective-permute-start | bytes 9437192 | tf_op jit(solution)/shard_map/ppermute | solution.py:75
  155.2 3.5 %fusion.5 = (f32[1,6144,128]{2,1,0:T(8,128)}, f32[6144,128]{1,0:T(8,128)}) fusion(s32[]{:T(128)S(6)} %select_n.251, f32[1,6144,128]{2,1,0:T(8,128)S(1)} %maximum_bitcast_fusion, f32[1,6144,128]{2,1,0:T(8,128)S(1)} %maximum_bitcast_fusion.1, s32[]{:T(128)S(6)} %select_n.252), kind=kLoop, calls=%fused_computation.16 | loop fusion | flops 1572864 | bytes 12582920 | tf_op jit(solution)/shard_map/stack | solution.py:110
  159.6 4.7 %collective-permute-done.42 = f32[64]{0:T(128)S(1)} collective-permute-done((f32[64]{0:T(128)S(1)}, f32[64]{0:T(128)S(1)}, u32[]{:S(2)}, u32[]{:S(2)}) %collective-permute-start.42) | collective-permute-done | bytes 288 | tf_op jit(solution)/shard_map/ppermute | solution.py:90
  164.3 1.5 collective-permute-start.43
  165.8 2.0 collective-permute-done.43
  167.8 2.8 %collective-permute-start.44 = (f32[64]{0:T(128)S(1)}, f32[64]{0:T(128)S(1)}, u32[]{:S(2)}, u32[]{:S(2)}) collective-permute-start(f32[64]{0:T(128)S(1)} %add.574), channel_id=1, source_target_pairs={{0,12},{1,5},{4,8},{5,1},{8,4},{9,13},{12,0},{13,9},{2,14},{3,7},{... | collective-permute-start | bytes 776 | tf_op jit(solution)/shard_map/ppermute | solution.py:93
  170.6 2.0 collective-permute-done.44
  172.6 2.3 collective-permute-start.45
  174.9 1.5 collective-permute-done.45
  176.4 4.4 %collective-permute-start.46 = (f32[64]{0:T(128)S(1)}, f32[64]{0:T(128)S(1)}, u32[]{:S(2)}, u32[]{:S(2)}) collective-permute-start(f32[64]{0:T(128)S(1)} %add.576), channel_id=1, source_target_pairs={{0,66},{1,3},{2,64},{3,1},{64,2},{65,67},{66,0},{67,65},{4,70},{5,... | collective-permute-start | bytes 776 | tf_op jit(solution)/shard_map/ppermute | solution.py:93
  180.8 1.5 collective-permute-done.46
  182.8 3.0 %collective-permute-done.47 = f32[64]{0:T(128)S(1)} collective-permute-done((f32[64]{0:T(128)S(1)}, f32[64]{0:T(128)S(1)}, u32[]{:S(2)}, u32[]{:S(2)}) %collective-permute-start.47) | collective-permute-done | bytes 288 | tf_op jit(solution)/shard_map/ppermute | solution.py:93
  185.8 5.9 %collective-permute-start.48 = (f32[64]{0:T(128)S(1)}, f32[64]{0:T(128)S(1)}, u32[]{:S(2)}, u32[]{:S(2)}) collective-permute-start(f32[64]{0:T(128)S(1)} %add.578), channel_id=1, source_target_pairs={{0,48},{1,17},{16,32},{17,1},{32,16},{33,49},{48,0},{49,33},{2,50}... | collective-permute-start | bytes 776 | tf_op jit(solution)/shard_map/ppermute | solution.py:93
  191.7 3.4 %add.484 = f32[384,8,128]{0,2,1:T(8,128)} add(f32[384,8,128]{0,2,1:T(8,128)} %get-tuple-element.11, f32[384,8,128]{0,2,1:T(8,128)} %bitcast.188) | non-fusion elementwise | flops 393216 | bytes 4718592 | tf_op jit(solution)/shard_map/add | solution.py:145
  195.1 3.0 %copy.116 = f32[384,8,128]{2,1,0:T(8,128)} copy(f32[384,8,128]{0,2,1:T(8,128)} %add.484) | data formatting | bytes 3145728
  198.6 2.2 slice_add_fusion.2
  202.7 2.2 slice_add_fusion.5
  204.9 1.4 collective-permute-start.5
  206.4 1.3 collective-permute-start.11
  207.7 5.0 %collective-permute-done.24 = f32[1024,128]{1,0:T(8,128)S(1)} collective-permute-done((f32[1024,128]{1,0:T(8,128)S(1)}, f32[1024,128]{1,0:T(8,128)S(1)}, u32[]{:S(2)}, u32[]{:S(2)}) %collective-permute-start.24) | collective-permute-done | bytes 524320 | tf_op jit(solution)/shard_map/ppermute | solution.py:83
  214.3 7.0 %collective-permute-done.5 = f32[1024,128]{1,0:T(8,128)S(1)} collective-permute-done((f32[1024,128]{1,0:T(8,128)S(1)}, f32[1024,128]{1,0:T(8,128)S(1)}, u32[]{:S(2)}, u32[]{:S(2)}) %collective-permute-start.5) | collective-permute-done | bytes 524320 | tf_op jit(solution)/shard_map/ppermute | solution.py:83
  221.7 1.6 collective-permute-start.6
  224.2 2.4 collective-permute-start.12
  227.4 2.9 %collective-permute-done.37 = f32[512,128]{1,0:T(8,128)S(1)} collective-permute-done((f32[512,128]{1,0:T(8,128)S(1)}, f32[512,128]{1,0:T(8,128)S(1)}, u32[]{:S(2)}, u32[]{:S(2)}) %collective-permute-start.37) | collective-permute-done | bytes 262176 | tf_op jit(solution)/shard_map/ppermute | solution.py:83
  232.3 2.1 collective-permute-done.18
  234.4 1.3 collective-permute-start.19
  235.8 1.5 collective-permute-start.27
  237.4 1.4 collective-permute-start.33
  238.8 1.9 collective-permute-start.39
  240.7 1.4 collective-permute-start.8
  242.2 2.0 collective-permute-start.14
  244.3 2.0 collective-permute-start.20
  251.0 2.1 collective-permute-start.21
  253.1 1.3 collective-permute-start.29
  254.5 1.4 collective-permute-start.35
  255.9 2.0 collective-permute-start.41
  257.9 1.6 collective-permute-start.10
  259.6 1.9 collective-permute-start.16
  261.5 1.9 collective-permute-start.22
  (288 shorter events, 37.1 us)
Async XLA Ops:
  0.6 42.8 %copy-start = (bf16[384,4096]{1,0:T(8,128)(2,1)S(1)}, bf16[384,4096]{1,0:T(8,128)(2,1)}, u32[]{:S(2)}) copy-start(bf16[384,4096]{1,0:T(8,128)(2,1)} %param.16) | copy-start | bytes 9437188
  3.8 16.8 %collective-permute-start = (f32[384,3,128]{2,0,1:T(8,128)}, f32[384,3,128]{2,0,1:T(8,128)}, u32[]{:S(2)}, u32[]{:S(2)}) collective-permute-start(f32[384,3,128]{2,0,1:T(8,128)} %copy.117), channel_id=1, source_target_pairs={{0,16},{16,32},{32,48},{48,64},{64,80},{80,96},{96,112},{1,17},{17... | collective-permute-start | bytes 1769480 | tf_op jit(solution)/shard_map/ppermute | solution.py:30
  8.6 8.1 %copy-start.19 = (s32[8,128]{1,0:T(8,128)S(1)}, s32[8,128]{1,0:T(8,128)}, u32[]{:S(2)}) copy-start(s32[8,128]{1,0:T(8,128)} %param.11) | copy-start | bytes 12292
  8.6 8.1 %copy-start.20 = (f32[384]{0:T(512)S(1)}, f32[384]{0:T(512)}, u32[]{:S(2)}) copy-start(f32[384]{0:T(512)} %param.15) | copy-start | bytes 4612
  8.6 8.1 %copy-start.21 = (f32[384]{0:T(512)S(1)}, f32[384]{0:T(512)}, u32[]{:S(2)}) copy-start(f32[384]{0:T(512)} %param.14) | copy-start | bytes 4612
  9.4 17.0 %collective-permute-start.1 = (f32[384,3,128]{2,0,1:T(8,128)}, f32[384,3,128]{2,0,1:T(8,128)}, u32[]{:S(2)}, u32[]{:S(2)}) collective-permute-start(f32[384,3,128]{2,0,1:T(8,128)} %copy.118), channel_id=1, source_target_pairs={{16,0},{32,16},{48,32},{64,48},{80,64},{96,80},{112,96},{17,1},{33... | collective-permute-start | bytes 1769480 | tf_op jit(solution)/shard_map/ppermute | solution.py:32
  31.1 3.5 %collective-permute-start.2 = (f32[384,14,3]{0,1,2:T(8,128)S(1)}, f32[384,14,3]{0,1,2:T(8,128)S(1)}, u32[]{:S(2)}, u32[]{:S(2)}) collective-permute-start(f32[384,14,3]{0,1,2:T(8,128)S(1)} %get-tuple-element.34), channel_id=1, source_target_pairs={{0,1},{1,2},{2,3},{3,4},{4,5},{5,6},{6,7},{7,8},{8,9},{9,10},{10,1... | collective-permute-start | bytes 193544 | tf_op jit(solution)/shard_map/ppermute | solution.py:30
  32.4 5.0 %collective-permute-start.3 = (f32[384,14,3]{0,1,2:T(8,128)S(1)}, f32[384,14,3]{0,1,2:T(8,128)S(1)}, u32[]{:S(2)}, u32[]{:S(2)}) collective-permute-start(f32[384,14,3]{0,1,2:T(8,128)S(1)} %get-tuple-element.35), channel_id=1, source_target_pairs={{1,0},{2,1},{3,2},{4,3},{5,4},{6,5},{7,6},{8,7},{9,8},{10,9},{11,1... | collective-permute-start | bytes 193544 | tf_op jit(solution)/shard_map/ppermute | solution.py:32
  34.6 3.0 %copy-start.18 = (f32[384]{0:T(512)S(1)}, f32[384]{0:T(512)}, u32[]{:S(2)}) copy-start(f32[384]{0:T(512)} %param.13) | copy-start | bytes 4612
  43.4 9.1 %copy-start.16 = (bf16[384,8,128]{0,2,1:T(8,128)(2,1)}, bf16[384,8,128]{0,2,1:T(8,128)(2,1)S(1)}, u32[]{:S(2)}) copy-start(bf16[384,8,128]{0,2,1:T(8,128)(2,1)S(1)} %get-tuple-element.10) | copy-start | bytes 2359300
  43.4 9.1 %copy-start.10 = (f32[384,8,128]{0,2,1:T(8,128)S(1)}, f32[384,8,128]{0,2,1:T(8,128)}, u32[]{:S(2)}) copy-start(f32[384,8,128]{0,2,1:T(8,128)} %copy.83) | copy-start | bytes 4718596
  43.4 9.1 %copy-start.22 = (bf16[4096,384]{1,0:T(8,128)(2,1)S(1)}, bf16[4096,384]{1,0:T(8,128)(2,1)}, u32[]{:S(2)}) copy-start(bf16[4096,384]{1,0:T(8,128)(2,1)} %param.17) | copy-start | bytes 9437188
  58.2 6.4 %copy-start.25 = (f32[1024,384]{1,0:T(8,128)}, f32[1024,384]{1,0:T(8,128)S(1)}, u32[]{:S(2)}) copy-start(f32[1024,384]{1,0:T(8,128)S(1)} %get-tuple-element.9) | copy-start | bytes 4718596
  89.7 2.5 copy-start.23
  89.8 2.9 %copy-start.26 = (f32[1024,384]{1,0:T(8,128)S(1)}, f32[1024,384]{1,0:T(8,128)}, u32[]{:S(2)}) copy-start(f32[1024,384]{1,0:T(8,128)} %copy-done.25) | copy-start | bytes 4718596
  92.7 13.2 %copy-start.17 = (bf16[384,8,128]{0,2,1:T(8,128)(2,1)S(1)}, bf16[384,8,128]{0,2,1:T(8,128)(2,1)}, u32[]{:S(2)}) copy-start(bf16[384,8,128]{0,2,1:T(8,128)(2,1)} %copy-done.16) | copy-start | bytes 2359300
  149.0 49.6 %collective-permute-start.23 = (f32[6144,128]{1,0:T(8,128)}, f32[6144,128]{1,0:T(8,128)}, u32[]{:S(2)}, u32[]{:S(2)}) collective-permute-start(f32[6144,128]{1,0:T(8,128)} %get-tuple-element.28), channel_id=1, source_target_pairs={{0,1},{1,0},{2,3},{3,2},{4,5},{5,4},{6,7},{7,6},{8,9},{9,8},{10,11... | collective-permute-start | bytes 9437192 | tf_op jit(solution)/shard_map/ppermute | solution.py:75
  155.2 3.5 %copy-start.24 = (s32[8,128]{1,0:T(8,128)S(1)}, s32[8,128]{1,0:T(8,128)}, u32[]{:S(2)}) copy-start(s32[8,128]{1,0:T(8,128)} %param.12) | copy-start | bytes 12292
  158.7 43.6 %collective-permute-start.4 = (f32[6144,128]{1,0:T(8,128)}, f32[6144,128]{1,0:T(8,128)}, u32[]{:S(2)}, u32[]{:S(2)}) collective-permute-start(f32[6144,128]{1,0:T(8,128)} %get-tuple-element.33), channel_id=1, source_target_pairs={{0,1},{1,0},{2,3},{3,2},{4,5},{5,4},{6,7},{7,6},{8,9},{9,8},{10,11... | collective-permute-start | bytes 9437192 | tf_op jit(solution)/shard_map/ppermute | solution.py:75
  159.0 5.2 %collective-permute-start.42 = (f32[64]{0:T(128)S(1)}, f32[64]{0:T(128)S(1)}, u32[]{:S(2)}, u32[]{:S(2)}) collective-permute-start(f32[64]{0:T(128)S(1)} %fusion.7), channel_id=1, source_target_pairs={{0,1},{1,0},{2,3},{3,2},{4,5},{5,4},{6,7},{7,6},{8,9},{9,8},{10,11... | collective-permute-start | bytes 776 | tf_op jit(solution)/shard_map/ppermute | solution.py:90
  164.3 3.5 %collective-permute-start.43 = (f32[64]{0:T(128)S(1)}, f32[64]{0:T(128)S(1)}, u32[]{:S(2)}, u32[]{:S(2)}) collective-permute-start(f32[64]{0:T(128)S(1)} %add.573), channel_id=1, source_target_pairs={{0,4},{1,13},{4,0},{5,9},{8,12},{9,5},{12,8},{13,1},{2,6},{3,15},{... | collective-permute-start | bytes 776 | tf_op jit(solution)/shard_map/ppermute | solution.py:93
  167.8 4.8 %collective-permute-start.44 = (f32[64]{0:T(128)S(1)}, f32[64]{0:T(128)S(1)}, u32[]{:S(2)}, u32[]{:S(2)}) collective-permute-start(f32[64]{0:T(128)S(1)} %add.574), channel_id=1, source_target_pairs={{0,12},{1,5},{4,8},{5,1},{8,4},{9,13},{12,0},{13,9},{2,14},{3,7},{... | collective-permute-start | bytes 776 | tf_op jit(solution)/shard_map/ppermute | solution.py:93
  172.6 3.8 %collective-permute-start.45 = (f32[64]{0:T(128)S(1)}, f32[64]{0:T(128)S(1)}, u32[]{:S(2)}, u32[]{:S(2)}) collective-permute-start(f32[64]{0:T(128)S(1)} %add.575), channel_id=1, source_target_pairs={{0,2},{1,67},{2,0},{3,65},{64,66},{65,3},{66,64},{67,1},{4,6},{5,7... | collective-permute-start | bytes 776 | tf_op jit(solution)/shard_map/ppermute | solution.py:93
  176.4 5.9 %collective-permute-start.46 = (f32[64]{0:T(128)S(1)}, f32[64]{0:T(128)S(1)}, u32[]{:S(2)}, u32[]{:S(2)}) collective-permute-start(f32[64]{0:T(128)S(1)} %add.576), channel_id=1, source_target_pairs={{0,66},{1,3},{2,64},{3,1},{64,2},{65,67},{66,0},{67,65},{4,70},{5,... | collective-permute-start | bytes 776 | tf_op jit(solution)/shard_map/ppermute | solution.py:93
  182.3 3.5 %collective-permute-start.47 = (f32[64]{0:T(128)S(1)}, f32[64]{0:T(128)S(1)}, u32[]{:S(2)}, u32[]{:S(2)}) collective-permute-start(f32[64]{0:T(128)S(1)} %add.577), channel_id=1, source_target_pairs={{0,16},{1,49},{16,0},{17,33},{32,48},{33,17},{48,32},{49,1},{2,18}... | collective-permute-start | bytes 776 | tf_op jit(solution)/shard_map/ppermute | solution.py:93
  185.8 12.3 %collective-permute-start.48 = (f32[64]{0:T(128)S(1)}, f32[64]{0:T(128)S(1)}, u32[]{:S(2)}, u32[]{:S(2)}) collective-permute-start(f32[64]{0:T(128)S(1)} %add.578), channel_id=1, source_target_pairs={{0,48},{1,17},{16,32},{17,1},{32,16},{33,49},{48,0},{49,33},{2,50}... | collective-permute-start | bytes 776 | tf_op jit(solution)/shard_map/ppermute | solution.py:93
  191.7 6.9 %copy-start.2 = (f32[1,6144,128]{2,1,0:T(8,128)S(1)}, f32[1,6144,128]{2,1,0:T(8,128)}, u32[]{:S(2)}) copy-start(f32[1,6144,128]{2,1,0:T(8,128)} %get-tuple-element.27) | copy-start | bytes 9437188
  200.8 11.9 %collective-permute-start.24 = (f32[1024,128]{1,0:T(8,128)S(1)}, f32[1024,128]{1,0:T(8,128)S(1)}, u32[]{:S(2)}, u32[]{:S(2)}) collective-permute-start(f32[1024,128]{1,0:T(8,128)S(1)} %constant_dynamic-slice_fusion.20), channel_id=1, source_target_pairs={{0,4},{1,13},{4,0},{5,9},{8,12},{9,5},{12,8},{13,1},{2,6},{3,15},{... | collective-permute-start | bytes 1572872 | tf_op jit(solution)/shard_map/ppermute | solution.py:83
  201.2 12.1 %collective-permute-start.30 = (f32[1024,128]{1,0:T(8,128)S(1)}, f32[1024,128]{1,0:T(8,128)S(1)}, u32[]{:S(2)}, u32[]{:S(2)}) collective-permute-start(f32[1024,128]{1,0:T(8,128)S(1)} %constant_dynamic-slice_fusion.13), channel_id=1, source_target_pairs={{0,2},{1,67},{2,0},{3,65},{64,66},{65,3},{66,64},{67,1},{4,6},{5,7... | collective-permute-start | bytes 1572872 | tf_op jit(solution)/shard_map/ppermute | solution.py:83
  202.2 12.0 %collective-permute-start.36 = (f32[1024,128]{1,0:T(8,128)S(1)}, f32[1024,128]{1,0:T(8,128)S(1)}, u32[]{:S(2)}, u32[]{:S(2)}) collective-permute-start(f32[1024,128]{1,0:T(8,128)S(1)} %constant_dynamic-slice_fusion.6), channel_id=1, source_target_pairs={{0,16},{1,49},{16,0},{17,33},{32,48},{33,17},{48,32},{49,1},{2,18}... | collective-permute-start | bytes 1572872 | tf_op jit(solution)/shard_map/ppermute | solution.py:83
  204.9 16.4 %collective-permute-start.5 = (f32[1024,128]{1,0:T(8,128)S(1)}, f32[1024,128]{1,0:T(8,128)S(1)}, u32[]{:S(2)}, u32[]{:S(2)}) collective-permute-start(f32[1024,128]{1,0:T(8,128)S(1)} %constant_dynamic-slice_fusion.41), channel_id=1, source_target_pairs={{0,4},{1,13},{4,0},{5,9},{8,12},{9,5},{12,8},{13,1},{2,6},{3,15},{... | collective-permute-start | bytes 1572872 | tf_op jit(solution)/shard_map/ppermute | solution.py:83
  206.4 15.4 %collective-permute-start.11 = (f32[1024,128]{1,0:T(8,128)S(1)}, f32[1024,128]{1,0:T(8,128)S(1)}, u32[]{:S(2)}, u32[]{:S(2)}) collective-permute-start(f32[1024,128]{1,0:T(8,128)S(1)} %constant_dynamic-slice_fusion.34), channel_id=1, source_target_pairs={{0,2},{1,67},{2,0},{3,65},{64,66},{65,3},{66,64},{67,1},{4,6},{5,7... | collective-permute-start | bytes 1572872 | tf_op jit(solution)/shard_map/ppermute | solution.py:83
  212.8 11.5 %collective-permute-start.17 = (f32[1024,128]{1,0:T(8,128)S(1)}, f32[1024,128]{1,0:T(8,128)S(1)}, u32[]{:S(2)}, u32[]{:S(2)}) collective-permute-start(f32[1024,128]{1,0:T(8,128)S(1)} %constant_dynamic-slice_fusion.27), channel_id=1, source_target_pairs={{0,16},{1,49},{16,0},{17,33},{32,48},{33,17},{48,32},{49,1},{2,18}... | collective-permute-start | bytes 1572872 | tf_op jit(solution)/shard_map/ppermute | solution.py:83
  213.3 13.4 %collective-permute-start.25 = (f32[512,128]{1,0:T(8,128)S(1)}, f32[512,128]{1,0:T(8,128)S(1)}, u32[]{:S(2)}, u32[]{:S(2)}) collective-permute-start(f32[512,128]{1,0:T(8,128)S(1)} %constant_dynamic-slice_fusion.19), channel_id=1, source_target_pairs={{0,12},{1,5},{4,8},{5,1},{8,4},{9,13},{12,0},{13,9},{2,14},{3,7},{... | collective-permute-start | bytes 786440 | tf_op jit(solution)/shard_map/ppermute | solution.py:83
  214.1 12.9 %collective-permute-start.31 = (f32[512,128]{1,0:T(8,128)S(1)}, f32[512,128]{1,0:T(8,128)S(1)}, u32[]{:S(2)}, u32[]{:S(2)}) collective-permute-start(f32[512,128]{1,0:T(8,128)S(1)} %constant_dynamic-slice_fusion.12), channel_id=1, source_target_pairs={{0,66},{1,3},{2,64},{3,1},{64,2},{65,67},{66,0},{67,65},{4,70},{5,... | collective-permute-start | bytes 786440 | tf_op jit(solution)/shard_map/ppermute | solution.py:83
  221.3 9.0 %collective-permute-start.37 = (f32[512,128]{1,0:T(8,128)S(1)}, f32[512,128]{1,0:T(8,128)S(1)}, u32[]{:S(2)}, u32[]{:S(2)}) collective-permute-start(f32[512,128]{1,0:T(8,128)S(1)} %constant_dynamic-slice_fusion.5), channel_id=1, source_target_pairs={{0,48},{1,17},{16,32},{17,1},{32,16},{33,49},{48,0},{49,33},{2,50}... | collective-permute-start | bytes 786440 | tf_op jit(solution)/shard_map/ppermute | solution.py:83
  221.7 8.7 %collective-permute-start.6 = (f32[512,128]{1,0:T(8,128)S(1)}, f32[512,128]{1,0:T(8,128)S(1)}, u32[]{:S(2)}, u32[]{:S(2)}) collective-permute-start(f32[512,128]{1,0:T(8,128)S(1)} %constant_dynamic-slice_fusion.40), channel_id=1, source_target_pairs={{0,12},{1,5},{4,8},{5,1},{8,4},{9,13},{12,0},{13,9},{2,14},{3,7},{... | collective-permute-start | bytes 786440 | tf_op jit(solution)/shard_map/ppermute | solution.py:83
  224.2 7.6 %collective-permute-start.12 = (f32[512,128]{1,0:T(8,128)S(1)}, f32[512,128]{1,0:T(8,128)S(1)}, u32[]{:S(2)}, u32[]{:S(2)}) collective-permute-start(f32[512,128]{1,0:T(8,128)S(1)} %constant_dynamic-slice_fusion.33), channel_id=1, source_target_pairs={{0,66},{1,3},{2,64},{3,1},{64,2},{65,67},{66,0},{67,65},{4,70},{5,... | collective-permute-start | bytes 786440 | tf_op jit(solution)/shard_map/ppermute | solution.py:83
  226.7 7.7 %collective-permute-start.18 = (f32[512,128]{1,0:T(8,128)S(1)}, f32[512,128]{1,0:T(8,128)S(1)}, u32[]{:S(2)}, u32[]{:S(2)}) collective-permute-start(f32[512,128]{1,0:T(8,128)S(1)} %constant_dynamic-slice_fusion.26), channel_id=1, source_target_pairs={{0,48},{1,17},{16,32},{17,1},{32,16},{33,49},{48,0},{49,33},{2,50}... | collective-permute-start | bytes 786440 | tf_op jit(solution)/shard_map/ppermute | solution.py:83
  227.1 7.4 %collective-permute-start.26 = (f32[256,128]{1,0:T(8,128)S(1)}, f32[256,128]{1,0:T(8,128)S(1)}, u32[]{:S(2)}, u32[]{:S(2)}) collective-permute-start(f32[256,128]{1,0:T(8,128)S(1)} %constant_dynamic-slice_fusion.18), channel_id=1, source_target_pairs={{0,2},{1,67},{2,0},{3,65},{64,66},{65,3},{66,64},{67,1},{4,6},{5,7... | collective-permute-start | bytes 393224 | tf_op jit(solution)/shard_map/ppermute | solution.py:83
  230.3 5.5 %collective-permute-start.32 = (f32[256,128]{1,0:T(8,128)S(1)}, f32[256,128]{1,0:T(8,128)S(1)}, u32[]{:S(2)}, u32[]{:S(2)}) collective-permute-start(f32[256,128]{1,0:T(8,128)S(1)} %constant_dynamic-slice_fusion.11), channel_id=1, source_target_pairs={{0,16},{1,49},{16,0},{17,33},{32,48},{33,17},{48,32},{49,1},{2,18}... | collective-permute-start | bytes 393224 | tf_op jit(solution)/shard_map/ppermute | solution.py:83
  230.5 6.9 %collective-permute-start.38 = (f32[256,128]{1,0:T(8,128)S(1)}, f32[256,128]{1,0:T(8,128)S(1)}, u32[]{:S(2)}, u32[]{:S(2)}) collective-permute-start(f32[256,128]{1,0:T(8,128)S(1)} %constant_dynamic-slice_fusion.4), channel_id=1, source_target_pairs={{0,4},{1,13},{4,0},{5,9},{8,12},{9,5},{12,8},{13,1},{2,6},{3,15},{... | collective-permute-start | bytes 393224 | tf_op jit(solution)/shard_map/ppermute | solution.py:83
  231.8 7.0 %collective-permute-start.7 = (f32[256,128]{1,0:T(8,128)S(1)}, f32[256,128]{1,0:T(8,128)S(1)}, u32[]{:S(2)}, u32[]{:S(2)}) collective-permute-start(f32[256,128]{1,0:T(8,128)S(1)} %constant_dynamic-slice_fusion.39), channel_id=1, source_target_pairs={{0,2},{1,67},{2,0},{3,65},{64,66},{65,3},{66,64},{67,1},{4,6},{5,7... | collective-permute-start | bytes 393224 | tf_op jit(solution)/shard_map/ppermute | solution.py:83
  234.4 6.4 %collective-permute-start.13 = (f32[256,128]{1,0:T(8,128)S(1)}, f32[256,128]{1,0:T(8,128)S(1)}, u32[]{:S(2)}, u32[]{:S(2)}) collective-permute-start(f32[256,128]{1,0:T(8,128)S(1)} %constant_dynamic-slice_fusion.32), channel_id=1, source_target_pairs={{0,16},{1,49},{16,0},{17,33},{32,48},{33,17},{48,32},{49,1},{2,18}... | collective-permute-start | bytes 393224 | tf_op jit(solution)/shard_map/ppermute | solution.py:83
  234.4 32.8 %copy-start.1 = (bf16[384,4096]{1,0:T(8,128)(2,1)S(1)}, bf16[384,4096]{1,0:T(8,128)(2,1)}, u32[]{:S(2)}) copy-start(bf16[384,4096]{1,0:T(8,128)(2,1)} %param.16) | copy-start | bytes 9437188
  234.4 7.7 %collective-permute-start.19 = (f32[256,128]{1,0:T(8,128)S(1)}, f32[256,128]{1,0:T(8,128)S(1)}, u32[]{:S(2)}, u32[]{:S(2)}) collective-permute-start(f32[256,128]{1,0:T(8,128)S(1)} %constant_dynamic-slice_fusion.25), channel_id=1, source_target_pairs={{0,4},{1,13},{4,0},{5,9},{8,12},{9,5},{12,8},{13,1},{2,6},{3,15},{... | collective-permute-start | bytes 393224 | tf_op jit(solution)/shard_map/ppermute | solution.py:83
  235.8 8.4 %collective-permute-start.27 = (f32[128,128]{1,0:T(8,128)S(1)}, f32[128,128]{1,0:T(8,128)S(1)}, u32[]{:S(2)}, u32[]{:S(2)}) collective-permute-start(f32[128,128]{1,0:T(8,128)S(1)} %constant_dynamic-slice_fusion.17), channel_id=1, source_target_pairs={{0,66},{1,3},{2,64},{3,1},{64,2},{65,67},{66,0},{67,65},{4,70},{5,... | collective-permute-start | bytes 196616 | tf_op jit(solution)/shard_map/ppermute | solution.py:83
  237.4 9.0 %collective-permute-start.33 = (f32[128,128]{1,0:T(8,128)S(1)}, f32[128,128]{1,0:T(8,128)S(1)}, u32[]{:S(2)}, u32[]{:S(2)}) collective-permute-start(f32[128,128]{1,0:T(8,128)S(1)} %constant_dynamic-slice_fusion.10), channel_id=1, source_target_pairs={{0,48},{1,17},{16,32},{17,1},{32,16},{33,49},{48,0},{49,33},{2,50}... | collective-permute-start | bytes 196616 | tf_op jit(solution)/shard_map/ppermute | solution.py:83
  238.8 7.7 %collective-permute-start.39 = (f32[128,128]{1,0:T(8,128)S(1)}, f32[128,128]{1,0:T(8,128)S(1)}, u32[]{:S(2)}, u32[]{:S(2)}) collective-permute-start(f32[128,128]{1,0:T(8,128)S(1)} %constant_dynamic-slice_fusion.3), channel_id=1, source_target_pairs={{0,12},{1,5},{4,8},{5,1},{8,4},{9,13},{12,0},{13,9},{2,14},{3,7},{... | collective-permute-start | bytes 196616 | tf_op jit(solution)/shard_map/ppermute | solution.py:83
  240.7 6.2 %collective-permute-start.8 = (f32[128,128]{1,0:T(8,128)S(1)}, f32[128,128]{1,0:T(8,128)S(1)}, u32[]{:S(2)}, u32[]{:S(2)}) collective-permute-start(f32[128,128]{1,0:T(8,128)S(1)} %constant_dynamic-slice_fusion.38), channel_id=1, source_target_pairs={{0,66},{1,3},{2,64},{3,1},{64,2},{65,67},{66,0},{67,65},{4,70},{5,... | collective-permute-start | bytes 196616 | tf_op jit(solution)/shard_map/ppermute | solution.py:83
  242.2 5.6 %collective-permute-start.14 = (f32[128,128]{1,0:T(8,128)S(1)}, f32[128,128]{1,0:T(8,128)S(1)}, u32[]{:S(2)}, u32[]{:S(2)}) collective-permute-start(f32[128,128]{1,0:T(8,128)S(1)} %constant_dynamic-slice_fusion.31), channel_id=1, source_target_pairs={{0,48},{1,17},{16,32},{17,1},{32,16},{33,49},{48,0},{49,33},{2,50}... | collective-permute-start | bytes 196616 | tf_op jit(solution)/shard_map/ppermute | solution.py:83
  244.3 5.6 %collective-permute-start.20 = (f32[128,128]{1,0:T(8,128)S(1)}, f32[128,128]{1,0:T(8,128)S(1)}, u32[]{:S(2)}, u32[]{:S(2)}) collective-permute-start(f32[128,128]{1,0:T(8,128)S(1)} %constant_dynamic-slice_fusion.24), channel_id=1, source_target_pairs={{0,12},{1,5},{4,8},{5,1},{8,4},{9,13},{12,0},{13,9},{2,14},{3,7},{... | collective-permute-start | bytes 196616 | tf_op jit(solution)/shard_map/ppermute | solution.py:83
  246.3 4.7 %collective-permute-start.28 = (f32[64,128]{1,0:T(8,128)S(1)}, f32[64,128]{1,0:T(8,128)S(1)}, u32[]{:S(2)}, u32[]{:S(2)}) collective-permute-start(f32[64,128]{1,0:T(8,128)S(1)} %constant_dynamic-slice_fusion.16), channel_id=1, source_target_pairs={{0,16},{1,49},{16,0},{17,33},{32,48},{33,17},{48,32},{49,1},{2,18}... | collective-permute-start | bytes 98312 | tf_op jit(solution)/shard_map/ppermute | solution.py:83
  246.5 6.6 %collective-permute-start.34 = (f32[64,128]{1,0:T(8,128)S(1)}, f32[64,128]{1,0:T(8,128)S(1)}, u32[]{:S(2)}, u32[]{:S(2)}) collective-permute-start(f32[64,128]{1,0:T(8,128)S(1)} %constant_dynamic-slice_fusion.9), channel_id=1, source_target_pairs={{0,4},{1,13},{4,0},{5,9},{8,12},{9,5},{12,8},{13,1},{2,6},{3,15},{... | collective-permute-start | bytes 98312 | tf_op jit(solution)/shard_map/ppermute | solution.py:83
  246.9 7.5 %collective-permute-start.40 = (f32[64,128]{1,0:T(8,128)S(1)}, f32[64,128]{1,0:T(8,128)S(1)}, u32[]{:S(2)}, u32[]{:S(2)}) collective-permute-start(f32[64,128]{1,0:T(8,128)S(1)} %constant_dynamic-slice_fusion.2), channel_id=1, source_target_pairs={{0,2},{1,67},{2,0},{3,65},{64,66},{65,3},{66,64},{67,1},{4,6},{5,7... | collective-permute-start | bytes 98312 | tf_op jit(solution)/shard_map/ppermute | solution.py:83
  247.7 8.2 %collective-permute-start.9 = (f32[64,128]{1,0:T(8,128)S(1)}, f32[64,128]{1,0:T(8,128)S(1)}, u32[]{:S(2)}, u32[]{:S(2)}) collective-permute-start(f32[64,128]{1,0:T(8,128)S(1)} %constant_dynamic-slice_fusion.37), channel_id=1, source_target_pairs={{0,16},{1,49},{16,0},{17,33},{32,48},{33,17},{48,32},{49,1},{2,18}... | collective-permute-start | bytes 98312 | tf_op jit(solution)/shard_map/ppermute | solution.py:83
  249.8 8.1 %collective-permute-start.15 = (f32[64,128]{1,0:T(8,128)S(1)}, f32[64,128]{1,0:T(8,128)S(1)}, u32[]{:S(2)}, u32[]{:S(2)}) collective-permute-start(f32[64,128]{1,0:T(8,128)S(1)} %constant_dynamic-slice_fusion.30), channel_id=1, source_target_pairs={{0,4},{1,13},{4,0},{5,9},{8,12},{9,5},{12,8},{13,1},{2,6},{3,15},{... | collective-permute-start | bytes 98312 | tf_op jit(solution)/shard_map/ppermute | solution.py:83
  251.0 8.5 %collective-permute-start.21 = (f32[64,128]{1,0:T(8,128)S(1)}, f32[64,128]{1,0:T(8,128)S(1)}, u32[]{:S(2)}, u32[]{:S(2)}) collective-permute-start(f32[64,128]{1,0:T(8,128)S(1)} %constant_dynamic-slice_fusion.23), channel_id=1, source_target_pairs={{0,2},{1,67},{2,0},{3,65},{64,66},{65,3},{66,64},{67,1},{4,6},{5,7... | collective-permute-start | bytes 98312 | tf_op jit(solution)/shard_map/ppermute | solution.py:83
  253.1 8.4 %collective-permute-start.29 = (f32[32,128]{1,0:T(8,128)S(1)}, f32[32,128]{1,0:T(8,128)S(1)}, u32[]{:S(2)}, u32[]{:S(2)}) collective-permute-start(f32[32,128]{1,0:T(8,128)S(1)} %constant_dynamic-slice_fusion.14), channel_id=1, source_target_pairs={{0,48},{1,17},{16,32},{17,1},{32,16},{33,49},{48,0},{49,33},{2,50}... | collective-permute-start | bytes 49160 | tf_op jit(solution)/shard_map/ppermute | solution.py:83
  254.5 9.0 %collective-permute-start.35 = (f32[32,128]{1,0:T(8,128)S(1)}, f32[32,128]{1,0:T(8,128)S(1)}, u32[]{:S(2)}, u32[]{:S(2)}) collective-permute-start(f32[32,128]{1,0:T(8,128)S(1)} %constant_dynamic-slice_fusion.7), channel_id=1, source_target_pairs={{0,12},{1,5},{4,8},{5,1},{8,4},{9,13},{12,0},{13,9},{2,14},{3,7},{... | collective-permute-start | bytes 49160 | tf_op jit(solution)/shard_map/ppermute | solution.py:83
  255.9 8.7 %collective-permute-start.41 = (f32[32,128]{1,0:T(8,128)S(1)}, f32[32,128]{1,0:T(8,128)S(1)}, u32[]{:S(2)}, u32[]{:S(2)}) collective-permute-start(f32[32,128]{1,0:T(8,128)S(1)} %constant_dynamic-slice_fusion), channel_id=1, source_target_pairs={{0,66},{1,3},{2,64},{3,1},{64,2},{65,67},{66,0},{67,65},{4,70},{5,... | collective-permute-start | bytes 49160 | tf_op jit(solution)/shard_map/ppermute | solution.py:83
  257.9 5.5 %collective-permute-start.10 = (f32[32,128]{1,0:T(8,128)S(1)}, f32[32,128]{1,0:T(8,128)S(1)}, u32[]{:S(2)}, u32[]{:S(2)}) collective-permute-start(f32[32,128]{1,0:T(8,128)S(1)} %constant_dynamic-slice_fusion.35), channel_id=1, source_target_pairs={{0,48},{1,17},{16,32},{17,1},{32,16},{33,49},{48,0},{49,33},{2,50}... | collective-permute-start | bytes 49160 | tf_op jit(solution)/shard_map/ppermute | solution.py:83
  259.6 5.0 %collective-permute-start.16 = (f32[32,128]{1,0:T(8,128)S(1)}, f32[32,128]{1,0:T(8,128)S(1)}, u32[]{:S(2)}, u32[]{:S(2)}) collective-permute-start(f32[32,128]{1,0:T(8,128)S(1)} %constant_dynamic-slice_fusion.28), channel_id=1, source_target_pairs={{0,12},{1,5},{4,8},{5,1},{8,4},{9,13},{12,0},{13,9},{2,14},{3,7},{... | collective-permute-start | bytes 49160 | tf_op jit(solution)/shard_map/ppermute | solution.py:83
  261.5 5.0 %collective-permute-start.22 = (f32[32,128]{1,0:T(8,128)S(1)}, f32[32,128]{1,0:T(8,128)S(1)}, u32[]{:S(2)}, u32[]{:S(2)}) collective-permute-start(f32[32,128]{1,0:T(8,128)S(1)} %constant_dynamic-slice_fusion.21), channel_id=1, source_target_pairs={{0,66},{1,3},{2,64},{3,1},{64,2},{65,67},{66,0},{67,65},{4,70},{5,... | collective-permute-start | bytes 49160 | tf_op jit(solution)/shard_map/ppermute | solution.py:83
  (18 other events, 20.5 us)

commit v2 on v1

v2 whole, which is shorter than its diff:
```python
import functools

import jax
import jax.numpy as jnp
import numpy as np
from jax import lax
from jax.experimental import pallas as pl
from jax.experimental.pallas import tpu as pltpu
from jax.sharding import Mesh
from jax.sharding import PartitionSpec as P

SUB = 3
BATCHES = 64
BX = ("bx_0", "bx_1")
BY = ("by_0", "by_1", "by_2")
CORE = "by_2"
AXES = {"x": ("by_0", CORE), "y": ("bx_0", "by_1", CORE), "z": ("bx_1", CORE)}
ORDERS = ("xyz", "yzx", "zxy")
DIGITS = ((0, 3, 1, 2), (0, 1, 2, 3))
RING = {
    1: [(2 * p + c, 2 * (p ^ 1 if c == 0 else 3 - p) + c) for p in range(4) for c in range(2)],
    2: [(2 * p + c, 2 * (3 - p if c == 0 else p ^ 1) + c) for p in range(4) for c in range(2)],
}
PAIR = [(0, 1), (1, 0)]


def extended(cells, sides, width):
    for axis, dim in sides:
        count = lax.axis_size(axis)
        ends = count - 1
        head = lax.slice_in_dim(cells, 0, width, axis=dim)
        tail = lax.slice_in_dim(cells, cells.shape[dim] - width, cells.shape[dim], axis=dim)
        cells = jnp.concatenate(
            [
                lax.ppermute(tail, axis, [(i, (i + 1) % count) for i in range(ends)]),
                cells,
                lax.ppermute(head, axis, [((i + 1) % count, i) for i in range(ends)]),
            ],
            axis=dim,
        )
    return cells


def advance(padded, kap, sxx, syy):
    centre = padded[:, 1:-1, 1:-1]
    east = padded[:, 2:, 1:-1]
    west = padded[:, :-2, 1:-1]
    north = padded[:, 1:-1, 2:]
    south = padded[:, 1:-1, :-2]
    return (
        centre
        + kap * (east + west + north + south - 4.0 * centre)
        - 0.5 * sxx * (east - west)
        - 0.5 * syy * (north - south)
    )


def position(axis):
    if axis == "y":
        return lax.axis_index("bx_0") * 2 + lax.axis_index("by_1")
    return lax.axis_index("by_0" if axis == "x" else "bx_1")


def ring_places():
    core = lax.axis_index(CORE)
    places = {}
    for axis in "xyz":
        at = position(axis)
        folded = jnp.where(at == 0, 0, jnp.where(at == 3, 1, at + 1))
        places[axis] = jnp.where(core == 0, folded, at)
    return places


def half_of(rows, bit):
    size = rows.shape[0] // 2
    return lax.dynamic_slice_in_dim(rows, bit * size, size, 0)


def ring_bits(places, axis):
    return (places[axis] // 2, places[axis] % 2)


def along_axis(mine, axis, places, riding=None):
    for turn, bit in enumerate(ring_bits(places, axis)):
        size = mine.shape[0] // 2
        leaving = half_of(mine, 1 - bit)
        if riding is not None:
            leaving = jnp.concatenate([leaving, riding], axis=0)
        coming = lax.ppermute(leaving, AXES[axis], RING[turn + 1])
        mine = half_of(mine, bit) + coming[:size]
        if riding is not None:
            riding = riding + coming[size:]
    return mine, riding


def scatter_sums(first, second, tile, places):
    from_core = [lax.ppermute(sent, CORE, PAIR) for _, sent in (first, second)]
    rows = first[0].shape[0] // len(ORDERS)
    riding = tile + from_core[0][first[0].shape[0] :]
    parts = []
    for (kept, _), received in zip((first, second), from_core):
        streams = []
        for stream, order in enumerate(ORDERS):
            at = slice(stream * rows, (stream + 1) * rows)
            carries = stream == 0 and kept is first[0]
            mine, carried = along_axis(
                kept[at] + received[at], order[0], places, riding if carries else None
            )
            riding = carried if carries else riding
            streams.append(mine)
        parts.append(streams)
    done = []
    riding = jnp.concatenate([riding, riding], axis=1)
    for stream, order in enumerate(ORDERS):
        mine = jnp.concatenate([parts[0][stream], parts[1][stream]], axis=1)
        for axis in order[1:]:
            mine, carried = along_axis(mine, axis, places, riding if stream == 0 else None)
            riding = carried if stream == 0 else riding
        done.append(mine)
    width = parts[0][0].shape[1]
    return (
        jnp.concatenate([d[:, :width] for d in done], axis=1),
        jnp.concatenate([d[:, width:] for d in done], axis=1),
        riding,
    )


def ring_rows():
    table = np.zeros((2, len(ORDERS), 64), np.int32)
    for core in range(2):
        for block in range(64):
            y_hi, z, x, y_lo = block // 32, block // 8 % 4, block // 2 % 4, block % 2
            at = {"x": x, "y": 2 * y_hi + y_lo, "z": z}
            for stream, order in enumerate(ORDERS):
                spot = 0
                for axis in order:
                    spot = spot * 4 + DIGITS[core].index(at[axis])
                table[core, stream, block] = (stream * 64 + spot) * 32
    return table.reshape(-1)


def put_rows(core_ref, table_ref, source_ref, base, right, kept_ref, sent_ref):
    core = core_ref[0]
    for slot, out_ref in enumerate((kept_ref, sent_ref)):
        digit = core if slot == 0 else 1 - core
        left = source_ref[:, digit].reshape(256, source_ref.shape[-1])
        sums = jnp.dot(left, right, preferred_element_type=jnp.float32)
        for block in range(8):
            for stream in range(3):
                row = table_ref[digit * 192 + stream * 64 + base + block]
                out_ref[pl.ds(pl.multiple_of(row, 32), 32), :] = sums[
                    block * 32 : (block + 1) * 32, stream * 128 : (stream + 1) * 128
                ]


def forward_kernel(
    scale, core_ref, table_ref, x_ref, win_ref, wout_t_ref, target_ref, mask_ref, batch_ref, field_ref,
    new_ref, slope_ref, dtend_ref, kept_ref, sent_ref, loss_ref, hidden_ref, tend_ref, right_ref,
):
    step = pl.program_id(0)

    @pl.when(step == 0)
    def _():
        tend_ref[...] = jnp.zeros_like(tend_ref)

    for part in range(2):
        rows = slice(part * 256, (part + 1) * 256)
        pre = jnp.dot(win_ref[rows, :], x_ref[...], preferred_element_type=jnp.float32)
        sig = 0.5 * jnp.tanh(0.5 * pre) + 0.5
        act = pre * sig
        slope_ref[rows, :] = sig + act * (1.0 - sig)
        hid = act.astype(jnp.bfloat16)
        hidden_ref[pl.ds(step * 8 + part * 4, 4)] = hid.reshape(4, 2, 32, hid.shape[-1])
        tend_ref[...] += jnp.dot(wout_t_ref[:, rows], hid, preferred_element_type=jnp.float32)

    @pl.when(step == pl.num_programs(0) - 1)
    def _():
        tend = tend_ref[...]
        mask = mask_ref[...].astype(jnp.float32)
        err = mask * (tend - target_ref[...].astype(jnp.float32))
        new_ref[...] = field_ref[...] + 0.5 * (mask * tend)
        persq = 0.5 * jnp.sum(err * err, axis=0, keepdims=True)
        batch = lax.broadcasted_iota(jnp.int32, (128, persq.shape[1]), 0)
        onehot = (batch == batch_ref[...]).astype(jnp.float32)
        loss = lax.dot_general(
            jnp.broadcast_to(persq, (8, persq.shape[1])),
            onehot,
            (((1,), (1,)), ((), ())),
            precision=lax.Precision.HIGHEST,
            preferred_element_type=jnp.float32,
        ) * scale[0]
        loss_ref[...] = loss
        sent_ref[pl.ds(kept_ref.shape[0], 8), :] = loss
        dtend = (err * scale[1]).astype(jnp.bfloat16)
        dtend_ref[...] = dtend
        right_ref[...] = dtend.T

        @pl.loop(0, 8)
        def _(piece):
            put_rows(
                core_ref, table_ref, hidden_ref.at[pl.ds(piece * 8, 8)], piece * 8, right_ref[...], kept_ref, sent_ref
            )


def backward_kernel(core_ref, table_ref, x_ref, wout_ref, slope_ref, dtend_ref, kept_ref, sent_ref, dpre_ref, right_ref):
    step = pl.program_id(0)

    @pl.when(step == 0)
    def _():
        right_ref[...] = x_ref[...].T

    for part in range(2):
        rows = slice(part * 256, (part + 1) * 256)
        dhid = jnp.dot(wout_ref[rows, :], dtend_ref[...], preferred_element_type=jnp.float32)
        dpre = (dhid * slope_ref[rows, :]).astype(jnp.bfloat16)
        dpre_ref[part * 4 : (part + 1) * 4] = dpre.reshape(4, 2, 32, dpre.shape[-1])
    put_rows(core_ref, table_ref, dpre_ref, step * 8, right_ref[...], kept_ref, sent_ref)


def whole(shape):
    return pl.BlockSpec(shape, lambda i, *_: (0,) * len(shape))


def network(x, field, target, mask, batch, w_in_t, w_out, total):
    feats, cols = x.shape
    hid = w_out.shape[0]
    core = lax.axis_index(CORE).astype(jnp.int32).reshape(1)
    table = jnp.asarray(ring_rows())
    rows = 3 * 2048
    f32, bf16 = jnp.float32, jnp.bfloat16
    new, slope, dtend, kept, sent, tile = pl.pallas_call(
        functools.partial(forward_kernel, (BATCHES / (total * feats), total ** (-0.5))),
        grid_spec=pltpu.PrefetchScalarGridSpec(
            num_scalar_prefetch=2,
            grid=(8,),
            in_specs=[
                whole((feats, cols)),
                pl.BlockSpec((512, feats), lambda i, *_: (i, 0)),
                pl.BlockSpec((feats, 512), lambda i, *_: (0, i)),
                whole((feats, cols)),
                whole((1, cols)),
                whole((1, cols)),
                whole((feats, cols)),
            ],
            out_specs=[
                whole((feats, cols)),
                pl.BlockSpec((512, cols), lambda i, *_: (i, 0)),
                whole((feats, cols)),
                whole((rows, 128)),
                whole((rows + 8, 128)),
                whole((8, 128)),
            ],
            scratch_shapes=[
                pltpu.VMEM((64, 2, 32, cols), bf16),
                pltpu.VMEM((feats, cols), f32),
                pltpu.VMEM((cols, feats), bf16),
            ],
        ),
        out_shape=[
            jax.ShapeDtypeStruct((feats, cols), f32),
            jax.ShapeDtypeStruct((hid, cols), f32),
            jax.ShapeDtypeStruct((feats, cols), bf16),
            jax.ShapeDtypeStruct((rows, 128), f32),
            jax.ShapeDtypeStruct((rows + 8, 128), f32),
            jax.ShapeDtypeStruct((8, 128), f32),
        ],
        compiler_params=pltpu.CompilerParams(
            dimension_semantics=("arbitrary",), vmem_limit_bytes=56 * 2**20
        ),
        cost_estimate=pl.CostEstimate(flops=6 * cols * feats * hid, bytes_accessed=30 * 2**20, transcendentals=cols * hid),
        name="forward",
    )(core, table, x, w_in_t, w_out.T, target, mask, batch, field)
    kept_in, sent_in = pl.pallas_call(
        backward_kernel,
        grid_spec=pltpu.PrefetchScalarGridSpec(
            num_scalar_prefetch=2,
            grid=(8,),
            in_specs=[
                whole((feats, cols)),
                pl.BlockSpec((512, feats), lambda i, *_: (i, 0)),
                pl.BlockSpec((512, cols), lambda i, *_: (i, 0)),
                whole((feats, cols)),
            ],
            out_specs=[whole((rows, 128)), whole((rows, 128))],
            scratch_shapes=[
                pltpu.VMEM((8, 2, 32, cols), bf16),
                pltpu.VMEM((cols, feats), bf16),
            ],
        ),
        out_shape=[jax.ShapeDtypeStruct((rows, 128), f32), jax.ShapeDtypeStruct((rows, 128), f32)],
        compiler_params=pltpu.CompilerParams(
            dimension_semantics=("arbitrary",), vmem_limit_bytes=32 * 2**20
        ),
        cost_estimate=pl.CostEstimate(flops=4 * cols * feats * hid, bytes_accessed=28 * 2**20, transcendentals=0),
        name="backward",
    )(core, table, x, w_out, slope, dtend)
    return new, (kept, sent), (kept_in, sent_in), tile


def on_device(state, target, land_mask, batch_map, diffusion, speed_x, speed_y, w_in, w_out):
    feats, rows_x, rows_y = state.shape
    kap = diffusion[:, None, None]
    sxx = speed_x[:, None, None]
    syy = speed_y[:, None, None]
    field = extended(state, ((BX, 1), (BY, 2)), SUB)
    for substep in range(SUB):
        field = advance(field, kap, sxx, syy)
        margin = SUB - substep - 1
        if margin > 0:
            along_x = (
                lax.axis_index(BX) * rows_x
                + jnp.arange(rows_x + 2 * margin, dtype=jnp.int32)
                - margin
            )
            along_y = (
                lax.axis_index(BY) * rows_y
                + jnp.arange(rows_y + 2 * margin, dtype=jnp.int32)
                - margin
            )
            inside_x = ((along_x >= 0) & (along_x < rows_x * lax.axis_size(BX))).astype(jnp.float32)
            inside_y = ((along_y >= 0) & (along_y < rows_y * lax.axis_size(BY))).astype(jnp.float32)
            field = field * inside_x[None, :, None] * inside_y[None, None, :]
    local_cols = rows_x * rows_y
    total = local_cols * lax.axis_size(BX) * lax.axis_size(BY)
    flat = field.reshape(feats, local_cols)
    new, first, second, tile = network(
        flat.astype(jnp.bfloat16),
        flat,
        target.reshape(feats, local_cols),
        land_mask.reshape(1, local_cols),
        batch_map.reshape(1, local_cols),
        w_in.T,
        w_out,
        total,
    )
    grad_out, grad_in, losses = scatter_sums(first, second, tile, ring_places())
    return (new.reshape(feats, rows_x, rows_y), grad_in, grad_out, losses[0, :BATCHES])


def solution(mesh):
    torus = Mesh(mesh.devices.reshape(2, 4, 4, 2, 2), BX + BY)
    return jax.shard_map(
        on_device,
        mesh=torus,
        in_specs=(P(None, BX, BY), P(None, BX, BY), P(BX, BY), P(BX, BY), P(), P(), P(), P(), P()),
        out_specs=(P(None, BX, BY), P(BX + BY, None), P(BX + BY, None), P()),
        check_vma=False,
    )
```

time: 272 us -> 171 us (0.63); the launches traced: 268 us -> 170 us
  local copies, waits for them, and re-layouts: 78 us -> 30.9 us
  matrix products: 44.5 us -> 0 us
  Pallas kernels: 0 us -> 43 us
  waiting for transfers between devices: 48.2 us -> 21.5 us
  starting transfers between devices: 66.7 us -> 55.3 us
  other arithmetic: 27.6 us -> 18.1 us
    dot_general x6 -> x0, matrix products: 44.5 us -> none  [the longest x1 13.2 us: on_device(): dhid = jnp.dot(dtend, w_out.T, preferred_element_type=jnp.float32)]
    pallas_call x0 -> x2, Pallas kernels: none -> 43 us  [the longest x1 27 us: network(): pl.pallas_call(functools.partial(forward_kernel, (BATCHES / (total * feat...]
    slice x48 -> x4, local copies, waits for them, and re-layouts: 32 us -> 0.02 us  [the longest x3 0.02 us: scatter_sums(): d[:, :width]]
    ppermute x45 -> x26, waiting for transfers between devices: 38 us -> 17.3 us  [the longest x24 14.6 us: along_axis(): coming = lax.ppermute(leaving, AXES[axis], RING[turn + 1])]
    reshape x2 -> x1, local copies, waits for them, and re-layouts: 20.6 us -> 3.02 us  [on_device(): flat = field.reshape(feats, local_cols)]
    ppermute x45 -> x26, starting transfers between devices: 58.1 us -> 46.5 us  [the longest x24 43.5 us: along_axis(): coming = lax.ppermute(leaving, AXES[axis], RING[turn + 1])]
    another operation x6 -> x0, other arithmetic: 7.68 us -> none  [in_ring_order(): both = jnp.stack(cores)]
    unnamed x58 -> x31, local copies, waits for them, and re-layouts: 12.8 us -> 19.6 us
  transfers between devices with their start and end apart: 49 -> 30, of which waited for: 22 -> 14; matrix products, arithmetic and copies ran while one was open for 11% -> 15% of each run, Pallas kernels for 0% -> 0%
where the time goes in v2:
time: 171 us; the launch traced here: 170 us
  starting transfers between devices  55.3 us (32%)
  Pallas kernels  43 us (25%)
  local copies, waits for them, and re-layouts  30.9 us (18%)
  waiting for transfers between devices  21.5 us (13%)
  other arithmetic  18.1 us (11%)
    ppermute x24, starting transfers between devices, along_axis(): coming = lax.ppermute(leaving, AXES[axis], RING[turn + 1])  43.5 us
    pallas_call x1, Pallas kernels, network(): pl.pallas_call(functools.partial(forward_kernel, (BATCHES / (total * feat...  27 us
    unnamed x31, local copies, waits for them, and re-layouts  19.6 us
    pallas_call x1, Pallas kernels, network(): pl.pallas_call(backward_kernel, grid_spec=pltpu.PrefetchScalarGridSpec(nu...  16 us
    ppermute x24, waiting for transfers between devices, along_axis(): coming = lax.ppermute(leaving, AXES[axis], RING[turn + 1])  14.6 us
    ppermute x2, starting transfers between devices, extended(): lax.ppermute(tail, axis, [(i, (i + 1) % count) for i in range(ends)])  6.03 us
    add x2, other arithmetic, scatter_sums(): kept[at] + received[at]  4.36 us
    ppermute x2, waiting for transfers between devices, extended(): lax.ppermute(head, axis, [((i + 1) % count, i) for i in range(ends)])  4.15 us
  transfers between devices with their start and end apart: 30, of which 14 were waited for; matrix products, arithmetic and copies ran while one was open for 15% of the time, Pallas kernels for 0%

profile of v2, /device:TPU:0, one launch (start us, length us, event | category | flops | bytes accessed | tf_op | source)
XLA Modules:
  0.0 170.0 jit_solution(16076009025133251058)
XLA Ops:
  0.6 2.3 %fusion.11 = (f32[384,3,128]{2,1,0:T(4,128)S(1)}, f32[384,3,128]{2,1,0:T(4,128)S(1)}) fusion(f32[384,8,128]{2,1,0:T(8,128)} %param.10), kind=kLoop, calls=%fused_computation.98 | loop fusion | bytes 2359296 | tf_op jit(solution)/shard_map/slice | solution.py:32
  2.9 0.9 copy.28
  3.8 4.7 %collective-permute-start = (f32[384,3,128]{2,0,1:T(8,128)}, f32[384,3,128]{2,0,1:T(8,128)}, u32[]{:S(2)}, u32[]{:S(2)}) collective-permute-start(f32[384,3,128]{2,0,1:T(8,128)} %copy.28), channel_id=1, source_target_pairs={{0,16},{16,32},{32,48},{48,64},{64,80},{80,96},{96,112},{1,17},{17... | collective-permute-start | bytes 1769480 | tf_op jit(solution)/shard_map/ppermute | solution.py:35
  8.6 0.9 copy.29
  9.4 1.3 collective-permute-start.1
  10.7 1.7 %copy.19 = f32[384,8,128]{0,1,2:T(8,128)} copy(f32[384,8,128]{2,1,0:T(8,128)S(1)} %copy-done.6) | data formatting | bytes 3145728 | tf_op args[0]
  12.4 4.8 %copy.25 = bf16[384,4096]{0,1:T(8,128)(2,1)} copy(bf16[384,4096]{1,0:T(8,128)(2,1)} %param.17) | data formatting | bytes 6291456 | tf_op args[7]
  17.2 3.0 %copy.26 = bf16[4096,384]{0,1:T(8,128)(2,1)} copy(bf16[4096,384]{1,0:T(8,128)(2,1)S(1)} %copy-done) | data formatting | bytes 6291456 | tf_op args[8]
  20.2 2.2 %copy.33 = bf16[48,8,8,128]{3,1,2,0:T(8,128)(2,1)} copy(bf16[48,8,8,128]{3,2,1,0:T(8,128)(2,1)} %bitcast.19) | data formatting | bytes 1572864
  22.5 2.2 %copy.18 = f32[384,3,128]{0,1,2:T(4,128)} copy(f32[384,3,128]{2,0,1:T(8,128)} %collective-permute-done) | data formatting | bytes 1179648 | tf_op jit(solution)/shard_map/ppermute | solution.py:35
  24.8 1.6 collective-permute-done.1
  26.4 2.2 %copy.20 = f32[384,3,128]{0,1,2:T(4,128)} copy(f32[384,3,128]{2,0,1:T(8,128)} %collective-permute-done.1) | data formatting | bytes 1179648 | tf_op jit(solution)/shard_map/ppermute | solution.py:37
  28.6 2.4 %pad_maximum_fusion = f32[384,14,128]{0,1,2:T(8,128)S(1)} fusion(f32[384,3,128]{0,1,2:T(4,128)} %copy.20, f32[384,8,128]{0,1,2:T(8,128)} %copy.19, f32[384,3,128]{0,1,2:T(4,128)} %copy.18), kind=kLoop, calls=%fused_computation | loop fusion | flops 1376256 | bytes 5505024 | tf_op jit(solution)/shard_map/concatenate | solution.py:33
  31.0 1.3 collective-permute-start.2
  32.3 1.5 collective-permute-start.3
  33.8 0.9 copy.22
  34.8 2.5 %collective-permute-done.3 = f32[384,14,3]{0,1,2:T(8,128)S(1)} collective-permute-done((f32[384,14,3]{0,1,2:T(8,128)S(1)}, f32[384,14,3]{0,1,2:T(8,128)S(1)}, u32[]{:S(2)}, u32[]{:S(2)}) %collective-permute-start.3) | collective-permute-done | bytes 64544 | tf_op jit(solution)/shard_map/ppermute | solution.py:37
  37.3 0.2 pad_maximum_fusion.1
  37.6 0.4 copy-done.8
  38.0 1.9 %multiply_multiply_fusion = f32[384,12,132]{0,2,1:T(8,128)S(1)} fusion(f32[384,14,134]{0,2,1:T(8,128)S(1)} %pad_maximum_fusion.1, f32[132]{0:T(256)S(1)} %and_convert_fusion.2, f32[12]{0:T(128)S(1)} %and_convert_fusion.3, f32[384]{0:T(512)S(1)} %get-tuple-element.36, f32[384]{0:T(512)S(1)} %get-tuple-element.37, f32[384]{0:T(512)S(1)} %copy-done.8), kind=kLoop, calls=%fused_computation.2 | loop fusion | flops 9123840 | bytes 14603328 | tf_op jit(solution)/shard_map/mul | solution.py:322
  40.0 1.3 multiply_multiply_fusion.1
  41.3 2.0 %multiply_subtract_fusion = f32[384,8,128]{0,2,1:T(8,128)} fusion(f32[384,10,130]{0,2,1:T(8,128)S(1)} %multiply_multiply_fusion.1, f32[384]{0:T(512)S(1)} %get-tuple-element.36, f32[384]{0:T(512)S(1)} %get-tuple-element.37, f32[384]{0:T(512)S(1)} %copy-done.8), kind=kLoop, calls=%fused_computation.4 | loop fusion | flops 5111808 | bytes 9441792 | tf_op jit(solution)/shard_map/sub | solution.py:51
  43.3 3.0 %copy.27.field_ref = f32[384,1024]{1,0:T(8,128)} copy(f32[384,1024]{0,1:T(8,128)} %bitcast.14) | data formatting | bytes 3145728 | tf_op jit(solution)/shard_map/reshape | solution.py:325
  46.3 2.4 %convert_element_type.35.x_ref = bf16[384,1024]{1,0:T(8,128)(2,1)} convert(f32[384,1024]{1,0:T(8,128)} %copy.27.field_ref) | non-fusion elementwise | flops 393216 | bytes 2359296 | tf_op jit(solution)/shard_map/convert_element_type | solution.py:327
  48.7 27.0 %forward.1 = (f32[384,1024]{1,0:T(8,128)}, f32[4096,1024]{1,0:T(8,128)}, bf16[384,1024]{1,0:T(8,128)(2,1)}, f32[6144,128]{1,0:T(8,128)}, f32[6152,128]{1,0:T(8,128)}, /*index=5*/f32[8,128]{1,0:T(8,128)}) custom-call(s32[1]{0:T(128)} %bitcast.core_ref, s32[384]{0:T(512)} %constant.148.clone.table_ref, bf16[384,1024]{1,0:T(8,128)(2,1)} %convert_element_type.35.x_ref, ...), custom_call_target="tpu_custom_call" | custom-call | flops 9663676416 | bytes 31457280 | tf_op jit(solution)/shard_map/forward/pallas_call | solution.py:231
  75.8 1.1 copy-done.5
  76.9 16.0 %backward.1 = (f32[6144,128]{1,0:T(8,128)S(1)}, f32[6144,128]{1,0:T(8,128)}) custom-call(s32[1]{0:T(128)} %bitcast.core_ref, s32[384]{0:T(512)S(1)} %copy-done.4, bf16[384,1024]{1,0:T(8,128)(2,1)S(1)} %copy-done.3, bf16[4096,384]{1,0:T(8,128)(2,1)S(1)} %copy-done, f32[4096,1024]{1,0:T(8,128)} %get-tuple-element.16.slope_ref, bf16[384,1024]{1,0:T(8,128)(2,1)S(1)} %copy-done.5), custom_call_target="tpu_custom_call" | custom-call | flops 6442450944 | bytes 29360128 | tf_op jit(solution)/shard_map/backward/pallas_call | solution.py:273
  92.9 1.7 copy-done.1
  94.6 3.0 %collective-permute-start.7 = (f32[6144,128]{1,0:T(8,128)}, f32[6144,128]{1,0:T(8,128)}, u32[]{:S(2)}, u32[]{:S(2)}) collective-permute-start(f32[6144,128]{1,0:T(8,128)} %get-tuple-element.19), channel_id=1, source_target_pairs={{0,1},{1,0},{2,3},{3,2},{4,5},{5,4},{6,7},{7,6},{8,9},{9,8},{10,11... | collective-permute-start | bytes 9437192 | tf_op jit(solution)/shard_map/ppermute | solution.py:97
  97.6 2.9 %copy.31 = f32[48,8,8,128]{3,2,1,0:T(8,128)} copy(f32[48,8,8,128]{3,1,2,0:T(8,128)} %bitcast.17) | data formatting | bytes 3145728
  100.5 2.7 %collective-permute-done.7 = f32[6144,128]{1,0:T(8,128)} collective-permute-done((f32[6144,128]{1,0:T(8,128)}, f32[6144,128]{1,0:T(8,128)}, u32[]{:S(2)}, u32[]{:S(2)}) %collective-permute-start.7) | collective-permute-done | bytes 3145760 | tf_op jit(solution)/shard_map/ppermute | solution.py:97
  103.2 2.2 %slice_add_fusion.4 = (f32[2048,128]{1,0:T(8,128)S(1)}, f32[2048,128]{1,0:T(8,128)S(1)}, f32[2048,128]{1,0:T(8,128)S(1)}) fusion(f32[6144,128]{1,0:T(8,128)} %collective-permute-done.7, f32[6144,128]{1,0:T(8,128)S(1)} %copy-done.2), kind=kLoop, calls=%fused_computation.9 | loop fusion | flops 786432 | bytes 9437184 | tf_op jit(solution)/shard_map/add | solution.py:107
  105.5 1.6 collective-permute-start.8
  107.1 2.3 %collective-permute-start.16 = (f32[1024,128]{1,0:T(8,128)S(1)}, f32[1024,128]{1,0:T(8,128)S(1)}, u32[]{:S(2)}, u32[]{:S(2)}) collective-permute-start(f32[1024,128]{1,0:T(8,128)S(1)} %constant_dynamic-slice_fusion.11), channel_id=1, source_target_pairs={{0,2},{1,67},{2,0},{3,65},{64,66},{65,3},{66,64},{67,1},{4,6},{5,7... | collective-permute-start | bytes 1572872 | tf_op jit(solution)/shard_map/ppermute | solution.py:89
  109.5 1.4 collective-permute-start.24
  110.9 2.2 %slice_add_fusion.5 = (f32[2048,128]{1,0:T(8,128)S(1)}, f32[2048,128]{1,0:T(8,128)S(1)}, f32[2048,128]{1,0:T(8,128)S(1)}) fusion(f32[6152,128]{1,0:T(8,128)} %collective-permute-done.4, f32[6144,128]{1,0:T(8,128)S(1)} %copy-done.7), kind=kLoop, calls=%fused_computation.10 | loop fusion | flops 786432 | bytes 9437184 | tf_op jit(solution)/shard_map/add | solution.py:107
  113.1 0.7 slice_add_fusion.16
  113.8 0.6 collective-permute-start.5
  114.7 1.1 collective-permute-start.22
  116.0 0.6 collective-permute-done.16
  116.6 2.2 %collective-permute-start.9 = (f32[512,128]{1,0:T(8,128)S(1)}, f32[512,128]{1,0:T(8,128)S(1)}, u32[]{:S(2)}, u32[]{:S(2)}) collective-permute-start(f32[512,128]{1,0:T(8,128)S(1)} %constant_dynamic-slice_fusion.17), channel_id=1, source_target_pairs={{0,12},{1,5},{4,8},{5,1},{8,4},{9,13},{12,0},{13,9},{2,14},{3,7},{... | collective-permute-start | bytes 786440 | tf_op jit(solution)/shard_map/ppermute | solution.py:89
  118.9 5.3 %collective-permute-start.17 = (f32[512,128]{1,0:T(8,128)S(1)}, f32[512,128]{1,0:T(8,128)S(1)}, u32[]{:S(2)}, u32[]{:S(2)}) collective-permute-start(f32[512,128]{1,0:T(8,128)S(1)} %constant_dynamic-slice_fusion.10), channel_id=1, source_target_pairs={{0,66},{1,3},{2,64},{3,1},{64,2},{65,67},{66,0},{67,65},{4,70},{5,... | collective-permute-start | bytes 786440 | tf_op jit(solution)/shard_map/ppermute | solution.py:89
  124.3 7.7 %collective-permute-start.25 = (f32[512,128]{1,0:T(8,128)S(1)}, f32[512,128]{1,0:T(8,128)S(1)}, u32[]{:S(2)}, u32[]{:S(2)}) collective-permute-start(f32[512,128]{1,0:T(8,128)S(1)} %constant_dynamic-slice_fusion.3), channel_id=1, source_target_pairs={{0,48},{1,17},{16,32},{17,1},{32,16},{33,49},{48,0},{49,33},{2,50}... | collective-permute-start | bytes 786440 | tf_op jit(solution)/shard_map/ppermute | solution.py:89
  132.7 2.0 %collective-permute-start.6 = (f32[520,128]{1,0:T(8,128)S(1)}, f32[520,128]{1,0:T(8,128)S(1)}, u32[]{:S(2)}, u32[]{:S(2)}) collective-permute-start(f32[520,128]{1,0:T(8,128)S(1)} %pad_maximum_fusion.3), channel_id=1, source_target_pairs={{0,12},{1,5},{4,8},{5,1},{8,4},{9,13},{12,0},{13,9},{2,14},{3,7},{... | collective-permute-start | bytes 798728 | tf_op jit(solution)/shard_map/ppermute | solution.py:89
  134.8 1.6 collective-permute-done.25
  136.4 3.4 %collective-permute-done.15 = f32[512,128]{1,0:T(8,128)S(1)} collective-permute-done((f32[512,128]{1,0:T(8,128)S(1)}, f32[512,128]{1,0:T(8,128)S(1)}, u32[]{:S(2)}, u32[]{:S(2)}) %collective-permute-start.15) | collective-permute-done | bytes 262176 | tf_op jit(solution)/shard_map/ppermute | solution.py:89
  139.8 0.5 collective-permute-start.18
  140.4 2.5 %collective-permute-start.26 = (f32[256,256]{1,0:T(8,128)S(1)}, f32[256,256]{1,0:T(8,128)S(1)}, u32[]{:S(2)}, u32[]{:S(2)}) collective-permute-start(f32[256,256]{1,0:T(8,128)S(1)} %fusion), channel_id=1, source_target_pairs={{0,4},{1,13},{4,0},{5,9},{8,12},{9,5},{12,8},{13,1},{2,6},{3,15},{... | collective-permute-start | bytes 786440 | tf_op jit(solution)/shard_map/ppermute | solution.py:89
  143.1 3.2 %collective-permute-done.18 = f32[256,256]{1,0:T(8,128)S(1)} collective-permute-done((f32[256,256]{1,0:T(8,128)S(1)}, f32[256,256]{1,0:T(8,128)S(1)}, u32[]{:S(2)}, u32[]{:S(2)}) %collective-permute-start.18) | collective-permute-done | bytes 262176 | tf_op jit(solution)/shard_map/ppermute | solution.py:89
  146.4 0.9 collective-permute-done.26
  147.4 2.0 %collective-permute-start.27 = (f32[128,256]{1,0:T(8,128)S(1)}, f32[128,256]{1,0:T(8,128)S(1)}, u32[]{:S(2)}, u32[]{:S(2)}) collective-permute-start(f32[128,256]{1,0:T(8,128)S(1)} %constant_dynamic-slice_fusion.2), channel_id=1, source_target_pairs={{0,12},{1,5},{4,8},{5,1},{8,4},{9,13},{12,0},{13,9},{2,14},{3,7},{... | collective-permute-start | bytes 393224 | tf_op jit(solution)/shard_map/ppermute | solution.py:89
  149.7 3.9 %collective-permute-start.11 = (f32[136,256]{1,0:T(8,128)S(1)}, f32[136,256]{1,0:T(8,128)S(1)}, u32[]{:S(2)}, u32[]{:S(2)}) collective-permute-start(f32[136,256]{1,0:T(8,128)S(1)} %pad_maximum_fusion.4), channel_id=1, source_target_pairs={{0,66},{1,3},{2,64},{3,1},{64,2},{65,67},{66,0},{67,65},{4,70},{5,... | collective-permute-start | bytes 417800 | tf_op jit(solution)/shard_map/ppermute | solution.py:89
  153.6 1.4 collective-permute-start.20
  155.0 0.5 collective-permute-start.28
  155.5 1.1 collective-permute-done.11
  156.7 0.6 collective-permute-start.12
  157.3 0.7 collective-permute-done.20
  158.0 2.1 %collective-permute-start.21 = (f32[32,256]{1,0:T(8,128)S(1)}, f32[32,256]{1,0:T(8,128)S(1)}, u32[]{:S(2)}, u32[]{:S(2)}) collective-permute-start(f32[32,256]{1,0:T(8,128)S(1)} %constant_dynamic-slice_fusion.7), channel_id=1, source_target_pairs={{0,12},{1,5},{4,8},{5,1},{8,4},{9,13},{12,0},{13,9},{2,14},{3,7},{... | collective-permute-start | bytes 98312 | tf_op jit(solution)/shard_map/ppermute | solution.py:89
  160.1 2.7 %collective-permute-start.29 = (f32[32,256]{1,0:T(8,128)S(1)}, f32[32,256]{1,0:T(8,128)S(1)}, u32[]{:S(2)}, u32[]{:S(2)}) collective-permute-start(f32[32,256]{1,0:T(8,128)S(1)} %constant_dynamic-slice_fusion), channel_id=1, source_target_pairs={{0,66},{1,3},{2,64},{3,1},{64,2},{65,67},{66,0},{67,65},{4,70},{5,... | collective-permute-start | bytes 98312 | tf_op jit(solution)/shard_map/ppermute | solution.py:89
  162.9 2.3 %collective-permute-start.13 = (f32[40,256]{1,0:T(8,128)S(1)}, f32[40,256]{1,0:T(8,128)S(1)}, u32[]{:S(2)}, u32[]{:S(2)}) collective-permute-start(f32[40,256]{1,0:T(8,128)S(1)} %pad_maximum_fusion.8), channel_id=1, source_target_pairs={{0,48},{1,17},{16,32},{17,1},{32,16},{33,49},{48,0},{49,33},{2,50}... | collective-permute-start | bytes 122888 | tf_op jit(solution)/shard_map/ppermute | solution.py:89
  165.3 2.9 %collective-permute-done.13 = f32[40,256]{1,0:T(8,128)S(1)} collective-permute-done((f32[40,256]{1,0:T(8,128)S(1)}, f32[40,256]{1,0:T(8,128)S(1)}, u32[]{:S(2)}, u32[]{:S(2)}) %collective-permute-start.13) | collective-permute-done | bytes 40992 | tf_op jit(solution)/shard_map/ppermute | solution.py:89
  168.2 0.5 fusion.9
  168.7 0.6 pad_maximum_fusion.7
  169.4 0.6 pad_maximum_fusion.6
  (117 shorter events, 2.6 us)
Async XLA Ops:
  0.6 10.1 %copy-start.6 = (f32[384,8,128]{2,1,0:T(8,128)S(1)}, f32[384,8,128]{2,1,0:T(8,128)}, u32[]{:S(2)}) copy-start(f32[384,8,128]{2,1,0:T(8,128)} %param.10) | copy-start | bytes 4718596
  3.8 18.7 %collective-permute-start = (f32[384,3,128]{2,0,1:T(8,128)}, f32[384,3,128]{2,0,1:T(8,128)}, u32[]{:S(2)}, u32[]{:S(2)}) collective-permute-start(f32[384,3,128]{2,0,1:T(8,128)} %copy.28), channel_id=1, source_target_pairs={{0,16},{16,32},{32,48},{48,64},{64,80},{80,96},{96,112},{1,17},{17... | collective-permute-start | bytes 1769480 | tf_op jit(solution)/shard_map/ppermute | solution.py:35
  9.4 17.0 %collective-permute-start.1 = (f32[384,3,128]{2,0,1:T(8,128)}, f32[384,3,128]{2,0,1:T(8,128)}, u32[]{:S(2)}, u32[]{:S(2)}) collective-permute-start(f32[384,3,128]{2,0,1:T(8,128)} %copy.29), channel_id=1, source_target_pairs={{16,0},{32,16},{48,32},{64,48},{80,64},{96,80},{112,96},{17,1},{33... | collective-permute-start | bytes 1769480 | tf_op jit(solution)/shard_map/ppermute | solution.py:37
  12.4 4.8 %copy-start = (bf16[4096,384]{1,0:T(8,128)(2,1)S(1)}, bf16[4096,384]{1,0:T(8,128)(2,1)}, u32[]{:S(2)}) copy-start(bf16[4096,384]{1,0:T(8,128)(2,1)} %wout_ref.1) | copy-start | bytes 9437188
  17.2 5.3 %copy-start.10 = (f32[384]{0:T(512)S(1)}, f32[384]{0:T(512)}, u32[]{:S(2)}) copy-start(f32[384]{0:T(512)} %param.16) | copy-start | bytes 4612
  17.2 5.3 %copy-start.11 = (f32[384]{0:T(512)S(1)}, f32[384]{0:T(512)}, u32[]{:S(2)}) copy-start(f32[384]{0:T(512)} %param.15) | copy-start | bytes 4612
  31.0 3.7 %collective-permute-start.2 = (f32[384,14,3]{0,1,2:T(8,128)S(1)}, f32[384,14,3]{0,1,2:T(8,128)S(1)}, u32[]{:S(2)}, u32[]{:S(2)}) collective-permute-start(f32[384,14,3]{0,1,2:T(8,128)S(1)} %get-tuple-element.26), channel_id=1, source_target_pairs={{0,1},{1,2},{2,3},{3,4},{4,5},{5,6},{6,7},{7,8},{8,9},{9,10},{10,1... | collective-permute-start | bytes 193544 | tf_op jit(solution)/shard_map/ppermute | solution.py:35
  32.3 5.0 %collective-permute-start.3 = (f32[384,14,3]{0,1,2:T(8,128)S(1)}, f32[384,14,3]{0,1,2:T(8,128)S(1)}, u32[]{:S(2)}, u32[]{:S(2)}) collective-permute-start(f32[384,14,3]{0,1,2:T(8,128)S(1)} %get-tuple-element.27), channel_id=1, source_target_pairs={{1,0},{2,1},{3,2},{4,3},{5,4},{6,5},{7,6},{8,7},{9,8},{10,9},{11,1... | collective-permute-start | bytes 193544 | tf_op jit(solution)/shard_map/ppermute | solution.py:37
  37.3 0.7 copy-start.8
  48.7 27.1 %copy-start.3 = (bf16[384,1024]{1,0:T(8,128)(2,1)S(1)}, bf16[384,1024]{1,0:T(8,128)(2,1)}, u32[]{:S(2)}) copy-start(bf16[384,1024]{1,0:T(8,128)(2,1)} %convert_element_type.35.x_ref) | copy-start | bytes 2359300
  48.7 27.1 %copy-start.4 = (s32[384]{0:T(512)S(1)}, s32[384]{0:T(512)}, u32[]{:S(2)}) copy-start(s32[384]{0:T(512)} %constant.148.clone.table_ref) | copy-start | bytes 4612
  75.8 1.1 copy-start.5
  92.9 1.7 copy-start.1
  94.6 8.6 %copy-start.2 = (f32[6144,128]{1,0:T(8,128)S(1)}, f32[6144,128]{1,0:T(8,128)}, u32[]{:S(2)}) copy-start(f32[6144,128]{1,0:T(8,128)} %copy-done.1) | copy-start | bytes 9437188
  94.6 8.6 %collective-permute-start.7 = (f32[6144,128]{1,0:T(8,128)}, f32[6144,128]{1,0:T(8,128)}, u32[]{:S(2)}, u32[]{:S(2)}) collective-permute-start(f32[6144,128]{1,0:T(8,128)} %get-tuple-element.19), channel_id=1, source_target_pairs={{0,1},{1,0},{2,3},{3,2},{4,5},{5,4},{6,7},{7,6},{8,9},{9,8},{10,11... | collective-permute-start | bytes 9437192 | tf_op jit(solution)/shard_map/ppermute | solution.py:97
  97.6 13.3 %collective-permute-start.4 = (f32[6152,128]{1,0:T(8,128)}, f32[6152,128]{1,0:T(8,128)}, u32[]{:S(2)}, u32[]{:S(2)}) collective-permute-start(f32[6152,128]{1,0:T(8,128)} %get-tuple-element.14), channel_id=1, source_target_pairs={{0,1},{1,0},{2,3},{3,2},{4,5},{5,4},{6,7},{7,6},{8,9},{9,8},{10,11... | collective-permute-start | bytes 9449480 | tf_op jit(solution)/shard_map/ppermute | solution.py:97
  105.4 5.5 %copy-start.7 = (f32[6144,128]{1,0:T(8,128)S(1)}, f32[6144,128]{1,0:T(8,128)}, u32[]{:S(2)}) copy-start(f32[6144,128]{1,0:T(8,128)} %get-tuple-element.13) | copy-start | bytes 9437188
  105.5 9.3 %collective-permute-start.8 = (f32[1024,128]{1,0:T(8,128)S(1)}, f32[1024,128]{1,0:T(8,128)S(1)}, u32[]{:S(2)}, u32[]{:S(2)}) collective-permute-start(f32[1024,128]{1,0:T(8,128)S(1)} %constant_dynamic-slice_fusion.18), channel_id=1, source_target_pairs={{0,4},{1,13},{4,0},{5,9},{8,12},{9,5},{12,8},{13,1},{2,6},{3,15},{... | collective-permute-start | bytes 1572872 | tf_op jit(solution)/shard_map/ppermute | solution.py:89
  107.1 9.5 %collective-permute-start.16 = (f32[1024,128]{1,0:T(8,128)S(1)}, f32[1024,128]{1,0:T(8,128)S(1)}, u32[]{:S(2)}, u32[]{:S(2)}) collective-permute-start(f32[1024,128]{1,0:T(8,128)S(1)} %constant_dynamic-slice_fusion.11), channel_id=1, source_target_pairs={{0,2},{1,67},{2,0},{3,65},{64,66},{65,3},{66,64},{67,1},{4,6},{5,7... | collective-permute-start | bytes 1572872 | tf_op jit(solution)/shard_map/ppermute | solution.py:89
  109.5 9.5 %collective-permute-start.24 = (f32[1024,128]{1,0:T(8,128)S(1)}, f32[1024,128]{1,0:T(8,128)S(1)}, u32[]{:S(2)}, u32[]{:S(2)}) collective-permute-start(f32[1024,128]{1,0:T(8,128)S(1)} %constant_dynamic-slice_fusion.4), channel_id=1, source_target_pairs={{0,16},{1,49},{16,0},{17,33},{32,48},{33,17},{48,32},{49,1},{2,18}... | collective-permute-start | bytes 1572872 | tf_op jit(solution)/shard_map/ppermute | solution.py:89
  110.9 2.2 %copy-start.9 = (f32[8,128]{1,0:T(8,128)S(1)}, f32[8,128]{1,0:T(8,128)}, u32[]{:S(2)}) copy-start(f32[8,128]{1,0:T(8,128)} %get-tuple-element.15) | copy-start | bytes 12292
  113.8 18.5 %collective-permute-start.5 = (f32[1032,128]{1,0:T(8,128)S(1)}, f32[1032,128]{1,0:T(8,128)S(1)}, u32[]{:S(2)}, u32[]{:S(2)}) collective-permute-start(f32[1032,128]{1,0:T(8,128)S(1)} %pad_maximum_fusion.2), channel_id=1, source_target_pairs={{0,4},{1,13},{4,0},{5,9},{8,12},{9,5},{12,8},{13,1},{2,6},{3,15},{... | collective-permute-start | bytes 1585160 | tf_op jit(solution)/shard_map/ppermute | solution.py:89
  114.5 9.8 %collective-permute-start.14 = (f32[1024,128]{1,0:T(8,128)S(1)}, f32[1024,128]{1,0:T(8,128)S(1)}, u32[]{:S(2)}, u32[]{:S(2)}) collective-permute-start(f32[1024,128]{1,0:T(8,128)S(1)} %constant_dynamic-slice_fusion.13), channel_id=1, source_target_pairs={{0,2},{1,67},{2,0},{3,65},{64,66},{65,3},{66,64},{67,1},{4,6},{5,7... | collective-permute-start | bytes 1572872 | tf_op jit(solution)/shard_map/ppermute | solution.py:89
  114.7 17.4 %collective-permute-start.22 = (f32[1024,128]{1,0:T(8,128)S(1)}, f32[1024,128]{1,0:T(8,128)S(1)}, u32[]{:S(2)}, u32[]{:S(2)}) collective-permute-start(f32[1024,128]{1,0:T(8,128)S(1)} %constant_dynamic-slice_fusion.6), channel_id=1, source_target_pairs={{0,16},{1,49},{16,0},{17,33},{32,48},{33,17},{48,32},{49,1},{2,18}... | collective-permute-start | bytes 1572872 | tf_op jit(solution)/shard_map/ppermute | solution.py:89
  116.6 16.1 %collective-permute-start.9 = (f32[512,128]{1,0:T(8,128)S(1)}, f32[512,128]{1,0:T(8,128)S(1)}, u32[]{:S(2)}, u32[]{:S(2)}) collective-permute-start(f32[512,128]{1,0:T(8,128)S(1)} %constant_dynamic-slice_fusion.17), channel_id=1, source_target_pairs={{0,12},{1,5},{4,8},{5,1},{8,4},{9,13},{12,0},{13,9},{2,14},{3,7},{... | collective-permute-start | bytes 786440 | tf_op jit(solution)/shard_map/ppermute | solution.py:89
  118.9 15.8 %collective-permute-start.17 = (f32[512,128]{1,0:T(8,128)S(1)}, f32[512,128]{1,0:T(8,128)S(1)}, u32[]{:S(2)}, u32[]{:S(2)}) collective-permute-start(f32[512,128]{1,0:T(8,128)S(1)} %constant_dynamic-slice_fusion.10), channel_id=1, source_target_pairs={{0,66},{1,3},{2,64},{3,1},{64,2},{65,67},{66,0},{67,65},{4,70},{5,... | collective-permute-start | bytes 786440 | tf_op jit(solution)/shard_map/ppermute | solution.py:89
  124.3 12.0 %collective-permute-start.25 = (f32[512,128]{1,0:T(8,128)S(1)}, f32[512,128]{1,0:T(8,128)S(1)}, u32[]{:S(2)}, u32[]{:S(2)}) collective-permute-start(f32[512,128]{1,0:T(8,128)S(1)} %constant_dynamic-slice_fusion.3), channel_id=1, source_target_pairs={{0,48},{1,17},{16,32},{17,1},{32,16},{33,49},{48,0},{49,33},{2,50}... | collective-permute-start | bytes 786440 | tf_op jit(solution)/shard_map/ppermute | solution.py:89
  132.1 7.7 %collective-permute-start.15 = (f32[512,128]{1,0:T(8,128)S(1)}, f32[512,128]{1,0:T(8,128)S(1)}, u32[]{:S(2)}, u32[]{:S(2)}) collective-permute-start(f32[512,128]{1,0:T(8,128)S(1)} %constant_dynamic-slice_fusion.12), channel_id=1, source_target_pairs={{0,66},{1,3},{2,64},{3,1},{64,2},{65,67},{66,0},{67,65},{4,70},{5,... | collective-permute-start | bytes 786440 | tf_op jit(solution)/shard_map/ppermute | solution.py:89
  132.3 8.0 %collective-permute-start.23 = (f32[512,128]{1,0:T(8,128)S(1)}, f32[512,128]{1,0:T(8,128)S(1)}, u32[]{:S(2)}, u32[]{:S(2)}) collective-permute-start(f32[512,128]{1,0:T(8,128)S(1)} %constant_dynamic-slice_fusion.5), channel_id=1, source_target_pairs={{0,48},{1,17},{16,32},{17,1},{32,16},{33,49},{48,0},{49,33},{2,50}... | collective-permute-start | bytes 786440 | tf_op jit(solution)/shard_map/ppermute | solution.py:89
  132.7 10.3 %collective-permute-start.6 = (f32[520,128]{1,0:T(8,128)S(1)}, f32[520,128]{1,0:T(8,128)S(1)}, u32[]{:S(2)}, u32[]{:S(2)}) collective-permute-start(f32[520,128]{1,0:T(8,128)S(1)} %pad_maximum_fusion.3), channel_id=1, source_target_pairs={{0,12},{1,5},{4,8},{5,1},{8,4},{9,13},{12,0},{13,9},{2,14},{3,7},{... | collective-permute-start | bytes 798728 | tf_op jit(solution)/shard_map/ppermute | solution.py:89
  139.8 6.5 %collective-permute-start.18 = (f32[256,256]{1,0:T(8,128)S(1)}, f32[256,256]{1,0:T(8,128)S(1)}, u32[]{:S(2)}, u32[]{:S(2)}) collective-permute-start(f32[256,256]{1,0:T(8,128)S(1)} %fusion.3), channel_id=1, source_target_pairs={{0,16},{1,49},{16,0},{17,33},{32,48},{33,17},{48,32},{49,1},{2,18}... | collective-permute-start | bytes 786440 | tf_op jit(solution)/shard_map/ppermute | solution.py:89
  140.4 7.0 %collective-permute-start.26 = (f32[256,256]{1,0:T(8,128)S(1)}, f32[256,256]{1,0:T(8,128)S(1)}, u32[]{:S(2)}, u32[]{:S(2)}) collective-permute-start(f32[256,256]{1,0:T(8,128)S(1)} %fusion), channel_id=1, source_target_pairs={{0,4},{1,13},{4,0},{5,9},{8,12},{9,5},{12,8},{13,1},{2,6},{3,15},{... | collective-permute-start | bytes 786440 | tf_op jit(solution)/shard_map/ppermute | solution.py:89
  143.0 6.5 %collective-permute-start.10 = (f32[264,256]{1,0:T(8,128)S(1)}, f32[264,256]{1,0:T(8,128)S(1)}, u32[]{:S(2)}, u32[]{:S(2)}) collective-permute-start(f32[264,256]{1,0:T(8,128)S(1)} %maximum_maximum_fusion), channel_id=1, source_target_pairs={{0,2},{1,67},{2,0},{3,65},{64,66},{65,3},{66,64},{67,1},{4,6},{5,7... | collective-permute-start | bytes 811016 | tf_op jit(solution)/shard_map/ppermute | solution.py:89
  146.4 7.2 %collective-permute-start.19 = (f32[128,256]{1,0:T(8,128)S(1)}, f32[128,256]{1,0:T(8,128)S(1)}, u32[]{:S(2)}, u32[]{:S(2)}) collective-permute-start(f32[128,256]{1,0:T(8,128)S(1)} %constant_dynamic-slice_fusion.9), channel_id=1, source_target_pairs={{0,48},{1,17},{16,32},{17,1},{32,16},{33,49},{48,0},{49,33},{2,50}... | collective-permute-start | bytes 393224 | tf_op jit(solution)/shard_map/ppermute | solution.py:89
  147.4 7.5 %collective-permute-start.27 = (f32[128,256]{1,0:T(8,128)S(1)}, f32[128,256]{1,0:T(8,128)S(1)}, u32[]{:S(2)}, u32[]{:S(2)}) collective-permute-start(f32[128,256]{1,0:T(8,128)S(1)} %constant_dynamic-slice_fusion.2), channel_id=1, source_target_pairs={{0,12},{1,5},{4,8},{5,1},{8,4},{9,13},{12,0},{13,9},{2,14},{3,7},{... | collective-permute-start | bytes 393224 | tf_op jit(solution)/shard_map/ppermute | solution.py:89
  149.7 6.9 %collective-permute-start.11 = (f32[136,256]{1,0:T(8,128)S(1)}, f32[136,256]{1,0:T(8,128)S(1)}, u32[]{:S(2)}, u32[]{:S(2)}) collective-permute-start(f32[136,256]{1,0:T(8,128)S(1)} %pad_maximum_fusion.4), channel_id=1, source_target_pairs={{0,66},{1,3},{2,64},{3,1},{64,2},{65,67},{66,0},{67,65},{4,70},{5,... | collective-permute-start | bytes 417800 | tf_op jit(solution)/shard_map/ppermute | solution.py:89
  153.6 4.3 %collective-permute-start.20 = (f32[64,256]{1,0:T(8,128)S(1)}, f32[64,256]{1,0:T(8,128)S(1)}, u32[]{:S(2)}, u32[]{:S(2)}) collective-permute-start(f32[64,256]{1,0:T(8,128)S(1)} %constant_dynamic-slice_fusion.8), channel_id=1, source_target_pairs={{0,4},{1,13},{4,0},{5,9},{8,12},{9,5},{12,8},{13,1},{2,6},{3,15},{... | collective-permute-start | bytes 196616 | tf_op jit(solution)/shard_map/ppermute | solution.py:89
  155.0 5.1 %collective-permute-start.28 = (f32[64,256]{1,0:T(8,128)S(1)}, f32[64,256]{1,0:T(8,128)S(1)}, u32[]{:S(2)}, u32[]{:S(2)}) collective-permute-start(f32[64,256]{1,0:T(8,128)S(1)} %constant_dynamic-slice_fusion.1), channel_id=1, source_target_pairs={{0,2},{1,67},{2,0},{3,65},{64,66},{65,3},{66,64},{67,1},{4,6},{5,7... | collective-permute-start | bytes 196616 | tf_op jit(solution)/shard_map/ppermute | solution.py:89
  156.7 6.2 %collective-permute-start.12 = (f32[72,256]{1,0:T(8,128)S(1)}, f32[72,256]{1,0:T(8,128)S(1)}, u32[]{:S(2)}, u32[]{:S(2)}) collective-permute-start(f32[72,256]{1,0:T(8,128)S(1)} %pad_maximum_fusion.5), channel_id=1, source_target_pairs={{0,16},{1,49},{16,0},{17,33},{32,48},{33,17},{48,32},{49,1},{2,18}... | collective-permute-start | bytes 221192 | tf_op jit(solution)/shard_map/ppermute | solution.py:89
  158.0 7.2 %collective-permute-start.21 = (f32[32,256]{1,0:T(8,128)S(1)}, f32[32,256]{1,0:T(8,128)S(1)}, u32[]{:S(2)}, u32[]{:S(2)}) collective-permute-start(f32[32,256]{1,0:T(8,128)S(1)} %constant_dynamic-slice_fusion.7), channel_id=1, source_target_pairs={{0,12},{1,5},{4,8},{5,1},{8,4},{9,13},{12,0},{13,9},{2,14},{3,7},{... | collective-permute-start | bytes 98312 | tf_op jit(solution)/shard_map/ppermute | solution.py:89
  160.1 5.2 %collective-permute-start.29 = (f32[32,256]{1,0:T(8,128)S(1)}, f32[32,256]{1,0:T(8,128)S(1)}, u32[]{:S(2)}, u32[]{:S(2)}) collective-permute-start(f32[32,256]{1,0:T(8,128)S(1)} %constant_dynamic-slice_fusion), channel_id=1, source_target_pairs={{0,66},{1,3},{2,64},{3,1},{64,2},{65,67},{66,0},{67,65},{4,70},{5,... | collective-permute-start | bytes 98312 | tf_op jit(solution)/shard_map/ppermute | solution.py:89
  162.9 5.3 %collective-permute-start.13 = (f32[40,256]{1,0:T(8,128)S(1)}, f32[40,256]{1,0:T(8,128)S(1)}, u32[]{:S(2)}, u32[]{:S(2)}) collective-permute-start(f32[40,256]{1,0:T(8,128)S(1)} %pad_maximum_fusion.8), channel_id=1, source_target_pairs={{0,48},{1,17},{16,32},{17,1},{32,16},{33,49},{48,0},{49,33},{2,50}... | collective-permute-start | bytes 122888 | tf_op jit(solution)/shard_map/ppermute | solution.py:89

commit v3 on v1

v3 whole, which is shorter than its diff:
```python
import functools

import jax
import jax.numpy as jnp
import numpy as np
from jax import lax
from jax.experimental import pallas as pl
from jax.experimental.pallas import tpu as pltpu
from jax.sharding import Mesh
from jax.sharding import PartitionSpec as P

SUB = 3
BATCHES = 64
FEW = 640
BX = ("bx_0", "bx_1")
BY = ("by_0", "by_1", "by_2")
CORE = "by_2"
AXES = {"x": ("by_0", CORE), "y": ("bx_0", "by_1", CORE), "z": ("bx_1", CORE)}
ORDERS = ("xyz", "yzx", "zxy")
DIGITS = ((0, 3, 1, 2), (0, 1, 2, 3))
RING = {
    1: [(2 * p + c, 2 * (p ^ 1 if c == 0 else 3 - p) + c) for p in range(4) for c in range(2)],
    2: [(2 * p + c, 2 * (3 - p if c == 0 else p ^ 1) + c) for p in range(4) for c in range(2)],
}
PAIR = [(0, 1), (1, 0)]


def extended(cells, sides, width):
    for axis, dim in sides:
        count = lax.axis_size(axis)
        ends = count - 1
        head = lax.slice_in_dim(cells, 0, width, axis=dim)
        tail = lax.slice_in_dim(cells, cells.shape[dim] - width, cells.shape[dim], axis=dim)
        cells = jnp.concatenate(
            [
                lax.ppermute(tail, axis, [(i, (i + 1) % count) for i in range(ends)]),
                cells,
                lax.ppermute(head, axis, [((i + 1) % count, i) for i in range(ends)]),
            ],
            axis=dim,
        )
    return cells


def advance(padded, kap, sxx, syy):
    centre = padded[:, 1:-1, 1:-1]
    east = padded[:, 2:, 1:-1]
    west = padded[:, :-2, 1:-1]
    north = padded[:, 1:-1, 2:]
    south = padded[:, 1:-1, :-2]
    return (
        centre
        + kap * (east + west + north + south - 4.0 * centre)
        - 0.5 * sxx * (east - west)
        - 0.5 * syy * (north - south)
    )


def position(axis):
    if axis == "y":
        return lax.axis_index("bx_0") * 2 + lax.axis_index("by_1")
    return lax.axis_index("by_0" if axis == "x" else "bx_1")


def ring_places():
    core = lax.axis_index(CORE)
    places = {}
    for axis in "xyz":
        at = position(axis)
        folded = jnp.where(at == 0, 0, jnp.where(at == 3, 1, at + 1))
        places[axis] = jnp.where(core == 0, folded, at)
    return places


def half_of(rows, bit):
    size = rows.shape[0] // 2
    return lax.dynamic_slice_in_dim(rows, bit * size, size, 0)


def ring_bits(places, axis):
    return (places[axis] // 2, places[axis] % 2)


def ring_turn(mine, axis, turn, places, riding=None):
    bit = places[axis] % 2 if turn else places[axis] // 2
    size = mine.shape[0] // 2
    leaving = half_of(mine, 1 - bit)
    if riding is not None:
        leaving = jnp.concatenate([leaving, riding], axis=0)
    coming = lax.ppermute(leaving, AXES[axis], RING[turn + 1])
    mine = half_of(mine, bit) + coming[:size]
    return mine, (None if riding is None else riding + coming[size:])


def ring_round(streams, stage, turn, places, riding=None):
    moved = []
    for stream, order in enumerate(ORDERS):
        mine, carried = ring_turn(
            streams[stream], order[stage], turn, places, riding if stream == 0 else None
        )
        riding = carried if stream == 0 else riding
        moved.append(mine)
    return moved, riding


def core_sums(kept, received):
    rows = kept.shape[0] // len(ORDERS)
    return [
        kept[stream * rows : (stream + 1) * rows] + received[stream * rows : (stream + 1) * rows]
        for stream in range(len(ORDERS))
    ]


def ring_rows():
    table = np.zeros((2, len(ORDERS), 64), np.int32)
    for core in range(2):
        for block in range(64):
            y_hi, z, x, y_lo = block // 32, block // 8 % 4, block // 2 % 4, block % 2
            at = {"x": x, "y": 2 * y_hi + y_lo, "z": z}
            for stream, order in enumerate(ORDERS):
                spot = 0
                for axis in order:
                    spot = spot * 4 + DIGITS[core].index(at[axis])
                table[core, stream, block] = (stream * 64 + spot) * 32
    return table.reshape(-1)


def put_rows(scalar_ref, table_ref, source_ref, base, right, kept_ref, sent_ref):
    core = scalar_ref[0]
    for slot, out_ref in enumerate((kept_ref, sent_ref)):
        digit = core if slot == 0 else 1 - core
        left = source_ref[:, digit, :, : right.shape[0]].reshape(256, right.shape[0])
        sums = jnp.dot(left, right, preferred_element_type=jnp.float32)
        for block in range(8):
            for stream in range(3):
                row = table_ref[digit * 192 + stream * 64 + base + block]
                out_ref[pl.ds(pl.multiple_of(row, 32), 32), :] = sums[
                    block * 32 : (block + 1) * 32, stream * 128 : (stream + 1) * 128
                ]


def by_width(scalar_ref, most, body):
    land = scalar_ref[1]
    pl.when(land <= FEW)(functools.partial(body, FEW))
    pl.when(land > FEW)(functools.partial(body, most))


ROWS = (((1,), (1,)), ((), ()))


def forward_kernel(
    scale, scalar_ref, table_ref, x_ref, win_ref, wout_t_ref, target_ref, rank_ref, batch_ref, field_ref,
    new_ref, slope_ref, dtend_ref, xn_ref, kept_ref, sent_ref, hidden_ref, tend_ref, right_ref, pick_ref, xc_ref,
):
    step = pl.program_id(0)
    cols = x_ref.shape[1]

    def start(n):
        for at in range(0, n, 128):
            slot = lax.broadcasted_iota(jnp.int32, (128, cols), 0) + at
            pick_ref[at : at + 128, :] = jnp.where(slot == rank_ref[...], 1.0, 0.0).astype(jnp.bfloat16)
        packed = lax.dot_general(x_ref[...], pick_ref[:n, :], ROWS, preferred_element_type=jnp.float32)
        packed = packed.astype(jnp.bfloat16)
        xc_ref[:, :n] = packed
        xn_ref[:n, :] = packed.T
        tend_ref[:, :n] = jnp.zeros((tend_ref.shape[0], n), jnp.float32)

    def run(n):
        for part in range(2):
            rows = slice(part * 256, (part + 1) * 256)
            pre = jnp.dot(win_ref[rows, :], xc_ref[:, :n], preferred_element_type=jnp.float32)
            sig = 0.5 * jnp.tanh(0.5 * pre) + 0.5
            act = pre * sig
            slope_ref[rows, :n] = sig + act * (1.0 - sig)
            hid = act.astype(jnp.bfloat16)
            hidden_ref[pl.ds(step * 8 + part * 4, 4), :, :, :n] = hid.reshape(4, 2, 32, n)
            tend_ref[:, :n] += jnp.dot(wout_t_ref[:, rows], hid, preferred_element_type=jnp.float32)

    def finish(n):
        pick = pick_ref[:n, :]
        tend = tend_ref[:, :n]
        wanted = lax.dot_general(target_ref[...], pick, ROWS, preferred_element_type=jnp.float32)
        err = tend - wanted
        coarse = tend.astype(jnp.bfloat16)
        fine = (tend - coarse.astype(jnp.float32)).astype(jnp.bfloat16)
        spread = jnp.dot(coarse, pick, preferred_element_type=jnp.float32)
        spread += jnp.dot(fine, pick, preferred_element_type=jnp.float32)
        new_ref[...] = field_ref[...] + 0.5 * spread
        persq = 0.5 * jnp.sum(err * err, axis=0, keepdims=True)
        batch = lax.dot_general(batch_ref[...], pick, ROWS, preferred_element_type=jnp.float32)
        which = lax.broadcasted_iota(jnp.int32, (128, n), 0).astype(jnp.float32)
        onehot = jnp.where(which == batch[0:1, :], 1.0, 0.0)
        sent_ref[pl.ds(kept_ref.shape[0], 8), :] = scale[0] * lax.dot_general(
            jnp.broadcast_to(persq, (8, n)),
            onehot,
            ROWS,
            precision=lax.Precision.HIGHEST,
            preferred_element_type=jnp.float32,
        )
        dtend = (err * scale[1]).astype(jnp.bfloat16)
        dtend_ref[:, :n] = dtend
        right_ref[:n, :] = dtend.T

        @pl.loop(0, 8)
        def _(piece):
            put_rows(
                scalar_ref, table_ref, hidden_ref.at[pl.ds(piece * 8, 8)], piece * 8, right_ref[:n, :], kept_ref, sent_ref
            )

    pl.when(step == 0)(lambda: by_width(scalar_ref, cols, start))
    by_width(scalar_ref, cols, run)
    pl.when(step == pl.num_programs(0) - 1)(lambda: by_width(scalar_ref, cols, finish))


def dpre_kernel(scalar_ref, wout_ref, slope_ref, dtend_ref, dpre_ref):
    def run(n):
        for part in range(2):
            rows = slice(part * 256, (part + 1) * 256)
            dhid = jnp.dot(wout_ref[rows, :], dtend_ref[:, :n], preferred_element_type=jnp.float32)
            dpre = (dhid * slope_ref[rows, :n]).astype(jnp.bfloat16)
            dpre_ref[part * 4 : (part + 1) * 4, :, :, :n] = dpre.reshape(4, 2, 32, n)

    by_width(scalar_ref, dtend_ref.shape[1], run)


def grad_kernel(scalar_ref, table_ref, dpre_ref, xn_ref, kept_ref, sent_ref):
    base = pl.program_id(0) * 8

    def run(n):
        put_rows(scalar_ref, table_ref, dpre_ref, base, xn_ref[:n, :], kept_ref, sent_ref)

    by_width(scalar_ref, xn_ref.shape[0], run)


def whole(*shape):
    return pl.BlockSpec(shape, lambda i, *_: (0,) * len(shape))


def shaped(dtype, *shape):
    return jax.ShapeDtypeStruct(shape, dtype)


def params(megabytes):
    return pltpu.CompilerParams(dimension_semantics=("arbitrary",), vmem_limit_bytes=megabytes * 2**20)


def land_ranks(mask):
    rows, cols = mask.shape
    ones = mask.astype(jnp.float32)
    before = jnp.triu(jnp.ones((cols, cols), jnp.float32), 1)
    within = jnp.dot(ones, before)
    above = jnp.dot(jnp.tril(jnp.ones((rows, rows), jnp.float32), -1), jnp.sum(ones, axis=1, keepdims=True))
    ranks = jnp.where(mask > 0, (within + above).astype(jnp.int32), -1)
    return ranks.reshape(1, rows * cols), jnp.sum(mask).astype(jnp.int32)


def network(x, field, target, mask, batch, w_in_t, w_out, total, places):
    feats, cols = x.shape
    hid = w_out.shape[0]
    ranks, land = land_ranks(mask)
    scalars = jnp.stack([lax.axis_index(CORE).astype(jnp.int32), land])
    table = jnp.asarray(ring_rows())
    rows = len(ORDERS) * 2048
    f32, bf16 = jnp.float32, jnp.bfloat16
    cut = lambda *shape: pl.BlockSpec(shape, lambda i, *_: (i,) + (0,) * (len(shape) - 1))
    new, slope, dtend, xn, kept, sent = pl.pallas_call(
        functools.partial(forward_kernel, (BATCHES / (total * feats), total ** (-0.5))),
        grid_spec=pltpu.PrefetchScalarGridSpec(
            num_scalar_prefetch=2,
            grid=(8,),
            in_specs=[
                whole(feats, cols),
                cut(512, feats),
                pl.BlockSpec((feats, 512), lambda i, *_: (0, i)),
                whole(feats, cols),
                whole(1, cols),
                whole(8, cols),
                whole(feats, cols),
            ],
            out_specs=[
                whole(feats, cols),
                cut(512, cols),
                whole(feats, cols),
                whole(cols, feats),
                whole(rows, 128),
                whole(rows + 8, 128),
            ],
            scratch_shapes=[
                pltpu.VMEM((64, 2, 32, cols), bf16),
                pltpu.VMEM((feats, cols), f32),
                pltpu.VMEM((cols, feats), bf16),
                pltpu.VMEM((cols, cols), bf16),
                pltpu.VMEM((feats, cols), bf16),
            ],
        ),
        out_shape=[
            shaped(f32, feats, cols),
            shaped(f32, hid, cols),
            shaped(bf16, feats, cols),
            shaped(bf16, cols, feats),
            shaped(f32, rows, 128),
            shaped(f32, rows + 8, 128),
        ],
        compiler_params=params(56),
        cost_estimate=pl.CostEstimate(
            flops=4 * cols * feats * hid, bytes_accessed=40 * 2**20, transcendentals=cols * hid
        ),
        name="forward",
    )(scalars, table, x, w_in_t, w_out.T, target, ranks, batch, field)
    from_core = lax.ppermute(sent, CORE, PAIR)
    dpre = pl.pallas_call(
        dpre_kernel,
        grid_spec=pltpu.PrefetchScalarGridSpec(
            num_scalar_prefetch=1,
            grid=(8,),
            in_specs=[cut(512, feats), cut(512, cols), whole(feats, cols)],
            out_specs=cut(8, 2, 32, cols),
        ),
        out_shape=shaped(bf16, 64, 2, 32, cols),
        compiler_params=params(24),
        cost_estimate=pl.CostEstimate(flops=2 * cols * feats * hid, bytes_accessed=28 * 2**20, transcendentals=0),
        name="dpre",
    )(scalars, w_out, slope, dtend)
    dpre, from_core = lax.optimization_barrier((dpre, from_core))
    first = core_sums(kept, from_core[:rows])
    first, losses = ring_round(first, 0, 0, places, from_core[rows:] + sent[rows:])
    kept_in, sent_in = pl.pallas_call(
        grad_kernel,
        grid_spec=pltpu.PrefetchScalarGridSpec(
            num_scalar_prefetch=2,
            grid=(8,),
            in_specs=[cut(8, 2, 32, cols), whole(cols, feats)],
            out_specs=[whole(rows, 128), whole(rows, 128)],
        ),
        out_shape=[shaped(f32, rows, 128), shaped(f32, rows, 128)],
        compiler_params=params(24),
        cost_estimate=pl.CostEstimate(flops=2 * cols * feats * hid, bytes_accessed=14 * 2**20, transcendentals=0),
        name="grad",
    )(scalars, table, dpre, xn)
    kept_in, sent_in, *first, losses = lax.optimization_barrier((kept_in, sent_in, *first, losses))
    from_core = lax.ppermute(sent_in, CORE, PAIR)
    first, losses = ring_round(first, 0, 1, places, losses)
    second = core_sums(kept_in, from_core)
    for turn in range(2):
        second, _ = ring_round(second, 0, turn, places)
    both = [jnp.concatenate(pair, axis=1) for pair in zip(first, second)]
    losses = jnp.concatenate([losses, losses], axis=1)
    for stage in (1, 2):
        for turn in range(2):
            both, losses = ring_round(both, stage, turn, places, losses)
    grad_out = jnp.concatenate([b[:, :128] for b in both], axis=1)
    grad_in = jnp.concatenate([b[:, 128:] for b in both], axis=1)
    return new, grad_in, grad_out, losses[0, :BATCHES]


def on_device(state, target, land_mask, batch_map, diffusion, speed_x, speed_y, w_in, w_out):
    feats, rows_x, rows_y = state.shape
    kap = diffusion[:, None, None]
    sxx = speed_x[:, None, None]
    syy = speed_y[:, None, None]
    field = extended(state, ((BX, 1), (BY, 2)), SUB)
    for substep in range(SUB):
        field = advance(field, kap, sxx, syy)
        margin = SUB - substep - 1
        if margin > 0:
            along_x = (
                lax.axis_index(BX) * rows_x
                + jnp.arange(rows_x + 2 * margin, dtype=jnp.int32)
                - margin
            )
            along_y = (
                lax.axis_index(BY) * rows_y
                + jnp.arange(rows_y + 2 * margin, dtype=jnp.int32)
                - margin
            )
            inside_x = ((along_x >= 0) & (along_x < rows_x * lax.axis_size(BX))).astype(jnp.float32)
            inside_y = ((along_y >= 0) & (along_y < rows_y * lax.axis_size(BY))).astype(jnp.float32)
            field = field * inside_x[None, :, None] * inside_y[None, None, :]
    local_cols = rows_x * rows_y
    total = local_cols * lax.axis_size(BX) * lax.axis_size(BY)
    flat = field.reshape(feats, local_cols)
    new, grad_in, grad_out, batch_loss = network(
        flat.astype(jnp.bfloat16),
        flat,
        target.reshape(feats, local_cols),
        land_mask,
        jnp.broadcast_to(batch_map.reshape(1, local_cols), (8, local_cols)).astype(jnp.bfloat16),
        w_in.T,
        w_out,
        total,
        ring_places(),
    )
    return (new.reshape(feats, rows_x, rows_y), grad_in, grad_out, batch_loss)


def solution(mesh):
    torus = Mesh(mesh.devices.reshape(2, 4, 4, 2, 2), BX + BY)
    return jax.shard_map(
        on_device,
        mesh=torus,
        in_specs=(P(None, BX, BY), P(None, BX, BY), P(BX, BY), P(BX, BY), P(), P(), P(), P(), P()),
        out_specs=(P(None, BX, BY), P(BX + BY, None), P(BX + BY, None), P()),
        check_vma=False,
    )
```

time: 272 us -> 181 us (0.67); the launches traced: 268 us -> 180 us
  matrix products: 44.5 us -> 0.91 us
  local copies, waits for them, and re-layouts: 78 us -> 35.8 us
  Pallas kernels: 0 us -> 38.4 us
  starting transfers between devices: 66.7 us -> 43.5 us
  waiting for transfers between devices: 48.2 us -> 37.2 us
  other arithmetic: 27.6 us -> 22.7 us
    dot_general x6 -> x2, matrix products: 44.5 us -> 0.91 us  [the longest x1 0.73 us: land_ranks(): within = jnp.dot(ones, before)]
    pallas_call x0 -> x3, Pallas kernels: none -> 38.4 us  [the longest x1 26.6 us: network(): pl.pallas_call(functools.partial(forward_kernel, (BATCHES / (total * feat...]
    slice x48 -> x4, local copies, waits for them, and re-layouts: 32 us -> 0.02 us  [the longest x3 0.02 us: network(): grad_out = jnp.concatenate([b[:, :128] for b in both], axis=1)]
    ppermute x45 -> x26, starting transfers between devices: 58.1 us -> 34.7 us  [the longest x24 27.4 us: ring_turn(): coming = lax.ppermute(leaving, AXES[axis], RING[turn + 1])]
    reshape x2 -> x1, local copies, waits for them, and re-layouts: 20.6 us -> 3.03 us  [on_device(): flat = field.reshape(feats, local_cols)]
    unnamed x58 -> x39, local copies, waits for them, and re-layouts: 12.8 us -> 23.9 us
    another operation x6 -> x1, other arithmetic: 7.68 us -> 1.31 us  [network(): scalars = jnp.stack([lax.axis_index(CORE).astype(jnp.int32), land])]
    ppermute x2, waiting for transfers between devices: 6.27 us -> 1.25 us  [extended(): lax.ppermute(head, axis, [((i + 1) % count, i) for i in range(ends)])]
  transfers between devices with their start and end apart: 49 -> 30, of which waited for: 22 -> 17; matrix products, arithmetic and copies ran while one was open for 11% -> 15% of each run, Pallas kernels for 0% -> 7%
where the time goes in v3:
time: 181 us; the launch traced here: 180 us
  starting transfers between devices  43.5 us (24%)
  Pallas kernels  38.4 us (21%)
  waiting for transfers between devices  37.2 us (21%)
  local copies, waits for them, and re-layouts  35.8 us (20%)
  other arithmetic  22.7 us (13%)
    ppermute x24, waiting for transfers between devices, ring_turn(): coming = lax.ppermute(leaving, AXES[axis], RING[turn + 1])  36 us
    ppermute x24, starting transfers between devices, ring_turn(): coming = lax.ppermute(leaving, AXES[axis], RING[turn + 1])  27.4 us
    pallas_call x1, Pallas kernels, network(): pl.pallas_call(functools.partial(forward_kernel, (BATCHES / (total * feat...  26.6 us
    unnamed x39, local copies, waits for them, and re-layouts  23.9 us
    pallas_call x1, Pallas kernels, network(): pl.pallas_call(grad_kernel, grid_spec=pltpu.PrefetchScalarGridSpec(num_sc...  6.58 us
    ppermute x2, starting transfers between devices, extended(): lax.ppermute(tail, axis, [(i, (i + 1) % count) for i in range(ends)])  6.2 us
    pallas_call x1, Pallas kernels, network(): pl.pallas_call(dpre_kernel, grid_spec=pltpu.PrefetchScalarGridSpec(num_sc...  5.22 us
    add x2, other arithmetic, core_sums(): kept[stream * rows:(stream + 1) * rows]  4.35 us
  transfers between devices with their start and end apart: 30, of which 17 were waited for; matrix products, arithmetic and copies ran while one was open for 15% of the time, Pallas kernels for 7%

profile of v3, /device:TPU:0, one launch (start us, length us, event | category | flops | bytes accessed | tf_op | source)
XLA Modules:
  0.0 179.8 jit_solution(12262541731815949364)
XLA Ops:
  0.7 2.3 %fusion.27 = (f32[384,3,128]{2,1,0:T(4,128)S(1)}, f32[384,3,128]{2,1,0:T(4,128)S(1)}) fusion(f32[384,8,128]{2,1,0:T(8,128)} %param.10), kind=kLoop, calls=%fused_computation.122 | loop fusion | bytes 2359296 | tf_op jit(solution)/shard_map/slice | solution.py:33
  3.0 0.9 copy.28
  3.8 4.7 %collective-permute-start = (f32[384,3,128]{2,0,1:T(8,128)}, f32[384,3,128]{2,0,1:T(8,128)}, u32[]{:S(2)}, u32[]{:S(2)}) collective-permute-start(f32[384,3,128]{2,0,1:T(8,128)} %copy.28), channel_id=1, source_target_pairs={{0,16},{16,32},{32,48},{48,64},{64,80},{80,96},{96,112},{1,17},{17... | collective-permute-start | bytes 1769480 | tf_op jit(solution)/shard_map/ppermute | solution.py:36
  8.6 0.9 copy.29
  9.5 1.3 collective-permute-start.1
  11.0 1.7 copy.19
  13.3 4.8 %copy.25 = bf16[384,4096]{0,1:T(8,128)(2,1)} copy(bf16[384,4096]{1,0:T(8,128)(2,1)} %param.17) | data formatting | bytes 6291456 | tf_op args[7]
  18.1 3.0 %copy.26 = bf16[4096,384]{0,1:T(8,128)(2,1)} copy(bf16[4096,384]{1,0:T(8,128)(2,1)S(1)} %copy-done.1) | data formatting | bytes 6291456 | tf_op args[8]
  21.1 2.2 %copy.33 = bf16[48,8,8,128]{3,1,2,0:T(8,128)(2,1)} copy(bf16[48,8,8,128]{3,2,1,0:T(8,128)(2,1)} %bitcast.30) | data formatting | bytes 1572864
  24.3 2.2 %copy.18 = f32[384,3,128]{0,1,2:T(4,128)} copy(f32[384,3,128]{2,0,1:T(8,128)} %collective-permute-done) | data formatting | bytes 1179648 | tf_op jit(solution)/shard_map/ppermute | solution.py:36
  26.6 2.2 %copy.20 = f32[384,3,128]{0,1,2:T(4,128)} copy(f32[384,3,128]{2,0,1:T(8,128)} %collective-permute-done.1) | data formatting | bytes 1179648 | tf_op jit(solution)/shard_map/ppermute | solution.py:38
  28.8 2.4 %pad_maximum_fusion = f32[384,14,128]{0,1,2:T(8,128)S(1)} fusion(f32[384,3,128]{0,1,2:T(4,128)} %copy.20, f32[384,8,128]{0,1,2:T(8,128)} %copy.19, f32[384,3,128]{0,1,2:T(4,128)} %copy.18), kind=kLoop, calls=%fused_computation | loop fusion | flops 1376256 | bytes 5505024 | tf_op jit(solution)/shard_map/concatenate | solution.py:34
  31.2 1.5 collective-permute-start.2
  32.6 1.3 collective-permute-start.3
  33.9 1.3 pad_add_fusion.scalar_ref
  35.2 0.9 copy.22
  36.2 1.2 collective-permute-done.3
  38.2 1.9 %multiply_multiply_fusion = f32[384,12,132]{0,2,1:T(8,128)S(1)} fusion(f32[384,14,134]{0,2,1:T(8,128)S(1)} %pad_maximum_fusion.1, f32[132]{0:T(256)S(1)} %and_convert_fusion.2, f32[12]{0:T(128)S(1)} %and_convert_fusion.3, f32[384]{0:T(512)S(1)} %get-tuple-element.52, f32[384]{0:T(512)S(1)} %get-tuple-element.53, f32[384]{0:T(512)S(1)} %copy-done.11), kind=kLoop, calls=%fused_computation.2 | loop fusion | flops 9123840 | bytes 14603328 | tf_op jit(solution)/shard_map/mul | solution.py:378
  40.1 1.3 multiply_multiply_fusion.1
  41.4 2.0 %multiply_subtract_fusion = f32[384,8,128]{0,2,1:T(8,128)} fusion(f32[384,10,130]{0,2,1:T(8,128)S(1)} %multiply_multiply_fusion.1, f32[384]{0:T(512)S(1)} %get-tuple-element.52, f32[384]{0:T(512)S(1)} %get-tuple-element.53, f32[384]{0:T(512)S(1)} %copy-done.11), kind=kLoop, calls=%fused_computation.4 | loop fusion | flops 5111808 | bytes 9441792 | tf_op jit(solution)/shard_map/sub | solution.py:52
  43.4 3.0 %copy.27.field_ref = f32[384,1024]{1,0:T(8,128)} copy(f32[384,1024]{0,1:T(8,128)} %bitcast.25) | data formatting | bytes 3145728 | tf_op jit(solution)/shard_map/reshape | solution.py:381
  46.5 2.4 %convert_element_type.49.x_ref = bf16[384,1024]{1,0:T(8,128)(2,1)} convert(f32[384,1024]{1,0:T(8,128)} %copy.27.field_ref) | non-fusion elementwise | flops 393216 | bytes 2359296 | tf_op jit(solution)/shard_map/convert_element_type | solution.py:383
  49.5 26.6 %forward.1 = (f32[384,1024]{1,0:T(8,128)}, f32[4096,1024]{1,0:T(8,128)}, bf16[384,1024]{1,0:T(8,128)(2,1)}, bf16[1024,384]{1,0:T(8,128)(2,1)}, f32[6144,128]{1,0:T(8,128)}, /*index=5*/f32[6152,128]{1,0:T(8,128)}) custom-call(s32[2]{0:T(128)} %pad_add_fusion.scalar_ref, s32[384]{0:T(512)} %constant.161.clone.table_ref, ...), custom_call_target="tpu_custom_call" | custom-call | flops 6442450944 | bytes 41943040 | tf_op jit(solution)/shard_map/forward/pallas_call | solution.py:266
  76.1 3.1 %collective-permute-start.4 = (f32[6152,128]{1,0:T(8,128)}, f32[6152,128]{1,0:T(8,128)}, u32[]{:S(2)}, u32[]{:S(2)}) collective-permute-start(f32[6152,128]{1,0:T(8,128)} %get-tuple-element.23), channel_id=1, source_target_pairs={{0,1},{1,0},{2,3},{3,2},{4,5},{5,4},{6,7},{7,6},{8,9},{9,8},{10,11... | collective-permute-start | bytes 9449480 | tf_op jit(solution)/shard_map/ppermute | solution.py:310
  79.2 5.8 %copy-done = f32[4096,1024]{1,0:T(8,128)S(1)} copy-done((f32[4096,1024]{1,0:T(8,128)S(1)}, f32[4096,1024]{1,0:T(8,128)}, u32[]{:S(2)}) %copy-start) | copy-done | bytes 16777240
  85.0 1.1 copy-done.2
  86.1 5.2 %dpre.1.dpre_ref = bf16[64,2,32,1024]{3,2,1,0:T(8,128)(2,1)S(1)} custom-call(s32[2]{0:T(128)S(1)} %copy-done.3, bf16[4096,384]{1,0:T(8,128)(2,1)S(1)} %copy-done.1, f32[4096,1024]{1,0:T(8,128)S(1)} %copy-done, bf16[384,1024]{1,0:T(8,128)(2,1)S(1)} %copy-done.2), custom_call_target="tpu_custom_call" | custom-call | flops 3221225472 | bytes 29360128 | tf_op jit(solution)/shard_map/dpre/pallas_call | solution.py:311
  92.0 2.2 %slice_add_fusion.3 = (f32[2048,128]{1,0:T(8,128)S(1)}, f32[2048,128]{1,0:T(8,128)S(1)}, f32[2048,128]{1,0:T(8,128)S(1)}) fusion(f32[6152,128]{1,0:T(8,128)} %collective-permute-done.4, f32[6144,128]{1,0:T(8,128)S(1)} %copy-done.7), kind=kLoop, calls=%fused_computation.13 | loop fusion | flops 786432 | bytes 9437184 | tf_op jit(solution)/shard_map/add | solution.py:109
  94.3 2.7 %collective-permute-start.7 = (f32[1024,128]{1,0:T(8,128)S(1)}, f32[1024,128]{1,0:T(8,128)S(1)}, u32[]{:S(2)}, u32[]{:S(2)}) collective-permute-start(f32[1024,128]{1,0:T(8,128)S(1)} %constant_dynamic-slice_fusion.18), channel_id=1, source_target_pairs={{0,16},{1,49},{16,0},{17,33},{32,48},{33,17},{48,32},{49,1},{2,18}... | collective-permute-start | bytes 1572872 | tf_op jit(solution)/shard_map/ppermute | solution.py:90
  97.1 1.6 collective-permute-start.5
  98.7 2.4 %collective-permute-start.6 = (f32[1024,128]{1,0:T(8,128)S(1)}, f32[1024,128]{1,0:T(8,128)S(1)}, u32[]{:S(2)}, u32[]{:S(2)}) collective-permute-start(f32[1024,128]{1,0:T(8,128)S(1)} %constant_dynamic-slice_fusion.19), channel_id=1, source_target_pairs={{0,2},{1,67},{2,0},{3,65},{64,66},{65,3},{66,64},{67,1},{4,6},{5,7... | collective-permute-start | bytes 1572872 | tf_op jit(solution)/shard_map/ppermute | solution.py:90
  101.1 6.6 %grad.1 = (f32[6144,128]{1,0:T(8,128)S(1)}, f32[6144,128]{1,0:T(8,128)}) custom-call(s32[2]{0:T(128)S(1)} %copy-done.3, s32[384]{0:T(512)S(1)} %copy-done.4, bf16[64,2,32,1024]{3,2,1,0:T(8,128)(2,1)S(1)} %dpre.1.dpre_ref, bf16[1024,384]{1,0:T(8,128)(2,1)S(1)} %copy-done.5), custom_call_target="tpu_custom_call" | custom-call | flops 3221225472 | bytes 14680064 | tf_op jit(solution)/shard_map/grad/pallas_call | solution.py:327
  107.7 0.8 dynamic-slice_add_fusion.3
  108.5 0.9 dynamic-slice_add_fusion.4
  109.4 0.9 slice_add_fusion.6
  110.3 4.2 %collective-permute-start.9 = (f32[6144,128]{1,0:T(8,128)}, f32[6144,128]{1,0:T(8,128)}, u32[]{:S(2)}, u32[]{:S(2)}) collective-permute-start(f32[6144,128]{1,0:T(8,128)} %get-tuple-element.33), channel_id=1, source_target_pairs={{0,1},{1,0},{2,3},{3,2},{4,5},{5,4},{6,7},{7,6},{8,9},{9,8},{10,11... | collective-permute-start | bytes 9437192 | tf_op jit(solution)/shard_map/ppermute | solution.py:341
  114.5 3.0 %copy.31 = f32[48,8,8,128]{3,2,1,0:T(8,128)} copy(f32[48,8,8,128]{3,1,2,0:T(8,128)} %bitcast.28) | data formatting | bytes 3145728
  117.5 1.2 collective-permute-start.16
  118.8 1.2 collective-permute-start.23
  120.0 2.6 %collective-permute-start.8 = (f32[520,128]{1,0:T(8,128)S(1)}, f32[520,128]{1,0:T(8,128)S(1)}, u32[]{:S(2)}, u32[]{:S(2)}) collective-permute-start(f32[520,128]{1,0:T(8,128)S(1)} %pad_maximum_fusion.3), channel_id=1, source_target_pairs={{0,12},{1,5},{4,8},{5,1},{8,4},{9,13},{12,0},{13,9},{2,14},{3,7},{... | collective-permute-start | bytes 798728 | tf_op jit(solution)/shard_map/ppermute | solution.py:90
  122.6 2.6 %collective-permute-done.16 = f32[512,128]{1,0:T(8,128)S(1)} collective-permute-done((f32[512,128]{1,0:T(8,128)S(1)}, f32[512,128]{1,0:T(8,128)S(1)}, u32[]{:S(2)}, u32[]{:S(2)}) %collective-permute-start.16) | collective-permute-done | bytes 262176 | tf_op jit(solution)/shard_map/ppermute | solution.py:90
  125.2 1.2 collective-permute-done.23
  126.5 2.2 %slice_add_fusion.2 = (f32[2048,128]{1,0:T(8,128)S(1)}, f32[2048,128]{1,0:T(8,128)S(1)}, f32[2048,128]{1,0:T(8,128)S(1)}) fusion(f32[6144,128]{1,0:T(8,128)} %collective-permute-done.9, f32[6144,128]{1,0:T(8,128)S(1)} %get-tuple-element.32), kind=kLoop, calls=%fused_computation.12 | loop fusion | flops 786432 | bytes 9437184 | tf_op jit(solution)/shard_map/add | solution.py:109
  128.7 1.1 collective-permute-start.10
  130.3 8.0 %collective-permute-done.10 = f32[1024,128]{1,0:T(8,128)S(1)} collective-permute-done((f32[1024,128]{1,0:T(8,128)S(1)}, f32[1024,128]{1,0:T(8,128)S(1)}, u32[]{:S(2)}, u32[]{:S(2)}) %collective-permute-start.10) | collective-permute-done | bytes 524320 | tf_op jit(solution)/shard_map/ppermute | solution.py:90
  138.3 1.8 %collective-permute-start.11 = (f32[512,128]{1,0:T(8,128)S(1)}, f32[512,128]{1,0:T(8,128)S(1)}, u32[]{:S(2)}, u32[]{:S(2)}) collective-permute-start(f32[512,128]{1,0:T(8,128)S(1)} %constant_dynamic-slice_fusion.15), channel_id=1, source_target_pairs={{0,12},{1,5},{4,8},{5,1},{8,4},{9,13},{12,0},{13,9},{2,14},{3,7},{... | collective-permute-start | bytes 786440 | tf_op jit(solution)/shard_map/ppermute | solution.py:90
  140.3 1.4 collective-permute-start.18
  141.8 1.8 %collective-permute-start.25 = (f32[512,128]{1,0:T(8,128)S(1)}, f32[512,128]{1,0:T(8,128)S(1)}, u32[]{:S(2)}, u32[]{:S(2)}) collective-permute-start(f32[512,128]{1,0:T(8,128)S(1)} %constant_dynamic-slice_fusion.3), channel_id=1, source_target_pairs={{0,48},{1,17},{16,32},{17,1},{32,16},{33,49},{48,0},{49,33},{2,50}... | collective-permute-start | bytes 786440 | tf_op jit(solution)/shard_map/ppermute | solution.py:90
  143.6 2.4 %collective-permute-done.11 = f32[512,128]{1,0:T(8,128)S(1)} collective-permute-done((f32[512,128]{1,0:T(8,128)S(1)}, f32[512,128]{1,0:T(8,128)S(1)}, u32[]{:S(2)}, u32[]{:S(2)}) %collective-permute-start.11) | collective-permute-done | bytes 262176 | tf_op jit(solution)/shard_map/ppermute | solution.py:90
  146.2 4.1 %collective-permute-done.18 = f32[512,128]{1,0:T(8,128)S(1)} collective-permute-done((f32[512,128]{1,0:T(8,128)S(1)}, f32[512,128]{1,0:T(8,128)S(1)}, u32[]{:S(2)}, u32[]{:S(2)}) %collective-permute-start.18) | collective-permute-done | bytes 262176 | tf_op jit(solution)/shard_map/ppermute | solution.py:90
  150.5 1.7 collective-permute-done.25
  152.8 5.4 %collective-permute-done.19 = f32[256,256]{1,0:T(8,128)S(1)} collective-permute-done((f32[256,256]{1,0:T(8,128)S(1)}, f32[256,256]{1,0:T(8,128)S(1)}, u32[]{:S(2)}, u32[]{:S(2)}) %collective-permute-start.19) | collective-permute-done | bytes 262176 | tf_op jit(solution)/shard_map/ppermute | solution.py:90
  158.3 1.7 collective-permute-start.20
  160.1 1.6 collective-permute-start.27
  161.8 1.6 collective-permute-start.13
  163.4 2.0 %collective-permute-done.20 = f32[128,256]{1,0:T(8,128)S(1)} collective-permute-done((f32[128,256]{1,0:T(8,128)S(1)}, f32[128,256]{1,0:T(8,128)S(1)}, u32[]{:S(2)}, u32[]{:S(2)}) %collective-permute-start.20) | collective-permute-done | bytes 131104 | tf_op jit(solution)/shard_map/ppermute | solution.py:90
  165.5 0.9 collective-permute-done.27
  166.5 1.6 collective-permute-done.13
  168.3 1.5 collective-permute-done.21
  170.8 1.2 collective-permute-start.29
  172.7 1.5 collective-permute-start.15
  174.2 0.8 collective-permute-done.22
  175.0 1.0 collective-permute-done.29
  176.0 1.9 %collective-permute-done.15 = f32[40,256]{1,0:T(8,128)S(1)} collective-permute-done((f32[40,256]{1,0:T(8,128)S(1)}, f32[40,256]{1,0:T(8,128)S(1)}, u32[]{:S(2)}, u32[]{:S(2)}) %collective-permute-start.15) | collective-permute-done | bytes 40992 | tf_op jit(solution)/shard_map/ppermute | solution.py:90
  (134 shorter events, 9.9 us)
Async XLA Ops:
  0.6 10.3 %copy-start.6 = (f32[384,8,128]{2,1,0:T(8,128)S(1)}, f32[384,8,128]{2,1,0:T(8,128)}, u32[]{:S(2)}) copy-start(f32[384,8,128]{2,1,0:T(8,128)} %param.10) | copy-start | bytes 4718596
  0.6 10.2 %copy-start.13 = (s32[8,128]{1,0:T(8,128)S(1)}, s32[8,128]{1,0:T(8,128)}, u32[]{:S(2)}) copy-start(s32[8,128]{1,0:T(8,128)} %param.13) | copy-start | bytes 12292
  0.7 10.2 %copy-start.12 = (s32[8,128]{1,0:T(8,128)S(1)}, s32[8,128]{1,0:T(8,128)}, u32[]{:S(2)}) copy-start(s32[8,128]{1,0:T(8,128)} %param.12) | copy-start | bytes 12292
  3.8 20.5 %collective-permute-start = (f32[384,3,128]{2,0,1:T(8,128)}, f32[384,3,128]{2,0,1:T(8,128)}, u32[]{:S(2)}, u32[]{:S(2)}) collective-permute-start(f32[384,3,128]{2,0,1:T(8,128)} %copy.28), channel_id=1, source_target_pairs={{0,16},{16,32},{32,48},{48,64},{64,80},{80,96},{96,112},{1,17},{17... | collective-permute-start | bytes 1769480 | tf_op jit(solution)/shard_map/ppermute | solution.py:36
  9.5 17.1 %collective-permute-start.1 = (f32[384,3,128]{2,0,1:T(8,128)}, f32[384,3,128]{2,0,1:T(8,128)}, u32[]{:S(2)}, u32[]{:S(2)}) collective-permute-start(f32[384,3,128]{2,0,1:T(8,128)} %copy.29), channel_id=1, source_target_pairs={{16,0},{32,16},{48,32},{64,48},{80,64},{96,80},{112,96},{17,1},{33... | collective-permute-start | bytes 1769480 | tf_op jit(solution)/shard_map/ppermute | solution.py:38
  13.3 4.8 %copy-start.1 = (bf16[4096,384]{1,0:T(8,128)(2,1)S(1)}, bf16[4096,384]{1,0:T(8,128)(2,1)}, u32[]{:S(2)}) copy-start(bf16[4096,384]{1,0:T(8,128)(2,1)} %wout_ref.1) | copy-start | bytes 9437188
  18.1 5.4 %copy-start.14 = (f32[384]{0:T(512)S(1)}, f32[384]{0:T(512)}, u32[]{:S(2)}) copy-start(f32[384]{0:T(512)} %param.16) | copy-start | bytes 4612
  18.1 5.4 %copy-start.15 = (f32[384]{0:T(512)S(1)}, f32[384]{0:T(512)}, u32[]{:S(2)}) copy-start(f32[384]{0:T(512)} %param.15) | copy-start | bytes 4612
  31.2 5.0 %collective-permute-start.2 = (f32[384,14,3]{0,1,2:T(8,128)S(1)}, f32[384,14,3]{0,1,2:T(8,128)S(1)}, u32[]{:S(2)}, u32[]{:S(2)}) collective-permute-start(f32[384,14,3]{0,1,2:T(8,128)S(1)} %get-tuple-element.42), channel_id=1, source_target_pairs={{0,1},{1,2},{2,3},{3,4},{4,5},{5,6},{6,7},{7,8},{8,9},{9,10},{10,1... | collective-permute-start | bytes 193544 | tf_op jit(solution)/shard_map/ppermute | solution.py:36
  32.6 4.8 %collective-permute-start.3 = (f32[384,14,3]{0,1,2:T(8,128)S(1)}, f32[384,14,3]{0,1,2:T(8,128)S(1)}, u32[]{:S(2)}, u32[]{:S(2)}) collective-permute-start(f32[384,14,3]{0,1,2:T(8,128)S(1)} %get-tuple-element.43), channel_id=1, source_target_pairs={{1,0},{2,1},{3,2},{4,3},{5,4},{6,5},{7,6},{8,7},{9,8},{10,9},{11,1... | collective-permute-start | bytes 193544 | tf_op jit(solution)/shard_map/ppermute | solution.py:38
  37.5 0.7 copy-start.11
  49.5 29.7 %copy-start.3 = (s32[2]{0:T(128)S(1)}, s32[2]{0:T(128)}, u32[]{:S(2)}) copy-start(s32[2]{0:T(128)} %pad_add_fusion.scalar_ref) | copy-start | bytes 28
  76.1 15.2 %collective-permute-start.4 = (f32[6152,128]{1,0:T(8,128)}, f32[6152,128]{1,0:T(8,128)}, u32[]{:S(2)}, u32[]{:S(2)}) collective-permute-start(f32[6152,128]{1,0:T(8,128)} %get-tuple-element.23), channel_id=1, source_target_pairs={{0,1},{1,0},{2,3},{3,2},{4,5},{5,4},{6,7},{7,6},{8,9},{9,8},{10,11... | collective-permute-start | bytes 9449480 | tf_op jit(solution)/shard_map/ppermute | solution.py:310
  79.2 5.8 %copy-start = (f32[4096,1024]{1,0:T(8,128)S(1)}, f32[4096,1024]{1,0:T(8,128)}, u32[]{:S(2)}) copy-start(f32[4096,1024]{1,0:T(8,128)} %get-tuple-element.21.slope_ref) | copy-start | bytes 50331652
  85.0 1.1 copy-start.2
  86.1 5.9 %copy-start.7 = (f32[6144,128]{1,0:T(8,128)S(1)}, f32[6144,128]{1,0:T(8,128)}, u32[]{:S(2)}) copy-start(f32[6144,128]{1,0:T(8,128)} %get-tuple-element.28) | copy-start | bytes 9437188
  94.2 6.8 %copy-start.4 = (s32[384]{0:T(512)S(1)}, s32[384]{0:T(512)}, u32[]{:S(2)}) copy-start(s32[384]{0:T(512)} %constant.161.clone.table_ref) | copy-start | bytes 4612
  94.2 6.8 %copy-start.5 = (bf16[1024,384]{1,0:T(8,128)(2,1)S(1)}, bf16[1024,384]{1,0:T(8,128)(2,1)}, u32[]{:S(2)}) copy-start(bf16[1024,384]{1,0:T(8,128)(2,1)} %get-tuple-element.25.xn_ref) | copy-start | bytes 2359300
  94.3 13.4 %collective-permute-start.7 = (f32[1024,128]{1,0:T(8,128)S(1)}, f32[1024,128]{1,0:T(8,128)S(1)}, u32[]{:S(2)}, u32[]{:S(2)}) collective-permute-start(f32[1024,128]{1,0:T(8,128)S(1)} %constant_dynamic-slice_fusion.18), channel_id=1, source_target_pairs={{0,16},{1,49},{16,0},{17,33},{32,48},{33,17},{48,32},{49,1},{2,18}... | collective-permute-start | bytes 1572872 | tf_op jit(solution)/shard_map/ppermute | solution.py:90
  97.1 12.3 %collective-permute-start.5 = (f32[1032,128]{1,0:T(8,128)S(1)}, f32[1032,128]{1,0:T(8,128)S(1)}, u32[]{:S(2)}, u32[]{:S(2)}) collective-permute-start(f32[1032,128]{1,0:T(8,128)S(1)} %pad_maximum_fusion.2), channel_id=1, source_target_pairs={{0,4},{1,13},{4,0},{5,9},{8,12},{9,5},{12,8},{13,1},{2,6},{3,15},{... | collective-permute-start | bytes 1585160 | tf_op jit(solution)/shard_map/ppermute | solution.py:90
  98.7 9.8 %collective-permute-start.6 = (f32[1024,128]{1,0:T(8,128)S(1)}, f32[1024,128]{1,0:T(8,128)S(1)}, u32[]{:S(2)}, u32[]{:S(2)}) collective-permute-start(f32[1024,128]{1,0:T(8,128)S(1)} %constant_dynamic-slice_fusion.19), channel_id=1, source_target_pairs={{0,2},{1,67},{2,0},{3,65},{64,66},{65,3},{66,64},{67,1},{4,6},{5,7... | collective-permute-start | bytes 1572872 | tf_op jit(solution)/shard_map/ppermute | solution.py:90
  110.3 16.2 %collective-permute-start.9 = (f32[6144,128]{1,0:T(8,128)}, f32[6144,128]{1,0:T(8,128)}, u32[]{:S(2)}, u32[]{:S(2)}) collective-permute-start(f32[6144,128]{1,0:T(8,128)} %get-tuple-element.33), channel_id=1, source_target_pairs={{0,1},{1,0},{2,3},{3,2},{4,5},{5,4},{6,7},{7,6},{8,9},{9,8},{10,11... | collective-permute-start | bytes 9437192 | tf_op jit(solution)/shard_map/ppermute | solution.py:341
  114.5 3.0 %copy-start.10 = (f32[1024,128]{1,0:T(8,128)S(1)}, f32[1024,128]{1,0:T(8,128)}, u32[]{:S(2)}) copy-start(f32[1024,128]{1,0:T(8,128)} %dynamic-slice_add_fusion.4) | copy-start | bytes 1572868
  114.5 4.3 %copy-start.9 = (f32[1024,128]{1,0:T(8,128)S(1)}, f32[1024,128]{1,0:T(8,128)}, u32[]{:S(2)}) copy-start(f32[1024,128]{1,0:T(8,128)} %dynamic-slice_add_fusion.3) | copy-start | bytes 1572868
  114.5 5.5 %copy-start.8 = (f32[1024,128]{1,0:T(8,128)S(1)}, f32[1024,128]{1,0:T(8,128)}, u32[]{:S(2)}) copy-start(f32[1024,128]{1,0:T(8,128)} %slice_add_fusion.6) | copy-start | bytes 1572868
  117.5 7.7 %collective-permute-start.16 = (f32[512,128]{1,0:T(8,128)S(1)}, f32[512,128]{1,0:T(8,128)S(1)}, u32[]{:S(2)}, u32[]{:S(2)}) collective-permute-start(f32[512,128]{1,0:T(8,128)S(1)} %constant_dynamic-slice_fusion.11), channel_id=1, source_target_pairs={{0,66},{1,3},{2,64},{3,1},{64,2},{65,67},{66,0},{67,65},{4,70},{5,... | collective-permute-start | bytes 786440 | tf_op jit(solution)/shard_map/ppermute | solution.py:90
  118.8 7.7 %collective-permute-start.23 = (f32[512,128]{1,0:T(8,128)S(1)}, f32[512,128]{1,0:T(8,128)S(1)}, u32[]{:S(2)}, u32[]{:S(2)}) collective-permute-start(f32[512,128]{1,0:T(8,128)S(1)} %constant_dynamic-slice_fusion.5), channel_id=1, source_target_pairs={{0,48},{1,17},{16,32},{17,1},{32,16},{33,49},{48,0},{49,33},{2,50}... | collective-permute-start | bytes 786440 | tf_op jit(solution)/shard_map/ppermute | solution.py:90
  120.0 9.8 %collective-permute-start.8 = (f32[520,128]{1,0:T(8,128)S(1)}, f32[520,128]{1,0:T(8,128)S(1)}, u32[]{:S(2)}, u32[]{:S(2)}) collective-permute-start(f32[520,128]{1,0:T(8,128)S(1)} %pad_maximum_fusion.3), channel_id=1, source_target_pairs={{0,12},{1,5},{4,8},{5,1},{8,4},{9,13},{12,0},{13,9},{2,14},{3,7},{... | collective-permute-start | bytes 798728 | tf_op jit(solution)/shard_map/ppermute | solution.py:90
  128.7 9.5 %collective-permute-start.10 = (f32[1024,128]{1,0:T(8,128)S(1)}, f32[1024,128]{1,0:T(8,128)S(1)}, u32[]{:S(2)}, u32[]{:S(2)}) collective-permute-start(f32[1024,128]{1,0:T(8,128)S(1)} %constant_dynamic-slice_fusion.16), channel_id=1, source_target_pairs={{0,4},{1,13},{4,0},{5,9},{8,12},{9,5},{12,8},{13,1},{2,6},{3,15},{... | collective-permute-start | bytes 1572872 | tf_op jit(solution)/shard_map/ppermute | solution.py:90
  129.9 10.3 %collective-permute-start.17 = (f32[1024,128]{1,0:T(8,128)S(1)}, f32[1024,128]{1,0:T(8,128)S(1)}, u32[]{:S(2)}, u32[]{:S(2)}) collective-permute-start(f32[1024,128]{1,0:T(8,128)S(1)} %constant_dynamic-slice_fusion.10), channel_id=1, source_target_pairs={{0,2},{1,67},{2,0},{3,65},{64,66},{65,3},{66,64},{67,1},{4,6},{5,7... | collective-permute-start | bytes 1572872 | tf_op jit(solution)/shard_map/ppermute | solution.py:90
  130.2 11.5 %collective-permute-start.24 = (f32[1024,128]{1,0:T(8,128)S(1)}, f32[1024,128]{1,0:T(8,128)S(1)}, u32[]{:S(2)}, u32[]{:S(2)}) collective-permute-start(f32[1024,128]{1,0:T(8,128)S(1)} %constant_dynamic-slice_fusion.4), channel_id=1, source_target_pairs={{0,16},{1,49},{16,0},{17,33},{32,48},{33,17},{48,32},{49,1},{2,18}... | collective-permute-start | bytes 1572872 | tf_op jit(solution)/shard_map/ppermute | solution.py:90
  138.3 7.7 %collective-permute-start.11 = (f32[512,128]{1,0:T(8,128)S(1)}, f32[512,128]{1,0:T(8,128)S(1)}, u32[]{:S(2)}, u32[]{:S(2)}) collective-permute-start(f32[512,128]{1,0:T(8,128)S(1)} %constant_dynamic-slice_fusion.15), channel_id=1, source_target_pairs={{0,12},{1,5},{4,8},{5,1},{8,4},{9,13},{12,0},{13,9},{2,14},{3,7},{... | collective-permute-start | bytes 786440 | tf_op jit(solution)/shard_map/ppermute | solution.py:90
  140.3 10.0 %collective-permute-start.18 = (f32[512,128]{1,0:T(8,128)S(1)}, f32[512,128]{1,0:T(8,128)S(1)}, u32[]{:S(2)}, u32[]{:S(2)}) collective-permute-start(f32[512,128]{1,0:T(8,128)S(1)} %constant_dynamic-slice_fusion.9), channel_id=1, source_target_pairs={{0,66},{1,3},{2,64},{3,1},{64,2},{65,67},{66,0},{67,65},{4,70},{5,... | collective-permute-start | bytes 786440 | tf_op jit(solution)/shard_map/ppermute | solution.py:90
  141.8 10.4 %collective-permute-start.25 = (f32[512,128]{1,0:T(8,128)S(1)}, f32[512,128]{1,0:T(8,128)S(1)}, u32[]{:S(2)}, u32[]{:S(2)}) collective-permute-start(f32[512,128]{1,0:T(8,128)S(1)} %constant_dynamic-slice_fusion.3), channel_id=1, source_target_pairs={{0,48},{1,17},{16,32},{17,1},{32,16},{33,49},{48,0},{49,33},{2,50}... | collective-permute-start | bytes 786440 | tf_op jit(solution)/shard_map/ppermute | solution.py:90
  146.1 15.6 %collective-permute-start.12 = (f32[264,256]{1,0:T(8,128)S(1)}, f32[264,256]{1,0:T(8,128)S(1)}, u32[]{:S(2)}, u32[]{:S(2)}) collective-permute-start(f32[264,256]{1,0:T(8,128)S(1)} %maximum_maximum_fusion), channel_id=1, source_target_pairs={{0,2},{1,67},{2,0},{3,65},{64,66},{65,3},{66,64},{67,1},{4,6},{5,7... | collective-permute-start | bytes 811016 | tf_op jit(solution)/shard_map/ppermute | solution.py:90
  150.4 7.9 %collective-permute-start.19 = (f32[256,256]{1,0:T(8,128)S(1)}, f32[256,256]{1,0:T(8,128)S(1)}, u32[]{:S(2)}, u32[]{:S(2)}) collective-permute-start(f32[256,256]{1,0:T(8,128)S(1)} %fusion.6), channel_id=1, source_target_pairs={{0,16},{1,49},{16,0},{17,33},{32,48},{33,17},{48,32},{49,1},{2,18}... | collective-permute-start | bytes 786440 | tf_op jit(solution)/shard_map/ppermute | solution.py:90
  152.2 7.8 %collective-permute-start.26 = (f32[256,256]{1,0:T(8,128)S(1)}, f32[256,256]{1,0:T(8,128)S(1)}, u32[]{:S(2)}, u32[]{:S(2)}) collective-permute-start(f32[256,256]{1,0:T(8,128)S(1)} %fusion.3), channel_id=1, source_target_pairs={{0,4},{1,13},{4,0},{5,9},{8,12},{9,5},{12,8},{13,1},{2,6},{3,15},{... | collective-permute-start | bytes 786440 | tf_op jit(solution)/shard_map/ppermute | solution.py:90
  158.3 7.0 %collective-permute-start.20 = (f32[128,256]{1,0:T(8,128)S(1)}, f32[128,256]{1,0:T(8,128)S(1)}, u32[]{:S(2)}, u32[]{:S(2)}) collective-permute-start(f32[128,256]{1,0:T(8,128)S(1)} %constant_dynamic-slice_fusion.8), channel_id=1, source_target_pairs={{0,48},{1,17},{16,32},{17,1},{32,16},{33,49},{48,0},{49,33},{2,50}... | collective-permute-start | bytes 393224 | tf_op jit(solution)/shard_map/ppermute | solution.py:90
  160.1 6.3 %collective-permute-start.27 = (f32[128,256]{1,0:T(8,128)S(1)}, f32[128,256]{1,0:T(8,128)S(1)}, u32[]{:S(2)}, u32[]{:S(2)}) collective-permute-start(f32[128,256]{1,0:T(8,128)S(1)} %constant_dynamic-slice_fusion.2), channel_id=1, source_target_pairs={{0,12},{1,5},{4,8},{5,1},{8,4},{9,13},{12,0},{13,9},{2,14},{3,7},{... | collective-permute-start | bytes 393224 | tf_op jit(solution)/shard_map/ppermute | solution.py:90
  161.8 6.3 %collective-permute-start.13 = (f32[136,256]{1,0:T(8,128)S(1)}, f32[136,256]{1,0:T(8,128)S(1)}, u32[]{:S(2)}, u32[]{:S(2)}) collective-permute-start(f32[136,256]{1,0:T(8,128)S(1)} %pad_maximum_fusion.4), channel_id=1, source_target_pairs={{0,66},{1,3},{2,64},{3,1},{64,2},{65,67},{66,0},{67,65},{4,70},{5,... | collective-permute-start | bytes 417800 | tf_op jit(solution)/shard_map/ppermute | solution.py:90
  165.4 4.3 %collective-permute-start.21 = (f32[64,256]{1,0:T(8,128)S(1)}, f32[64,256]{1,0:T(8,128)S(1)}, u32[]{:S(2)}, u32[]{:S(2)}) collective-permute-start(f32[64,256]{1,0:T(8,128)S(1)} %constant_dynamic-slice_fusion.7), channel_id=1, source_target_pairs={{0,4},{1,13},{4,0},{5,9},{8,12},{9,5},{12,8},{13,1},{2,6},{3,15},{... | collective-permute-start | bytes 196616 | tf_op jit(solution)/shard_map/ppermute | solution.py:90
  166.4 4.3 %collective-permute-start.28 = (f32[64,256]{1,0:T(8,128)S(1)}, f32[64,256]{1,0:T(8,128)S(1)}, u32[]{:S(2)}, u32[]{:S(2)}) collective-permute-start(f32[64,256]{1,0:T(8,128)S(1)} %constant_dynamic-slice_fusion.1), channel_id=1, source_target_pairs={{0,2},{1,67},{2,0},{3,65},{64,66},{65,3},{66,64},{67,1},{4,6},{5,7... | collective-permute-start | bytes 196616 | tf_op jit(solution)/shard_map/ppermute | solution.py:90
  168.2 4.4 %collective-permute-start.14 = (f32[72,256]{1,0:T(8,128)S(1)}, f32[72,256]{1,0:T(8,128)S(1)}, u32[]{:S(2)}, u32[]{:S(2)}) collective-permute-start(f32[72,256]{1,0:T(8,128)S(1)} %pad_maximum_fusion.5), channel_id=1, source_target_pairs={{0,16},{1,49},{16,0},{17,33},{32,48},{33,17},{48,32},{49,1},{2,18}... | collective-permute-start | bytes 221192 | tf_op jit(solution)/shard_map/ppermute | solution.py:90
  169.8 5.2 %collective-permute-start.22 = (f32[32,256]{1,0:T(8,128)S(1)}, f32[32,256]{1,0:T(8,128)S(1)}, u32[]{:S(2)}, u32[]{:S(2)}) collective-permute-start(f32[32,256]{1,0:T(8,128)S(1)} %constant_dynamic-slice_fusion.6), channel_id=1, source_target_pairs={{0,12},{1,5},{4,8},{5,1},{8,4},{9,13},{12,0},{13,9},{2,14},{3,7},{... | collective-permute-start | bytes 98312 | tf_op jit(solution)/shard_map/ppermute | solution.py:90
  170.8 5.2 %collective-permute-start.29 = (f32[32,256]{1,0:T(8,128)S(1)}, f32[32,256]{1,0:T(8,128)S(1)}, u32[]{:S(2)}, u32[]{:S(2)}) collective-permute-start(f32[32,256]{1,0:T(8,128)S(1)} %constant_dynamic-slice_fusion), channel_id=1, source_target_pairs={{0,66},{1,3},{2,64},{3,1},{64,2},{65,67},{66,0},{67,65},{4,70},{5,... | collective-permute-start | bytes 98312 | tf_op jit(solution)/shard_map/ppermute | solution.py:90
  172.7 5.3 %collective-permute-start.15 = (f32[40,256]{1,0:T(8,128)S(1)}, f32[40,256]{1,0:T(8,128)S(1)}, u32[]{:S(2)}, u32[]{:S(2)}) collective-permute-start(f32[40,256]{1,0:T(8,128)S(1)} %pad_maximum_fusion.8), channel_id=1, source_target_pairs={{0,48},{1,17},{16,32},{17,1},{32,16},{33,49},{48,0},{49,33},{2,50}... | collective-permute-start | bytes 122888 | tf_op jit(solution)/shard_map/ppermute | solution.py:90

commit v4 on v3

v4 whole, which is shorter than its diff:
```python
import functools

import jax
import jax.numpy as jnp
import numpy as np
from jax import lax
from jax.experimental import pallas as pl
from jax.experimental.pallas import tpu as pltpu
from jax.sharding import Mesh
from jax.sharding import PartitionSpec as P

SUB = 3
BATCHES = 64
FEW = 640
BX = ("bx_0", "bx_1")
BY = ("by_0", "by_1", "by_2")
CORE = "by_2"
AXES = {"x": ("by_0", CORE), "y": ("bx_0", "by_1", CORE), "z": ("bx_1", CORE)}
ORDERS = ("xyz", "yzx", "zxy")
DIGITS = ((0, 3, 1, 2), (0, 1, 2, 3))
RING = {
    1: [(2 * p + c, 2 * (p ^ 1 if c == 0 else 3 - p) + c) for p in range(4) for c in range(2)],
    2: [(2 * p + c, 2 * (3 - p if c == 0 else p ^ 1) + c) for p in range(4) for c in range(2)],
}
PAIR = [(0, 1), (1, 0)]


def edge_kernel(state_ref, low_ref, high_ref, left_ref, right_ref):
    for row in range(8):
        cells = state_ref[pl.ds(row, 128, stride=8), :]
        if row < SUB:
            low_ref[0, row * 128 : (row + 1) * 128, :] = cells
        if row >= 8 - SUB:
            high_ref[0, (row - 8 + SUB) * 128 : (row - 7 + SUB) * 128, :] = cells
        turned = cells.T
        left_ref[0, row * 8 : (row + 1) * 8, :] = turned[:8, :]
        right_ref[0, row * 8 : (row + 1) * 8, :] = turned[120:, :]


def transport_kernel(
    state_ref, above_ref, below_ref, left_ref, right_ref,
    coef_0, coef_1, coef_2, coef_3, coef_4, field_ref, x_ref, even_ref, odd_ref,
):
    lane = lax.broadcasted_iota(jnp.int32, (128, 128), 1)
    gap = jnp.zeros((112, 128), jnp.float32)
    at_x, at_y = lax.axis_index(BX), lax.axis_index(BY)
    inside = [jnp.where(at_x > 0, 1.0, 0.0), jnp.where(at_x < lax.axis_size(BX) - 1, 1.0, 0.0)]
    beside = jnp.where(
        lane < 64, jnp.where(at_y < lax.axis_size(BY) - 1, 1.0, 0.0), jnp.where(at_y > 0, 1.0, 0.0)
    )
    for row in range(-SUB, 8 + SUB):
        if 0 <= row < 8:
            cells = state_ref[pl.ds(row, 128, stride=8), :]
            left, right = (ref[0, row * 8 : (row + 1) * 8, :] for ref in (left_ref, right_ref))
        else:
            far_ref, at = (above_ref, row + SUB) if row < 0 else (below_ref, row - 8)
            cells = far_ref[0, at * 128 : (at + 1) * 128, :]
            left, right = (
                far_ref[0, side + at * 8 : side + (at + 1) * 8, :]
                for side in (SUB * 128, SUB * 136)
            )
        even_ref[row + SUB, 0] = cells
        even_ref[row + SUB, 1] = jnp.concatenate([right, gap, left], axis=0).T
    here, there = even_ref, odd_ref
    for substep in range(SUB):
        margin = SUB - substep - 1
        for row in range(-margin, 8 + margin):
            at = row + SUB
            main, side = here[at, 0], here[at, 1]
            main_up, side_up = pltpu.roll(main, 127, 1), pltpu.roll(side, 127, 1)
            main_down, side_down = pltpu.roll(main, 1, 1), pltpu.roll(side, 1, 1)
            new = (
                coef_0[...] * main
                + coef_1[...] * here[at + 1, 0]
                + coef_2[...] * here[at - 1, 0]
                + coef_3[...] * jnp.where(lane == 127, side_up, main_up)
                + coef_4[...] * jnp.where(lane == 0, side_down, main_down)
            )
            if margin == 0:
                field_ref[:, row * 128 : (row + 1) * 128] = new
                x_ref[:, row * 128 : (row + 1) * 128] = new.astype(jnp.bfloat16)
                continue
            near = (
                coef_0[...] * side
                + coef_1[...] * here[at + 1, 1]
                + coef_2[...] * here[at - 1, 1]
                + coef_3[...] * jnp.where(lane == 127, main_up, side_up)
                + coef_4[...] * jnp.where(lane == 0, main_down, side_down)
            ) * beside
            if row < 0 or row > 7:
                new = new * inside[0 if row < 0 else 1]
                near = near * inside[0 if row < 0 else 1]
            there[at, 0] = new
            there[at, 1] = near
        here, there = there, here


def shifted(value, axis, step):
    count = lax.axis_size(axis)
    pairs = [(i, i + step) for i in range(count) if 0 <= i + step < count]
    return lax.ppermute(value, axis, pairs)


def transported(state, diffusion, speed_x, speed_y):
    feats = state.shape[0]
    f32 = jnp.float32
    flat = in_hbm(state.reshape(feats * 8, 128))
    chunk = lambda rows: pl.BlockSpec((1, rows, 128), lambda i: (i, 0, 0))
    low, high, left, right = pl.pallas_call(
        edge_kernel,
        grid=(feats // 128,),
        in_specs=[pl.BlockSpec((1024, 128), lambda i: (i, 0))],
        out_specs=[chunk(SUB * 144), chunk(SUB * 144), chunk(64), chunk(64)],
        out_shape=[shaped(f32, feats // 128, rows, 128) for rows in (SUB * 144, SUB * 144, 64, 64)],
        compiler_params=params(16),
        cost_estimate=pl.CostEstimate(flops=2**20, bytes_accessed=3 * 2**20, transcendentals=0),
        name="edges",
    )(flat)
    from_left = shifted(right, BY, 1)
    from_right = shifted(left, BY, -1)
    low, high = (
        lax.dynamic_update_slice(
            edge, jnp.concatenate([from_left[:, rows], from_right[:, rows]], axis=1), (0, SUB * 128, 0)
        )
        for edge, rows in ((low, slice(0, SUB * 8)), (high, slice((8 - SUB) * 8, 64)))
    )
    above = shifted(high, BX, 1)
    below = shifted(low, BX, -1)
    coefs = [
        jnp.broadcast_to(value[:, None], (feats, 128))
        for value in (
            1.0 - 4.0 * diffusion,
            diffusion - 0.5 * speed_x,
            diffusion + 0.5 * speed_x,
            diffusion - 0.5 * speed_y,
            diffusion + 0.5 * speed_y,
        )
    ]
    field, x = pl.pallas_call(
        transport_kernel,
        grid=(feats // 128,),
        in_specs=[
            pl.BlockSpec((1024, 128), lambda i: (i, 0)),
            chunk(SUB * 144),
            chunk(SUB * 144),
            chunk(64),
            chunk(64),
        ]
        + [pl.BlockSpec((128, 128), lambda i: (i, 0))] * 5,
        out_specs=[pl.BlockSpec((128, 1024), lambda i: (i, 0))] * 2,
        scratch_shapes=[pltpu.VMEM((14, 2, 128, 128), f32)] * 2,
        out_shape=[pltpu.HBM((feats, 1024), f32), pltpu.HBM((feats, 1024), jnp.bfloat16)],
        compiler_params=params(16),
        cost_estimate=pl.CostEstimate(flops=2**24, bytes_accessed=6 * 2**20, transcendentals=0),
        name="transport",
    )(flat, above, below, from_left, from_right, *coefs)
    return field, x, (from_left, from_right)


def position(axis):
    if axis == "y":
        return lax.axis_index("bx_0") * 2 + lax.axis_index("by_1")
    return lax.axis_index("by_0" if axis == "x" else "bx_1")


def ring_places():
    core = lax.axis_index(CORE)
    places = {}
    for axis in "xyz":
        at = position(axis)
        folded = jnp.where(at == 0, 0, jnp.where(at == 3, 1, at + 1))
        places[axis] = jnp.where(core == 0, folded, at)
    return places


def half_of(rows, size, bit):
    return lax.dynamic_slice_in_dim(rows, bit * size, size, 0)


def ring_turn(terms, axis, turn, places, riding=None):
    bit = places[axis] % 2 if turn else places[axis] // 2
    size = terms[0].shape[0] // 2
    leaving = sum(half_of(term, size, 1 - bit) for term in terms)
    if riding is not None:
        leaving = jnp.concatenate([leaving, riding], axis=0)
    coming = lax.ppermute(leaving, AXES[axis], RING[turn + 1])
    staying = sum(half_of(term, size, bit) for term in terms)
    return [staying + coming[:size]], (None if riding is None else riding + coming[size:])


def ring_round(streams, stage, turn, places, riding=None):
    moved = []
    for stream, order in enumerate(ORDERS):
        terms, carried = ring_turn(
            streams[stream], order[stage], turn, places, riding if stream == 0 else None
        )
        riding = carried if stream == 0 else riding
        moved.append(terms)
    return moved, riding


def ring_rows():
    table = np.zeros((2, len(ORDERS), 64), np.int32)
    for core in range(2):
        for block in range(64):
            y_hi, z, x, y_lo = block // 32, block // 8 % 4, block // 2 % 4, block % 2
            at = {"x": x, "y": 2 * y_hi + y_lo, "z": z}
            for stream, order in enumerate(ORDERS):
                spot = 0
                for axis in order:
                    spot = spot * 4 + DIGITS[core].index(at[axis])
                table[core, stream, block] = spot * 32
    return table.reshape(-1)


def put_rows(table_ref, source_ref, base, right, lanes, kept_refs, sent_refs):
    core = lax.axis_index(CORE)
    for slot, out_refs in enumerate((kept_refs, sent_refs)):
        digit = core if slot == 0 else 1 - core
        left = source_ref[:, digit, :, : right.shape[0]].reshape(256, right.shape[0])
        sums = jnp.dot(left, right, preferred_element_type=jnp.float32)
        for block in range(8):
            for stream in range(3):
                row = table_ref[digit * 192 + stream * 64 + base + block]
                out_refs[stream][pl.ds(pl.multiple_of(row, 32), 32), lanes] = sums[
                    block * 32 : (block + 1) * 32, stream * 128 : (stream + 1) * 128
                ]


def by_width(scalar_ref, most, body):
    land = scalar_ref[0]
    pl.when(land <= FEW)(functools.partial(body, FEW))
    pl.when(land > FEW)(functools.partial(body, most))


ROWS = (((1,), (1,)), ((), ()))


def network_kernel(
    scale, scalar_ref, table_ref, x_ref, win_ref, wout_f_ref, wout_ref, target_ref, rank_ref, batch_ref, field_ref,
    new_ref, kept_a, kept_b, kept_c, sent_a, sent_b, sent_c, loss_ref,
    slope_ref, hidden_ref, tend_ref, pick_ref, xc_ref, xn_ref, dtend_ref, dtn_ref, dpre_ref,
):
    step = pl.program_id(0)
    feats, cols = x_ref.shape
    kept, sent = (kept_a, kept_b, kept_c), (sent_a, sent_b, sent_c)

    def start(n):
        for at in range(0, n, 128):
            slot = lax.broadcasted_iota(jnp.int32, (128, cols), 0) + at
            pick_ref[at : at + 128, :] = jnp.where(slot == rank_ref[...], 1.0, 0.0).astype(jnp.bfloat16)
        packed = lax.dot_general(x_ref[...], pick_ref[:n, :], ROWS, preferred_element_type=jnp.float32)
        packed = packed.astype(jnp.bfloat16)
        xc_ref[:, :n] = packed
        xn_ref[:n, :] = packed.T
        tend_ref[:, :n] = jnp.zeros((feats, n), jnp.float32)

    def forward(n):
        for part in range(2):
            rows = slice(part * 256, (part + 1) * 256)
            pre = jnp.dot(win_ref[:, rows].T, xc_ref[:, :n], preferred_element_type=jnp.float32)
            sig = 0.5 * jnp.tanh(0.5 * pre) + 0.5
            act = pre * sig
            slope_ref[pl.ds(pl.multiple_of(step * 512 + part * 256, 256), 256), :n] = sig + act * (1.0 - sig)
            hid = act.astype(jnp.bfloat16)
            hidden_ref[pl.ds(step * 8 + part * 4, 4), :, :, :n] = hid.reshape(4, 2, 32, n)
            tend_ref[:, :n] += jnp.dot(wout_f_ref[rows, :].T, hid, preferred_element_type=jnp.float32)

    def middle(n):
        pick = pick_ref[:n, :]
        tend = tend_ref[:, :n]
        wanted = lax.dot_general(target_ref[...], pick, ROWS, preferred_element_type=jnp.float32)
        err = tend - wanted
        dtend = (err * scale[1]).astype(jnp.bfloat16)
        dtend_ref[:, :n] = dtend
        dtn_ref[:n, :] = dtend.T
        coarse = tend.astype(jnp.bfloat16)
        fine = (tend - coarse.astype(jnp.float32)).astype(jnp.bfloat16)
        spread = jnp.dot(coarse, pick, preferred_element_type=jnp.float32)
        spread += jnp.dot(fine, pick, preferred_element_type=jnp.float32)
        new = field_ref[...] + 0.5 * spread
        for row in range(8):
            new_ref[pl.ds(row, feats, stride=8), :] = new[:, row * 128 : (row + 1) * 128]
        persq = 0.5 * jnp.sum(err * err, axis=0, keepdims=True)
        batch = lax.dot_general(batch_ref[...], pick, ROWS, preferred_element_type=jnp.float32)
        which = lax.broadcasted_iota(jnp.int32, (128, n), 0).astype(jnp.float32)
        onehot = jnp.where(which == batch[0:1, :], 1.0, 0.0)
        loss = scale[0] * lax.dot_general(
            jnp.broadcast_to(persq, (8, n)),
            onehot,
            ROWS,
            precision=lax.Precision.HIGHEST,
            preferred_element_type=jnp.float32,
        )
        for side in (0, 128):
            sent_a[2048:, side : side + 128] = loss
            loss_ref[:, side : side + 128] = loss

    def backward(n):
        piece = step - 8
        for part in range(2):
            rows = slice(part * 256, (part + 1) * 256)
            dhid = jnp.dot(wout_ref[rows, :], dtend_ref[:, :n], preferred_element_type=jnp.float32)
            slope = slope_ref[pl.ds(pl.multiple_of(piece * 512 + part * 256, 256), 256), :n]
            dpre = (dhid * slope).astype(jnp.bfloat16)
            dpre_ref[part * 4 : (part + 1) * 4, :, :, :n] = dpre.reshape(4, 2, 32, n)
        base = piece * 8
        here = hidden_ref.at[pl.ds(base, 8)]
        put_rows(table_ref, here, base, dtn_ref[:n, :], slice(0, 128), kept, sent)
        put_rows(table_ref, dpre_ref, base, xn_ref[:n, :], slice(128, 256), kept, sent)

    pl.when(step == 0)(lambda: by_width(scalar_ref, cols, start))
    pl.when(step < 8)(lambda: by_width(scalar_ref, cols, forward))
    pl.when(step == 7)(lambda: by_width(scalar_ref, cols, middle))
    pl.when(step >= 8)(lambda: by_width(scalar_ref, cols, backward))


def in_hbm(value):
    return pltpu.with_memory_space_constraint(value, pltpu.HBM)


def whole(*shape):
    return pl.BlockSpec(shape, lambda i, *_: (0,) * len(shape), pipeline_mode=pl.Buffered(1))


def shaped(dtype, *shape):
    return jax.ShapeDtypeStruct(shape, dtype)


def params(megabytes):
    return pltpu.CompilerParams(dimension_semantics=("arbitrary",), vmem_limit_bytes=megabytes * 2**20)


def ranks_kernel(mask_ref, batch_ref, ranks_ref, batches_ref, land_ref):
    mask = mask_ref[...]
    ones = mask.astype(jnp.float32)
    first = lax.broadcasted_iota(jnp.int32, (128, 128), 0) < lax.broadcasted_iota(jnp.int32, (128, 128), 1)
    before = jnp.where(first, 1.0, 0.0).astype(jnp.bfloat16)
    within = jnp.dot(ones.astype(jnp.bfloat16), before, preferred_element_type=jnp.float32)
    batch = batch_ref[...].astype(jnp.float32)
    above = jnp.zeros((1, 1), jnp.float32)
    for row in range(8):
        lanes = slice(row * 128, (row + 1) * 128)
        rank = (within[row : row + 1, :] + above).astype(jnp.int32)
        ranks_ref[:, lanes] = jnp.where(mask[row : row + 1, :] > 0, rank, -1)
        batches_ref[:, lanes] = jnp.broadcast_to(batch[row : row + 1, :], (8, 128)).astype(jnp.bfloat16)
        above += jnp.sum(ones[row : row + 1, :], axis=1, keepdims=True)
    land_ref[0] = jnp.sum(ones).astype(jnp.int32)


def land_ranks(mask, batch):
    cols = mask.size
    return pl.pallas_call(
        ranks_kernel,
        in_specs=[pl.BlockSpec(memory_space=pltpu.VMEM)] * 2,
        out_specs=[pl.BlockSpec(memory_space=pltpu.VMEM)] * 2 + [pl.BlockSpec(memory_space=pltpu.SMEM)],
        out_shape=[shaped(jnp.int32, 1, cols), shaped(jnp.bfloat16, 8, cols), shaped(jnp.int32, 1)],
        compiler_params=pltpu.CompilerParams(vmem_limit_bytes=2**21),
        cost_estimate=pl.CostEstimate(flops=2**20, bytes_accessed=2**16, transcendentals=0),
        name="ranks",
    )(mask, batch)


def network(x, field, target, mask, batch, w_in, w_out, total, places):
    feats, cols = x.shape
    hid = w_out.shape[0]
    ranks, batch, land = land_ranks(mask, batch)
    table = jnp.asarray(ring_rows())
    f32, bf16 = jnp.float32, jnp.bfloat16
    tail = [2048, 2048, 2048, 2056, 2048, 2048]
    new, *halves = pl.pallas_call(
        functools.partial(network_kernel, (BATCHES / (total * feats), total ** (-0.5))),
        grid_spec=pltpu.PrefetchScalarGridSpec(
            num_scalar_prefetch=2,
            grid=(16,),
            in_specs=[
                whole(feats, cols),
                pl.BlockSpec((feats, 512), lambda i, *_: (0, jnp.minimum(i, 7))),
                pl.BlockSpec((512, feats), lambda i, *_: (jnp.minimum(i, 7), 0)),
                pl.BlockSpec((512, feats), lambda i, *_: (jnp.maximum(i - 8, 0), 0)),
                whole(feats, cols),
                whole(1, cols),
                whole(8, cols),
                whole(feats, cols),
            ],
            out_specs=[whole(feats * 8, cols // 8)]
            + [whole(size, 256) for size in tail + [8]],
            scratch_shapes=[
                pltpu.VMEM((hid, cols), f32),
                pltpu.VMEM((64, 2, 32, cols), bf16),
                pltpu.VMEM((feats, cols), f32),
                pltpu.VMEM((cols, cols), bf16),
                pltpu.VMEM((feats, cols), bf16),
                pltpu.VMEM((cols, feats), bf16),
                pltpu.VMEM((feats, cols), bf16),
                pltpu.VMEM((cols, feats), bf16),
                pltpu.VMEM((8, 2, 32, cols), bf16),
            ],
        ),
        out_shape=[shaped(f32, feats * 8, cols // 8)] + [shaped(f32, size, 256) for size in tail + [8]],
        compiler_params=params(58),
        cost_estimate=pl.CostEstimate(
            flops=10 * cols * feats * hid, bytes_accessed=20 * 2**20, transcendentals=cols * hid
        ),
        name="network",
    )(land, table, in_hbm(x), w_in, w_out, w_out, target, ranks, batch, in_hbm(field))
    streams = [[kept, lax.ppermute(sent, CORE, PAIR)] for kept, sent in zip(halves[:3], halves[3:6])]
    losses = halves[6] + streams[0][1][2048:]
    for stage in range(3):
        for turn in range(2):
            streams, losses = ring_round(streams, stage, turn, places, losses)
    grad_out = jnp.concatenate([part[:, :128] for (part,) in streams], axis=1)
    grad_in = jnp.concatenate([part[:, 128:] for (part,) in streams], axis=1)
    return new, grad_in, grad_out, losses[0, :BATCHES]


def on_device(state, target, land_mask, batch_map, diffusion, speed_x, speed_y, w_in, w_out):
    feats, rows_x, rows_y = state.shape
    field, x, strips = transported(state, diffusion, speed_x, speed_y)
    target, land_mask, batch_map, *_ = lax.optimization_barrier((target, land_mask, batch_map, *strips))
    local_cols = rows_x * rows_y
    total = local_cols * lax.axis_size(BX) * lax.axis_size(BY)
    new, grad_in, grad_out, batch_loss = network(
        x,
        field,
        target.reshape(feats, local_cols),
        land_mask,
        batch_map,
        w_in,
        w_out,
        total,
        ring_places(),
    )
    return (new.reshape(feats, rows_x, rows_y), grad_in, grad_out, batch_loss)


def solution(mesh):
    torus = Mesh(mesh.devices.reshape(2, 4, 4, 2, 2), BX + BY)
    return jax.shard_map(
        on_device,
        mesh=torus,
        in_specs=(P(None, BX, BY), P(None, BX, BY), P(BX, BY), P(BX, BY), P(), P(), P(), P(), P()),
        out_specs=(P(None, BX, BY), P(BX + BY, None), P(BX + BY, None), P()),
        check_vma=False,
    )
```

time: 181 us -> 155 us (0.86)
  local copies, waits for them, and re-layouts: 35.8 us -> 3.25 us
  other arithmetic: 22.7 us -> 12.3 us
  Pallas kernels: 38.4 us -> 47.6 us
  waiting for transfers between devices: 37.2 us -> 42.2 us
  starting transfers between devices: 43.5 us -> 47.6 us
    unnamed x39 -> x25, local copies, waits for them, and re-layouts: 23.9 us -> 2.33 us
    ppermute x6 -> x7, waiting for transfers between devices: 1.26 us -> 20.5 us  [the longest x4 15.5 us: shifted(): return lax.ppermute(value, axis, pairs)]
    ppermute x24 -> x18, waiting for transfers between devices: 36 us -> 21.7 us  [ring_turn(): coming = lax.ppermute(leaving, AXES[axis], RING[turn + 1])]
    ppermute x24 -> x18, starting transfers between devices: 27.4 us -> 37 us  [ring_turn(): coming = lax.ppermute(leaving, AXES[axis], RING[turn + 1])]
    pallas_call x3 -> x4, Pallas kernels: 38.4 us -> 47.6 us  [the longest x1 33.9 us: network(): pl.pallas_call(functools.partial(network_kernel, (BATCHES / (total * feat...]
    ppermute x6 -> x7, starting transfers between devices: 16.1 us -> 10.7 us  [the longest x4 9.57 us: shifted(): return lax.ppermute(value, axis, pairs)]
    ppermute x4 -> x0, local copies, waits for them, and re-layouts: 4.51 us -> none  [the longest x2 2.27 us: extended(): lax.ppermute(tail, axis, [(i, (i + 1) % count) for i in range(ends)])]
    concatenate x7 -> x1, other arithmetic: 3.98 us -> 0.64 us  [network(): grad_in = jnp.concatenate([part[:, 128:] for part, in streams], axis=1)]
  transfers between devices with their start and end apart: 30 -> 25, of which waited for: 17 -> 15; matrix products, arithmetic and copies ran while one was open for 15% -> 8% of each run, Pallas kernels for 7% -> 0%
where the time goes in v4:
time: 155 us; the launch traced here: 154 us
  Pallas kernels  47.6 us (31%)
  starting transfers between devices  47.6 us (31%)
  waiting for transfers between devices  42.2 us (27%)
  other arithmetic  12.3 us (8%)
  local copies, waits for them, and re-layouts  3.25 us (2%)
    ppermute x18, starting transfers between devices, ring_turn(): coming = lax.ppermute(leaving, AXES[axis], RING[turn + 1])  37 us
    pallas_call x1, Pallas kernels, network(): pl.pallas_call(functools.partial(network_kernel, (BATCHES / (total * feat...  33.9 us
    ppermute x18, waiting for transfers between devices, ring_turn(): coming = lax.ppermute(leaving, AXES[axis], RING[turn + 1])  21.7 us
    ppermute x4, waiting for transfers between devices, shifted(): return lax.ppermute(value, axis, pairs)  15.5 us
    pallas_call x1, Pallas kernels, transported(): pl.pallas_call(transport_kernel, grid=(feats // 128,), in_specs=[pl.Block...  10.5 us
    ppermute x4, starting transfers between devices, shifted(): return lax.ppermute(value, axis, pairs)  9.57 us
    add x3, other arithmetic, ring_turn(): leaving = sum((half_of(term, size, 1 - bit) for term in terms))  5.51 us
    ppermute x3, waiting for transfers between devices, network(): lax.ppermute(sent, CORE, PAIR)  5.06 us
  transfers between devices with their start and end apart: 25, of which 15 were waited for; matrix products, arithmetic and copies ran while one was open for 8% of the time, Pallas kernels for 0%

profile of v4, /device:TPU:0, one launch (start us, length us, event | category | flops | bytes accessed | tf_op | source)
XLA Modules:
  0.0 154.2 jit_solution(1247005096765670240)
XLA Ops:
  0.7 2.6 %edges.1 = (f32[3,432,128]{2,1,0:T(8,128)S(1)}, f32[3,432,128]{2,1,0:T(8,128)S(1)}, f32[3,64,128]{2,1,0:T(8,128)S(1)}, f32[3,64,128]{2,1,0:T(8,128)S(1)}) custom-call(f32[3072,128]{1,0:T(8,128)} %bitcast.8), custom_call_target="tpu_custom_call" | custom-call | flops 1048576 | bytes 3145728 | tf_op jit(solution)/shard_map/edges/pallas_call | solution.py:109
  3.3 1.3 collective-permute-start.1
  4.6 3.0 %collective-permute-start = (f32[3,64,128]{2,1,0:T(8,128)S(1)}, f32[3,64,128]{2,1,0:T(8,128)S(1)}, u32[]{:S(2)}, u32[]{:S(2)}) collective-permute-start(f32[3,64,128]{2,1,0:T(8,128)S(1)} %get-tuple-element.24), channel_id=1, source_target_pairs={{0,1},{1,2},{2,3},{3,4},{4,5},{5,6},{6,7},{7,8},{8,9},{9,10},{10,1... | collective-permute-start | bytes 294920 | tf_op jit(solution)/shard_map/ppermute | solution.py:101
  7.7 0.9 collective-permute-done.left_ref
  8.6 3.9 %collective-permute-start.2 = (f32[3,432,128]{2,1,0:T(8,128)S(1)}, f32[3,432,128]{2,1,0:T(8,128)S(1)}, u32[]{:S(2)}, u32[]{:S(2)}) collective-permute-start(f32[3,432,128]{2,1,0:T(8,128)S(1)} %maximum_dynamic-update-slice_fusion), channel_id=1, source_target_pairs={{0,16},{16,32},{32,48},{48,64},{64,80},{80,96},{96,112},{1,17},{17... | collective-permute-start | bytes 1990664 | tf_op jit(solution)/shard_map/ppermute | solution.py:101
  12.6 1.3 collective-permute-start.3
  13.9 1.1 copy.16
  15.0 0.7 ranks.1
  15.7 0.6 copy-done.2
  16.3 0.6 copy-done.3
  16.9 10.0 %collective-permute-done.2.above_ref = f32[3,432,128]{2,1,0:T(8,128)S(1)} collective-permute-done((f32[3,432,128]{2,1,0:T(8,128)S(1)}, f32[3,432,128]{2,1,0:T(8,128)S(1)}, u32[]{:S(2)}, u32[]{:S(2)}) %collective-permute-start.2) | collective-permute-done | bytes 663584 | tf_op jit(solution)/shard_map/ppermute | solution.py:101
  26.9 4.6 %collective-permute-done.3.below_ref = f32[3,432,128]{2,1,0:T(8,128)S(1)} collective-permute-done((f32[3,432,128]{2,1,0:T(8,128)S(1)}, f32[3,432,128]{2,1,0:T(8,128)S(1)}, u32[]{:S(2)}, u32[]{:S(2)}) %collective-permute-start.3) | collective-permute-done | bytes 663584 | tf_op jit(solution)/shard_map/ppermute | solution.py:101
  31.5 0.1 broadcast_in_dim.10.coef_0
  31.6 0.1 broadcast_in_dim.11.coef_1
  31.7 0.1 broadcast_in_dim.12.coef_2
  31.8 0.1 broadcast_in_dim.13.coef_3
  31.9 0.1 broadcast_in_dim.14.coef_4
  32.1 10.5 %transport.1 = (f32[384,1024]{1,0:T(8,128)}, bf16[384,1024]{1,0:T(8,128)(2,1)}) custom-call(f32[3072,128]{1,0:T(8,128)} %bitcast.9, f32[3,432,128]{2,1,0:T(8,128)S(1)} %collective-permute-done.2.above_ref, f32[3,432,128]{2,1,0:T(8,128)S(1)} %collective-permute-done.3.below_ref, f32[3,64,128]{2,1,0:T(8,128)S(1)} %collective-permute-done.left_ref, ...), custom_call_target="tpu_custom_call" | custom-call | flops 16777216 | bytes 6291456 | tf_op jit(solution)/shard_map/transport/pallas_call | solution.py:139
  42.5 33.9 %network.1 = (f32[3072,128]{1,0:T(8,128)}, f32[2048,256]{1,0:T(8,128)}, f32[2048,256]{1,0:T(8,128)}, f32[2048,256]{1,0:T(8,128)}, f32[2056,256]{1,0:T(8,128)}, /...) custom-call(s32[1]{0:T(128)} %get-tuple-element.28.scalar_ref, s32[384]{0:T(512)} %constant.119.clone.table_ref, ...), custom_call_target="tpu_custom_call" | custom-call | flops 16106127360 | bytes 20971520 | tf_op jit(solution)/shard_map/network/pallas_call | solution.py:371
  76.4 0.6 collective-permute-start.18
  77.0 0.1 collective-permute-start.11
  77.1 0.4 collective-permute-start.4
  77.5 3.6 %collective-permute-done.18 = f32[2048,256]{1,0:T(8,128)} collective-permute-done((f32[2048,256]{1,0:T(8,128)}, f32[2048,256]{1,0:T(8,128)}, u32[]{:S(2)}, u32[]{:S(2)}) %collective-permute-start.18) | collective-permute-done | bytes 2097184 | tf_op jit(solution)/shard_map/ppermute | solution.py:407
  81.1 2.7 %dynamic-slice_add_fusion = f32[1024,256]{1,0:T(8,128)} fusion(f32[2048,256]{1,0:T(8,128)} %collective-permute-done.18, s32[]{:T(128)S(6)} %select_n.231, f32[2048,256]{1,0:T(8,128)} %get-tuple-element.42), kind=kLoop, calls=%fused_computation.2 | loop fusion | flops 262144 | bytes 3145732 | tf_op jit(solution)/shard_map/add | solution.py:183
  83.8 1.9 %collective-permute-start.19 = (f32[1024,256]{1,0:T(8,128)}, f32[1024,256]{1,0:T(8,128)}, u32[]{:S(2)}, u32[]{:S(2)}) collective-permute-start(f32[1024,256]{1,0:T(8,128)} %dynamic-slice_add_fusion), channel_id=1, source_target_pairs={{0,16},{1,49},{16,0},{17,33},{32,48},{33,17},{48,32},{49,1},{2,18}... | collective-permute-start | bytes 3145736 | tf_op jit(solution)/shard_map/ppermute | solution.py:186
  85.7 1.4 collective-permute-done.11
  87.1 2.7 %dynamic-slice_add_fusion.1 = f32[1024,256]{1,0:T(8,128)} fusion(f32[2048,256]{1,0:T(8,128)} %collective-permute-done.11, s32[]{:T(128)S(6)} %select_n.219, f32[2048,256]{1,0:T(8,128)} %get-tuple-element.40), kind=kLoop, calls=%fused_computation.4 | loop fusion | flops 262144 | bytes 3145732 | tf_op jit(solution)/shard_map/add | solution.py:183
  89.8 3.7 %collective-permute-start.12 = (f32[1024,256]{1,0:T(8,128)}, f32[1024,256]{1,0:T(8,128)}, u32[]{:S(2)}, u32[]{:S(2)}) collective-permute-start(f32[1024,256]{1,0:T(8,128)} %dynamic-slice_add_fusion.1), channel_id=1, source_target_pairs={{0,2},{1,67},{2,0},{3,65},{64,66},{65,3},{66,64},{67,1},{4,6},{5,7... | collective-permute-start | bytes 3145736 | tf_op jit(solution)/shard_map/ppermute | solution.py:186
  93.6 0.1 dynamic-slice_add_fusion.2
  93.7 1.1 pad_maximum_fusion
  94.8 1.5 collective-permute-start.5
  96.3 2.6 %collective-permute-done.19 = f32[1024,256]{1,0:T(8,128)} collective-permute-done((f32[1024,256]{1,0:T(8,128)}, f32[1024,256]{1,0:T(8,128)}, u32[]{:S(2)}, u32[]{:S(2)}) %collective-permute-start.19) | collective-permute-done | bytes 1048608 | tf_op jit(solution)/shard_map/ppermute | solution.py:186
  98.9 2.1 %add_add_fusion = f32[1024,256]{1,0:T(8,128)S(1)} fusion(f32[1024,256]{1,0:T(8,128)} %collective-permute-done.19, f32[2048,256]{1,0:T(8,128)} %collective-permute-done.18, s32[]{:T(128)S(6)} %select_n.230, f32[2048,256]{1,0:T(8,128)} %get-tuple-element.42), kind=kLoop, calls=%fused_computation.3 | loop fusion | flops 524288 | bytes 4194308 | tf_op jit(solution)/shard_map/add | solution.py:188
  101.0 7.7 %collective-permute-start.20 = (f32[512,256]{1,0:T(8,128)S(1)}, f32[512,256]{1,0:T(8,128)S(1)}, u32[]{:S(2)}, u32[]{:S(2)}) collective-permute-start(f32[512,256]{1,0:T(8,128)S(1)} %constant_dynamic-slice_fusion.2), channel_id=1, source_target_pairs={{0,48},{1,17},{16,32},{17,1},{32,16},{33,49},{48,0},{49,33},{2,50}... | collective-permute-start | bytes 1572872 | tf_op jit(solution)/shard_map/ppermute | solution.py:186
  108.8 1.7 %add_add_fusion.1 = f32[1024,256]{1,0:T(8,128)S(1)} fusion(f32[1024,256]{1,0:T(8,128)} %collective-permute-done.12, f32[2048,256]{1,0:T(8,128)} %collective-permute-done.11, s32[]{:T(128)S(6)} %select_n.218, f32[2048,256]{1,0:T(8,128)S(1)} %copy-done.6), kind=kLoop, calls=%fused_computation.5 | loop fusion | flops 524288 | bytes 4194308 | tf_op jit(solution)/shard_map/add | solution.py:188
  110.6 2.5 %collective-permute-start.13 = (f32[512,256]{1,0:T(8,128)S(1)}, f32[512,256]{1,0:T(8,128)S(1)}, u32[]{:S(2)}, u32[]{:S(2)}) collective-permute-start(f32[512,256]{1,0:T(8,128)S(1)} %constant_dynamic-slice_fusion.8), channel_id=1, source_target_pairs={{0,66},{1,3},{2,64},{3,1},{64,2},{65,67},{66,0},{67,65},{4,70},{5,... | collective-permute-start | bytes 1572872 | tf_op jit(solution)/shard_map/ppermute | solution.py:186
  113.0 0.2 slice_add_fusion
  113.4 1.4 collective-permute-start.6
  114.8 1.1 collective-permute-done.20
  115.9 0.1 dynamic-slice_add_fusion.3
  116.0 2.5 %collective-permute-start.21 = (f32[256,256]{1,0:T(8,128)S(1)}, f32[256,256]{1,0:T(8,128)S(1)}, u32[]{:S(2)}, u32[]{:S(2)}) collective-permute-start(f32[256,256]{1,0:T(8,128)S(1)} %constant_dynamic-slice_fusion.1), channel_id=1, source_target_pairs={{0,4},{1,13},{4,0},{5,9},{8,12},{9,5},{12,8},{13,1},{2,6},{3,15},{... | collective-permute-start | bytes 786440 | tf_op jit(solution)/shard_map/ppermute | solution.py:186
  118.6 2.5 %collective-permute-done.13 = f32[512,256]{1,0:T(8,128)S(1)} collective-permute-done((f32[512,256]{1,0:T(8,128)S(1)}, f32[512,256]{1,0:T(8,128)S(1)}, u32[]{:S(2)}, u32[]{:S(2)}) %collective-permute-start.13) | collective-permute-done | bytes 524320 | tf_op jit(solution)/shard_map/ppermute | solution.py:186
  121.0 0.1 dynamic-slice_add_fusion.4
  121.1 0.1 collective-permute-start.14
  121.2 5.5 %collective-permute-done.6 = f32[520,256]{1,0:T(8,128)S(1)} collective-permute-done((f32[520,256]{1,0:T(8,128)S(1)}, f32[520,256]{1,0:T(8,128)S(1)}, u32[]{:S(2)}, u32[]{:S(2)}) %collective-permute-start.6) | collective-permute-done | bytes 532512 | tf_op jit(solution)/shard_map/ppermute | solution.py:186
  126.8 0.1 slice_add_fusion.1
  126.9 0.3 collective-permute-start.7
  127.2 1.9 %collective-permute-start.22 = (f32[128,256]{1,0:T(8,128)S(1)}, f32[128,256]{1,0:T(8,128)S(1)}, u32[]{:S(2)}, u32[]{:S(2)}) collective-permute-start(f32[128,256]{1,0:T(8,128)S(1)} %constant_dynamic-slice_fusion), channel_id=1, source_target_pairs={{0,12},{1,5},{4,8},{5,1},{8,4},{9,13},{12,0},{13,9},{2,14},{3,7},{... | collective-permute-start | bytes 393224 | tf_op jit(solution)/shard_map/ppermute | solution.py:186
  129.2 4.6 %collective-permute-start.15 = (f32[128,256]{1,0:T(8,128)S(1)}, f32[128,256]{1,0:T(8,128)S(1)}, u32[]{:S(2)}, u32[]{:S(2)}) collective-permute-start(f32[128,256]{1,0:T(8,128)S(1)} %constant_dynamic-slice_fusion.6), channel_id=1, source_target_pairs={{0,48},{1,17},{16,32},{17,1},{32,16},{33,49},{48,0},{49,33},{2,50}... | collective-permute-start | bytes 393224 | tf_op jit(solution)/shard_map/ppermute | solution.py:186
  133.8 0.5 collective-permute-done.7
  134.4 0.9 collective-permute-start.8
  135.3 0.6 collective-permute-start.23
  135.9 0.9 collective-permute-done.15
  136.8 0.3 collective-permute-start.16
  137.1 3.6 %collective-permute-done.8 = f32[136,256]{1,0:T(8,128)S(1)} collective-permute-done((f32[136,256]{1,0:T(8,128)S(1)}, f32[136,256]{1,0:T(8,128)S(1)}, u32[]{:S(2)}, u32[]{:S(2)}) %collective-permute-start.8) | collective-permute-done | bytes 139296 | tf_op jit(solution)/shard_map/ppermute | solution.py:186
  140.8 0.5 collective-permute-start.9
  141.3 0.9 collective-permute-start.24
  142.2 2.1 %collective-permute-start.17 = (f32[32,256]{1,0:T(8,128)S(1)}, f32[32,256]{1,0:T(8,128)S(1)}, u32[]{:S(2)}, u32[]{:S(2)}) collective-permute-start(f32[32,256]{1,0:T(8,128)S(1)} %constant_dynamic-slice_fusion.4), channel_id=1, source_target_pairs={{0,12},{1,5},{4,8},{5,1},{8,4},{9,13},{12,0},{13,9},{2,14},{3,7},{... | collective-permute-start | bytes 98312 | tf_op jit(solution)/shard_map/ppermute | solution.py:186
  144.4 2.2 %collective-permute-done.24 = f32[32,256]{1,0:T(8,128)S(1)} collective-permute-done((f32[32,256]{1,0:T(8,128)S(1)}, f32[32,256]{1,0:T(8,128)S(1)}, u32[]{:S(2)}, u32[]{:S(2)}) %collective-permute-start.24) | collective-permute-done | bytes 32800 | tf_op jit(solution)/shard_map/ppermute | solution.py:186
  146.5 0.9 collective-permute-done.17
  147.5 3.5 %collective-permute-start.10 = (f32[40,256]{1,0:T(8,128)S(1)}, f32[40,256]{1,0:T(8,128)S(1)}, u32[]{:S(2)}, u32[]{:S(2)}) collective-permute-start(f32[40,256]{1,0:T(8,128)S(1)} %pad_maximum_fusion.7), channel_id=1, source_target_pairs={{0,48},{1,17},{16,32},{17,1},{32,16},{33,49},{48,0},{49,33},{2,50}... | collective-permute-start | bytes 122888 | tf_op jit(solution)/shard_map/ppermute | solution.py:186
  151.1 2.0 %collective-permute-done.10 = f32[40,256]{1,0:T(8,128)S(1)} collective-permute-done((f32[40,256]{1,0:T(8,128)S(1)}, f32[40,256]{1,0:T(8,128)S(1)}, u32[]{:S(2)}, u32[]{:S(2)}) %collective-permute-start.10) | collective-permute-done | bytes 40992 | tf_op jit(solution)/shard_map/ppermute | solution.py:186
  153.1 0.5 fusion
  153.6 0.6 pad_maximum_fusion.5
  (79 shorter events, 0.8 us)
Async XLA Ops:
  0.6 13.2 %copy-start.9 = (f32[384]{0:T(512)S(1)}, f32[384]{0:T(512)}, u32[]{:S(2)}) copy-start(f32[384]{0:T(512)} %param.14) | copy-start | bytes 4612
  0.6 13.2 %copy-start.10 = (f32[384]{0:T(512)S(1)}, f32[384]{0:T(512)}, u32[]{:S(2)}) copy-start(f32[384]{0:T(512)} %param.16) | copy-start | bytes 4612
  0.7 13.2 %copy-start.11 = (f32[384]{0:T(512)S(1)}, f32[384]{0:T(512)}, u32[]{:S(2)}) copy-start(f32[384]{0:T(512)} %param.15) | copy-start | bytes 4612
  0.7 13.2 %copy-start.7 = (bf16[384,8,128]{2,1,0:T(8,128)(2,1)S(1)}, bf16[384,8,128]{2,1,0:T(8,128)(2,1)}, u32[]{:S(2)}) copy-start(bf16[384,8,128]{2,1,0:T(8,128)(2,1)} %param.11) | copy-start | bytes 2359300
  0.7 14.3 %copy-start = (s32[8,128]{1,0:T(8,128)S(1)}, s32[8,128]{1,0:T(8,128)}, u32[]{:S(2)}) copy-start(s32[8,128]{1,0:T(8,128)} %mask_ref) | copy-start | bytes 12292
  0.7 14.3 %copy-start.1 = (s32[8,128]{1,0:T(8,128)S(1)}, s32[8,128]{1,0:T(8,128)}, u32[]{:S(2)}) copy-start(s32[8,128]{1,0:T(8,128)} %batch_ref) | copy-start | bytes 12292
  3.3 4.3 %collective-permute-start.1 = (f32[3,64,128]{2,1,0:T(8,128)S(1)}, f32[3,64,128]{2,1,0:T(8,128)S(1)}, u32[]{:S(2)}, u32[]{:S(2)}) collective-permute-start(f32[3,64,128]{2,1,0:T(8,128)S(1)} %get-tuple-element.25), channel_id=1, source_target_pairs={{1,0},{2,1},{3,2},{4,3},{5,4},{6,5},{7,6},{8,7},{9,8},{10,9},{11,1... | collective-permute-start | bytes 294920 | tf_op jit(solution)/shard_map/ppermute | solution.py:101
  4.6 4.0 %collective-permute-start = (f32[3,64,128]{2,1,0:T(8,128)S(1)}, f32[3,64,128]{2,1,0:T(8,128)S(1)}, u32[]{:S(2)}, u32[]{:S(2)}) collective-permute-start(f32[3,64,128]{2,1,0:T(8,128)S(1)} %get-tuple-element.24), channel_id=1, source_target_pairs={{0,1},{1,2},{2,3},{3,4},{4,5},{5,6},{6,7},{7,8},{8,9},{9,10},{10,1... | collective-permute-start | bytes 294920 | tf_op jit(solution)/shard_map/ppermute | solution.py:101
  8.6 18.3 %collective-permute-start.2 = (f32[3,432,128]{2,1,0:T(8,128)S(1)}, f32[3,432,128]{2,1,0:T(8,128)S(1)}, u32[]{:S(2)}, u32[]{:S(2)}) collective-permute-start(f32[3,432,128]{2,1,0:T(8,128)S(1)} %maximum_dynamic-update-slice_fusion), channel_id=1, source_target_pairs={{0,16},{16,32},{32,48},{48,64},{64,80},{80,96},{96,112},{1,17},{17... | collective-permute-start | bytes 1990664 | tf_op jit(solution)/shard_map/ppermute | solution.py:101
  12.6 18.9 %collective-permute-start.3 = (f32[3,432,128]{2,1,0:T(8,128)S(1)}, f32[3,432,128]{2,1,0:T(8,128)S(1)}, u32[]{:S(2)}, u32[]{:S(2)}) collective-permute-start(f32[3,432,128]{2,1,0:T(8,128)S(1)} %maximum_dynamic-update-slice_fusion.1), channel_id=1, source_target_pairs={{16,0},{32,16},{48,32},{64,48},{80,64},{96,80},{112,96},{17,1},{33... | collective-permute-start | bytes 1990664 | tf_op jit(solution)/shard_map/ppermute | solution.py:101
  15.7 0.6 copy-start.2
  16.3 0.6 copy-start.3
  76.4 4.7 %collective-permute-start.18 = (f32[2048,256]{1,0:T(8,128)}, f32[2048,256]{1,0:T(8,128)}, u32[]{:S(2)}, u32[]{:S(2)}) collective-permute-start(f32[2048,256]{1,0:T(8,128)} %get-tuple-element.43), channel_id=1, source_target_pairs={{0,1},{1,0},{2,3},{3,2},{4,5},{5,4},{6,7},{7,6},{8,9},{9,8},{10,11... | collective-permute-start | bytes 6291464 | tf_op jit(solution)/shard_map/ppermute | solution.py:407
  77.0 10.1 %collective-permute-start.11 = (f32[2048,256]{1,0:T(8,128)}, f32[2048,256]{1,0:T(8,128)}, u32[]{:S(2)}, u32[]{:S(2)}) collective-permute-start(f32[2048,256]{1,0:T(8,128)} %get-tuple-element.41), channel_id=1, source_target_pairs={{0,1},{1,0},{2,3},{3,2},{4,5},{5,4},{6,7},{7,6},{8,9},{9,8},{10,11... | collective-permute-start | bytes 6291464 | tf_op jit(solution)/shard_map/ppermute | solution.py:407
  77.1 16.4 %collective-permute-start.4 = (f32[2056,256]{1,0:T(8,128)}, f32[2056,256]{1,0:T(8,128)S(1)}, u32[]{:S(2)}, u32[]{:S(2)}) collective-permute-start(f32[2056,256]{1,0:T(8,128)} %get-tuple-element.38), channel_id=1, source_target_pairs={{0,1},{1,0},{2,3},{3,2},{4,5},{5,4},{6,7},{7,6},{8,9},{9,8},{10,11... | collective-permute-start | bytes 6316040 | tf_op jit(solution)/shard_map/ppermute | solution.py:407
  83.8 9.8 %copy-start.8 = (f32[8,256]{1,0:T(8,128)S(1)}, f32[8,256]{1,0:T(8,128)}, u32[]{:S(2)}) copy-start(f32[8,256]{1,0:T(8,128)} %get-tuple-element.39) | copy-start | bytes 24580
  83.8 15.1 %collective-permute-start.19 = (f32[1024,256]{1,0:T(8,128)}, f32[1024,256]{1,0:T(8,128)}, u32[]{:S(2)}, u32[]{:S(2)}) collective-permute-start(f32[1024,256]{1,0:T(8,128)} %dynamic-slice_add_fusion), channel_id=1, source_target_pairs={{0,16},{1,49},{16,0},{17,33},{32,48},{33,17},{48,32},{49,1},{2,18}... | collective-permute-start | bytes 3145736 | tf_op jit(solution)/shard_map/ppermute | solution.py:186
  85.7 7.9 %copy-start.4 = (f32[2048,256]{1,0:T(8,128)S(1)}, f32[2048,256]{1,0:T(8,128)}, u32[]{:S(2)}) copy-start(f32[2048,256]{1,0:T(8,128)} %get-tuple-element.37) | copy-start | bytes 6291460
  89.8 18.9 %collective-permute-start.12 = (f32[1024,256]{1,0:T(8,128)}, f32[1024,256]{1,0:T(8,128)}, u32[]{:S(2)}, u32[]{:S(2)}) collective-permute-start(f32[1024,256]{1,0:T(8,128)} %dynamic-slice_add_fusion.1), channel_id=1, source_target_pairs={{0,2},{1,67},{2,0},{3,65},{64,66},{65,3},{66,64},{67,1},{4,6},{5,7... | collective-permute-start | bytes 3145736 | tf_op jit(solution)/shard_map/ppermute | solution.py:186
  94.8 18.2 %collective-permute-start.5 = (f32[1032,256]{1,0:T(8,128)}, f32[1032,256]{1,0:T(8,128)S(1)}, u32[]{:S(2)}, u32[]{:S(2)}) collective-permute-start(f32[1032,256]{1,0:T(8,128)} %pad_maximum_fusion), channel_id=1, source_target_pairs={{0,4},{1,13},{4,0},{5,9},{8,12},{9,5},{12,8},{13,1},{2,6},{3,15},{... | collective-permute-start | bytes 3170312 | tf_op jit(solution)/shard_map/ppermute | solution.py:186
  96.3 12.5 %copy-start.6 = (f32[2048,256]{1,0:T(8,128)S(1)}, f32[2048,256]{1,0:T(8,128)}, u32[]{:S(2)}) copy-start(f32[2048,256]{1,0:T(8,128)} %get-tuple-element.40) | copy-start | bytes 6291460
  101.0 12.0 %copy-start.5 = (f32[2048,256]{1,0:T(8,128)S(1)}, f32[2048,256]{1,0:T(8,128)}, u32[]{:S(2)}) copy-start(f32[2048,256]{1,0:T(8,128)} %get-tuple-element.37) | copy-start | bytes 6291460
  101.0 14.9 %collective-permute-start.20 = (f32[512,256]{1,0:T(8,128)S(1)}, f32[512,256]{1,0:T(8,128)S(1)}, u32[]{:S(2)}, u32[]{:S(2)}) collective-permute-start(f32[512,256]{1,0:T(8,128)S(1)} %constant_dynamic-slice_fusion.2), channel_id=1, source_target_pairs={{0,48},{1,17},{16,32},{17,1},{32,16},{33,49},{48,0},{49,33},{2,50}... | collective-permute-start | bytes 1572872 | tf_op jit(solution)/shard_map/ppermute | solution.py:186
  110.6 10.5 %collective-permute-start.13 = (f32[512,256]{1,0:T(8,128)S(1)}, f32[512,256]{1,0:T(8,128)S(1)}, u32[]{:S(2)}, u32[]{:S(2)}) collective-permute-start(f32[512,256]{1,0:T(8,128)S(1)} %constant_dynamic-slice_fusion.8), channel_id=1, source_target_pairs={{0,66},{1,3},{2,64},{3,1},{64,2},{65,67},{66,0},{67,65},{4,70},{5,... | collective-permute-start | bytes 1572872 | tf_op jit(solution)/shard_map/ppermute | solution.py:186
  113.4 13.4 %collective-permute-start.6 = (f32[520,256]{1,0:T(8,128)S(1)}, f32[520,256]{1,0:T(8,128)S(1)}, u32[]{:S(2)}, u32[]{:S(2)}) collective-permute-start(f32[520,256]{1,0:T(8,128)S(1)} %pad_maximum_fusion.1), channel_id=1, source_target_pairs={{0,12},{1,5},{4,8},{5,1},{8,4},{9,13},{12,0},{13,9},{2,14},{3,7},{... | collective-permute-start | bytes 1597448 | tf_op jit(solution)/shard_map/ppermute | solution.py:186
  116.0 11.1 %collective-permute-start.21 = (f32[256,256]{1,0:T(8,128)S(1)}, f32[256,256]{1,0:T(8,128)S(1)}, u32[]{:S(2)}, u32[]{:S(2)}) collective-permute-start(f32[256,256]{1,0:T(8,128)S(1)} %constant_dynamic-slice_fusion.1), channel_id=1, source_target_pairs={{0,4},{1,13},{4,0},{5,9},{8,12},{9,5},{12,8},{13,1},{2,6},{3,15},{... | collective-permute-start | bytes 786440 | tf_op jit(solution)/shard_map/ppermute | solution.py:186
  121.1 8.0 %collective-permute-start.14 = (f32[256,256]{1,0:T(8,128)S(1)}, f32[256,256]{1,0:T(8,128)S(1)}, u32[]{:S(2)}, u32[]{:S(2)}) collective-permute-start(f32[256,256]{1,0:T(8,128)S(1)} %constant_dynamic-slice_fusion.7), channel_id=1, source_target_pairs={{0,16},{1,49},{16,0},{17,33},{32,48},{33,17},{48,32},{49,1},{2,18}... | collective-permute-start | bytes 786440 | tf_op jit(solution)/shard_map/ppermute | solution.py:186
  126.9 7.4 %collective-permute-start.7 = (f32[264,256]{1,0:T(8,128)S(1)}, f32[264,256]{1,0:T(8,128)S(1)}, u32[]{:S(2)}, u32[]{:S(2)}) collective-permute-start(f32[264,256]{1,0:T(8,128)S(1)} %pad_maximum_fusion.2), channel_id=1, source_target_pairs={{0,2},{1,67},{2,0},{3,65},{64,66},{65,3},{66,64},{67,1},{4,6},{5,7... | collective-permute-start | bytes 811016 | tf_op jit(solution)/shard_map/ppermute | solution.py:186
  127.2 8.0 %collective-permute-start.22 = (f32[128,256]{1,0:T(8,128)S(1)}, f32[128,256]{1,0:T(8,128)S(1)}, u32[]{:S(2)}, u32[]{:S(2)}) collective-permute-start(f32[128,256]{1,0:T(8,128)S(1)} %constant_dynamic-slice_fusion), channel_id=1, source_target_pairs={{0,12},{1,5},{4,8},{5,1},{8,4},{9,13},{12,0},{13,9},{2,14},{3,7},{... | collective-permute-start | bytes 393224 | tf_op jit(solution)/shard_map/ppermute | solution.py:186
  129.2 7.6 %collective-permute-start.15 = (f32[128,256]{1,0:T(8,128)S(1)}, f32[128,256]{1,0:T(8,128)S(1)}, u32[]{:S(2)}, u32[]{:S(2)}) collective-permute-start(f32[128,256]{1,0:T(8,128)S(1)} %constant_dynamic-slice_fusion.6), channel_id=1, source_target_pairs={{0,48},{1,17},{16,32},{17,1},{32,16},{33,49},{48,0},{49,33},{2,50}... | collective-permute-start | bytes 393224 | tf_op jit(solution)/shard_map/ppermute | solution.py:186
  134.4 6.3 %collective-permute-start.8 = (f32[136,256]{1,0:T(8,128)S(1)}, f32[136,256]{1,0:T(8,128)S(1)}, u32[]{:S(2)}, u32[]{:S(2)}) collective-permute-start(f32[136,256]{1,0:T(8,128)S(1)} %pad_maximum_fusion.3), channel_id=1, source_target_pairs={{0,66},{1,3},{2,64},{3,1},{64,2},{65,67},{66,0},{67,65},{4,70},{5,... | collective-permute-start | bytes 417800 | tf_op jit(solution)/shard_map/ppermute | solution.py:186
  135.3 6.0 %collective-permute-start.23 = (f32[64,256]{1,0:T(8,128)S(1)}, f32[64,256]{1,0:T(8,128)S(1)}, u32[]{:S(2)}, u32[]{:S(2)}) collective-permute-start(f32[64,256]{1,0:T(8,128)S(1)} %constant_dynamic-slice_fusion.14), channel_id=1, source_target_pairs={{0,2},{1,67},{2,0},{3,65},{64,66},{65,3},{66,64},{67,1},{4,6},{5,7... | collective-permute-start | bytes 196616 | tf_op jit(solution)/shard_map/ppermute | solution.py:186
  136.8 5.4 %collective-permute-start.16 = (f32[64,256]{1,0:T(8,128)S(1)}, f32[64,256]{1,0:T(8,128)S(1)}, u32[]{:S(2)}, u32[]{:S(2)}) collective-permute-start(f32[64,256]{1,0:T(8,128)S(1)} %constant_dynamic-slice_fusion.5), channel_id=1, source_target_pairs={{0,4},{1,13},{4,0},{5,9},{8,12},{9,5},{12,8},{13,1},{2,6},{3,15},{... | collective-permute-start | bytes 196616 | tf_op jit(solution)/shard_map/ppermute | solution.py:186
  140.8 6.7 %collective-permute-start.9 = (f32[72,256]{1,0:T(8,128)S(1)}, f32[72,256]{1,0:T(8,128)S(1)}, u32[]{:S(2)}, u32[]{:S(2)}) collective-permute-start(f32[72,256]{1,0:T(8,128)S(1)} %pad_maximum_fusion.4), channel_id=1, source_target_pairs={{0,16},{1,49},{16,0},{17,33},{32,48},{33,17},{48,32},{49,1},{2,18}... | collective-permute-start | bytes 221192 | tf_op jit(solution)/shard_map/ppermute | solution.py:186
  141.3 5.2 %collective-permute-start.24 = (f32[32,256]{1,0:T(8,128)S(1)}, f32[32,256]{1,0:T(8,128)S(1)}, u32[]{:S(2)}, u32[]{:S(2)}) collective-permute-start(f32[32,256]{1,0:T(8,128)S(1)} %constant_dynamic-slice_fusion.3), channel_id=1, source_target_pairs={{0,66},{1,3},{2,64},{3,1},{64,2},{65,67},{66,0},{67,65},{4,70},{5,... | collective-permute-start | bytes 98312 | tf_op jit(solution)/shard_map/ppermute | solution.py:186
  142.2 5.2 %collective-permute-start.17 = (f32[32,256]{1,0:T(8,128)S(1)}, f32[32,256]{1,0:T(8,128)S(1)}, u32[]{:S(2)}, u32[]{:S(2)}) collective-permute-start(f32[32,256]{1,0:T(8,128)S(1)} %constant_dynamic-slice_fusion.4), channel_id=1, source_target_pairs={{0,12},{1,5},{4,8},{5,1},{8,4},{9,13},{12,0},{13,9},{2,14},{3,7},{... | collective-permute-start | bytes 98312 | tf_op jit(solution)/shard_map/ppermute | solution.py:186
  147.5 5.5 %collective-permute-start.10 = (f32[40,256]{1,0:T(8,128)S(1)}, f32[40,256]{1,0:T(8,128)S(1)}, u32[]{:S(2)}, u32[]{:S(2)}) collective-permute-start(f32[40,256]{1,0:T(8,128)S(1)} %pad_maximum_fusion.7), channel_id=1, source_target_pairs={{0,48},{1,17},{16,32},{17,1},{32,16},{33,49},{48,0},{49,33},{2,50}... | collective-permute-start | bytes 122888 | tf_op jit(solution)/shard_map/ppermute | solution.py:186

commit v5 on v4

--- a/solution.py
+++ b/solution.py
@@ -213,20 +213,6 @@
     return table.reshape(-1)
 
 
-def put_rows(table_ref, source_ref, base, right, lanes, kept_refs, sent_refs):
-    core = lax.axis_index(CORE)
-    for slot, out_refs in enumerate((kept_refs, sent_refs)):
-        digit = core if slot == 0 else 1 - core
-        left = source_ref[:, digit, :, : right.shape[0]].reshape(256, right.shape[0])
-        sums = jnp.dot(left, right, preferred_element_type=jnp.float32)
-        for block in range(8):
-            for stream in range(3):
-                row = table_ref[digit * 192 + stream * 64 + base + block]
-                out_refs[stream][pl.ds(pl.multiple_of(row, 32), 32), lanes] = sums[
-                    block * 32 : (block + 1) * 32, stream * 128 : (stream + 1) * 128
-                ]
-
-
 def by_width(scalar_ref, most, body):
     land = scalar_ref[0]
     pl.when(land <= FEW)(functools.partial(body, FEW))
@@ -237,38 +223,93 @@
 
 
 def network_kernel(
-    scale, scalar_ref, table_ref, x_ref, win_ref, wout_f_ref, wout_ref, target_ref, rank_ref, batch_ref, field_ref,
-    new_ref, kept_a, kept_b, kept_c, sent_a, sent_b, sent_c, loss_ref,
-    slope_ref, hidden_ref, tend_ref, pick_ref, xc_ref, xn_ref, dtend_ref, dtn_ref, dpre_ref,
+    scale, scalar_ref, table_ref, x_hbm, win_hbm, wout_hbm, target_hbm, field_hbm, rank_ref, batch_ref,
+    new_hbm, kept_hbm_a, kept_hbm_b, kept_hbm_c, sent_hbm_a, sent_hbm_b, sent_hbm_c, loss_ref,
+    x_ref, win_ref, wout_ref, target_ref, field_ref, new_ref, kept_a, kept_b, kept_c, sent_a, sent_b, sent_c,
+    slope_ref, hidden_ref, tend_ref, pick_ref, xc_ref, xn_ref, dtend_ref, dtn_ref,
+    win_sem, wout_sem, in_sem, out_sem,
 ):
-    step = pl.program_id(0)
     feats, cols = x_ref.shape
-    kept, sent = (kept_a, kept_b, kept_c), (sent_a, sent_b, sent_c)
-
-    def start(n):
+    core = lax.axis_index(CORE)
+    incoming = [
+        pltpu.make_async_copy(source, ref, in_sem.at[k])
+        for k, (source, ref) in enumerate(((x_hbm, x_ref), (target_hbm, target_ref), (field_hbm, field_ref)))
+    ]
+    outgoing = [
+        pltpu.make_async_copy(ref, dest, out_sem.at[k])
+        for k, (ref, dest) in enumerate(
+            (
+                (new_ref, new_hbm),
+                (sent_a, sent_hbm_a),
+                (sent_b, sent_hbm_b),
+                (sent_c, sent_hbm_c),
+                (kept_a, kept_hbm_a),
+                (kept_b, kept_hbm_b),
+                (kept_c, kept_hbm_c),
+            )
+        )
+    ]
+
+    def win_copy(piece):
+        return pltpu.make_async_copy(
+            win_hbm.at[:, pl.ds(pl.multiple_of(piece * 512, 512), 512)], win_ref.at[piece], win_sem.at[piece]
+        )
+
+    def wout_copy(piece):
+        at = pl.ds(piece * 8, 8)
+        return pltpu.make_async_copy(wout_hbm.at[at], wout_ref.at[at], wout_sem.at[piece])
+
+    incoming[0].start()
+    for piece in range(8):
+        win_copy(piece).start()
+        wout_copy(piece).start()
+    incoming[1].start()
+    incoming[2].start()
+
+    def run(n):
         for at in range(0, n, 128):
             slot = lax.broadcasted_iota(jnp.int32, (128, cols), 0) + at
             pick_ref[at : at + 128, :] = jnp.where(slot == rank_ref[...], 1.0, 0.0).astype(jnp.bfloat16)
+        incoming[0].wait()
         packed = lax.dot_general(x_ref[...], pick_ref[:n, :], ROWS, preferred_element_type=jnp.float32)
         packed = packed.astype(jnp.bfloat16)
         xc_ref[:, :n] = packed
         xn_ref[:n, :] = packed.T
         tend_ref[:, :n] = jnp.zeros((feats, n), jnp.float32)
 
-    def forward(n):
-        for part in range(2):
-            rows = slice(part * 256, (part + 1) * 256)
-            pre = jnp.dot(win_ref[:, rows].T, xc_ref[:, :n], preferred_element_type=jnp.float32)
-            sig = 0.5 * jnp.tanh(0.5 * pre) + 0.5
-            act = pre * sig
-            slope_ref[pl.ds(pl.multiple_of(step * 512 + part * 256, 256), 256), :n] = sig + act * (1.0 - sig)
-            hid = act.astype(jnp.bfloat16)
-            hidden_ref[pl.ds(step * 8 + part * 4, 4), :, :, :n] = hid.reshape(4, 2, 32, n)
-            tend_ref[:, :n] += jnp.dot(wout_f_ref[rows, :].T, hid, preferred_element_type=jnp.float32)
-
-    def middle(n):
+        def activate(piece):
+            for part in range(2):
+                rows = slice(part * 256, (part + 1) * 256)
+                pre = jnp.dot(win_ref[piece, :, rows].T, xc_ref[:, :n], preferred_element_type=jnp.float32)
+                sig = 0.5 * jnp.tanh(0.5 * pre) + 0.5
+                act = pre * sig
+                at = pl.ds(piece * 8 + part * 4, 4)
+                slope_ref[at, :, :, :n] = (sig + act * (1.0 - sig)).reshape(4, 2, 32, n)
+                hidden_ref[at, :, :, :n] = act.astype(jnp.bfloat16).reshape(4, 2, 32, n)
+
+        def project(piece):
+            at = pl.ds(piece * 8, 8)
+            tend_ref[:, :n] += jnp.dot(
+                wout_ref[at].reshape(512, feats).T,
+                hidden_ref[at, :, :, :n].reshape(512, n),
+                preferred_element_type=jnp.float32,
+            )
+
+        win_copy(0).wait()
+        activate(0)
+
+        @pl.loop(1, 8)
+        def _(piece):
+            win_copy(piece).wait()
+            wout_copy(piece - 1).wait()
+            project(piece - 1)
+            activate(piece)
+
+        wout_copy(7).wait()
+        project(7)
         pick = pick_ref[:n, :]
         tend = tend_ref[:, :n]
+        incoming[1].wait()
         wanted = lax.dot_general(target_ref[...], pick, ROWS, preferred_element_type=jnp.float32)
         err = tend - wanted
         dtend = (err * scale[1]).astype(jnp.bfloat16)
@@ -278,9 +319,11 @@
         fine = (tend - coarse.astype(jnp.float32)).astype(jnp.bfloat16)
         spread = jnp.dot(coarse, pick, preferred_element_type=jnp.float32)
         spread += jnp.dot(fine, pick, preferred_element_type=jnp.float32)
+        incoming[2].wait()
         new = field_ref[...] + 0.5 * spread
         for row in range(8):
             new_ref[pl.ds(row, feats, stride=8), :] = new[:, row * 128 : (row + 1) * 128]
+        outgoing[0].start()
         persq = 0.5 * jnp.sum(err * err, axis=0, keepdims=True)
         batch = lax.dot_general(batch_ref[...], pick, ROWS, preferred_element_type=jnp.float32)
         which = lax.broadcasted_iota(jnp.int32, (128, n), 0).astype(jnp.float32)
@@ -296,23 +339,38 @@
             sent_a[2048:, side : side + 128] = loss
             loss_ref[:, side : side + 128] = loss
 
-    def backward(n):
-        piece = step - 8
-        for part in range(2):
-            rows = slice(part * 256, (part + 1) * 256)
-            dhid = jnp.dot(wout_ref[rows, :], dtend_ref[:, :n], preferred_element_type=jnp.float32)
-            slope = slope_ref[pl.ds(pl.multiple_of(piece * 512 + part * 256, 256), 256), :n]
-            dpre = (dhid * slope).astype(jnp.bfloat16)
-            dpre_ref[part * 4 : (part + 1) * 4, :, :, :n] = dpre.reshape(4, 2, 32, n)
-        base = piece * 8
-        here = hidden_ref.at[pl.ds(base, 8)]
-        put_rows(table_ref, here, base, dtn_ref[:n, :], slice(0, 128), kept, sent)
-        put_rows(table_ref, dpre_ref, base, xn_ref[:n, :], slice(128, 256), kept, sent)
-
-    pl.when(step == 0)(lambda: by_width(scalar_ref, cols, start))
-    pl.when(step < 8)(lambda: by_width(scalar_ref, cols, forward))
-    pl.when(step == 7)(lambda: by_width(scalar_ref, cols, middle))
-    pl.when(step >= 8)(lambda: by_width(scalar_ref, cols, backward))
+        for digit, out_refs, copies in (
+            (1 - core, (sent_a, sent_b, sent_c), outgoing[1:4]),
+            (core, (kept_a, kept_b, kept_c), outgoing[4:]),
+        ):
+
+            @pl.loop(0, 4)
+            def _(piece, digit=digit, out_refs=out_refs):
+                at = pl.ds(piece * 16, 16)
+                dhid = jnp.dot(
+                    wout_ref[at, digit].reshape(512, feats), dtend_ref[:, :n], preferred_element_type=jnp.float32
+                )
+                dpre = (dhid * slope_ref[at, digit, :, :n].reshape(512, n)).astype(jnp.bfloat16)
+                sums = (
+                    jnp.dot(
+                        hidden_ref[at, digit, :, :n].reshape(512, n), dtn_ref[:n, :], preferred_element_type=jnp.float32
+                    ),
+                    jnp.dot(dpre, xn_ref[:n, :], preferred_element_type=jnp.float32),
+                )
+                for block in range(16):
+                    for stream in range(3):
+                        row = table_ref[digit * 192 + stream * 64 + piece * 16 + block]
+                        for which in range(2):
+                            out_refs[stream][
+                                pl.ds(pl.multiple_of(row, 32), 32), which * 128 : (which + 1) * 128
+                            ] = sums[which][block * 32 : (block + 1) * 32, stream * 128 : (stream + 1) * 128]
+
+            for copy in copies:
+                copy.start()
+
+    by_width(scalar_ref, cols, run)
+    for copy in outgoing:
+        copy.wait()
 
 
 def in_hbm(value):
@@ -368,42 +426,43 @@
     table = jnp.asarray(ring_rows())
     f32, bf16 = jnp.float32, jnp.bfloat16
     tail = [2048, 2048, 2048, 2056, 2048, 2048]
+    hbm = pl.BlockSpec(memory_space=pl.ANY)
+    vmem = pl.BlockSpec(memory_space=pltpu.VMEM)
+    smem = pl.BlockSpec(memory_space=pltpu.SMEM)
     new, *halves = pl.pallas_call(
         functools.partial(network_kernel, (BATCHES / (total * feats), total ** (-0.5))),
-        grid_spec=pltpu.PrefetchScalarGridSpec(
-            num_scalar_prefetch=2,
-            grid=(16,),
-            in_specs=[
-                whole(feats, cols),
-                pl.BlockSpec((feats, 512), lambda i, *_: (0, jnp.minimum(i, 7))),
-                pl.BlockSpec((512, feats), lambda i, *_: (jnp.minimum(i, 7), 0)),
-                pl.BlockSpec((512, feats), lambda i, *_: (jnp.maximum(i - 8, 0), 0)),
-                whole(feats, cols),
-                whole(1, cols),
-                whole(8, cols),
-                whole(feats, cols),
-            ],
-            out_specs=[whole(feats * 8, cols // 8)]
-            + [whole(size, 256) for size in tail + [8]],
-            scratch_shapes=[
-                pltpu.VMEM((hid, cols), f32),
-                pltpu.VMEM((64, 2, 32, cols), bf16),
-                pltpu.VMEM((feats, cols), f32),
-                pltpu.VMEM((cols, cols), bf16),
-                pltpu.VMEM((feats, cols), bf16),
-                pltpu.VMEM((cols, feats), bf16),
-                pltpu.VMEM((feats, cols), bf16),
-                pltpu.VMEM((cols, feats), bf16),
-                pltpu.VMEM((8, 2, 32, cols), bf16),
-            ],
-        ),
+        in_specs=[smem, smem, hbm, hbm, hbm, hbm, hbm, vmem, vmem],
+        out_specs=[hbm] * 7 + [vmem],
+        scratch_shapes=[
+            pltpu.VMEM((feats, cols), bf16),
+            pltpu.VMEM((8, feats, 512), bf16),
+            pltpu.VMEM((64, 2, 32, feats), bf16),
+            pltpu.VMEM((feats, cols), bf16),
+            pltpu.VMEM((feats, cols), f32),
+            pltpu.VMEM((feats * 8, cols // 8), f32),
+        ]
+        + [pltpu.VMEM((size, 256), f32) for size in tail]
+        + [
+            pltpu.VMEM((64, 2, 32, cols), f32),
+            pltpu.VMEM((64, 2, 32, cols), bf16),
+            pltpu.VMEM((feats, cols), f32),
+            pltpu.VMEM((cols, cols), bf16),
+            pltpu.VMEM((feats, cols), bf16),
+            pltpu.VMEM((cols, feats), bf16),
+            pltpu.VMEM((feats, cols), bf16),
+            pltpu.VMEM((cols, feats), bf16),
+            pltpu.SemaphoreType.DMA((8,)),
+            pltpu.SemaphoreType.DMA((8,)),
+            pltpu.SemaphoreType.DMA((3,)),
+            pltpu.SemaphoreType.DMA((7,)),
+        ],
         out_shape=[shaped(f32, feats * 8, cols // 8)] + [shaped(f32, size, 256) for size in tail + [8]],
-        compiler_params=params(58),
+        compiler_params=pltpu.CompilerParams(vmem_limit_bytes=60 * 2**20),
         cost_estimate=pl.CostEstimate(
             flops=10 * cols * feats * hid, bytes_accessed=20 * 2**20, transcendentals=cols * hid
         ),
         name="network",
-    )(land, table, in_hbm(x), w_in, w_out, w_out, target, ranks, batch, in_hbm(field))
+    )(land, table, x, w_in, w_out.reshape(64, 2, 32, feats), target, field, ranks, batch)
     streams = [[kept, lax.ppermute(sent, CORE, PAIR)] for kept, sent in zip(halves[:3], halves[3:6])]
     losses = halves[6] + streams[0][1][2048:]
     for stage in range(3):

time: 155 us -> 153 us (0.987)
    pallas_call x1, Pallas kernels: 33.9 us -> 31.2 us  [network(): pl.pallas_call(functools.partial(network_kernel, (BATCHES / (total * feat...]
where the time goes in v5:
time: 153 us
  starting transfers between devices  47.9 us (31%)
  Pallas kernels  46.3 us (30%)
  waiting for transfers between devices  42 us (27%)
  other arithmetic  12.3 us (8%)
  local copies, waits for them, and re-layouts  3.25 us (2%)
    ppermute x18, starting transfers between devices, ring_turn(): coming = lax.ppermute(leaving, AXES[axis], RING[turn + 1])  37.2 us
    pallas_call x1, Pallas kernels, network(): pl.pallas_call(functools.partial(network_kernel, (BATCHES / (total * feat...  31.2 us
    ppermute x18, waiting for transfers between devices, ring_turn(): coming = lax.ppermute(leaving, AXES[axis], RING[turn + 1])  21.5 us
    ppermute x4, waiting for transfers between devices, shifted(): return lax.ppermute(value, axis, pairs)  15.5 us
    pallas_call x1, Pallas kernels, transported(): pl.pallas_call(transport_kernel, grid=(feats // 128,), in_specs=[pl.Block...  11.8 us
    ppermute x4, starting transfers between devices, shifted(): return lax.ppermute(value, axis, pairs)  9.57 us
    add x3, other arithmetic, ring_turn(): leaving = sum((half_of(term, size, 1 - bit) for term in terms))  5.51 us
    ppermute x3, waiting for transfers between devices, network(): lax.ppermute(sent, CORE, PAIR)  5.07 us
  transfers between devices with their start and end apart: 25, of which 15 were waited for; matrix products, arithmetic and copies ran while one was open for 8% of the time, Pallas kernels for 0%

profile of v5, /device:TPU:0, one launch (start us, length us, event | category | flops | bytes accessed | tf_op | source)
XLA Modules:
  0.0 153.0 jit_solution(8518986703314603370)
XLA Ops:
  0.7 2.6 %edges.1 = (f32[3,432,128]{2,1,0:T(8,128)S(1)}, f32[3,432,128]{2,1,0:T(8,128)S(1)}, f32[3,64,128]{2,1,0:T(8,128)S(1)}, f32[3,64,128]{2,1,0:T(8,128)S(1)}) custom-call(f32[3072,128]{1,0:T(8,128)} %bitcast.9), custom_call_target="tpu_custom_call" | custom-call | flops 1048576 | bytes 3145728 | tf_op jit(solution)/shard_map/edges/pallas_call | solution.py:109
  3.3 1.3 collective-permute-start.1
  4.6 3.0 %collective-permute-start = (f32[3,64,128]{2,1,0:T(8,128)S(1)}, f32[3,64,128]{2,1,0:T(8,128)S(1)}, u32[]{:S(2)}, u32[]{:S(2)}) collective-permute-start(f32[3,64,128]{2,1,0:T(8,128)S(1)} %get-tuple-element.24), channel_id=1, source_target_pairs={{0,1},{1,2},{2,3},{3,4},{4,5},{5,6},{6,7},{7,8},{8,9},{9,10},{10,1... | collective-permute-start | bytes 294920 | tf_op jit(solution)/shard_map/ppermute | solution.py:101
  7.7 0.9 collective-permute-done.left_ref
  8.6 3.9 %collective-permute-start.2 = (f32[3,432,128]{2,1,0:T(8,128)S(1)}, f32[3,432,128]{2,1,0:T(8,128)S(1)}, u32[]{:S(2)}, u32[]{:S(2)}) collective-permute-start(f32[3,432,128]{2,1,0:T(8,128)S(1)} %maximum_dynamic-update-slice_fusion), channel_id=1, source_target_pairs={{0,16},{16,32},{32,48},{48,64},{64,80},{80,96},{96,112},{1,17},{17... | collective-permute-start | bytes 1990664 | tf_op jit(solution)/shard_map/ppermute | solution.py:101
  12.6 1.3 collective-permute-start.3
  13.9 1.1 copy.16
  15.0 0.7 ranks.1
  15.7 0.6 copy-done.2
  16.3 0.6 copy-done.3
  16.9 10.0 %collective-permute-done.2.above_ref = f32[3,432,128]{2,1,0:T(8,128)S(1)} collective-permute-done((f32[3,432,128]{2,1,0:T(8,128)S(1)}, f32[3,432,128]{2,1,0:T(8,128)S(1)}, u32[]{:S(2)}, u32[]{:S(2)}) %collective-permute-start.2) | collective-permute-done | bytes 663584 | tf_op jit(solution)/shard_map/ppermute | solution.py:101
  26.9 4.6 %collective-permute-done.3.below_ref = f32[3,432,128]{2,1,0:T(8,128)S(1)} collective-permute-done((f32[3,432,128]{2,1,0:T(8,128)S(1)}, f32[3,432,128]{2,1,0:T(8,128)S(1)}, u32[]{:S(2)}, u32[]{:S(2)}) %collective-permute-start.3) | collective-permute-done | bytes 663584 | tf_op jit(solution)/shard_map/ppermute | solution.py:101
  31.5 0.1 broadcast_in_dim.10.coef_0
  31.6 0.1 broadcast_in_dim.11.coef_1
  31.7 0.1 broadcast_in_dim.12.coef_2
  31.8 0.1 broadcast_in_dim.13.coef_3
  31.9 0.1 broadcast_in_dim.14.coef_4
  32.1 11.8 %transport.1 = (f32[384,1024]{1,0:T(8,128)}, bf16[384,1024]{1,0:T(8,128)(2,1)}) custom-call(f32[3072,128]{1,0:T(8,128)} %bitcast.10, f32[3,432,128]{2,1,0:T(8,128)S(1)} %collective-permute-done.2.above_ref, f32[3,432,128]{2,1,0:T(8,128)S(1)} %collective-permute-done.3.below_ref, f32[3,64,128]{2,1,0:T(8,128)S(1)} %collective-permute-done.left_ref, ...), custom_call_target="tpu_custom_call" | custom-call | flops 16777216 | bytes 6291456 | tf_op jit(solution)/shard_map/transport/pallas_call | solution.py:139
  43.9 31.2 %network.1 = (f32[3072,128]{1,0:T(8,128)}, f32[2048,256]{1,0:T(8,128)}, f32[2048,256]{1,0:T(8,128)}, f32[2048,256]{1,0:T(8,128)}, f32[2056,256]{1,0:T(8,128)}, /...) custom-call(s32[1]{0:T(128)} %get-tuple-element.28.scalar_ref, s32[384]{0:T(512)} %constant.119.clone.table_ref, ...), custom_call_target="tpu_custom_call" | custom-call | flops 16106127360 | bytes 20971520 | tf_op jit(solution)/shard_map/network/pallas_call | solution.py:432
  75.1 0.7 collective-permute-start.18
  75.8 0.1 collective-permute-start.11
  75.9 0.4 collective-permute-start.4
  76.3 3.6 %collective-permute-done.18 = f32[2048,256]{1,0:T(8,128)} collective-permute-done((f32[2048,256]{1,0:T(8,128)}, f32[2048,256]{1,0:T(8,128)}, u32[]{:S(2)}, u32[]{:S(2)}) %collective-permute-start.18) | collective-permute-done | bytes 2097184 | tf_op jit(solution)/shard_map/ppermute | solution.py:466
  79.9 2.7 %dynamic-slice_add_fusion = f32[1024,256]{1,0:T(8,128)} fusion(f32[2048,256]{1,0:T(8,128)} %collective-permute-done.18, s32[]{:T(128)S(6)} %select_n.231, f32[2048,256]{1,0:T(8,128)} %get-tuple-element.42), kind=kLoop, calls=%fused_computation.2 | loop fusion | flops 262144 | bytes 3145732 | tf_op jit(solution)/shard_map/add | solution.py:183
  82.6 1.9 %collective-permute-start.19 = (f32[1024,256]{1,0:T(8,128)}, f32[1024,256]{1,0:T(8,128)}, u32[]{:S(2)}, u32[]{:S(2)}) collective-permute-start(f32[1024,256]{1,0:T(8,128)} %dynamic-slice_add_fusion), channel_id=1, source_target_pairs={{0,16},{1,49},{16,0},{17,33},{32,48},{33,17},{48,32},{49,1},{2,18}... | collective-permute-start | bytes 3145736 | tf_op jit(solution)/shard_map/ppermute | solution.py:186
  84.5 1.5 collective-permute-done.11
  85.9 2.7 %dynamic-slice_add_fusion.1 = f32[1024,256]{1,0:T(8,128)} fusion(f32[2048,256]{1,0:T(8,128)} %collective-permute-done.11, s32[]{:T(128)S(6)} %select_n.219, f32[2048,256]{1,0:T(8,128)} %get-tuple-element.40), kind=kLoop, calls=%fused_computation.4 | loop fusion | flops 262144 | bytes 3145732 | tf_op jit(solution)/shard_map/add | solution.py:183
  88.6 3.7 %collective-permute-start.12 = (f32[1024,256]{1,0:T(8,128)}, f32[1024,256]{1,0:T(8,128)}, u32[]{:S(2)}, u32[]{:S(2)}) collective-permute-start(f32[1024,256]{1,0:T(8,128)} %dynamic-slice_add_fusion.1), channel_id=1, source_target_pairs={{0,2},{1,67},{2,0},{3,65},{64,66},{65,3},{66,64},{67,1},{4,6},{5,7... | collective-permute-start | bytes 3145736 | tf_op jit(solution)/shard_map/ppermute | solution.py:186
  92.3 0.1 dynamic-slice_add_fusion.2
  92.5 1.1 pad_maximum_fusion
  93.6 1.5 collective-permute-start.5
  95.1 2.6 %collective-permute-done.19 = f32[1024,256]{1,0:T(8,128)} collective-permute-done((f32[1024,256]{1,0:T(8,128)}, f32[1024,256]{1,0:T(8,128)}, u32[]{:S(2)}, u32[]{:S(2)}) %collective-permute-start.19) | collective-permute-done | bytes 1048608 | tf_op jit(solution)/shard_map/ppermute | solution.py:186
  97.7 2.1 %add_add_fusion = f32[1024,256]{1,0:T(8,128)S(1)} fusion(f32[1024,256]{1,0:T(8,128)} %collective-permute-done.19, f32[2048,256]{1,0:T(8,128)} %collective-permute-done.18, s32[]{:T(128)S(6)} %select_n.230, f32[2048,256]{1,0:T(8,128)} %get-tuple-element.42), kind=kLoop, calls=%fused_computation.3 | loop fusion | flops 524288 | bytes 4194308 | tf_op jit(solution)/shard_map/add | solution.py:188
  99.8 7.7 %collective-permute-start.20 = (f32[512,256]{1,0:T(8,128)S(1)}, f32[512,256]{1,0:T(8,128)S(1)}, u32[]{:S(2)}, u32[]{:S(2)}) collective-permute-start(f32[512,256]{1,0:T(8,128)S(1)} %constant_dynamic-slice_fusion.2), channel_id=1, source_target_pairs={{0,48},{1,17},{16,32},{17,1},{32,16},{33,49},{48,0},{49,33},{2,50}... | collective-permute-start | bytes 1572872 | tf_op jit(solution)/shard_map/ppermute | solution.py:186
  107.5 1.7 %add_add_fusion.1 = f32[1024,256]{1,0:T(8,128)S(1)} fusion(f32[1024,256]{1,0:T(8,128)} %collective-permute-done.12, f32[2048,256]{1,0:T(8,128)} %collective-permute-done.11, s32[]{:T(128)S(6)} %select_n.218, f32[2048,256]{1,0:T(8,128)S(1)} %copy-done.6), kind=kLoop, calls=%fused_computation.5 | loop fusion | flops 524288 | bytes 4194308 | tf_op jit(solution)/shard_map/add | solution.py:188
  109.3 2.5 %collective-permute-start.13 = (f32[512,256]{1,0:T(8,128)S(1)}, f32[512,256]{1,0:T(8,128)S(1)}, u32[]{:S(2)}, u32[]{:S(2)}) collective-permute-start(f32[512,256]{1,0:T(8,128)S(1)} %constant_dynamic-slice_fusion.8), channel_id=1, source_target_pairs={{0,66},{1,3},{2,64},{3,1},{64,2},{65,67},{66,0},{67,65},{4,70},{5,... | collective-permute-start | bytes 1572872 | tf_op jit(solution)/shard_map/ppermute | solution.py:186
  111.8 0.2 slice_add_fusion
  112.1 1.4 collective-permute-start.6
  113.6 1.1 collective-permute-done.20
  114.7 0.1 dynamic-slice_add_fusion.3
  114.8 2.5 %collective-permute-start.21 = (f32[256,256]{1,0:T(8,128)S(1)}, f32[256,256]{1,0:T(8,128)S(1)}, u32[]{:S(2)}, u32[]{:S(2)}) collective-permute-start(f32[256,256]{1,0:T(8,128)S(1)} %constant_dynamic-slice_fusion.1), channel_id=1, source_target_pairs={{0,4},{1,13},{4,0},{5,9},{8,12},{9,5},{12,8},{13,1},{2,6},{3,15},{... | collective-permute-start | bytes 786440 | tf_op jit(solution)/shard_map/ppermute | solution.py:186
  117.3 2.5 %collective-permute-done.13 = f32[512,256]{1,0:T(8,128)S(1)} collective-permute-done((f32[512,256]{1,0:T(8,128)S(1)}, f32[512,256]{1,0:T(8,128)S(1)}, u32[]{:S(2)}, u32[]{:S(2)}) %collective-permute-start.13) | collective-permute-done | bytes 524320 | tf_op jit(solution)/shard_map/ppermute | solution.py:186
  119.8 0.1 dynamic-slice_add_fusion.4
  119.9 0.1 collective-permute-start.14
  120.0 5.5 %collective-permute-done.6 = f32[520,256]{1,0:T(8,128)S(1)} collective-permute-done((f32[520,256]{1,0:T(8,128)S(1)}, f32[520,256]{1,0:T(8,128)S(1)}, u32[]{:S(2)}, u32[]{:S(2)}) %collective-permute-start.6) | collective-permute-done | bytes 532512 | tf_op jit(solution)/shard_map/ppermute | solution.py:186
  125.5 0.1 slice_add_fusion.1
  125.6 0.3 collective-permute-start.7
  126.0 1.9 %collective-permute-start.22 = (f32[128,256]{1,0:T(8,128)S(1)}, f32[128,256]{1,0:T(8,128)S(1)}, u32[]{:S(2)}, u32[]{:S(2)}) collective-permute-start(f32[128,256]{1,0:T(8,128)S(1)} %constant_dynamic-slice_fusion), channel_id=1, source_target_pairs={{0,12},{1,5},{4,8},{5,1},{8,4},{9,13},{12,0},{13,9},{2,14},{3,7},{... | collective-permute-start | bytes 393224 | tf_op jit(solution)/shard_map/ppermute | solution.py:186
  128.0 4.6 %collective-permute-start.15 = (f32[128,256]{1,0:T(8,128)S(1)}, f32[128,256]{1,0:T(8,128)S(1)}, u32[]{:S(2)}, u32[]{:S(2)}) collective-permute-start(f32[128,256]{1,0:T(8,128)S(1)} %constant_dynamic-slice_fusion.6), channel_id=1, source_target_pairs={{0,48},{1,17},{16,32},{17,1},{32,16},{33,49},{48,0},{49,33},{2,50}... | collective-permute-start | bytes 393224 | tf_op jit(solution)/shard_map/ppermute | solution.py:186
  132.6 0.4 collective-permute-done.7
  133.1 0.9 collective-permute-start.8
  134.0 0.6 collective-permute-start.23
  134.7 0.9 collective-permute-done.15
  135.5 0.3 collective-permute-start.16
  135.9 3.5 %collective-permute-done.8 = f32[136,256]{1,0:T(8,128)S(1)} collective-permute-done((f32[136,256]{1,0:T(8,128)S(1)}, f32[136,256]{1,0:T(8,128)S(1)}, u32[]{:S(2)}, u32[]{:S(2)}) %collective-permute-start.8) | collective-permute-done | bytes 139296 | tf_op jit(solution)/shard_map/ppermute | solution.py:186
  139.5 0.6 collective-permute-start.9
  140.1 0.8 collective-permute-start.24
  140.9 2.2 %collective-permute-start.17 = (f32[32,256]{1,0:T(8,128)S(1)}, f32[32,256]{1,0:T(8,128)S(1)}, u32[]{:S(2)}, u32[]{:S(2)}) collective-permute-start(f32[32,256]{1,0:T(8,128)S(1)} %constant_dynamic-slice_fusion.4), channel_id=1, source_target_pairs={{0,12},{1,5},{4,8},{5,1},{8,4},{9,13},{12,0},{13,9},{2,14},{3,7},{... | collective-permute-start | bytes 98312 | tf_op jit(solution)/shard_map/ppermute | solution.py:186
  143.2 2.2 %collective-permute-done.24 = f32[32,256]{1,0:T(8,128)S(1)} collective-permute-done((f32[32,256]{1,0:T(8,128)S(1)}, f32[32,256]{1,0:T(8,128)S(1)}, u32[]{:S(2)}, u32[]{:S(2)}) %collective-permute-start.24) | collective-permute-done | bytes 32800 | tf_op jit(solution)/shard_map/ppermute | solution.py:186
  145.3 0.8 collective-permute-done.17
  146.2 3.6 %collective-permute-start.10 = (f32[40,256]{1,0:T(8,128)S(1)}, f32[40,256]{1,0:T(8,128)S(1)}, u32[]{:S(2)}, u32[]{:S(2)}) collective-permute-start(f32[40,256]{1,0:T(8,128)S(1)} %pad_maximum_fusion.7), channel_id=1, source_target_pairs={{0,48},{1,17},{16,32},{17,1},{32,16},{33,49},{48,0},{49,33},{2,50}... | collective-permute-start | bytes 122888 | tf_op jit(solution)/shard_map/ppermute | solution.py:186
  149.8 2.0 %collective-permute-done.10 = f32[40,256]{1,0:T(8,128)S(1)} collective-permute-done((f32[40,256]{1,0:T(8,128)S(1)}, f32[40,256]{1,0:T(8,128)S(1)}, u32[]{:S(2)}, u32[]{:S(2)}) %collective-permute-start.10) | collective-permute-done | bytes 40992 | tf_op jit(solution)/shard_map/ppermute | solution.py:186
  151.8 0.5 fusion
  152.4 0.6 pad_maximum_fusion.5
  (79 shorter events, 0.8 us)
Async XLA Ops:
  0.6 13.2 %copy-start.9 = (f32[384]{0:T(512)S(1)}, f32[384]{0:T(512)}, u32[]{:S(2)}) copy-start(f32[384]{0:T(512)} %param.14) | copy-start | bytes 4612
  0.6 13.2 %copy-start.10 = (f32[384]{0:T(512)S(1)}, f32[384]{0:T(512)}, u32[]{:S(2)}) copy-start(f32[384]{0:T(512)} %param.16) | copy-start | bytes 4612
  0.7 13.2 %copy-start.11 = (f32[384]{0:T(512)S(1)}, f32[384]{0:T(512)}, u32[]{:S(2)}) copy-start(f32[384]{0:T(512)} %param.15) | copy-start | bytes 4612
  0.7 13.2 %copy-start.7 = (bf16[384,8,128]{2,1,0:T(8,128)(2,1)S(1)}, bf16[384,8,128]{2,1,0:T(8,128)(2,1)}, u32[]{:S(2)}) copy-start(bf16[384,8,128]{2,1,0:T(8,128)(2,1)} %param.11) | copy-start | bytes 2359300
  0.7 14.3 %copy-start = (s32[8,128]{1,0:T(8,128)S(1)}, s32[8,128]{1,0:T(8,128)}, u32[]{:S(2)}) copy-start(s32[8,128]{1,0:T(8,128)} %mask_ref) | copy-start | bytes 12292
  0.7 14.3 %copy-start.1 = (s32[8,128]{1,0:T(8,128)S(1)}, s32[8,128]{1,0:T(8,128)}, u32[]{:S(2)}) copy-start(s32[8,128]{1,0:T(8,128)} %batch_ref) | copy-start | bytes 12292
  3.3 4.3 %collective-permute-start.1 = (f32[3,64,128]{2,1,0:T(8,128)S(1)}, f32[3,64,128]{2,1,0:T(8,128)S(1)}, u32[]{:S(2)}, u32[]{:S(2)}) collective-permute-start(f32[3,64,128]{2,1,0:T(8,128)S(1)} %get-tuple-element.25), channel_id=1, source_target_pairs={{1,0},{2,1},{3,2},{4,3},{5,4},{6,5},{7,6},{8,7},{9,8},{10,9},{11,1... | collective-permute-start | bytes 294920 | tf_op jit(solution)/shard_map/ppermute | solution.py:101
  4.6 4.0 %collective-permute-start = (f32[3,64,128]{2,1,0:T(8,128)S(1)}, f32[3,64,128]{2,1,0:T(8,128)S(1)}, u32[]{:S(2)}, u32[]{:S(2)}) collective-permute-start(f32[3,64,128]{2,1,0:T(8,128)S(1)} %get-tuple-element.24), channel_id=1, source_target_pairs={{0,1},{1,2},{2,3},{3,4},{4,5},{5,6},{6,7},{7,8},{8,9},{9,10},{10,1... | collective-permute-start | bytes 294920 | tf_op jit(solution)/shard_map/ppermute | solution.py:101
  8.6 18.3 %collective-permute-start.2 = (f32[3,432,128]{2,1,0:T(8,128)S(1)}, f32[3,432,128]{2,1,0:T(8,128)S(1)}, u32[]{:S(2)}, u32[]{:S(2)}) collective-permute-start(f32[3,432,128]{2,1,0:T(8,128)S(1)} %maximum_dynamic-update-slice_fusion), channel_id=1, source_target_pairs={{0,16},{16,32},{32,48},{48,64},{64,80},{80,96},{96,112},{1,17},{17... | collective-permute-start | bytes 1990664 | tf_op jit(solution)/shard_map/ppermute | solution.py:101
  12.6 18.9 %collective-permute-start.3 = (f32[3,432,128]{2,1,0:T(8,128)S(1)}, f32[3,432,128]{2,1,0:T(8,128)S(1)}, u32[]{:S(2)}, u32[]{:S(2)}) collective-permute-start(f32[3,432,128]{2,1,0:T(8,128)S(1)} %maximum_dynamic-update-slice_fusion.1), channel_id=1, source_target_pairs={{16,0},{32,16},{48,32},{64,48},{80,64},{96,80},{112,96},{17,1},{33... | collective-permute-start | bytes 1990664 | tf_op jit(solution)/shard_map/ppermute | solution.py:101
  15.7 0.6 copy-start.2
  16.3 0.6 copy-start.3
  75.1 4.8 %collective-permute-start.18 = (f32[2048,256]{1,0:T(8,128)}, f32[2048,256]{1,0:T(8,128)}, u32[]{:S(2)}, u32[]{:S(2)}) collective-permute-start(f32[2048,256]{1,0:T(8,128)} %get-tuple-element.43), channel_id=1, source_target_pairs={{0,1},{1,0},{2,3},{3,2},{4,5},{5,4},{6,7},{7,6},{8,9},{9,8},{10,11... | collective-permute-start | bytes 6291464 | tf_op jit(solution)/shard_map/ppermute | solution.py:466
  75.8 10.1 %collective-permute-start.11 = (f32[2048,256]{1,0:T(8,128)}, f32[2048,256]{1,0:T(8,128)}, u32[]{:S(2)}, u32[]{:S(2)}) collective-permute-start(f32[2048,256]{1,0:T(8,128)} %get-tuple-element.41), channel_id=1, source_target_pairs={{0,1},{1,0},{2,3},{3,2},{4,5},{5,4},{6,7},{7,6},{8,9},{9,8},{10,11... | collective-permute-start | bytes 6291464 | tf_op jit(solution)/shard_map/ppermute | solution.py:466
  75.9 16.4 %collective-permute-start.4 = (f32[2056,256]{1,0:T(8,128)}, f32[2056,256]{1,0:T(8,128)S(1)}, u32[]{:S(2)}, u32[]{:S(2)}) collective-permute-start(f32[2056,256]{1,0:T(8,128)} %get-tuple-element.38), channel_id=1, source_target_pairs={{0,1},{1,0},{2,3},{3,2},{4,5},{5,4},{6,7},{7,6},{8,9},{9,8},{10,11... | collective-permute-start | bytes 6316040 | tf_op jit(solution)/shard_map/ppermute | solution.py:466
  82.6 9.8 %copy-start.8 = (f32[8,256]{1,0:T(8,128)S(1)}, f32[8,256]{1,0:T(8,128)}, u32[]{:S(2)}) copy-start(f32[8,256]{1,0:T(8,128)} %get-tuple-element.39) | copy-start | bytes 24580
  82.6 15.1 %collective-permute-start.19 = (f32[1024,256]{1,0:T(8,128)}, f32[1024,256]{1,0:T(8,128)}, u32[]{:S(2)}, u32[]{:S(2)}) collective-permute-start(f32[1024,256]{1,0:T(8,128)} %dynamic-slice_add_fusion), channel_id=1, source_target_pairs={{0,16},{1,49},{16,0},{17,33},{32,48},{33,17},{48,32},{49,1},{2,18}... | collective-permute-start | bytes 3145736 | tf_op jit(solution)/shard_map/ppermute | solution.py:186
  84.5 7.9 %copy-start.4 = (f32[2048,256]{1,0:T(8,128)S(1)}, f32[2048,256]{1,0:T(8,128)}, u32[]{:S(2)}) copy-start(f32[2048,256]{1,0:T(8,128)} %get-tuple-element.37) | copy-start | bytes 6291460
  88.6 18.9 %collective-permute-start.12 = (f32[1024,256]{1,0:T(8,128)}, f32[1024,256]{1,0:T(8,128)}, u32[]{:S(2)}, u32[]{:S(2)}) collective-permute-start(f32[1024,256]{1,0:T(8,128)} %dynamic-slice_add_fusion.1), channel_id=1, source_target_pairs={{0,2},{1,67},{2,0},{3,65},{64,66},{65,3},{66,64},{67,1},{4,6},{5,7... | collective-permute-start | bytes 3145736 | tf_op jit(solution)/shard_map/ppermute | solution.py:186
  93.6 18.2 %collective-permute-start.5 = (f32[1032,256]{1,0:T(8,128)}, f32[1032,256]{1,0:T(8,128)S(1)}, u32[]{:S(2)}, u32[]{:S(2)}) collective-permute-start(f32[1032,256]{1,0:T(8,128)} %pad_maximum_fusion), channel_id=1, source_target_pairs={{0,4},{1,13},{4,0},{5,9},{8,12},{9,5},{12,8},{13,1},{2,6},{3,15},{... | collective-permute-start | bytes 3170312 | tf_op jit(solution)/shard_map/ppermute | solution.py:186
  95.1 12.5 %copy-start.6 = (f32[2048,256]{1,0:T(8,128)S(1)}, f32[2048,256]{1,0:T(8,128)}, u32[]{:S(2)}) copy-start(f32[2048,256]{1,0:T(8,128)} %get-tuple-element.40) | copy-start | bytes 6291460
  99.8 12.0 %copy-start.5 = (f32[2048,256]{1,0:T(8,128)S(1)}, f32[2048,256]{1,0:T(8,128)}, u32[]{:S(2)}) copy-start(f32[2048,256]{1,0:T(8,128)} %get-tuple-element.37) | copy-start | bytes 6291460
  99.8 14.9 %collective-permute-start.20 = (f32[512,256]{1,0:T(8,128)S(1)}, f32[512,256]{1,0:T(8,128)S(1)}, u32[]{:S(2)}, u32[]{:S(2)}) collective-permute-start(f32[512,256]{1,0:T(8,128)S(1)} %constant_dynamic-slice_fusion.2), channel_id=1, source_target_pairs={{0,48},{1,17},{16,32},{17,1},{32,16},{33,49},{48,0},{49,33},{2,50}... | collective-permute-start | bytes 1572872 | tf_op jit(solution)/shard_map/ppermute | solution.py:186
  109.3 10.5 %collective-permute-start.13 = (f32[512,256]{1,0:T(8,128)S(1)}, f32[512,256]{1,0:T(8,128)S(1)}, u32[]{:S(2)}, u32[]{:S(2)}) collective-permute-start(f32[512,256]{1,0:T(8,128)S(1)} %constant_dynamic-slice_fusion.8), channel_id=1, source_target_pairs={{0,66},{1,3},{2,64},{3,1},{64,2},{65,67},{66,0},{67,65},{4,70},{5,... | collective-permute-start | bytes 1572872 | tf_op jit(solution)/shard_map/ppermute | solution.py:186
  112.1 13.4 %collective-permute-start.6 = (f32[520,256]{1,0:T(8,128)S(1)}, f32[520,256]{1,0:T(8,128)S(1)}, u32[]{:S(2)}, u32[]{:S(2)}) collective-permute-start(f32[520,256]{1,0:T(8,128)S(1)} %pad_maximum_fusion.1), channel_id=1, source_target_pairs={{0,12},{1,5},{4,8},{5,1},{8,4},{9,13},{12,0},{13,9},{2,14},{3,7},{... | collective-permute-start | bytes 1597448 | tf_op jit(solution)/shard_map/ppermute | solution.py:186
  114.8 11.1 %collective-permute-start.21 = (f32[256,256]{1,0:T(8,128)S(1)}, f32[256,256]{1,0:T(8,128)S(1)}, u32[]{:S(2)}, u32[]{:S(2)}) collective-permute-start(f32[256,256]{1,0:T(8,128)S(1)} %constant_dynamic-slice_fusion.1), channel_id=1, source_target_pairs={{0,4},{1,13},{4,0},{5,9},{8,12},{9,5},{12,8},{13,1},{2,6},{3,15},{... | collective-permute-start | bytes 786440 | tf_op jit(solution)/shard_map/ppermute | solution.py:186
  119.9 8.0 %collective-permute-start.14 = (f32[256,256]{1,0:T(8,128)S(1)}, f32[256,256]{1,0:T(8,128)S(1)}, u32[]{:S(2)}, u32[]{:S(2)}) collective-permute-start(f32[256,256]{1,0:T(8,128)S(1)} %constant_dynamic-slice_fusion.7), channel_id=1, source_target_pairs={{0,16},{1,49},{16,0},{17,33},{32,48},{33,17},{48,32},{49,1},{2,18}... | collective-permute-start | bytes 786440 | tf_op jit(solution)/shard_map/ppermute | solution.py:186
  125.6 7.3 %collective-permute-start.7 = (f32[264,256]{1,0:T(8,128)S(1)}, f32[264,256]{1,0:T(8,128)S(1)}, u32[]{:S(2)}, u32[]{:S(2)}) collective-permute-start(f32[264,256]{1,0:T(8,128)S(1)} %pad_maximum_fusion.2), channel_id=1, source_target_pairs={{0,2},{1,67},{2,0},{3,65},{64,66},{65,3},{66,64},{67,1},{4,6},{5,7... | collective-permute-start | bytes 811016 | tf_op jit(solution)/shard_map/ppermute | solution.py:186
  126.0 8.0 %collective-permute-start.22 = (f32[128,256]{1,0:T(8,128)S(1)}, f32[128,256]{1,0:T(8,128)S(1)}, u32[]{:S(2)}, u32[]{:S(2)}) collective-permute-start(f32[128,256]{1,0:T(8,128)S(1)} %constant_dynamic-slice_fusion), channel_id=1, source_target_pairs={{0,12},{1,5},{4,8},{5,1},{8,4},{9,13},{12,0},{13,9},{2,14},{3,7},{... | collective-permute-start | bytes 393224 | tf_op jit(solution)/shard_map/ppermute | solution.py:186
  128.0 7.6 %collective-permute-start.15 = (f32[128,256]{1,0:T(8,128)S(1)}, f32[128,256]{1,0:T(8,128)S(1)}, u32[]{:S(2)}, u32[]{:S(2)}) collective-permute-start(f32[128,256]{1,0:T(8,128)S(1)} %constant_dynamic-slice_fusion.6), channel_id=1, source_target_pairs={{0,48},{1,17},{16,32},{17,1},{32,16},{33,49},{48,0},{49,33},{2,50}... | collective-permute-start | bytes 393224 | tf_op jit(solution)/shard_map/ppermute | solution.py:186
  133.1 6.3 %collective-permute-start.8 = (f32[136,256]{1,0:T(8,128)S(1)}, f32[136,256]{1,0:T(8,128)S(1)}, u32[]{:S(2)}, u32[]{:S(2)}) collective-permute-start(f32[136,256]{1,0:T(8,128)S(1)} %pad_maximum_fusion.3), channel_id=1, source_target_pairs={{0,66},{1,3},{2,64},{3,1},{64,2},{65,67},{66,0},{67,65},{4,70},{5,... | collective-permute-start | bytes 417800 | tf_op jit(solution)/shard_map/ppermute | solution.py:186
  134.0 6.0 %collective-permute-start.23 = (f32[64,256]{1,0:T(8,128)S(1)}, f32[64,256]{1,0:T(8,128)S(1)}, u32[]{:S(2)}, u32[]{:S(2)}) collective-permute-start(f32[64,256]{1,0:T(8,128)S(1)} %constant_dynamic-slice_fusion.14), channel_id=1, source_target_pairs={{0,2},{1,67},{2,0},{3,65},{64,66},{65,3},{66,64},{67,1},{4,6},{5,7... | collective-permute-start | bytes 196616 | tf_op jit(solution)/shard_map/ppermute | solution.py:186
  135.5 5.3 %collective-permute-start.16 = (f32[64,256]{1,0:T(8,128)S(1)}, f32[64,256]{1,0:T(8,128)S(1)}, u32[]{:S(2)}, u32[]{:S(2)}) collective-permute-start(f32[64,256]{1,0:T(8,128)S(1)} %constant_dynamic-slice_fusion.5), channel_id=1, source_target_pairs={{0,4},{1,13},{4,0},{5,9},{8,12},{9,5},{12,8},{13,1},{2,6},{3,15},{... | collective-permute-start | bytes 196616 | tf_op jit(solution)/shard_map/ppermute | solution.py:186
  139.5 6.7 %collective-permute-start.9 = (f32[72,256]{1,0:T(8,128)S(1)}, f32[72,256]{1,0:T(8,128)S(1)}, u32[]{:S(2)}, u32[]{:S(2)}) collective-permute-start(f32[72,256]{1,0:T(8,128)S(1)} %pad_maximum_fusion.4), channel_id=1, source_target_pairs={{0,16},{1,49},{16,0},{17,33},{32,48},{33,17},{48,32},{49,1},{2,18}... | collective-permute-start | bytes 221192 | tf_op jit(solution)/shard_map/ppermute | solution.py:186
  140.1 5.2 %collective-permute-start.24 = (f32[32,256]{1,0:T(8,128)S(1)}, f32[32,256]{1,0:T(8,128)S(1)}, u32[]{:S(2)}, u32[]{:S(2)}) collective-permute-start(f32[32,256]{1,0:T(8,128)S(1)} %constant_dynamic-slice_fusion.3), channel_id=1, source_target_pairs={{0,66},{1,3},{2,64},{3,1},{64,2},{65,67},{66,0},{67,65},{4,70},{5,... | collective-permute-start | bytes 98312 | tf_op jit(solution)/shard_map/ppermute | solution.py:186
  140.9 5.2 %collective-permute-start.17 = (f32[32,256]{1,0:T(8,128)S(1)}, f32[32,256]{1,0:T(8,128)S(1)}, u32[]{:S(2)}, u32[]{:S(2)}) collective-permute-start(f32[32,256]{1,0:T(8,128)S(1)} %constant_dynamic-slice_fusion.4), channel_id=1, source_target_pairs={{0,12},{1,5},{4,8},{5,1},{8,4},{9,13},{12,0},{13,9},{2,14},{3,7},{... | collective-permute-start | bytes 98312 | tf_op jit(solution)/shard_map/ppermute | solution.py:186
  146.2 5.6 %collective-permute-start.10 = (f32[40,256]{1,0:T(8,128)S(1)}, f32[40,256]{1,0:T(8,128)S(1)}, u32[]{:S(2)}, u32[]{:S(2)}) collective-permute-start(f32[40,256]{1,0:T(8,128)S(1)} %pad_maximum_fusion.7), channel_id=1, source_target_pairs={{0,48},{1,17},{16,32},{17,1},{32,16},{33,49},{48,0},{49,33},{2,50}... | collective-permute-start | bytes 122888 | tf_op jit(solution)/shard_map/ppermute | solution.py:186

commit v6 on v5

--- a/solution.py
+++ b/solution.py
@@ -12,6 +12,7 @@
 SUB = 3
 BATCHES = 64
 FEW = 640
+FEW_ROWS = 32
 BX = ("bx_0", "bx_1")
 BY = ("by_0", "by_1", "by_2")
 CORE = "by_2"
@@ -61,38 +62,45 @@
             )
         even_ref[row + SUB, 0] = cells
         even_ref[row + SUB, 1] = jnp.concatenate([right, gap, left], axis=0).T
-    here, there = even_ref, odd_ref
-    for substep in range(SUB):
-        margin = SUB - substep - 1
-        for row in range(-margin, 8 + margin):
-            at = row + SUB
-            main, side = here[at, 0], here[at, 1]
-            main_up, side_up = pltpu.roll(main, 127, 1), pltpu.roll(side, 127, 1)
-            main_down, side_down = pltpu.roll(main, 1, 1), pltpu.roll(side, 1, 1)
-            new = (
-                coef_0[...] * main
-                + coef_1[...] * here[at + 1, 0]
-                + coef_2[...] * here[at - 1, 0]
-                + coef_3[...] * jnp.where(lane == 127, side_up, main_up)
-                + coef_4[...] * jnp.where(lane == 0, side_down, main_down)
-            )
-            if margin == 0:
-                field_ref[:, row * 128 : (row + 1) * 128] = new
-                x_ref[:, row * 128 : (row + 1) * 128] = new.astype(jnp.bfloat16)
-                continue
-            near = (
-                coef_0[...] * side
-                + coef_1[...] * here[at + 1, 1]
-                + coef_2[...] * here[at - 1, 1]
-                + coef_3[...] * jnp.where(lane == 127, main_up, side_up)
-                + coef_4[...] * jnp.where(lane == 0, main_down, side_down)
-            ) * beside
-            if row < 0 or row > 7:
-                new = new * inside[0 if row < 0 else 1]
-                near = near * inside[0 if row < 0 else 1]
-            there[at, 0] = new
-            there[at, 1] = near
-        here, there = there, here
+    lane = lane[:FEW_ROWS]
+    beside = beside[:FEW_ROWS]
+
+    @pl.loop(0, 128 // FEW_ROWS)
+    def _(piece):
+        feats = pl.ds(pl.multiple_of(piece * FEW_ROWS, FEW_ROWS), FEW_ROWS)
+        centre, east, west, north, south = (ref[feats, :] for ref in (coef_0, coef_1, coef_2, coef_3, coef_4))
+        here, there = even_ref, odd_ref
+        for substep in range(SUB):
+            margin = SUB - substep - 1
+            for row in range(-margin, 8 + margin):
+                at = row + SUB
+                main, side = here[at, 0, feats, :], here[at, 1, feats, :]
+                main_up, side_up = pltpu.roll(main, 127, 1), pltpu.roll(side, 127, 1)
+                main_down, side_down = pltpu.roll(main, 1, 1), pltpu.roll(side, 1, 1)
+                new = (
+                    centre * main
+                    + east * here[at + 1, 0, feats, :]
+                    + west * here[at - 1, 0, feats, :]
+                    + north * jnp.where(lane == 127, side_up, main_up)
+                    + south * jnp.where(lane == 0, side_down, main_down)
+                )
+                if margin == 0:
+                    field_ref[feats, row * 128 : (row + 1) * 128] = new
+                    x_ref[feats, row * 128 : (row + 1) * 128] = new.astype(jnp.bfloat16)
+                    continue
+                near = (
+                    centre * side
+                    + east * here[at + 1, 1, feats, :]
+                    + west * here[at - 1, 1, feats, :]
+                    + north * jnp.where(lane == 127, main_up, side_up)
+                    + south * jnp.where(lane == 0, main_down, side_down)
+                ) * beside
+                if row < 0 or row > 7:
+                    new = new * inside[0 if row < 0 else 1]
+                    near = near * inside[0 if row < 0 else 1]
+                there[at, 0, feats, :] = new
+                there[at, 1, feats, :] = near
+            here, there = there, here
 
 
 def shifted(value, axis, step):
@@ -226,7 +234,7 @@
     scale, scalar_ref, table_ref, x_hbm, win_hbm, wout_hbm, target_hbm, field_hbm, rank_ref, batch_ref,
     new_hbm, kept_hbm_a, kept_hbm_b, kept_hbm_c, sent_hbm_a, sent_hbm_b, sent_hbm_c, loss_ref,
     x_ref, win_ref, wout_ref, target_ref, field_ref, new_ref, kept_a, kept_b, kept_c, sent_a, sent_b, sent_c,
-    slope_ref, hidden_ref, tend_ref, pick_ref, xc_ref, xn_ref, dtend_ref, dtn_ref,
+    slope_ref, hidden_ref, tend_ref, pick_ref, xc_ref, xn_ref, dtend_ref, dtn_ref, persq_ref,
     win_sem, wout_sem, in_sem, out_sem,
 ):
     feats, cols = x_ref.shape
@@ -267,15 +275,23 @@
     incoming[2].start()
 
     def run(n):
-        for at in range(0, n, 128):
-            slot = lax.broadcasted_iota(jnp.int32, (128, cols), 0) + at
-            pick_ref[at : at + 128, :] = jnp.where(slot == rank_ref[...], 1.0, 0.0).astype(jnp.bfloat16)
+        @pl.loop(0, n // 128)
+        def _(block):
+            slot = lax.broadcasted_iota(jnp.int32, (128, cols), 0) + block * 128
+            pick_ref[pl.ds(pl.multiple_of(block * 128, 128), 128), :] = jnp.where(
+                slot == rank_ref[...], 1.0, 0.0
+            ).astype(jnp.bfloat16)
+
         incoming[0].wait()
-        packed = lax.dot_general(x_ref[...], pick_ref[:n, :], ROWS, preferred_element_type=jnp.float32)
-        packed = packed.astype(jnp.bfloat16)
-        xc_ref[:, :n] = packed
-        xn_ref[:n, :] = packed.T
-        tend_ref[:, :n] = jnp.zeros((feats, n), jnp.float32)
+
+        @pl.loop(0, feats // 128)
+        def _(block):
+            some = pl.ds(pl.multiple_of(block * 128, 128), 128)
+            packed = lax.dot_general(x_ref[some, :], pick_ref[:n, :], ROWS, preferred_element_type=jnp.float32)
+            packed = packed.astype(jnp.bfloat16)
+            xc_ref[some, :n] = packed
+            xn_ref[:n, some] = packed.T
+            tend_ref[some, :n] = jnp.zeros((128, n), jnp.float32)
 
         def activate(piece):
             for part in range(2):
@@ -308,23 +324,30 @@
         wout_copy(7).wait()
         project(7)
         pick = pick_ref[:n, :]
-        tend = tend_ref[:, :n]
+        persq_ref[:, :n] = jnp.zeros((1, n), jnp.float32)
         incoming[1].wait()
-        wanted = lax.dot_general(target_ref[...], pick, ROWS, preferred_element_type=jnp.float32)
-        err = tend - wanted
-        dtend = (err * scale[1]).astype(jnp.bfloat16)
-        dtend_ref[:, :n] = dtend
-        dtn_ref[:n, :] = dtend.T
-        coarse = tend.astype(jnp.bfloat16)
-        fine = (tend - coarse.astype(jnp.float32)).astype(jnp.bfloat16)
-        spread = jnp.dot(coarse, pick, preferred_element_type=jnp.float32)
-        spread += jnp.dot(fine, pick, preferred_element_type=jnp.float32)
         incoming[2].wait()
-        new = field_ref[...] + 0.5 * spread
-        for row in range(8):
-            new_ref[pl.ds(row, feats, stride=8), :] = new[:, row * 128 : (row + 1) * 128]
+
+        @pl.loop(0, feats // 128)
+        def _(block):
+            some = pl.ds(pl.multiple_of(block * 128, 128), 128)
+            tend = tend_ref[some, :n]
+            wanted = lax.dot_general(target_ref[some, :], pick_ref[:n, :], ROWS, preferred_element_type=jnp.float32)
+            err = tend - wanted
+            persq_ref[:, :n] += 0.5 * jnp.sum(err * err, axis=0, keepdims=True)
+            dtend = (err * scale[1]).astype(jnp.bfloat16)
+            dtend_ref[some, :n] = dtend
+            dtn_ref[:n, some] = dtend.T
+            coarse = tend.astype(jnp.bfloat16)
+            fine = (tend - coarse.astype(jnp.float32)).astype(jnp.bfloat16)
+            spread = jnp.dot(coarse, pick_ref[:n, :], preferred_element_type=jnp.float32)
+            spread += jnp.dot(fine, pick_ref[:n, :], preferred_element_type=jnp.float32)
+            new = field_ref[some, :] + 0.5 * spread
+            for row in range(8):
+                new_ref[pl.ds(block * 1024 + row, 128, stride=8), :] = new[:, row * 128 : (row + 1) * 128]
+
         outgoing[0].start()
-        persq = 0.5 * jnp.sum(err * err, axis=0, keepdims=True)
+        persq = persq_ref[:, :n]
         batch = lax.dot_general(batch_ref[...], pick, ROWS, preferred_element_type=jnp.float32)
         which = lax.broadcasted_iota(jnp.int32, (128, n), 0).astype(jnp.float32)
         onehot = jnp.where(which == batch[0:1, :], 1.0, 0.0)
@@ -451,6 +474,7 @@
             pltpu.VMEM((cols, feats), bf16),
             pltpu.VMEM((feats, cols), bf16),
             pltpu.VMEM((cols, feats), bf16),
+            pltpu.VMEM((1, cols), f32),
             pltpu.SemaphoreType.DMA((8,)),
             pltpu.SemaphoreType.DMA((8,)),
             pltpu.SemaphoreType.DMA((3,)),

time: 153 us -> 152 us (level)
  no operation moved by 1% of the time
where the time goes in v6:
time: 152 us
  starting transfers between devices  49 us (32%)
  Pallas kernels  45.3 us (30%)
  waiting for transfers between devices  40.9 us (27%)
  other arithmetic  12.3 us (8%)
  local copies, waits for them, and re-layouts  3.25 us (2%)
    ppermute x18, starting transfers between devices, ring_turn(): coming = lax.ppermute(leaving, AXES[axis], RING[turn + 1])  38.3 us
    pallas_call x1, Pallas kernels, network(): pl.pallas_call(functools.partial(network_kernel, (BATCHES / (total * feat...  31.6 us
    ppermute x18, waiting for transfers between devices, ring_turn(): coming = lax.ppermute(leaving, AXES[axis], RING[turn + 1])  20.4 us
    ppermute x4, waiting for transfers between devices, shifted(): return lax.ppermute(value, axis, pairs)  15.5 us
    pallas_call x1, Pallas kernels, transported(): pl.pallas_call(transport_kernel, grid=(feats // 128,), in_specs=[pl.Block...  10.4 us
    ppermute x4, starting transfers between devices, shifted(): return lax.ppermute(value, axis, pairs)  9.57 us
    add x3, other arithmetic, ring_turn(): leaving = sum((half_of(term, size, 1 - bit) for term in terms))  5.51 us
    ppermute x3, waiting for transfers between devices, network(): lax.ppermute(sent, CORE, PAIR)  5.09 us
  transfers between devices with their start and end apart: 25, of which 15 were waited for; matrix products, arithmetic and copies ran while one was open for 8% of the time, Pallas kernels for 0%

profile of v6, /device:TPU:0, one launch (start us, length us, event | category | flops | bytes accessed | tf_op | source)
XLA Modules:
  0.0 151.9 jit_solution(18164676080430078470)
XLA Ops:
  0.7 2.6 %edges.1 = (f32[3,432,128]{2,1,0:T(8,128)S(1)}, f32[3,432,128]{2,1,0:T(8,128)S(1)}, f32[3,64,128]{2,1,0:T(8,128)S(1)}, f32[3,64,128]{2,1,0:T(8,128)S(1)}) custom-call(f32[3072,128]{1,0:T(8,128)} %bitcast.9), custom_call_target="tpu_custom_call" | custom-call | flops 1048576 | bytes 3145728 | tf_op jit(solution)/shard_map/edges/pallas_call | solution.py:117
  3.3 1.3 collective-permute-start.1
  4.6 3.0 %collective-permute-start = (f32[3,64,128]{2,1,0:T(8,128)S(1)}, f32[3,64,128]{2,1,0:T(8,128)S(1)}, u32[]{:S(2)}, u32[]{:S(2)}) collective-permute-start(f32[3,64,128]{2,1,0:T(8,128)S(1)} %get-tuple-element.24), channel_id=1, source_target_pairs={{0,1},{1,2},{2,3},{3,4},{4,5},{5,6},{6,7},{7,8},{8,9},{9,10},{10,1... | collective-permute-start | bytes 294920 | tf_op jit(solution)/shard_map/ppermute | solution.py:109
  7.7 0.9 collective-permute-done.left_ref
  8.6 3.9 %collective-permute-start.2 = (f32[3,432,128]{2,1,0:T(8,128)S(1)}, f32[3,432,128]{2,1,0:T(8,128)S(1)}, u32[]{:S(2)}, u32[]{:S(2)}) collective-permute-start(f32[3,432,128]{2,1,0:T(8,128)S(1)} %maximum_dynamic-update-slice_fusion), channel_id=1, source_target_pairs={{0,16},{16,32},{32,48},{48,64},{64,80},{80,96},{96,112},{1,17},{17... | collective-permute-start | bytes 1990664 | tf_op jit(solution)/shard_map/ppermute | solution.py:109
  12.6 1.3 collective-permute-start.3
  13.9 1.1 copy.16
  15.0 0.7 ranks.1
  15.7 0.6 copy-done.2
  16.3 0.6 copy-done.3
  16.9 10.0 %collective-permute-done.2.above_ref = f32[3,432,128]{2,1,0:T(8,128)S(1)} collective-permute-done((f32[3,432,128]{2,1,0:T(8,128)S(1)}, f32[3,432,128]{2,1,0:T(8,128)S(1)}, u32[]{:S(2)}, u32[]{:S(2)}) %collective-permute-start.2) | collective-permute-done | bytes 663584 | tf_op jit(solution)/shard_map/ppermute | solution.py:109
  26.9 4.6 %collective-permute-done.3.below_ref = f32[3,432,128]{2,1,0:T(8,128)S(1)} collective-permute-done((f32[3,432,128]{2,1,0:T(8,128)S(1)}, f32[3,432,128]{2,1,0:T(8,128)S(1)}, u32[]{:S(2)}, u32[]{:S(2)}) %collective-permute-start.3) | collective-permute-done | bytes 663584 | tf_op jit(solution)/shard_map/ppermute | solution.py:109
  31.5 0.1 broadcast_in_dim.10.coef_0
  31.6 0.1 broadcast_in_dim.11.coef_1
  31.7 0.1 broadcast_in_dim.12.coef_2
  31.8 0.1 broadcast_in_dim.13.coef_3
  31.9 0.1 broadcast_in_dim.14.coef_4
  32.1 10.4 %transport.1 = (f32[384,1024]{1,0:T(8,128)}, bf16[384,1024]{1,0:T(8,128)(2,1)}) custom-call(f32[3072,128]{1,0:T(8,128)} %bitcast.10, f32[3,432,128]{2,1,0:T(8,128)S(1)} %collective-permute-done.2.above_ref, f32[3,432,128]{2,1,0:T(8,128)S(1)} %collective-permute-done.3.below_ref, f32[3,64,128]{2,1,0:T(8,128)S(1)} %collective-permute-done.left_ref, ...), custom_call_target="tpu_custom_call" | custom-call | flops 16777216 | bytes 6291456 | tf_op jit(solution)/shard_map/transport/pallas_call | solution.py:147
  42.4 31.6 %network.1 = (f32[3072,128]{1,0:T(8,128)}, f32[2048,256]{1,0:T(8,128)}, f32[2048,256]{1,0:T(8,128)}, f32[2048,256]{1,0:T(8,128)}, f32[2056,256]{1,0:T(8,128)}, /...) custom-call(s32[1]{0:T(128)} %get-tuple-element.28.scalar_ref, s32[384]{0:T(512)} %constant.119.clone.table_ref, ...), custom_call_target="tpu_custom_call" | custom-call | flops 16106127360 | bytes 20971520 | tf_op jit(solution)/shard_map/network/pallas_call | solution.py:455
  74.0 0.7 collective-permute-start.18
  74.7 0.1 collective-permute-start.11
  74.8 0.4 collective-permute-start.4
  75.2 3.6 %collective-permute-done.18 = f32[2048,256]{1,0:T(8,128)} collective-permute-done((f32[2048,256]{1,0:T(8,128)}, f32[2048,256]{1,0:T(8,128)}, u32[]{:S(2)}, u32[]{:S(2)}) %collective-permute-start.18) | collective-permute-done | bytes 2097184 | tf_op jit(solution)/shard_map/ppermute | solution.py:490
  78.8 2.7 %dynamic-slice_add_fusion = f32[1024,256]{1,0:T(8,128)} fusion(f32[2048,256]{1,0:T(8,128)} %collective-permute-done.18, s32[]{:T(128)S(6)} %select_n.231, f32[2048,256]{1,0:T(8,128)} %get-tuple-element.42), kind=kLoop, calls=%fused_computation.2 | loop fusion | flops 262144 | bytes 3145732 | tf_op jit(solution)/shard_map/add | solution.py:191
  81.5 1.9 %collective-permute-start.19 = (f32[1024,256]{1,0:T(8,128)}, f32[1024,256]{1,0:T(8,128)}, u32[]{:S(2)}, u32[]{:S(2)}) collective-permute-start(f32[1024,256]{1,0:T(8,128)} %dynamic-slice_add_fusion), channel_id=1, source_target_pairs={{0,16},{1,49},{16,0},{17,33},{32,48},{33,17},{48,32},{49,1},{2,18}... | collective-permute-start | bytes 3145736 | tf_op jit(solution)/shard_map/ppermute | solution.py:194
  83.4 1.5 collective-permute-done.11
  84.8 2.7 %dynamic-slice_add_fusion.1 = f32[1024,256]{1,0:T(8,128)} fusion(f32[2048,256]{1,0:T(8,128)} %collective-permute-done.11, s32[]{:T(128)S(6)} %select_n.219, f32[2048,256]{1,0:T(8,128)} %get-tuple-element.40), kind=kLoop, calls=%fused_computation.4 | loop fusion | flops 262144 | bytes 3145732 | tf_op jit(solution)/shard_map/add | solution.py:191
  87.5 3.7 %collective-permute-start.12 = (f32[1024,256]{1,0:T(8,128)}, f32[1024,256]{1,0:T(8,128)}, u32[]{:S(2)}, u32[]{:S(2)}) collective-permute-start(f32[1024,256]{1,0:T(8,128)} %dynamic-slice_add_fusion.1), channel_id=1, source_target_pairs={{0,2},{1,67},{2,0},{3,65},{64,66},{65,3},{66,64},{67,1},{4,6},{5,7... | collective-permute-start | bytes 3145736 | tf_op jit(solution)/shard_map/ppermute | solution.py:194
  91.2 0.1 dynamic-slice_add_fusion.2
  91.4 1.1 pad_maximum_fusion
  92.5 1.5 collective-permute-start.5
  94.0 2.6 %collective-permute-done.19 = f32[1024,256]{1,0:T(8,128)} collective-permute-done((f32[1024,256]{1,0:T(8,128)}, f32[1024,256]{1,0:T(8,128)}, u32[]{:S(2)}, u32[]{:S(2)}) %collective-permute-start.19) | collective-permute-done | bytes 1048608 | tf_op jit(solution)/shard_map/ppermute | solution.py:194
  96.6 2.1 %add_add_fusion = f32[1024,256]{1,0:T(8,128)S(1)} fusion(f32[1024,256]{1,0:T(8,128)} %collective-permute-done.19, f32[2048,256]{1,0:T(8,128)} %collective-permute-done.18, s32[]{:T(128)S(6)} %select_n.230, f32[2048,256]{1,0:T(8,128)} %get-tuple-element.42), kind=kLoop, calls=%fused_computation.3 | loop fusion | flops 524288 | bytes 4194308 | tf_op jit(solution)/shard_map/add | solution.py:196
  98.7 7.7 %collective-permute-start.20 = (f32[512,256]{1,0:T(8,128)S(1)}, f32[512,256]{1,0:T(8,128)S(1)}, u32[]{:S(2)}, u32[]{:S(2)}) collective-permute-start(f32[512,256]{1,0:T(8,128)S(1)} %constant_dynamic-slice_fusion.2), channel_id=1, source_target_pairs={{0,48},{1,17},{16,32},{17,1},{32,16},{33,49},{48,0},{49,33},{2,50}... | collective-permute-start | bytes 1572872 | tf_op jit(solution)/shard_map/ppermute | solution.py:194
  106.4 1.7 %add_add_fusion.1 = f32[1024,256]{1,0:T(8,128)S(1)} fusion(f32[1024,256]{1,0:T(8,128)} %collective-permute-done.12, f32[2048,256]{1,0:T(8,128)} %collective-permute-done.11, s32[]{:T(128)S(6)} %select_n.218, f32[2048,256]{1,0:T(8,128)S(1)} %copy-done.6), kind=kLoop, calls=%fused_computation.5 | loop fusion | flops 524288 | bytes 4194308 | tf_op jit(solution)/shard_map/add | solution.py:196
  108.2 2.5 %collective-permute-start.13 = (f32[512,256]{1,0:T(8,128)S(1)}, f32[512,256]{1,0:T(8,128)S(1)}, u32[]{:S(2)}, u32[]{:S(2)}) collective-permute-start(f32[512,256]{1,0:T(8,128)S(1)} %constant_dynamic-slice_fusion.8), channel_id=1, source_target_pairs={{0,66},{1,3},{2,64},{3,1},{64,2},{65,67},{66,0},{67,65},{4,70},{5,... | collective-permute-start | bytes 1572872 | tf_op jit(solution)/shard_map/ppermute | solution.py:194
  110.7 0.2 slice_add_fusion
  111.0 1.4 collective-permute-start.6
  112.5 1.1 collective-permute-done.20
  113.6 0.1 dynamic-slice_add_fusion.3
  113.7 2.5 %collective-permute-start.21 = (f32[256,256]{1,0:T(8,128)S(1)}, f32[256,256]{1,0:T(8,128)S(1)}, u32[]{:S(2)}, u32[]{:S(2)}) collective-permute-start(f32[256,256]{1,0:T(8,128)S(1)} %constant_dynamic-slice_fusion.1), channel_id=1, source_target_pairs={{0,4},{1,13},{4,0},{5,9},{8,12},{9,5},{12,8},{13,1},{2,6},{3,15},{... | collective-permute-start | bytes 786440 | tf_op jit(solution)/shard_map/ppermute | solution.py:194
  116.2 2.5 %collective-permute-done.13 = f32[512,256]{1,0:T(8,128)S(1)} collective-permute-done((f32[512,256]{1,0:T(8,128)S(1)}, f32[512,256]{1,0:T(8,128)S(1)}, u32[]{:S(2)}, u32[]{:S(2)}) %collective-permute-start.13) | collective-permute-done | bytes 524320 | tf_op jit(solution)/shard_map/ppermute | solution.py:194
  118.7 0.1 dynamic-slice_add_fusion.4
  118.8 0.3 collective-permute-start.14
  119.1 5.3 %collective-permute-done.6 = f32[520,256]{1,0:T(8,128)S(1)} collective-permute-done((f32[520,256]{1,0:T(8,128)S(1)}, f32[520,256]{1,0:T(8,128)S(1)}, u32[]{:S(2)}, u32[]{:S(2)}) %collective-permute-start.6) | collective-permute-done | bytes 532512 | tf_op jit(solution)/shard_map/ppermute | solution.py:194
  124.4 0.1 slice_add_fusion.1
  124.5 0.3 collective-permute-start.7
  124.9 1.9 %collective-permute-start.22 = (f32[128,256]{1,0:T(8,128)S(1)}, f32[128,256]{1,0:T(8,128)S(1)}, u32[]{:S(2)}, u32[]{:S(2)}) collective-permute-start(f32[128,256]{1,0:T(8,128)S(1)} %constant_dynamic-slice_fusion), channel_id=1, source_target_pairs={{0,12},{1,5},{4,8},{5,1},{8,4},{9,13},{12,0},{13,9},{2,14},{3,7},{... | collective-permute-start | bytes 393224 | tf_op jit(solution)/shard_map/ppermute | solution.py:194
  126.8 4.6 %collective-permute-start.15 = (f32[128,256]{1,0:T(8,128)S(1)}, f32[128,256]{1,0:T(8,128)S(1)}, u32[]{:S(2)}, u32[]{:S(2)}) collective-permute-start(f32[128,256]{1,0:T(8,128)S(1)} %constant_dynamic-slice_fusion.6), channel_id=1, source_target_pairs={{0,48},{1,17},{16,32},{17,1},{32,16},{33,49},{48,0},{49,33},{2,50}... | collective-permute-start | bytes 393224 | tf_op jit(solution)/shard_map/ppermute | solution.py:194
  131.5 0.2 collective-permute-done.7
  131.7 1.2 collective-permute-start.8
  132.9 0.6 collective-permute-start.23
  133.6 0.9 collective-permute-done.15
  134.4 0.6 collective-permute-start.16
  135.0 3.1 %collective-permute-done.8 = f32[136,256]{1,0:T(8,128)S(1)} collective-permute-done((f32[136,256]{1,0:T(8,128)S(1)}, f32[136,256]{1,0:T(8,128)S(1)}, u32[]{:S(2)}, u32[]{:S(2)}) %collective-permute-start.8) | collective-permute-done | bytes 139296 | tf_op jit(solution)/shard_map/ppermute | solution.py:194
  138.2 0.8 collective-permute-start.9
  139.0 0.6 collective-permute-start.24
  139.6 2.5 %collective-permute-start.17 = (f32[32,256]{1,0:T(8,128)S(1)}, f32[32,256]{1,0:T(8,128)S(1)}, u32[]{:S(2)}, u32[]{:S(2)}) collective-permute-start(f32[32,256]{1,0:T(8,128)S(1)} %constant_dynamic-slice_fusion.4), channel_id=1, source_target_pairs={{0,12},{1,5},{4,8},{5,1},{8,4},{9,13},{12,0},{13,9},{2,14},{3,7},{... | collective-permute-start | bytes 98312 | tf_op jit(solution)/shard_map/ppermute | solution.py:194
  142.1 2.2 %collective-permute-done.24 = f32[32,256]{1,0:T(8,128)S(1)} collective-permute-done((f32[32,256]{1,0:T(8,128)S(1)}, f32[32,256]{1,0:T(8,128)S(1)}, u32[]{:S(2)}, u32[]{:S(2)}) %collective-permute-start.24) | collective-permute-done | bytes 32800 | tf_op jit(solution)/shard_map/ppermute | solution.py:194
  144.2 0.6 collective-permute-done.17
  144.9 3.8 %collective-permute-start.10 = (f32[40,256]{1,0:T(8,128)S(1)}, f32[40,256]{1,0:T(8,128)S(1)}, u32[]{:S(2)}, u32[]{:S(2)}) collective-permute-start(f32[40,256]{1,0:T(8,128)S(1)} %pad_maximum_fusion.7), channel_id=1, source_target_pairs={{0,48},{1,17},{16,32},{17,1},{32,16},{33,49},{48,0},{49,33},{2,50}... | collective-permute-start | bytes 122888 | tf_op jit(solution)/shard_map/ppermute | solution.py:194
  148.7 2.0 %collective-permute-done.10 = f32[40,256]{1,0:T(8,128)S(1)} collective-permute-done((f32[40,256]{1,0:T(8,128)S(1)}, f32[40,256]{1,0:T(8,128)S(1)}, u32[]{:S(2)}, u32[]{:S(2)}) %collective-permute-start.10) | collective-permute-done | bytes 40992 | tf_op jit(solution)/shard_map/ppermute | solution.py:194
  150.7 0.5 fusion
  151.3 0.6 pad_maximum_fusion.5
  (79 shorter events, 0.8 us)
Async XLA Ops:
  0.6 13.2 %copy-start.9 = (f32[384]{0:T(512)S(1)}, f32[384]{0:T(512)}, u32[]{:S(2)}) copy-start(f32[384]{0:T(512)} %param.14) | copy-start | bytes 4612
  0.6 13.2 %copy-start.10 = (f32[384]{0:T(512)S(1)}, f32[384]{0:T(512)}, u32[]{:S(2)}) copy-start(f32[384]{0:T(512)} %param.16) | copy-start | bytes 4612
  0.7 13.2 %copy-start.11 = (f32[384]{0:T(512)S(1)}, f32[384]{0:T(512)}, u32[]{:S(2)}) copy-start(f32[384]{0:T(512)} %param.15) | copy-start | bytes 4612
  0.7 13.2 %copy-start.7 = (bf16[384,8,128]{2,1,0:T(8,128)(2,1)S(1)}, bf16[384,8,128]{2,1,0:T(8,128)(2,1)}, u32[]{:S(2)}) copy-start(bf16[384,8,128]{2,1,0:T(8,128)(2,1)} %param.11) | copy-start | bytes 2359300
  0.7 14.3 %copy-start = (s32[8,128]{1,0:T(8,128)S(1)}, s32[8,128]{1,0:T(8,128)}, u32[]{:S(2)}) copy-start(s32[8,128]{1,0:T(8,128)} %mask_ref) | copy-start | bytes 12292
  0.7 14.3 %copy-start.1 = (s32[8,128]{1,0:T(8,128)S(1)}, s32[8,128]{1,0:T(8,128)}, u32[]{:S(2)}) copy-start(s32[8,128]{1,0:T(8,128)} %batch_ref) | copy-start | bytes 12292
  3.3 4.3 %collective-permute-start.1 = (f32[3,64,128]{2,1,0:T(8,128)S(1)}, f32[3,64,128]{2,1,0:T(8,128)S(1)}, u32[]{:S(2)}, u32[]{:S(2)}) collective-permute-start(f32[3,64,128]{2,1,0:T(8,128)S(1)} %get-tuple-element.25), channel_id=1, source_target_pairs={{1,0},{2,1},{3,2},{4,3},{5,4},{6,5},{7,6},{8,7},{9,8},{10,9},{11,1... | collective-permute-start | bytes 294920 | tf_op jit(solution)/shard_map/ppermute | solution.py:109
  4.6 4.0 %collective-permute-start = (f32[3,64,128]{2,1,0:T(8,128)S(1)}, f32[3,64,128]{2,1,0:T(8,128)S(1)}, u32[]{:S(2)}, u32[]{:S(2)}) collective-permute-start(f32[3,64,128]{2,1,0:T(8,128)S(1)} %get-tuple-element.24), channel_id=1, source_target_pairs={{0,1},{1,2},{2,3},{3,4},{4,5},{5,6},{6,7},{7,8},{8,9},{9,10},{10,1... | collective-permute-start | bytes 294920 | tf_op jit(solution)/shard_map/ppermute | solution.py:109
  8.6 18.3 %collective-permute-start.2 = (f32[3,432,128]{2,1,0:T(8,128)S(1)}, f32[3,432,128]{2,1,0:T(8,128)S(1)}, u32[]{:S(2)}, u32[]{:S(2)}) collective-permute-start(f32[3,432,128]{2,1,0:T(8,128)S(1)} %maximum_dynamic-update-slice_fusion), channel_id=1, source_target_pairs={{0,16},{16,32},{32,48},{48,64},{64,80},{80,96},{96,112},{1,17},{17... | collective-permute-start | bytes 1990664 | tf_op jit(solution)/shard_map/ppermute | solution.py:109
  12.6 18.9 %collective-permute-start.3 = (f32[3,432,128]{2,1,0:T(8,128)S(1)}, f32[3,432,128]{2,1,0:T(8,128)S(1)}, u32[]{:S(2)}, u32[]{:S(2)}) collective-permute-start(f32[3,432,128]{2,1,0:T(8,128)S(1)} %maximum_dynamic-update-slice_fusion.1), channel_id=1, source_target_pairs={{16,0},{32,16},{48,32},{64,48},{80,64},{96,80},{112,96},{17,1},{33... | collective-permute-start | bytes 1990664 | tf_op jit(solution)/shard_map/ppermute | solution.py:109
  15.7 0.6 copy-start.2
  16.3 0.6 copy-start.3
  74.0 4.8 %collective-permute-start.18 = (f32[2048,256]{1,0:T(8,128)}, f32[2048,256]{1,0:T(8,128)}, u32[]{:S(2)}, u32[]{:S(2)}) collective-permute-start(f32[2048,256]{1,0:T(8,128)} %get-tuple-element.43), channel_id=1, source_target_pairs={{0,1},{1,0},{2,3},{3,2},{4,5},{5,4},{6,7},{7,6},{8,9},{9,8},{10,11... | collective-permute-start | bytes 6291464 | tf_op jit(solution)/shard_map/ppermute | solution.py:490
  74.7 10.1 %collective-permute-start.11 = (f32[2048,256]{1,0:T(8,128)}, f32[2048,256]{1,0:T(8,128)}, u32[]{:S(2)}, u32[]{:S(2)}) collective-permute-start(f32[2048,256]{1,0:T(8,128)} %get-tuple-element.41), channel_id=1, source_target_pairs={{0,1},{1,0},{2,3},{3,2},{4,5},{5,4},{6,7},{7,6},{8,9},{9,8},{10,11... | collective-permute-start | bytes 6291464 | tf_op jit(solution)/shard_map/ppermute | solution.py:490
  74.8 16.4 %collective-permute-start.4 = (f32[2056,256]{1,0:T(8,128)}, f32[2056,256]{1,0:T(8,128)S(1)}, u32[]{:S(2)}, u32[]{:S(2)}) collective-permute-start(f32[2056,256]{1,0:T(8,128)} %get-tuple-element.38), channel_id=1, source_target_pairs={{0,1},{1,0},{2,3},{3,2},{4,5},{5,4},{6,7},{7,6},{8,9},{9,8},{10,11... | collective-permute-start | bytes 6316040 | tf_op jit(solution)/shard_map/ppermute | solution.py:490
  81.5 9.7 %copy-start.8 = (f32[8,256]{1,0:T(8,128)S(1)}, f32[8,256]{1,0:T(8,128)}, u32[]{:S(2)}) copy-start(f32[8,256]{1,0:T(8,128)} %get-tuple-element.39) | copy-start | bytes 24580
  81.5 15.1 %collective-permute-start.19 = (f32[1024,256]{1,0:T(8,128)}, f32[1024,256]{1,0:T(8,128)}, u32[]{:S(2)}, u32[]{:S(2)}) collective-permute-start(f32[1024,256]{1,0:T(8,128)} %dynamic-slice_add_fusion), channel_id=1, source_target_pairs={{0,16},{1,49},{16,0},{17,33},{32,48},{33,17},{48,32},{49,1},{2,18}... | collective-permute-start | bytes 3145736 | tf_op jit(solution)/shard_map/ppermute | solution.py:194
  83.4 7.9 %copy-start.4 = (f32[2048,256]{1,0:T(8,128)S(1)}, f32[2048,256]{1,0:T(8,128)}, u32[]{:S(2)}) copy-start(f32[2048,256]{1,0:T(8,128)} %get-tuple-element.37) | copy-start | bytes 6291460
  87.5 18.9 %collective-permute-start.12 = (f32[1024,256]{1,0:T(8,128)}, f32[1024,256]{1,0:T(8,128)}, u32[]{:S(2)}, u32[]{:S(2)}) collective-permute-start(f32[1024,256]{1,0:T(8,128)} %dynamic-slice_add_fusion.1), channel_id=1, source_target_pairs={{0,2},{1,67},{2,0},{3,65},{64,66},{65,3},{66,64},{67,1},{4,6},{5,7... | collective-permute-start | bytes 3145736 | tf_op jit(solution)/shard_map/ppermute | solution.py:194
  92.5 18.2 %collective-permute-start.5 = (f32[1032,256]{1,0:T(8,128)}, f32[1032,256]{1,0:T(8,128)S(1)}, u32[]{:S(2)}, u32[]{:S(2)}) collective-permute-start(f32[1032,256]{1,0:T(8,128)} %pad_maximum_fusion), channel_id=1, source_target_pairs={{0,4},{1,13},{4,0},{5,9},{8,12},{9,5},{12,8},{13,1},{2,6},{3,15},{... | collective-permute-start | bytes 3170312 | tf_op jit(solution)/shard_map/ppermute | solution.py:194
  94.0 12.5 %copy-start.6 = (f32[2048,256]{1,0:T(8,128)S(1)}, f32[2048,256]{1,0:T(8,128)}, u32[]{:S(2)}) copy-start(f32[2048,256]{1,0:T(8,128)} %get-tuple-element.40) | copy-start | bytes 6291460
  98.7 12.0 %copy-start.5 = (f32[2048,256]{1,0:T(8,128)S(1)}, f32[2048,256]{1,0:T(8,128)}, u32[]{:S(2)}) copy-start(f32[2048,256]{1,0:T(8,128)} %get-tuple-element.37) | copy-start | bytes 6291460
  98.7 14.9 %collective-permute-start.20 = (f32[512,256]{1,0:T(8,128)S(1)}, f32[512,256]{1,0:T(8,128)S(1)}, u32[]{:S(2)}, u32[]{:S(2)}) collective-permute-start(f32[512,256]{1,0:T(8,128)S(1)} %constant_dynamic-slice_fusion.2), channel_id=1, source_target_pairs={{0,48},{1,17},{16,32},{17,1},{32,16},{33,49},{48,0},{49,33},{2,50}... | collective-permute-start | bytes 1572872 | tf_op jit(solution)/shard_map/ppermute | solution.py:194
  108.2 10.5 %collective-permute-start.13 = (f32[512,256]{1,0:T(8,128)S(1)}, f32[512,256]{1,0:T(8,128)S(1)}, u32[]{:S(2)}, u32[]{:S(2)}) collective-permute-start(f32[512,256]{1,0:T(8,128)S(1)} %constant_dynamic-slice_fusion.8), channel_id=1, source_target_pairs={{0,66},{1,3},{2,64},{3,1},{64,2},{65,67},{66,0},{67,65},{4,70},{5,... | collective-permute-start | bytes 1572872 | tf_op jit(solution)/shard_map/ppermute | solution.py:194
  111.0 13.4 %collective-permute-start.6 = (f32[520,256]{1,0:T(8,128)S(1)}, f32[520,256]{1,0:T(8,128)S(1)}, u32[]{:S(2)}, u32[]{:S(2)}) collective-permute-start(f32[520,256]{1,0:T(8,128)S(1)} %pad_maximum_fusion.1), channel_id=1, source_target_pairs={{0,12},{1,5},{4,8},{5,1},{8,4},{9,13},{12,0},{13,9},{2,14},{3,7},{... | collective-permute-start | bytes 1597448 | tf_op jit(solution)/shard_map/ppermute | solution.py:194
  113.7 11.1 %collective-permute-start.21 = (f32[256,256]{1,0:T(8,128)S(1)}, f32[256,256]{1,0:T(8,128)S(1)}, u32[]{:S(2)}, u32[]{:S(2)}) collective-permute-start(f32[256,256]{1,0:T(8,128)S(1)} %constant_dynamic-slice_fusion.1), channel_id=1, source_target_pairs={{0,4},{1,13},{4,0},{5,9},{8,12},{9,5},{12,8},{13,1},{2,6},{3,15},{... | collective-permute-start | bytes 786440 | tf_op jit(solution)/shard_map/ppermute | solution.py:194
  118.8 8.0 %collective-permute-start.14 = (f32[256,256]{1,0:T(8,128)S(1)}, f32[256,256]{1,0:T(8,128)S(1)}, u32[]{:S(2)}, u32[]{:S(2)}) collective-permute-start(f32[256,256]{1,0:T(8,128)S(1)} %constant_dynamic-slice_fusion.7), channel_id=1, source_target_pairs={{0,16},{1,49},{16,0},{17,33},{32,48},{33,17},{48,32},{49,1},{2,18}... | collective-permute-start | bytes 786440 | tf_op jit(solution)/shard_map/ppermute | solution.py:194
  124.5 7.1 %collective-permute-start.7 = (f32[264,256]{1,0:T(8,128)S(1)}, f32[264,256]{1,0:T(8,128)S(1)}, u32[]{:S(2)}, u32[]{:S(2)}) collective-permute-start(f32[264,256]{1,0:T(8,128)S(1)} %pad_maximum_fusion.2), channel_id=1, source_target_pairs={{0,2},{1,67},{2,0},{3,65},{64,66},{65,3},{66,64},{67,1},{4,6},{5,7... | collective-permute-start | bytes 811016 | tf_op jit(solution)/shard_map/ppermute | solution.py:194
  124.9 8.0 %collective-permute-start.22 = (f32[128,256]{1,0:T(8,128)S(1)}, f32[128,256]{1,0:T(8,128)S(1)}, u32[]{:S(2)}, u32[]{:S(2)}) collective-permute-start(f32[128,256]{1,0:T(8,128)S(1)} %constant_dynamic-slice_fusion), channel_id=1, source_target_pairs={{0,12},{1,5},{4,8},{5,1},{8,4},{9,13},{12,0},{13,9},{2,14},{3,7},{... | collective-permute-start | bytes 393224 | tf_op jit(solution)/shard_map/ppermute | solution.py:194
  126.8 7.6 %collective-permute-start.15 = (f32[128,256]{1,0:T(8,128)S(1)}, f32[128,256]{1,0:T(8,128)S(1)}, u32[]{:S(2)}, u32[]{:S(2)}) collective-permute-start(f32[128,256]{1,0:T(8,128)S(1)} %constant_dynamic-slice_fusion.6), channel_id=1, source_target_pairs={{0,48},{1,17},{16,32},{17,1},{32,16},{33,49},{48,0},{49,33},{2,50}... | collective-permute-start | bytes 393224 | tf_op jit(solution)/shard_map/ppermute | solution.py:194
  131.7 6.3 %collective-permute-start.8 = (f32[136,256]{1,0:T(8,128)S(1)}, f32[136,256]{1,0:T(8,128)S(1)}, u32[]{:S(2)}, u32[]{:S(2)}) collective-permute-start(f32[136,256]{1,0:T(8,128)S(1)} %pad_maximum_fusion.3), channel_id=1, source_target_pairs={{0,66},{1,3},{2,64},{3,1},{64,2},{65,67},{66,0},{67,65},{4,70},{5,... | collective-permute-start | bytes 417800 | tf_op jit(solution)/shard_map/ppermute | solution.py:194
  132.9 6.0 %collective-permute-start.23 = (f32[64,256]{1,0:T(8,128)S(1)}, f32[64,256]{1,0:T(8,128)S(1)}, u32[]{:S(2)}, u32[]{:S(2)}) collective-permute-start(f32[64,256]{1,0:T(8,128)S(1)} %constant_dynamic-slice_fusion.14), channel_id=1, source_target_pairs={{0,2},{1,67},{2,0},{3,65},{64,66},{65,3},{66,64},{67,1},{4,6},{5,7... | collective-permute-start | bytes 196616 | tf_op jit(solution)/shard_map/ppermute | solution.py:194
  134.4 5.1 %collective-permute-start.16 = (f32[64,256]{1,0:T(8,128)S(1)}, f32[64,256]{1,0:T(8,128)S(1)}, u32[]{:S(2)}, u32[]{:S(2)}) collective-permute-start(f32[64,256]{1,0:T(8,128)S(1)} %constant_dynamic-slice_fusion.5), channel_id=1, source_target_pairs={{0,4},{1,13},{4,0},{5,9},{8,12},{9,5},{12,8},{13,1},{2,6},{3,15},{... | collective-permute-start | bytes 196616 | tf_op jit(solution)/shard_map/ppermute | solution.py:194
  138.2 6.7 %collective-permute-start.9 = (f32[72,256]{1,0:T(8,128)S(1)}, f32[72,256]{1,0:T(8,128)S(1)}, u32[]{:S(2)}, u32[]{:S(2)}) collective-permute-start(f32[72,256]{1,0:T(8,128)S(1)} %pad_maximum_fusion.4), channel_id=1, source_target_pairs={{0,16},{1,49},{16,0},{17,33},{32,48},{33,17},{48,32},{49,1},{2,18}... | collective-permute-start | bytes 221192 | tf_op jit(solution)/shard_map/ppermute | solution.py:194
  139.0 5.2 %collective-permute-start.24 = (f32[32,256]{1,0:T(8,128)S(1)}, f32[32,256]{1,0:T(8,128)S(1)}, u32[]{:S(2)}, u32[]{:S(2)}) collective-permute-start(f32[32,256]{1,0:T(8,128)S(1)} %constant_dynamic-slice_fusion.3), channel_id=1, source_target_pairs={{0,66},{1,3},{2,64},{3,1},{64,2},{65,67},{66,0},{67,65},{4,70},{5,... | collective-permute-start | bytes 98312 | tf_op jit(solution)/shard_map/ppermute | solution.py:194
  139.6 5.2 %collective-permute-start.17 = (f32[32,256]{1,0:T(8,128)S(1)}, f32[32,256]{1,0:T(8,128)S(1)}, u32[]{:S(2)}, u32[]{:S(2)}) collective-permute-start(f32[32,256]{1,0:T(8,128)S(1)} %constant_dynamic-slice_fusion.4), channel_id=1, source_target_pairs={{0,12},{1,5},{4,8},{5,1},{8,4},{9,13},{12,0},{13,9},{2,14},{3,7},{... | collective-permute-start | bytes 98312 | tf_op jit(solution)/shard_map/ppermute | solution.py:194
  144.9 5.8 %collective-permute-start.10 = (f32[40,256]{1,0:T(8,128)S(1)}, f32[40,256]{1,0:T(8,128)S(1)}, u32[]{:S(2)}, u32[]{:S(2)}) collective-permute-start(f32[40,256]{1,0:T(8,128)S(1)} %pad_maximum_fusion.7), channel_id=1, source_target_pairs={{0,48},{1,17},{16,32},{17,1},{32,16},{33,49},{48,0},{49,33},{2,50}... | collective-permute-start | bytes 122888 | tf_op jit(solution)/shard_map/ppermute | solution.py:194

commit v7 on v6

--- a/solution.py
+++ b/solution.py
@@ -61,7 +61,8 @@
                 for side in (SUB * 128, SUB * 136)
             )
         even_ref[row + SUB, 0] = cells
-        even_ref[row + SUB, 1] = jnp.concatenate([right, gap, left], axis=0).T
+        if -SUB < row < 7 + SUB:
+            even_ref[row + SUB, 1] = jnp.concatenate([right, gap, left], axis=0).T
     lane = lane[:FEW_ROWS]
     beside = beside[:FEW_ROWS]
 
@@ -75,30 +76,32 @@
             for row in range(-margin, 8 + margin):
                 at = row + SUB
                 main, side = here[at, 0, feats, :], here[at, 1, feats, :]
-                main_up, side_up = pltpu.roll(main, 127, 1), pltpu.roll(side, 127, 1)
-                main_down, side_down = pltpu.roll(main, 1, 1), pltpu.roll(side, 1, 1)
                 new = (
                     centre * main
                     + east * here[at + 1, 0, feats, :]
                     + west * here[at - 1, 0, feats, :]
-                    + north * jnp.where(lane == 127, side_up, main_up)
-                    + south * jnp.where(lane == 0, side_down, main_down)
+                    + north * pltpu.roll(jnp.where(lane == 0, side, main), 127, 1)
+                    + south * pltpu.roll(jnp.where(lane == 127, side, main), 1, 1)
                 )
                 if margin == 0:
                     field_ref[feats, row * 128 : (row + 1) * 128] = new
                     x_ref[feats, row * 128 : (row + 1) * 128] = new.astype(jnp.bfloat16)
                     continue
+                outside = row < 0 or row > 7
+                if outside:
+                    new = new * inside[0 if row < 0 else 1]
+                there[at, 0, feats, :] = new
+                if not -margin < row < 7 + margin:
+                    continue
                 near = (
                     centre * side
                     + east * here[at + 1, 1, feats, :]
                     + west * here[at - 1, 1, feats, :]
-                    + north * jnp.where(lane == 127, main_up, side_up)
-                    + south * jnp.where(lane == 0, main_down, side_down)
+                    + north * pltpu.roll(jnp.where(lane == 0, main, side), 127, 1)
+                    + south * pltpu.roll(jnp.where(lane == 127, main, side), 1, 1)
                 ) * beside
-                if row < 0 or row > 7:
-                    new = new * inside[0 if row < 0 else 1]
+                if outside:
                     near = near * inside[0 if row < 0 else 1]
-                there[at, 0, feats, :] = new
                 there[at, 1, feats, :] = near
             here, there = there, here
 

time: 152 us -> 151 us (level)
  no operation moved by 1% of the time
where the time goes in v7:
time: 151 us
  starting transfers between devices  49 us (32%)
  Pallas kernels  44.3 us (29%)
  waiting for transfers between devices  40.9 us (27%)
  other arithmetic  12.3 us (8%)
  local copies, waits for them, and re-layouts  3.25 us (2%)
    ppermute x18, starting transfers between devices, ring_turn(): coming = lax.ppermute(leaving, AXES[axis], RING[turn + 1])  38.3 us
    pallas_call x1, Pallas kernels, network(): pl.pallas_call(functools.partial(network_kernel, (BATCHES / (total * feat...  31.6 us
    ppermute x18, waiting for transfers between devices, ring_turn(): coming = lax.ppermute(leaving, AXES[axis], RING[turn + 1])  20.4 us
    ppermute x4, waiting for transfers between devices, shifted(): return lax.ppermute(value, axis, pairs)  15.5 us
    ppermute x4, starting transfers between devices, shifted(): return lax.ppermute(value, axis, pairs)  9.57 us
    pallas_call x1, Pallas kernels, transported(): pl.pallas_call(transport_kernel, grid=(feats // 128,), in_specs=[pl.Block...  9.44 us
    add x3, other arithmetic, ring_turn(): leaving = sum((half_of(term, size, 1 - bit) for term in terms))  5.51 us
    ppermute x3, waiting for transfers between devices, network(): lax.ppermute(sent, CORE, PAIR)  5.08 us
  transfers between devices with their start and end apart: 25, of which 15 were waited for; matrix products, arithmetic and copies ran while one was open for 8% of the time, Pallas kernels for 0%

profile of v7, /device:TPU:0, one launch (start us, length us, event | category | flops | bytes accessed | tf_op | source)
XLA Modules:
  0.0 151.0 jit_solution(5581860214241602620)
XLA Ops:
  0.7 2.6 %edges.1 = (f32[3,432,128]{2,1,0:T(8,128)S(1)}, f32[3,432,128]{2,1,0:T(8,128)S(1)}, f32[3,64,128]{2,1,0:T(8,128)S(1)}, f32[3,64,128]{2,1,0:T(8,128)S(1)}) custom-call(f32[3072,128]{1,0:T(8,128)} %bitcast.9), custom_call_target="tpu_custom_call" | custom-call | flops 1048576 | bytes 3145728 | tf_op jit(solution)/shard_map/edges/pallas_call | solution.py:120
  3.3 1.3 collective-permute-start.1
  4.6 3.0 %collective-permute-start = (f32[3,64,128]{2,1,0:T(8,128)S(1)}, f32[3,64,128]{2,1,0:T(8,128)S(1)}, u32[]{:S(2)}, u32[]{:S(2)}) collective-permute-start(f32[3,64,128]{2,1,0:T(8,128)S(1)} %get-tuple-element.24), channel_id=1, source_target_pairs={{0,1},{1,2},{2,3},{3,4},{4,5},{5,6},{6,7},{7,8},{8,9},{9,10},{10,1... | collective-permute-start | bytes 294920 | tf_op jit(solution)/shard_map/ppermute | solution.py:112
  7.7 0.9 collective-permute-done.left_ref
  8.6 3.9 %collective-permute-start.2 = (f32[3,432,128]{2,1,0:T(8,128)S(1)}, f32[3,432,128]{2,1,0:T(8,128)S(1)}, u32[]{:S(2)}, u32[]{:S(2)}) collective-permute-start(f32[3,432,128]{2,1,0:T(8,128)S(1)} %maximum_dynamic-update-slice_fusion), channel_id=1, source_target_pairs={{0,16},{16,32},{32,48},{48,64},{64,80},{80,96},{96,112},{1,17},{17... | collective-permute-start | bytes 1990664 | tf_op jit(solution)/shard_map/ppermute | solution.py:112
  12.6 1.3 collective-permute-start.3
  13.9 1.1 copy.16
  15.0 0.7 ranks.1
  15.7 0.6 copy-done.2
  16.3 0.6 copy-done.3
  16.9 10.0 %collective-permute-done.2.above_ref = f32[3,432,128]{2,1,0:T(8,128)S(1)} collective-permute-done((f32[3,432,128]{2,1,0:T(8,128)S(1)}, f32[3,432,128]{2,1,0:T(8,128)S(1)}, u32[]{:S(2)}, u32[]{:S(2)}) %collective-permute-start.2) | collective-permute-done | bytes 663584 | tf_op jit(solution)/shard_map/ppermute | solution.py:112
  26.9 4.6 %collective-permute-done.3.below_ref = f32[3,432,128]{2,1,0:T(8,128)S(1)} collective-permute-done((f32[3,432,128]{2,1,0:T(8,128)S(1)}, f32[3,432,128]{2,1,0:T(8,128)S(1)}, u32[]{:S(2)}, u32[]{:S(2)}) %collective-permute-start.3) | collective-permute-done | bytes 663584 | tf_op jit(solution)/shard_map/ppermute | solution.py:112
  31.5 0.1 broadcast_in_dim.10.coef_0
  31.6 0.1 broadcast_in_dim.11.coef_1
  31.7 0.1 broadcast_in_dim.12.coef_2
  31.8 0.1 broadcast_in_dim.13.coef_3
  31.9 0.1 broadcast_in_dim.14.coef_4
  32.1 9.4 %transport.1 = (f32[384,1024]{1,0:T(8,128)}, bf16[384,1024]{1,0:T(8,128)(2,1)}) custom-call(f32[3072,128]{1,0:T(8,128)} %bitcast.10, f32[3,432,128]{2,1,0:T(8,128)S(1)} %collective-permute-done.2.above_ref, f32[3,432,128]{2,1,0:T(8,128)S(1)} %collective-permute-done.3.below_ref, f32[3,64,128]{2,1,0:T(8,128)S(1)} %collective-permute-done.left_ref, ...), custom_call_target="tpu_custom_call" | custom-call | flops 16777216 | bytes 6291456 | tf_op jit(solution)/shard_map/transport/pallas_call | solution.py:150
  41.5 31.6 %network.1 = (f32[3072,128]{1,0:T(8,128)}, f32[2048,256]{1,0:T(8,128)}, f32[2048,256]{1,0:T(8,128)}, f32[2048,256]{1,0:T(8,128)}, f32[2056,256]{1,0:T(8,128)}, /...) custom-call(s32[1]{0:T(128)} %get-tuple-element.28.scalar_ref, s32[384]{0:T(512)} %constant.119.clone.table_ref, ...), custom_call_target="tpu_custom_call" | custom-call | flops 16106127360 | bytes 20971520 | tf_op jit(solution)/shard_map/network/pallas_call | solution.py:458
  73.1 0.7 collective-permute-start.18
  73.8 0.1 collective-permute-start.11
  73.9 0.4 collective-permute-start.4
  74.3 3.6 %collective-permute-done.18 = f32[2048,256]{1,0:T(8,128)} collective-permute-done((f32[2048,256]{1,0:T(8,128)}, f32[2048,256]{1,0:T(8,128)}, u32[]{:S(2)}, u32[]{:S(2)}) %collective-permute-start.18) | collective-permute-done | bytes 2097184 | tf_op jit(solution)/shard_map/ppermute | solution.py:493
  77.9 2.7 %dynamic-slice_add_fusion = f32[1024,256]{1,0:T(8,128)} fusion(f32[2048,256]{1,0:T(8,128)} %collective-permute-done.18, s32[]{:T(128)S(6)} %select_n.231, f32[2048,256]{1,0:T(8,128)} %get-tuple-element.42), kind=kLoop, calls=%fused_computation.2 | loop fusion | flops 262144 | bytes 3145732 | tf_op jit(solution)/shard_map/add | solution.py:194
  80.6 1.9 %collective-permute-start.19 = (f32[1024,256]{1,0:T(8,128)}, f32[1024,256]{1,0:T(8,128)}, u32[]{:S(2)}, u32[]{:S(2)}) collective-permute-start(f32[1024,256]{1,0:T(8,128)} %dynamic-slice_add_fusion), channel_id=1, source_target_pairs={{0,16},{1,49},{16,0},{17,33},{32,48},{33,17},{48,32},{49,1},{2,18}... | collective-permute-start | bytes 3145736 | tf_op jit(solution)/shard_map/ppermute | solution.py:197
  82.5 1.5 collective-permute-done.11
  83.9 2.7 %dynamic-slice_add_fusion.1 = f32[1024,256]{1,0:T(8,128)} fusion(f32[2048,256]{1,0:T(8,128)} %collective-permute-done.11, s32[]{:T(128)S(6)} %select_n.219, f32[2048,256]{1,0:T(8,128)} %get-tuple-element.40), kind=kLoop, calls=%fused_computation.4 | loop fusion | flops 262144 | bytes 3145732 | tf_op jit(solution)/shard_map/add | solution.py:194
  86.6 3.7 %collective-permute-start.12 = (f32[1024,256]{1,0:T(8,128)}, f32[1024,256]{1,0:T(8,128)}, u32[]{:S(2)}, u32[]{:S(2)}) collective-permute-start(f32[1024,256]{1,0:T(8,128)} %dynamic-slice_add_fusion.1), channel_id=1, source_target_pairs={{0,2},{1,67},{2,0},{3,65},{64,66},{65,3},{66,64},{67,1},{4,6},{5,7... | collective-permute-start | bytes 3145736 | tf_op jit(solution)/shard_map/ppermute | solution.py:197
  90.3 0.1 dynamic-slice_add_fusion.2
  90.5 1.1 pad_maximum_fusion
  91.6 1.5 collective-permute-start.5
  93.1 2.6 %collective-permute-done.19 = f32[1024,256]{1,0:T(8,128)} collective-permute-done((f32[1024,256]{1,0:T(8,128)}, f32[1024,256]{1,0:T(8,128)}, u32[]{:S(2)}, u32[]{:S(2)}) %collective-permute-start.19) | collective-permute-done | bytes 1048608 | tf_op jit(solution)/shard_map/ppermute | solution.py:197
  95.7 2.1 %add_add_fusion = f32[1024,256]{1,0:T(8,128)S(1)} fusion(f32[1024,256]{1,0:T(8,128)} %collective-permute-done.19, f32[2048,256]{1,0:T(8,128)} %collective-permute-done.18, s32[]{:T(128)S(6)} %select_n.230, f32[2048,256]{1,0:T(8,128)} %get-tuple-element.42), kind=kLoop, calls=%fused_computation.3 | loop fusion | flops 524288 | bytes 4194308 | tf_op jit(solution)/shard_map/add | solution.py:199
  97.8 7.7 %collective-permute-start.20 = (f32[512,256]{1,0:T(8,128)S(1)}, f32[512,256]{1,0:T(8,128)S(1)}, u32[]{:S(2)}, u32[]{:S(2)}) collective-permute-start(f32[512,256]{1,0:T(8,128)S(1)} %constant_dynamic-slice_fusion.2), channel_id=1, source_target_pairs={{0,48},{1,17},{16,32},{17,1},{32,16},{33,49},{48,0},{49,33},{2,50}... | collective-permute-start | bytes 1572872 | tf_op jit(solution)/shard_map/ppermute | solution.py:197
  105.5 1.7 %add_add_fusion.1 = f32[1024,256]{1,0:T(8,128)S(1)} fusion(f32[1024,256]{1,0:T(8,128)} %collective-permute-done.12, f32[2048,256]{1,0:T(8,128)} %collective-permute-done.11, s32[]{:T(128)S(6)} %select_n.218, f32[2048,256]{1,0:T(8,128)S(1)} %copy-done.6), kind=kLoop, calls=%fused_computation.5 | loop fusion | flops 524288 | bytes 4194308 | tf_op jit(solution)/shard_map/add | solution.py:199
  107.3 2.5 %collective-permute-start.13 = (f32[512,256]{1,0:T(8,128)S(1)}, f32[512,256]{1,0:T(8,128)S(1)}, u32[]{:S(2)}, u32[]{:S(2)}) collective-permute-start(f32[512,256]{1,0:T(8,128)S(1)} %constant_dynamic-slice_fusion.8), channel_id=1, source_target_pairs={{0,66},{1,3},{2,64},{3,1},{64,2},{65,67},{66,0},{67,65},{4,70},{5,... | collective-permute-start | bytes 1572872 | tf_op jit(solution)/shard_map/ppermute | solution.py:197
  109.8 0.2 slice_add_fusion
  110.1 1.4 collective-permute-start.6
  111.6 1.1 collective-permute-done.20
  112.7 0.1 dynamic-slice_add_fusion.3
  112.8 2.5 %collective-permute-start.21 = (f32[256,256]{1,0:T(8,128)S(1)}, f32[256,256]{1,0:T(8,128)S(1)}, u32[]{:S(2)}, u32[]{:S(2)}) collective-permute-start(f32[256,256]{1,0:T(8,128)S(1)} %constant_dynamic-slice_fusion.1), channel_id=1, source_target_pairs={{0,4},{1,13},{4,0},{5,9},{8,12},{9,5},{12,8},{13,1},{2,6},{3,15},{... | collective-permute-start | bytes 786440 | tf_op jit(solution)/shard_map/ppermute | solution.py:197
  115.3 2.5 %collective-permute-done.13 = f32[512,256]{1,0:T(8,128)S(1)} collective-permute-done((f32[512,256]{1,0:T(8,128)S(1)}, f32[512,256]{1,0:T(8,128)S(1)}, u32[]{:S(2)}, u32[]{:S(2)}) %collective-permute-start.13) | collective-permute-done | bytes 524320 | tf_op jit(solution)/shard_map/ppermute | solution.py:197
  117.8 0.1 dynamic-slice_add_fusion.4
  117.9 0.3 collective-permute-start.14
  118.2 5.3 %collective-permute-done.6 = f32[520,256]{1,0:T(8,128)S(1)} collective-permute-done((f32[520,256]{1,0:T(8,128)S(1)}, f32[520,256]{1,0:T(8,128)S(1)}, u32[]{:S(2)}, u32[]{:S(2)}) %collective-permute-start.6) | collective-permute-done | bytes 532512 | tf_op jit(solution)/shard_map/ppermute | solution.py:197
  123.5 0.1 slice_add_fusion.1
  123.6 0.3 collective-permute-start.7
  124.0 1.9 %collective-permute-start.22 = (f32[128,256]{1,0:T(8,128)S(1)}, f32[128,256]{1,0:T(8,128)S(1)}, u32[]{:S(2)}, u32[]{:S(2)}) collective-permute-start(f32[128,256]{1,0:T(8,128)S(1)} %constant_dynamic-slice_fusion), channel_id=1, source_target_pairs={{0,12},{1,5},{4,8},{5,1},{8,4},{9,13},{12,0},{13,9},{2,14},{3,7},{... | collective-permute-start | bytes 393224 | tf_op jit(solution)/shard_map/ppermute | solution.py:197
  125.9 4.6 %collective-permute-start.15 = (f32[128,256]{1,0:T(8,128)S(1)}, f32[128,256]{1,0:T(8,128)S(1)}, u32[]{:S(2)}, u32[]{:S(2)}) collective-permute-start(f32[128,256]{1,0:T(8,128)S(1)} %constant_dynamic-slice_fusion.6), channel_id=1, source_target_pairs={{0,48},{1,17},{16,32},{17,1},{32,16},{33,49},{48,0},{49,33},{2,50}... | collective-permute-start | bytes 393224 | tf_op jit(solution)/shard_map/ppermute | solution.py:197
  130.6 0.2 collective-permute-done.7
  130.8 1.2 collective-permute-start.8
  132.0 0.6 collective-permute-start.23
  132.7 0.9 collective-permute-done.15
  133.5 0.5 collective-permute-start.16
  134.1 3.1 %collective-permute-done.8 = f32[136,256]{1,0:T(8,128)S(1)} collective-permute-done((f32[136,256]{1,0:T(8,128)S(1)}, f32[136,256]{1,0:T(8,128)S(1)}, u32[]{:S(2)}, u32[]{:S(2)}) %collective-permute-start.8) | collective-permute-done | bytes 139296 | tf_op jit(solution)/shard_map/ppermute | solution.py:197
  137.3 0.8 collective-permute-start.9
  138.1 0.6 collective-permute-start.24
  138.7 2.5 %collective-permute-start.17 = (f32[32,256]{1,0:T(8,128)S(1)}, f32[32,256]{1,0:T(8,128)S(1)}, u32[]{:S(2)}, u32[]{:S(2)}) collective-permute-start(f32[32,256]{1,0:T(8,128)S(1)} %constant_dynamic-slice_fusion.4), channel_id=1, source_target_pairs={{0,12},{1,5},{4,8},{5,1},{8,4},{9,13},{12,0},{13,9},{2,14},{3,7},{... | collective-permute-start | bytes 98312 | tf_op jit(solution)/shard_map/ppermute | solution.py:197
  141.2 2.1 %collective-permute-done.24 = f32[32,256]{1,0:T(8,128)S(1)} collective-permute-done((f32[32,256]{1,0:T(8,128)S(1)}, f32[32,256]{1,0:T(8,128)S(1)}, u32[]{:S(2)}, u32[]{:S(2)}) %collective-permute-start.24) | collective-permute-done | bytes 32800 | tf_op jit(solution)/shard_map/ppermute | solution.py:197
  143.3 0.6 collective-permute-done.17
  144.0 3.8 %collective-permute-start.10 = (f32[40,256]{1,0:T(8,128)S(1)}, f32[40,256]{1,0:T(8,128)S(1)}, u32[]{:S(2)}, u32[]{:S(2)}) collective-permute-start(f32[40,256]{1,0:T(8,128)S(1)} %pad_maximum_fusion.7), channel_id=1, source_target_pairs={{0,48},{1,17},{16,32},{17,1},{32,16},{33,49},{48,0},{49,33},{2,50}... | collective-permute-start | bytes 122888 | tf_op jit(solution)/shard_map/ppermute | solution.py:197
  147.8 2.0 %collective-permute-done.10 = f32[40,256]{1,0:T(8,128)S(1)} collective-permute-done((f32[40,256]{1,0:T(8,128)S(1)}, f32[40,256]{1,0:T(8,128)S(1)}, u32[]{:S(2)}, u32[]{:S(2)}) %collective-permute-start.10) | collective-permute-done | bytes 40992 | tf_op jit(solution)/shard_map/ppermute | solution.py:197
  149.8 0.5 fusion
  150.3 0.6 pad_maximum_fusion.5
  (79 shorter events, 0.8 us)
Async XLA Ops:
  0.6 13.2 %copy-start.9 = (f32[384]{0:T(512)S(1)}, f32[384]{0:T(512)}, u32[]{:S(2)}) copy-start(f32[384]{0:T(512)} %param.14) | copy-start | bytes 4612
  0.6 13.2 %copy-start.10 = (f32[384]{0:T(512)S(1)}, f32[384]{0:T(512)}, u32[]{:S(2)}) copy-start(f32[384]{0:T(512)} %param.16) | copy-start | bytes 4612
  0.7 13.2 %copy-start.11 = (f32[384]{0:T(512)S(1)}, f32[384]{0:T(512)}, u32[]{:S(2)}) copy-start(f32[384]{0:T(512)} %param.15) | copy-start | bytes 4612
  0.7 13.2 %copy-start.7 = (bf16[384,8,128]{2,1,0:T(8,128)(2,1)S(1)}, bf16[384,8,128]{2,1,0:T(8,128)(2,1)}, u32[]{:S(2)}) copy-start(bf16[384,8,128]{2,1,0:T(8,128)(2,1)} %param.11) | copy-start | bytes 2359300
  0.7 14.3 %copy-start = (s32[8,128]{1,0:T(8,128)S(1)}, s32[8,128]{1,0:T(8,128)}, u32[]{:S(2)}) copy-start(s32[8,128]{1,0:T(8,128)} %mask_ref) | copy-start | bytes 12292
  0.7 14.3 %copy-start.1 = (s32[8,128]{1,0:T(8,128)S(1)}, s32[8,128]{1,0:T(8,128)}, u32[]{:S(2)}) copy-start(s32[8,128]{1,0:T(8,128)} %batch_ref) | copy-start | bytes 12292
  3.3 4.3 %collective-permute-start.1 = (f32[3,64,128]{2,1,0:T(8,128)S(1)}, f32[3,64,128]{2,1,0:T(8,128)S(1)}, u32[]{:S(2)}, u32[]{:S(2)}) collective-permute-start(f32[3,64,128]{2,1,0:T(8,128)S(1)} %get-tuple-element.25), channel_id=1, source_target_pairs={{1,0},{2,1},{3,2},{4,3},{5,4},{6,5},{7,6},{8,7},{9,8},{10,9},{11,1... | collective-permute-start | bytes 294920 | tf_op jit(solution)/shard_map/ppermute | solution.py:112
  4.6 4.0 %collective-permute-start = (f32[3,64,128]{2,1,0:T(8,128)S(1)}, f32[3,64,128]{2,1,0:T(8,128)S(1)}, u32[]{:S(2)}, u32[]{:S(2)}) collective-permute-start(f32[3,64,128]{2,1,0:T(8,128)S(1)} %get-tuple-element.24), channel_id=1, source_target_pairs={{0,1},{1,2},{2,3},{3,4},{4,5},{5,6},{6,7},{7,8},{8,9},{9,10},{10,1... | collective-permute-start | bytes 294920 | tf_op jit(solution)/shard_map/ppermute | solution.py:112
  8.6 18.3 %collective-permute-start.2 = (f32[3,432,128]{2,1,0:T(8,128)S(1)}, f32[3,432,128]{2,1,0:T(8,128)S(1)}, u32[]{:S(2)}, u32[]{:S(2)}) collective-permute-start(f32[3,432,128]{2,1,0:T(8,128)S(1)} %maximum_dynamic-update-slice_fusion), channel_id=1, source_target_pairs={{0,16},{16,32},{32,48},{48,64},{64,80},{80,96},{96,112},{1,17},{17... | collective-permute-start | bytes 1990664 | tf_op jit(solution)/shard_map/ppermute | solution.py:112
  12.6 18.9 %collective-permute-start.3 = (f32[3,432,128]{2,1,0:T(8,128)S(1)}, f32[3,432,128]{2,1,0:T(8,128)S(1)}, u32[]{:S(2)}, u32[]{:S(2)}) collective-permute-start(f32[3,432,128]{2,1,0:T(8,128)S(1)} %maximum_dynamic-update-slice_fusion.1), channel_id=1, source_target_pairs={{16,0},{32,16},{48,32},{64,48},{80,64},{96,80},{112,96},{17,1},{33... | collective-permute-start | bytes 1990664 | tf_op jit(solution)/shard_map/ppermute | solution.py:112
  15.7 0.6 copy-start.2
  16.3 0.6 copy-start.3
  73.1 4.8 %collective-permute-start.18 = (f32[2048,256]{1,0:T(8,128)}, f32[2048,256]{1,0:T(8,128)}, u32[]{:S(2)}, u32[]{:S(2)}) collective-permute-start(f32[2048,256]{1,0:T(8,128)} %get-tuple-element.43), channel_id=1, source_target_pairs={{0,1},{1,0},{2,3},{3,2},{4,5},{5,4},{6,7},{7,6},{8,9},{9,8},{10,11... | collective-permute-start | bytes 6291464 | tf_op jit(solution)/shard_map/ppermute | solution.py:493
  73.8 10.1 %collective-permute-start.11 = (f32[2048,256]{1,0:T(8,128)}, f32[2048,256]{1,0:T(8,128)}, u32[]{:S(2)}, u32[]{:S(2)}) collective-permute-start(f32[2048,256]{1,0:T(8,128)} %get-tuple-element.41), channel_id=1, source_target_pairs={{0,1},{1,0},{2,3},{3,2},{4,5},{5,4},{6,7},{7,6},{8,9},{9,8},{10,11... | collective-permute-start | bytes 6291464 | tf_op jit(solution)/shard_map/ppermute | solution.py:493
  73.9 16.4 %collective-permute-start.4 = (f32[2056,256]{1,0:T(8,128)}, f32[2056,256]{1,0:T(8,128)S(1)}, u32[]{:S(2)}, u32[]{:S(2)}) collective-permute-start(f32[2056,256]{1,0:T(8,128)} %get-tuple-element.38), channel_id=1, source_target_pairs={{0,1},{1,0},{2,3},{3,2},{4,5},{5,4},{6,7},{7,6},{8,9},{9,8},{10,11... | collective-permute-start | bytes 6316040 | tf_op jit(solution)/shard_map/ppermute | solution.py:493
  80.6 9.8 %copy-start.8 = (f32[8,256]{1,0:T(8,128)S(1)}, f32[8,256]{1,0:T(8,128)}, u32[]{:S(2)}) copy-start(f32[8,256]{1,0:T(8,128)} %get-tuple-element.39) | copy-start | bytes 24580
  80.6 15.1 %collective-permute-start.19 = (f32[1024,256]{1,0:T(8,128)}, f32[1024,256]{1,0:T(8,128)}, u32[]{:S(2)}, u32[]{:S(2)}) collective-permute-start(f32[1024,256]{1,0:T(8,128)} %dynamic-slice_add_fusion), channel_id=1, source_target_pairs={{0,16},{1,49},{16,0},{17,33},{32,48},{33,17},{48,32},{49,1},{2,18}... | collective-permute-start | bytes 3145736 | tf_op jit(solution)/shard_map/ppermute | solution.py:197
  82.5 7.9 %copy-start.4 = (f32[2048,256]{1,0:T(8,128)S(1)}, f32[2048,256]{1,0:T(8,128)}, u32[]{:S(2)}) copy-start(f32[2048,256]{1,0:T(8,128)} %get-tuple-element.37) | copy-start | bytes 6291460
  86.6 18.9 %collective-permute-start.12 = (f32[1024,256]{1,0:T(8,128)}, f32[1024,256]{1,0:T(8,128)}, u32[]{:S(2)}, u32[]{:S(2)}) collective-permute-start(f32[1024,256]{1,0:T(8,128)} %dynamic-slice_add_fusion.1), channel_id=1, source_target_pairs={{0,2},{1,67},{2,0},{3,65},{64,66},{65,3},{66,64},{67,1},{4,6},{5,7... | collective-permute-start | bytes 3145736 | tf_op jit(solution)/shard_map/ppermute | solution.py:197
  91.6 18.2 %collective-permute-start.5 = (f32[1032,256]{1,0:T(8,128)}, f32[1032,256]{1,0:T(8,128)S(1)}, u32[]{:S(2)}, u32[]{:S(2)}) collective-permute-start(f32[1032,256]{1,0:T(8,128)} %pad_maximum_fusion), channel_id=1, source_target_pairs={{0,4},{1,13},{4,0},{5,9},{8,12},{9,5},{12,8},{13,1},{2,6},{3,15},{... | collective-permute-start | bytes 3170312 | tf_op jit(solution)/shard_map/ppermute | solution.py:197
  93.1 12.5 %copy-start.6 = (f32[2048,256]{1,0:T(8,128)S(1)}, f32[2048,256]{1,0:T(8,128)}, u32[]{:S(2)}) copy-start(f32[2048,256]{1,0:T(8,128)} %get-tuple-element.40) | copy-start | bytes 6291460
  97.8 12.0 %copy-start.5 = (f32[2048,256]{1,0:T(8,128)S(1)}, f32[2048,256]{1,0:T(8,128)}, u32[]{:S(2)}) copy-start(f32[2048,256]{1,0:T(8,128)} %get-tuple-element.37) | copy-start | bytes 6291460
  97.8 14.9 %collective-permute-start.20 = (f32[512,256]{1,0:T(8,128)S(1)}, f32[512,256]{1,0:T(8,128)S(1)}, u32[]{:S(2)}, u32[]{:S(2)}) collective-permute-start(f32[512,256]{1,0:T(8,128)S(1)} %constant_dynamic-slice_fusion.2), channel_id=1, source_target_pairs={{0,48},{1,17},{16,32},{17,1},{32,16},{33,49},{48,0},{49,33},{2,50}... | collective-permute-start | bytes 1572872 | tf_op jit(solution)/shard_map/ppermute | solution.py:197
  107.3 10.5 %collective-permute-start.13 = (f32[512,256]{1,0:T(8,128)S(1)}, f32[512,256]{1,0:T(8,128)S(1)}, u32[]{:S(2)}, u32[]{:S(2)}) collective-permute-start(f32[512,256]{1,0:T(8,128)S(1)} %constant_dynamic-slice_fusion.8), channel_id=1, source_target_pairs={{0,66},{1,3},{2,64},{3,1},{64,2},{65,67},{66,0},{67,65},{4,70},{5,... | collective-permute-start | bytes 1572872 | tf_op jit(solution)/shard_map/ppermute | solution.py:197
  110.1 13.4 %collective-permute-start.6 = (f32[520,256]{1,0:T(8,128)S(1)}, f32[520,256]{1,0:T(8,128)S(1)}, u32[]{:S(2)}, u32[]{:S(2)}) collective-permute-start(f32[520,256]{1,0:T(8,128)S(1)} %pad_maximum_fusion.1), channel_id=1, source_target_pairs={{0,12},{1,5},{4,8},{5,1},{8,4},{9,13},{12,0},{13,9},{2,14},{3,7},{... | collective-permute-start | bytes 1597448 | tf_op jit(solution)/shard_map/ppermute | solution.py:197
  112.8 11.1 %collective-permute-start.21 = (f32[256,256]{1,0:T(8,128)S(1)}, f32[256,256]{1,0:T(8,128)S(1)}, u32[]{:S(2)}, u32[]{:S(2)}) collective-permute-start(f32[256,256]{1,0:T(8,128)S(1)} %constant_dynamic-slice_fusion.1), channel_id=1, source_target_pairs={{0,4},{1,13},{4,0},{5,9},{8,12},{9,5},{12,8},{13,1},{2,6},{3,15},{... | collective-permute-start | bytes 786440 | tf_op jit(solution)/shard_map/ppermute | solution.py:197
  117.9 8.0 %collective-permute-start.14 = (f32[256,256]{1,0:T(8,128)S(1)}, f32[256,256]{1,0:T(8,128)S(1)}, u32[]{:S(2)}, u32[]{:S(2)}) collective-permute-start(f32[256,256]{1,0:T(8,128)S(1)} %constant_dynamic-slice_fusion.7), channel_id=1, source_target_pairs={{0,16},{1,49},{16,0},{17,33},{32,48},{33,17},{48,32},{49,1},{2,18}... | collective-permute-start | bytes 786440 | tf_op jit(solution)/shard_map/ppermute | solution.py:197
  123.6 7.1 %collective-permute-start.7 = (f32[264,256]{1,0:T(8,128)S(1)}, f32[264,256]{1,0:T(8,128)S(1)}, u32[]{:S(2)}, u32[]{:S(2)}) collective-permute-start(f32[264,256]{1,0:T(8,128)S(1)} %pad_maximum_fusion.2), channel_id=1, source_target_pairs={{0,2},{1,67},{2,0},{3,65},{64,66},{65,3},{66,64},{67,1},{4,6},{5,7... | collective-permute-start | bytes 811016 | tf_op jit(solution)/shard_map/ppermute | solution.py:197
  124.0 8.0 %collective-permute-start.22 = (f32[128,256]{1,0:T(8,128)S(1)}, f32[128,256]{1,0:T(8,128)S(1)}, u32[]{:S(2)}, u32[]{:S(2)}) collective-permute-start(f32[128,256]{1,0:T(8,128)S(1)} %constant_dynamic-slice_fusion), channel_id=1, source_target_pairs={{0,12},{1,5},{4,8},{5,1},{8,4},{9,13},{12,0},{13,9},{2,14},{3,7},{... | collective-permute-start | bytes 393224 | tf_op jit(solution)/shard_map/ppermute | solution.py:197
  125.9 7.6 %collective-permute-start.15 = (f32[128,256]{1,0:T(8,128)S(1)}, f32[128,256]{1,0:T(8,128)S(1)}, u32[]{:S(2)}, u32[]{:S(2)}) collective-permute-start(f32[128,256]{1,0:T(8,128)S(1)} %constant_dynamic-slice_fusion.6), channel_id=1, source_target_pairs={{0,48},{1,17},{16,32},{17,1},{32,16},{33,49},{48,0},{49,33},{2,50}... | collective-permute-start | bytes 393224 | tf_op jit(solution)/shard_map/ppermute | solution.py:197
  130.8 6.3 %collective-permute-start.8 = (f32[136,256]{1,0:T(8,128)S(1)}, f32[136,256]{1,0:T(8,128)S(1)}, u32[]{:S(2)}, u32[]{:S(2)}) collective-permute-start(f32[136,256]{1,0:T(8,128)S(1)} %pad_maximum_fusion.3), channel_id=1, source_target_pairs={{0,66},{1,3},{2,64},{3,1},{64,2},{65,67},{66,0},{67,65},{4,70},{5,... | collective-permute-start | bytes 417800 | tf_op jit(solution)/shard_map/ppermute | solution.py:197
  132.0 6.0 %collective-permute-start.23 = (f32[64,256]{1,0:T(8,128)S(1)}, f32[64,256]{1,0:T(8,128)S(1)}, u32[]{:S(2)}, u32[]{:S(2)}) collective-permute-start(f32[64,256]{1,0:T(8,128)S(1)} %constant_dynamic-slice_fusion.14), channel_id=1, source_target_pairs={{0,2},{1,67},{2,0},{3,65},{64,66},{65,3},{66,64},{67,1},{4,6},{5,7... | collective-permute-start | bytes 196616 | tf_op jit(solution)/shard_map/ppermute | solution.py:197
  133.5 5.1 %collective-permute-start.16 = (f32[64,256]{1,0:T(8,128)S(1)}, f32[64,256]{1,0:T(8,128)S(1)}, u32[]{:S(2)}, u32[]{:S(2)}) collective-permute-start(f32[64,256]{1,0:T(8,128)S(1)} %constant_dynamic-slice_fusion.5), channel_id=1, source_target_pairs={{0,4},{1,13},{4,0},{5,9},{8,12},{9,5},{12,8},{13,1},{2,6},{3,15},{... | collective-permute-start | bytes 196616 | tf_op jit(solution)/shard_map/ppermute | solution.py:197
  137.3 6.7 %collective-permute-start.9 = (f32[72,256]{1,0:T(8,128)S(1)}, f32[72,256]{1,0:T(8,128)S(1)}, u32[]{:S(2)}, u32[]{:S(2)}) collective-permute-start(f32[72,256]{1,0:T(8,128)S(1)} %pad_maximum_fusion.4), channel_id=1, source_target_pairs={{0,16},{1,49},{16,0},{17,33},{32,48},{33,17},{48,32},{49,1},{2,18}... | collective-permute-start | bytes 221192 | tf_op jit(solution)/shard_map/ppermute | solution.py:197
  138.1 5.2 %collective-permute-start.24 = (f32[32,256]{1,0:T(8,128)S(1)}, f32[32,256]{1,0:T(8,128)S(1)}, u32[]{:S(2)}, u32[]{:S(2)}) collective-permute-start(f32[32,256]{1,0:T(8,128)S(1)} %constant_dynamic-slice_fusion.3), channel_id=1, source_target_pairs={{0,66},{1,3},{2,64},{3,1},{64,2},{65,67},{66,0},{67,65},{4,70},{5,... | collective-permute-start | bytes 98312 | tf_op jit(solution)/shard_map/ppermute | solution.py:197
  138.7 5.2 %collective-permute-start.17 = (f32[32,256]{1,0:T(8,128)S(1)}, f32[32,256]{1,0:T(8,128)S(1)}, u32[]{:S(2)}, u32[]{:S(2)}) collective-permute-start(f32[32,256]{1,0:T(8,128)S(1)} %constant_dynamic-slice_fusion.4), channel_id=1, source_target_pairs={{0,12},{1,5},{4,8},{5,1},{8,4},{9,13},{12,0},{13,9},{2,14},{3,7},{... | collective-permute-start | bytes 98312 | tf_op jit(solution)/shard_map/ppermute | solution.py:197
  144.0 5.8 %collective-permute-start.10 = (f32[40,256]{1,0:T(8,128)S(1)}, f32[40,256]{1,0:T(8,128)S(1)}, u32[]{:S(2)}, u32[]{:S(2)}) collective-permute-start(f32[40,256]{1,0:T(8,128)S(1)} %pad_maximum_fusion.7), channel_id=1, source_target_pairs={{0,48},{1,17},{16,32},{17,1},{32,16},{33,49},{48,0},{49,33},{2,50}... | collective-permute-start | bytes 122888 | tf_op jit(solution)/shard_map/ppermute | solution.py:197

commit v8 on v7

--- a/solution.py
+++ b/solution.py
@@ -12,7 +12,7 @@
 SUB = 3
 BATCHES = 64
 FEW = 640
-FEW_ROWS = 32
+FEW_ROWS = 64
 BX = ("bx_0", "bx_1")
 BY = ("by_0", "by_1", "by_2")
 CORE = "by_2"

time: 151 us -> 151 us (level)
  no operation moved by 1% of the time
where the time goes in v8:
time: 151 us; the launch traced here: 150 us
  starting transfers between devices  49 us (32%)
  Pallas kernels  43.8 us (29%)
  waiting for transfers between devices  41 us (27%)
  other arithmetic  12.3 us (8%)
  local copies, waits for them, and re-layouts  3.25 us (2%)
    ppermute x18, starting transfers between devices, ring_turn(): coming = lax.ppermute(leaving, AXES[axis], RING[turn + 1])  38.2 us
    pallas_call x1, Pallas kernels, network(): pl.pallas_call(functools.partial(network_kernel, (BATCHES / (total * feat...  31.6 us
    ppermute x18, waiting for transfers between devices, ring_turn(): coming = lax.ppermute(leaving, AXES[axis], RING[turn + 1])  20.4 us
    ppermute x4, waiting for transfers between devices, shifted(): return lax.ppermute(value, axis, pairs)  15.5 us
    ppermute x4, starting transfers between devices, shifted(): return lax.ppermute(value, axis, pairs)  9.57 us
    pallas_call x1, Pallas kernels, transported(): pl.pallas_call(transport_kernel, grid=(feats // 128,), in_specs=[pl.Block...  8.92 us
    add x3, other arithmetic, ring_turn(): leaving = sum((half_of(term, size, 1 - bit) for term in terms))  5.51 us
    ppermute x3, waiting for transfers between devices, network(): lax.ppermute(sent, CORE, PAIR)  5.08 us
  transfers between devices with their start and end apart: 25, of which 15 were waited for; matrix products, arithmetic and copies ran while one was open for 8% of the time, Pallas kernels for 0%

profile of v8, /device:TPU:0, one launch (start us, length us, event | category | flops | bytes accessed | tf_op | source)
XLA Modules:
  0.0 150.5 jit_solution(7809713019944129367)
XLA Ops:
  0.7 2.6 %edges.1 = (f32[3,432,128]{2,1,0:T(8,128)S(1)}, f32[3,432,128]{2,1,0:T(8,128)S(1)}, f32[3,64,128]{2,1,0:T(8,128)S(1)}, f32[3,64,128]{2,1,0:T(8,128)S(1)}) custom-call(f32[3072,128]{1,0:T(8,128)} %bitcast.9), custom_call_target="tpu_custom_call" | custom-call | flops 1048576 | bytes 3145728 | tf_op jit(solution)/shard_map/edges/pallas_call | solution.py:120
  3.3 1.3 collective-permute-start.1
  4.6 3.0 %collective-permute-start = (f32[3,64,128]{2,1,0:T(8,128)S(1)}, f32[3,64,128]{2,1,0:T(8,128)S(1)}, u32[]{:S(2)}, u32[]{:S(2)}) collective-permute-start(f32[3,64,128]{2,1,0:T(8,128)S(1)} %get-tuple-element.24), channel_id=1, source_target_pairs={{0,1},{1,2},{2,3},{3,4},{4,5},{5,6},{6,7},{7,8},{8,9},{9,10},{10,1... | collective-permute-start | bytes 294920 | tf_op jit(solution)/shard_map/ppermute | solution.py:112
  7.7 0.9 collective-permute-done.left_ref
  8.6 3.9 %collective-permute-start.2 = (f32[3,432,128]{2,1,0:T(8,128)S(1)}, f32[3,432,128]{2,1,0:T(8,128)S(1)}, u32[]{:S(2)}, u32[]{:S(2)}) collective-permute-start(f32[3,432,128]{2,1,0:T(8,128)S(1)} %maximum_dynamic-update-slice_fusion), channel_id=1, source_target_pairs={{0,16},{16,32},{32,48},{48,64},{64,80},{80,96},{96,112},{1,17},{17... | collective-permute-start | bytes 1990664 | tf_op jit(solution)/shard_map/ppermute | solution.py:112
  12.6 1.3 collective-permute-start.3
  13.9 1.1 copy.16
  15.0 0.7 ranks.1
  15.7 0.6 copy-done.2
  16.3 0.6 copy-done.3
  16.9 10.0 %collective-permute-done.2.above_ref = f32[3,432,128]{2,1,0:T(8,128)S(1)} collective-permute-done((f32[3,432,128]{2,1,0:T(8,128)S(1)}, f32[3,432,128]{2,1,0:T(8,128)S(1)}, u32[]{:S(2)}, u32[]{:S(2)}) %collective-permute-start.2) | collective-permute-done | bytes 663584 | tf_op jit(solution)/shard_map/ppermute | solution.py:112
  26.9 4.6 %collective-permute-done.3.below_ref = f32[3,432,128]{2,1,0:T(8,128)S(1)} collective-permute-done((f32[3,432,128]{2,1,0:T(8,128)S(1)}, f32[3,432,128]{2,1,0:T(8,128)S(1)}, u32[]{:S(2)}, u32[]{:S(2)}) %collective-permute-start.3) | collective-permute-done | bytes 663584 | tf_op jit(solution)/shard_map/ppermute | solution.py:112
  31.5 0.1 broadcast_in_dim.10.coef_0
  31.6 0.1 broadcast_in_dim.11.coef_1
  31.7 0.1 broadcast_in_dim.12.coef_2
  31.8 0.1 broadcast_in_dim.13.coef_3
  31.9 0.1 broadcast_in_dim.14.coef_4
  32.1 8.9 %transport.1 = (f32[384,1024]{1,0:T(8,128)}, bf16[384,1024]{1,0:T(8,128)(2,1)}) custom-call(f32[3072,128]{1,0:T(8,128)} %bitcast.10, f32[3,432,128]{2,1,0:T(8,128)S(1)} %collective-permute-done.2.above_ref, f32[3,432,128]{2,1,0:T(8,128)S(1)} %collective-permute-done.3.below_ref, f32[3,64,128]{2,1,0:T(8,128)S(1)} %collective-permute-done.left_ref, ...), custom_call_target="tpu_custom_call" | custom-call | flops 16777216 | bytes 6291456 | tf_op jit(solution)/shard_map/transport/pallas_call | solution.py:150
  41.0 31.6 %network.1 = (f32[3072,128]{1,0:T(8,128)}, f32[2048,256]{1,0:T(8,128)}, f32[2048,256]{1,0:T(8,128)}, f32[2048,256]{1,0:T(8,128)}, f32[2056,256]{1,0:T(8,128)}, /...) custom-call(s32[1]{0:T(128)} %get-tuple-element.28.scalar_ref, s32[384]{0:T(512)} %constant.119.clone.table_ref, ...), custom_call_target="tpu_custom_call" | custom-call | flops 16106127360 | bytes 20971520 | tf_op jit(solution)/shard_map/network/pallas_call | solution.py:458
  72.6 0.7 collective-permute-start.18
  73.3 0.1 collective-permute-start.11
  73.4 0.4 collective-permute-start.4
  73.8 3.6 %collective-permute-done.18 = f32[2048,256]{1,0:T(8,128)} collective-permute-done((f32[2048,256]{1,0:T(8,128)}, f32[2048,256]{1,0:T(8,128)}, u32[]{:S(2)}, u32[]{:S(2)}) %collective-permute-start.18) | collective-permute-done | bytes 2097184 | tf_op jit(solution)/shard_map/ppermute | solution.py:493
  77.4 2.7 %dynamic-slice_add_fusion = f32[1024,256]{1,0:T(8,128)} fusion(f32[2048,256]{1,0:T(8,128)} %collective-permute-done.18, s32[]{:T(128)S(6)} %select_n.231, f32[2048,256]{1,0:T(8,128)} %get-tuple-element.42), kind=kLoop, calls=%fused_computation.2 | loop fusion | flops 262144 | bytes 3145732 | tf_op jit(solution)/shard_map/add | solution.py:194
  80.0 1.9 %collective-permute-start.19 = (f32[1024,256]{1,0:T(8,128)}, f32[1024,256]{1,0:T(8,128)}, u32[]{:S(2)}, u32[]{:S(2)}) collective-permute-start(f32[1024,256]{1,0:T(8,128)} %dynamic-slice_add_fusion), channel_id=1, source_target_pairs={{0,16},{1,49},{16,0},{17,33},{32,48},{33,17},{48,32},{49,1},{2,18}... | collective-permute-start | bytes 3145736 | tf_op jit(solution)/shard_map/ppermute | solution.py:197
  81.9 1.5 collective-permute-done.11
  83.4 2.7 %dynamic-slice_add_fusion.1 = f32[1024,256]{1,0:T(8,128)} fusion(f32[2048,256]{1,0:T(8,128)} %collective-permute-done.11, s32[]{:T(128)S(6)} %select_n.219, f32[2048,256]{1,0:T(8,128)} %get-tuple-element.40), kind=kLoop, calls=%fused_computation.4 | loop fusion | flops 262144 | bytes 3145732 | tf_op jit(solution)/shard_map/add | solution.py:194
  86.1 3.7 %collective-permute-start.12 = (f32[1024,256]{1,0:T(8,128)}, f32[1024,256]{1,0:T(8,128)}, u32[]{:S(2)}, u32[]{:S(2)}) collective-permute-start(f32[1024,256]{1,0:T(8,128)} %dynamic-slice_add_fusion.1), channel_id=1, source_target_pairs={{0,2},{1,67},{2,0},{3,65},{64,66},{65,3},{66,64},{67,1},{4,6},{5,7... | collective-permute-start | bytes 3145736 | tf_op jit(solution)/shard_map/ppermute | solution.py:197
  89.8 0.1 dynamic-slice_add_fusion.2
  90.0 1.1 pad_maximum_fusion
  91.0 1.5 collective-permute-start.5
  92.5 2.6 %collective-permute-done.19 = f32[1024,256]{1,0:T(8,128)} collective-permute-done((f32[1024,256]{1,0:T(8,128)}, f32[1024,256]{1,0:T(8,128)}, u32[]{:S(2)}, u32[]{:S(2)}) %collective-permute-start.19) | collective-permute-done | bytes 1048608 | tf_op jit(solution)/shard_map/ppermute | solution.py:197
  95.2 2.1 %add_add_fusion = f32[1024,256]{1,0:T(8,128)S(1)} fusion(f32[1024,256]{1,0:T(8,128)} %collective-permute-done.19, f32[2048,256]{1,0:T(8,128)} %collective-permute-done.18, s32[]{:T(128)S(6)} %select_n.230, f32[2048,256]{1,0:T(8,128)} %get-tuple-element.42), kind=kLoop, calls=%fused_computation.3 | loop fusion | flops 524288 | bytes 4194308 | tf_op jit(solution)/shard_map/add | solution.py:199
  97.3 7.7 %collective-permute-start.20 = (f32[512,256]{1,0:T(8,128)S(1)}, f32[512,256]{1,0:T(8,128)S(1)}, u32[]{:S(2)}, u32[]{:S(2)}) collective-permute-start(f32[512,256]{1,0:T(8,128)S(1)} %constant_dynamic-slice_fusion.2), channel_id=1, source_target_pairs={{0,48},{1,17},{16,32},{17,1},{32,16},{33,49},{48,0},{49,33},{2,50}... | collective-permute-start | bytes 1572872 | tf_op jit(solution)/shard_map/ppermute | solution.py:197
  105.0 1.7 %add_add_fusion.1 = f32[1024,256]{1,0:T(8,128)S(1)} fusion(f32[1024,256]{1,0:T(8,128)} %collective-permute-done.12, f32[2048,256]{1,0:T(8,128)} %collective-permute-done.11, s32[]{:T(128)S(6)} %select_n.218, f32[2048,256]{1,0:T(8,128)S(1)} %copy-done.6), kind=kLoop, calls=%fused_computation.5 | loop fusion | flops 524288 | bytes 4194308 | tf_op jit(solution)/shard_map/add | solution.py:199
  106.8 2.5 %collective-permute-start.13 = (f32[512,256]{1,0:T(8,128)S(1)}, f32[512,256]{1,0:T(8,128)S(1)}, u32[]{:S(2)}, u32[]{:S(2)}) collective-permute-start(f32[512,256]{1,0:T(8,128)S(1)} %constant_dynamic-slice_fusion.8), channel_id=1, source_target_pairs={{0,66},{1,3},{2,64},{3,1},{64,2},{65,67},{66,0},{67,65},{4,70},{5,... | collective-permute-start | bytes 1572872 | tf_op jit(solution)/shard_map/ppermute | solution.py:197
  109.3 0.2 slice_add_fusion
  109.6 1.4 collective-permute-start.6
  111.0 1.1 collective-permute-done.20
  112.2 0.1 dynamic-slice_add_fusion.3
  112.3 2.5 %collective-permute-start.21 = (f32[256,256]{1,0:T(8,128)S(1)}, f32[256,256]{1,0:T(8,128)S(1)}, u32[]{:S(2)}, u32[]{:S(2)}) collective-permute-start(f32[256,256]{1,0:T(8,128)S(1)} %constant_dynamic-slice_fusion.1), channel_id=1, source_target_pairs={{0,4},{1,13},{4,0},{5,9},{8,12},{9,5},{12,8},{13,1},{2,6},{3,15},{... | collective-permute-start | bytes 786440 | tf_op jit(solution)/shard_map/ppermute | solution.py:197
  114.8 2.5 %collective-permute-done.13 = f32[512,256]{1,0:T(8,128)S(1)} collective-permute-done((f32[512,256]{1,0:T(8,128)S(1)}, f32[512,256]{1,0:T(8,128)S(1)}, u32[]{:S(2)}, u32[]{:S(2)}) %collective-permute-start.13) | collective-permute-done | bytes 524320 | tf_op jit(solution)/shard_map/ppermute | solution.py:197
  117.3 0.1 dynamic-slice_add_fusion.4
  117.4 0.3 collective-permute-start.14
  117.7 5.3 %collective-permute-done.6 = f32[520,256]{1,0:T(8,128)S(1)} collective-permute-done((f32[520,256]{1,0:T(8,128)S(1)}, f32[520,256]{1,0:T(8,128)S(1)}, u32[]{:S(2)}, u32[]{:S(2)}) %collective-permute-start.6) | collective-permute-done | bytes 532512 | tf_op jit(solution)/shard_map/ppermute | solution.py:197
  123.0 0.1 slice_add_fusion.1
  123.1 0.3 collective-permute-start.7
  123.4 1.9 %collective-permute-start.22 = (f32[128,256]{1,0:T(8,128)S(1)}, f32[128,256]{1,0:T(8,128)S(1)}, u32[]{:S(2)}, u32[]{:S(2)}) collective-permute-start(f32[128,256]{1,0:T(8,128)S(1)} %constant_dynamic-slice_fusion), channel_id=1, source_target_pairs={{0,12},{1,5},{4,8},{5,1},{8,4},{9,13},{12,0},{13,9},{2,14},{3,7},{... | collective-permute-start | bytes 393224 | tf_op jit(solution)/shard_map/ppermute | solution.py:197
  125.4 4.6 %collective-permute-start.15 = (f32[128,256]{1,0:T(8,128)S(1)}, f32[128,256]{1,0:T(8,128)S(1)}, u32[]{:S(2)}, u32[]{:S(2)}) collective-permute-start(f32[128,256]{1,0:T(8,128)S(1)} %constant_dynamic-slice_fusion.6), channel_id=1, source_target_pairs={{0,48},{1,17},{16,32},{17,1},{32,16},{33,49},{48,0},{49,33},{2,50}... | collective-permute-start | bytes 393224 | tf_op jit(solution)/shard_map/ppermute | solution.py:197
  130.0 0.2 collective-permute-done.7
  130.3 1.1 collective-permute-start.8
  131.5 0.6 collective-permute-start.23
  132.1 0.9 collective-permute-done.15
  133.0 0.5 collective-permute-start.16
  133.6 3.1 %collective-permute-done.8 = f32[136,256]{1,0:T(8,128)S(1)} collective-permute-done((f32[136,256]{1,0:T(8,128)S(1)}, f32[136,256]{1,0:T(8,128)S(1)}, u32[]{:S(2)}, u32[]{:S(2)}) %collective-permute-start.8) | collective-permute-done | bytes 139296 | tf_op jit(solution)/shard_map/ppermute | solution.py:197
  136.7 0.8 collective-permute-start.9
  137.6 0.6 collective-permute-start.24
  138.2 2.4 %collective-permute-start.17 = (f32[32,256]{1,0:T(8,128)S(1)}, f32[32,256]{1,0:T(8,128)S(1)}, u32[]{:S(2)}, u32[]{:S(2)}) collective-permute-start(f32[32,256]{1,0:T(8,128)S(1)} %constant_dynamic-slice_fusion.4), channel_id=1, source_target_pairs={{0,12},{1,5},{4,8},{5,1},{8,4},{9,13},{12,0},{13,9},{2,14},{3,7},{... | collective-permute-start | bytes 98312 | tf_op jit(solution)/shard_map/ppermute | solution.py:197
  140.6 2.2 %collective-permute-done.24 = f32[32,256]{1,0:T(8,128)S(1)} collective-permute-done((f32[32,256]{1,0:T(8,128)S(1)}, f32[32,256]{1,0:T(8,128)S(1)}, u32[]{:S(2)}, u32[]{:S(2)}) %collective-permute-start.24) | collective-permute-done | bytes 32800 | tf_op jit(solution)/shard_map/ppermute | solution.py:197
  142.8 0.6 collective-permute-done.17
  143.5 3.8 %collective-permute-start.10 = (f32[40,256]{1,0:T(8,128)S(1)}, f32[40,256]{1,0:T(8,128)S(1)}, u32[]{:S(2)}, u32[]{:S(2)}) collective-permute-start(f32[40,256]{1,0:T(8,128)S(1)} %pad_maximum_fusion.7), channel_id=1, source_target_pairs={{0,48},{1,17},{16,32},{17,1},{32,16},{33,49},{48,0},{49,33},{2,50}... | collective-permute-start | bytes 122888 | tf_op jit(solution)/shard_map/ppermute | solution.py:197
  147.3 2.0 %collective-permute-done.10 = f32[40,256]{1,0:T(8,128)S(1)} collective-permute-done((f32[40,256]{1,0:T(8,128)S(1)}, f32[40,256]{1,0:T(8,128)S(1)}, u32[]{:S(2)}, u32[]{:S(2)}) %collective-permute-start.10) | collective-permute-done | bytes 40992 | tf_op jit(solution)/shard_map/ppermute | solution.py:197
  149.3 0.5 fusion
  149.8 0.6 pad_maximum_fusion.5
  (79 shorter events, 0.8 us)
Async XLA Ops:
  0.6 13.2 %copy-start.9 = (f32[384]{0:T(512)S(1)}, f32[384]{0:T(512)}, u32[]{:S(2)}) copy-start(f32[384]{0:T(512)} %param.14) | copy-start | bytes 4612
  0.6 13.2 %copy-start.10 = (f32[384]{0:T(512)S(1)}, f32[384]{0:T(512)}, u32[]{:S(2)}) copy-start(f32[384]{0:T(512)} %param.16) | copy-start | bytes 4612
  0.7 13.2 %copy-start.11 = (f32[384]{0:T(512)S(1)}, f32[384]{0:T(512)}, u32[]{:S(2)}) copy-start(f32[384]{0:T(512)} %param.15) | copy-start | bytes 4612
  0.7 13.2 %copy-start.7 = (bf16[384,8,128]{2,1,0:T(8,128)(2,1)S(1)}, bf16[384,8,128]{2,1,0:T(8,128)(2,1)}, u32[]{:S(2)}) copy-start(bf16[384,8,128]{2,1,0:T(8,128)(2,1)} %param.11) | copy-start | bytes 2359300
  0.7 14.3 %copy-start = (s32[8,128]{1,0:T(8,128)S(1)}, s32[8,128]{1,0:T(8,128)}, u32[]{:S(2)}) copy-start(s32[8,128]{1,0:T(8,128)} %mask_ref) | copy-start | bytes 12292
  0.7 14.3 %copy-start.1 = (s32[8,128]{1,0:T(8,128)S(1)}, s32[8,128]{1,0:T(8,128)}, u32[]{:S(2)}) copy-start(s32[8,128]{1,0:T(8,128)} %batch_ref) | copy-start | bytes 12292
  3.3 4.3 %collective-permute-start.1 = (f32[3,64,128]{2,1,0:T(8,128)S(1)}, f32[3,64,128]{2,1,0:T(8,128)S(1)}, u32[]{:S(2)}, u32[]{:S(2)}) collective-permute-start(f32[3,64,128]{2,1,0:T(8,128)S(1)} %get-tuple-element.25), channel_id=1, source_target_pairs={{1,0},{2,1},{3,2},{4,3},{5,4},{6,5},{7,6},{8,7},{9,8},{10,9},{11,1... | collective-permute-start | bytes 294920 | tf_op jit(solution)/shard_map/ppermute | solution.py:112
  4.6 4.0 %collective-permute-start = (f32[3,64,128]{2,1,0:T(8,128)S(1)}, f32[3,64,128]{2,1,0:T(8,128)S(1)}, u32[]{:S(2)}, u32[]{:S(2)}) collective-permute-start(f32[3,64,128]{2,1,0:T(8,128)S(1)} %get-tuple-element.24), channel_id=1, source_target_pairs={{0,1},{1,2},{2,3},{3,4},{4,5},{5,6},{6,7},{7,8},{8,9},{9,10},{10,1... | collective-permute-start | bytes 294920 | tf_op jit(solution)/shard_map/ppermute | solution.py:112
  8.6 18.3 %collective-permute-start.2 = (f32[3,432,128]{2,1,0:T(8,128)S(1)}, f32[3,432,128]{2,1,0:T(8,128)S(1)}, u32[]{:S(2)}, u32[]{:S(2)}) collective-permute-start(f32[3,432,128]{2,1,0:T(8,128)S(1)} %maximum_dynamic-update-slice_fusion), channel_id=1, source_target_pairs={{0,16},{16,32},{32,48},{48,64},{64,80},{80,96},{96,112},{1,17},{17... | collective-permute-start | bytes 1990664 | tf_op jit(solution)/shard_map/ppermute | solution.py:112
  12.6 18.9 %collective-permute-start.3 = (f32[3,432,128]{2,1,0:T(8,128)S(1)}, f32[3,432,128]{2,1,0:T(8,128)S(1)}, u32[]{:S(2)}, u32[]{:S(2)}) collective-permute-start(f32[3,432,128]{2,1,0:T(8,128)S(1)} %maximum_dynamic-update-slice_fusion.1), channel_id=1, source_target_pairs={{16,0},{32,16},{48,32},{64,48},{80,64},{96,80},{112,96},{17,1},{33... | collective-permute-start | bytes 1990664 | tf_op jit(solution)/shard_map/ppermute | solution.py:112
  15.7 0.6 copy-start.2
  16.3 0.6 copy-start.3
  72.6 4.8 %collective-permute-start.18 = (f32[2048,256]{1,0:T(8,128)}, f32[2048,256]{1,0:T(8,128)}, u32[]{:S(2)}, u32[]{:S(2)}) collective-permute-start(f32[2048,256]{1,0:T(8,128)} %get-tuple-element.43), channel_id=1, source_target_pairs={{0,1},{1,0},{2,3},{3,2},{4,5},{5,4},{6,7},{7,6},{8,9},{9,8},{10,11... | collective-permute-start | bytes 6291464 | tf_op jit(solution)/shard_map/ppermute | solution.py:493
  73.3 10.1 %collective-permute-start.11 = (f32[2048,256]{1,0:T(8,128)}, f32[2048,256]{1,0:T(8,128)}, u32[]{:S(2)}, u32[]{:S(2)}) collective-permute-start(f32[2048,256]{1,0:T(8,128)} %get-tuple-element.41), channel_id=1, source_target_pairs={{0,1},{1,0},{2,3},{3,2},{4,5},{5,4},{6,7},{7,6},{8,9},{9,8},{10,11... | collective-permute-start | bytes 6291464 | tf_op jit(solution)/shard_map/ppermute | solution.py:493
  73.4 16.4 %collective-permute-start.4 = (f32[2056,256]{1,0:T(8,128)}, f32[2056,256]{1,0:T(8,128)S(1)}, u32[]{:S(2)}, u32[]{:S(2)}) collective-permute-start(f32[2056,256]{1,0:T(8,128)} %get-tuple-element.38), channel_id=1, source_target_pairs={{0,1},{1,0},{2,3},{3,2},{4,5},{5,4},{6,7},{7,6},{8,9},{9,8},{10,11... | collective-permute-start | bytes 6316040 | tf_op jit(solution)/shard_map/ppermute | solution.py:493
  80.0 9.8 %copy-start.8 = (f32[8,256]{1,0:T(8,128)S(1)}, f32[8,256]{1,0:T(8,128)}, u32[]{:S(2)}) copy-start(f32[8,256]{1,0:T(8,128)} %get-tuple-element.39) | copy-start | bytes 24580
  80.0 15.1 %collective-permute-start.19 = (f32[1024,256]{1,0:T(8,128)}, f32[1024,256]{1,0:T(8,128)}, u32[]{:S(2)}, u32[]{:S(2)}) collective-permute-start(f32[1024,256]{1,0:T(8,128)} %dynamic-slice_add_fusion), channel_id=1, source_target_pairs={{0,16},{1,49},{16,0},{17,33},{32,48},{33,17},{48,32},{49,1},{2,18}... | collective-permute-start | bytes 3145736 | tf_op jit(solution)/shard_map/ppermute | solution.py:197
  81.9 7.9 %copy-start.4 = (f32[2048,256]{1,0:T(8,128)S(1)}, f32[2048,256]{1,0:T(8,128)}, u32[]{:S(2)}) copy-start(f32[2048,256]{1,0:T(8,128)} %get-tuple-element.37) | copy-start | bytes 6291460
  86.1 18.9 %collective-permute-start.12 = (f32[1024,256]{1,0:T(8,128)}, f32[1024,256]{1,0:T(8,128)}, u32[]{:S(2)}, u32[]{:S(2)}) collective-permute-start(f32[1024,256]{1,0:T(8,128)} %dynamic-slice_add_fusion.1), channel_id=1, source_target_pairs={{0,2},{1,67},{2,0},{3,65},{64,66},{65,3},{66,64},{67,1},{4,6},{5,7... | collective-permute-start | bytes 3145736 | tf_op jit(solution)/shard_map/ppermute | solution.py:197
  91.0 18.2 %collective-permute-start.5 = (f32[1032,256]{1,0:T(8,128)}, f32[1032,256]{1,0:T(8,128)S(1)}, u32[]{:S(2)}, u32[]{:S(2)}) collective-permute-start(f32[1032,256]{1,0:T(8,128)} %pad_maximum_fusion), channel_id=1, source_target_pairs={{0,4},{1,13},{4,0},{5,9},{8,12},{9,5},{12,8},{13,1},{2,6},{3,15},{... | collective-permute-start | bytes 3170312 | tf_op jit(solution)/shard_map/ppermute | solution.py:197
  92.5 12.5 %copy-start.6 = (f32[2048,256]{1,0:T(8,128)S(1)}, f32[2048,256]{1,0:T(8,128)}, u32[]{:S(2)}) copy-start(f32[2048,256]{1,0:T(8,128)} %get-tuple-element.40) | copy-start | bytes 6291460
  97.3 12.0 %copy-start.5 = (f32[2048,256]{1,0:T(8,128)S(1)}, f32[2048,256]{1,0:T(8,128)}, u32[]{:S(2)}) copy-start(f32[2048,256]{1,0:T(8,128)} %get-tuple-element.37) | copy-start | bytes 6291460
  97.3 14.9 %collective-permute-start.20 = (f32[512,256]{1,0:T(8,128)S(1)}, f32[512,256]{1,0:T(8,128)S(1)}, u32[]{:S(2)}, u32[]{:S(2)}) collective-permute-start(f32[512,256]{1,0:T(8,128)S(1)} %constant_dynamic-slice_fusion.2), channel_id=1, source_target_pairs={{0,48},{1,17},{16,32},{17,1},{32,16},{33,49},{48,0},{49,33},{2,50}... | collective-permute-start | bytes 1572872 | tf_op jit(solution)/shard_map/ppermute | solution.py:197
  106.8 10.5 %collective-permute-start.13 = (f32[512,256]{1,0:T(8,128)S(1)}, f32[512,256]{1,0:T(8,128)S(1)}, u32[]{:S(2)}, u32[]{:S(2)}) collective-permute-start(f32[512,256]{1,0:T(8,128)S(1)} %constant_dynamic-slice_fusion.8), channel_id=1, source_target_pairs={{0,66},{1,3},{2,64},{3,1},{64,2},{65,67},{66,0},{67,65},{4,70},{5,... | collective-permute-start | bytes 1572872 | tf_op jit(solution)/shard_map/ppermute | solution.py:197
  109.6 13.4 %collective-permute-start.6 = (f32[520,256]{1,0:T(8,128)S(1)}, f32[520,256]{1,0:T(8,128)S(1)}, u32[]{:S(2)}, u32[]{:S(2)}) collective-permute-start(f32[520,256]{1,0:T(8,128)S(1)} %pad_maximum_fusion.1), channel_id=1, source_target_pairs={{0,12},{1,5},{4,8},{5,1},{8,4},{9,13},{12,0},{13,9},{2,14},{3,7},{... | collective-permute-start | bytes 1597448 | tf_op jit(solution)/shard_map/ppermute | solution.py:197
  112.3 11.1 %collective-permute-start.21 = (f32[256,256]{1,0:T(8,128)S(1)}, f32[256,256]{1,0:T(8,128)S(1)}, u32[]{:S(2)}, u32[]{:S(2)}) collective-permute-start(f32[256,256]{1,0:T(8,128)S(1)} %constant_dynamic-slice_fusion.1), channel_id=1, source_target_pairs={{0,4},{1,13},{4,0},{5,9},{8,12},{9,5},{12,8},{13,1},{2,6},{3,15},{... | collective-permute-start | bytes 786440 | tf_op jit(solution)/shard_map/ppermute | solution.py:197
  117.4 8.0 %collective-permute-start.14 = (f32[256,256]{1,0:T(8,128)S(1)}, f32[256,256]{1,0:T(8,128)S(1)}, u32[]{:S(2)}, u32[]{:S(2)}) collective-permute-start(f32[256,256]{1,0:T(8,128)S(1)} %constant_dynamic-slice_fusion.7), channel_id=1, source_target_pairs={{0,16},{1,49},{16,0},{17,33},{32,48},{33,17},{48,32},{49,1},{2,18}... | collective-permute-start | bytes 786440 | tf_op jit(solution)/shard_map/ppermute | solution.py:197
  123.1 7.1 %collective-permute-start.7 = (f32[264,256]{1,0:T(8,128)S(1)}, f32[264,256]{1,0:T(8,128)S(1)}, u32[]{:S(2)}, u32[]{:S(2)}) collective-permute-start(f32[264,256]{1,0:T(8,128)S(1)} %pad_maximum_fusion.2), channel_id=1, source_target_pairs={{0,2},{1,67},{2,0},{3,65},{64,66},{65,3},{66,64},{67,1},{4,6},{5,7... | collective-permute-start | bytes 811016 | tf_op jit(solution)/shard_map/ppermute | solution.py:197
  123.4 8.0 %collective-permute-start.22 = (f32[128,256]{1,0:T(8,128)S(1)}, f32[128,256]{1,0:T(8,128)S(1)}, u32[]{:S(2)}, u32[]{:S(2)}) collective-permute-start(f32[128,256]{1,0:T(8,128)S(1)} %constant_dynamic-slice_fusion), channel_id=1, source_target_pairs={{0,12},{1,5},{4,8},{5,1},{8,4},{9,13},{12,0},{13,9},{2,14},{3,7},{... | collective-permute-start | bytes 393224 | tf_op jit(solution)/shard_map/ppermute | solution.py:197
  125.4 7.6 %collective-permute-start.15 = (f32[128,256]{1,0:T(8,128)S(1)}, f32[128,256]{1,0:T(8,128)S(1)}, u32[]{:S(2)}, u32[]{:S(2)}) collective-permute-start(f32[128,256]{1,0:T(8,128)S(1)} %constant_dynamic-slice_fusion.6), channel_id=1, source_target_pairs={{0,48},{1,17},{16,32},{17,1},{32,16},{33,49},{48,0},{49,33},{2,50}... | collective-permute-start | bytes 393224 | tf_op jit(solution)/shard_map/ppermute | solution.py:197
  130.3 6.3 %collective-permute-start.8 = (f32[136,256]{1,0:T(8,128)S(1)}, f32[136,256]{1,0:T(8,128)S(1)}, u32[]{:S(2)}, u32[]{:S(2)}) collective-permute-start(f32[136,256]{1,0:T(8,128)S(1)} %pad_maximum_fusion.3), channel_id=1, source_target_pairs={{0,66},{1,3},{2,64},{3,1},{64,2},{65,67},{66,0},{67,65},{4,70},{5,... | collective-permute-start | bytes 417800 | tf_op jit(solution)/shard_map/ppermute | solution.py:197
  131.5 6.0 %collective-permute-start.23 = (f32[64,256]{1,0:T(8,128)S(1)}, f32[64,256]{1,0:T(8,128)S(1)}, u32[]{:S(2)}, u32[]{:S(2)}) collective-permute-start(f32[64,256]{1,0:T(8,128)S(1)} %constant_dynamic-slice_fusion.14), channel_id=1, source_target_pairs={{0,2},{1,67},{2,0},{3,65},{64,66},{65,3},{66,64},{67,1},{4,6},{5,7... | collective-permute-start | bytes 196616 | tf_op jit(solution)/shard_map/ppermute | solution.py:197
  133.0 5.1 %collective-permute-start.16 = (f32[64,256]{1,0:T(8,128)S(1)}, f32[64,256]{1,0:T(8,128)S(1)}, u32[]{:S(2)}, u32[]{:S(2)}) collective-permute-start(f32[64,256]{1,0:T(8,128)S(1)} %constant_dynamic-slice_fusion.5), channel_id=1, source_target_pairs={{0,4},{1,13},{4,0},{5,9},{8,12},{9,5},{12,8},{13,1},{2,6},{3,15},{... | collective-permute-start | bytes 196616 | tf_op jit(solution)/shard_map/ppermute | solution.py:197
  136.7 6.7 %collective-permute-start.9 = (f32[72,256]{1,0:T(8,128)S(1)}, f32[72,256]{1,0:T(8,128)S(1)}, u32[]{:S(2)}, u32[]{:S(2)}) collective-permute-start(f32[72,256]{1,0:T(8,128)S(1)} %pad_maximum_fusion.4), channel_id=1, source_target_pairs={{0,16},{1,49},{16,0},{17,33},{32,48},{33,17},{48,32},{49,1},{2,18}... | collective-permute-start | bytes 221192 | tf_op jit(solution)/shard_map/ppermute | solution.py:197
  137.6 5.2 %collective-permute-start.24 = (f32[32,256]{1,0:T(8,128)S(1)}, f32[32,256]{1,0:T(8,128)S(1)}, u32[]{:S(2)}, u32[]{:S(2)}) collective-permute-start(f32[32,256]{1,0:T(8,128)S(1)} %constant_dynamic-slice_fusion.3), channel_id=1, source_target_pairs={{0,66},{1,3},{2,64},{3,1},{64,2},{65,67},{66,0},{67,65},{4,70},{5,... | collective-permute-start | bytes 98312 | tf_op jit(solution)/shard_map/ppermute | solution.py:197
  138.2 5.2 %collective-permute-start.17 = (f32[32,256]{1,0:T(8,128)S(1)}, f32[32,256]{1,0:T(8,128)S(1)}, u32[]{:S(2)}, u32[]{:S(2)}) collective-permute-start(f32[32,256]{1,0:T(8,128)S(1)} %constant_dynamic-slice_fusion.4), channel_id=1, source_target_pairs={{0,12},{1,5},{4,8},{5,1},{8,4},{9,13},{12,0},{13,9},{2,14},{3,7},{... | collective-permute-start | bytes 98312 | tf_op jit(solution)/shard_map/ppermute | solution.py:197
  143.5 5.8 %collective-permute-start.10 = (f32[40,256]{1,0:T(8,128)S(1)}, f32[40,256]{1,0:T(8,128)S(1)}, u32[]{:S(2)}, u32[]{:S(2)}) collective-permute-start(f32[40,256]{1,0:T(8,128)S(1)} %pad_maximum_fusion.7), channel_id=1, source_target_pairs={{0,48},{1,17},{16,32},{17,1},{32,16},{33,49},{48,0},{49,33},{2,50}... | collective-permute-start | bytes 122888 | tf_op jit(solution)/shard_map/ppermute | solution.py:197
